TPU v7x, 32 devices: a whole 2x2x4 slice. The times are simulated.
32 devices in a mesh: grp: 4 (over y, x), dev: 8 (over z, core).
Axes of the slice: x: 2, y: 2, z: 4, core: 2. Of those that a mesh axis runs over, the one named last changes fastest.
Arguments:
- points: float32 [64, 49152], P(None, 'dev'), may hold values from -6 to 6
- weights: float32 [49152, 128], P('dev'), may hold values from -4 to 4
- proj: float32 [256, 49152], P(None, 'dev'), may hold values from -0.078125 to 0.078125
- fetch_table: int32 [3, 8, 8, 2], P(None, 'dev'), may hold values from 0 to 11, as said below
- near_list: int32 [96, 16], P('dev'), may hold values from 0 to 15, as said below
- far_list: int32 [96, 8], P('dev'), may hold values from 0 to 7, as said below
- skel_idx: int32 [8, 256], P('dev'), may hold values from 0 to 6143, as said below
Outputs:
- potential: float32 [49152, 128], P('dev')
Inputs may be any that keep to these rules, and one draw needn't show every extreme that they name: Entries of fetch_table[r, d, e] are distinct local leaf numbers of column e. `near_list`: the 16 slots of one target leaf are distinct. `far_list`: the 8 nodes of one target leaf are distinct, and one of them is node (c + 1) mod 8 for the leaf's column c. `skel_idx`: the 256 skeleton points of one node are distinct.
All inputs are finite; a program needn't handle non-finite values.
Results may differ from a plain program's by a relative error of at most 0.0003.
Values sent between devices are 32-bit elements; how exact they have to be, the bound alone decides.
No kernel may reach another device: no remote copies, remote signals or barrier semaphores. Data moves between devices by JAX's collectives and lax.ppermute only.
A program may use at most 192 MiB of HBM per device.

v0:
```python
import functools
import math

import jax
import jax.numpy as jnp
from jax import lax
from jax.experimental import pallas as pl
from jax.experimental.pallas import tpu as pltpu
from jax.sharding import PartitionSpec as P

F32 = jnp.float32
BF16 = jnp.bfloat16


def two_terms(v):
    high = v.astype(BF16)
    return high.astype(F32), v - high.astype(F32)


def three_terms(v):
    high, rest = two_terms(v)
    middle, low = two_terms(rest)
    return high, middle, low


def stacked(coords, gain, scale, is_target):
    features, count = coords.shape
    norm = jnp.sum(coords * coords, axis=0, keepdims=True) * (-scale)
    high, low = two_terms(coords * gain if gain is not None else coords)
    norms = jnp.concatenate(three_terms(norm), axis=0)
    ones = jnp.ones_like(norms)
    rest = jnp.zeros((features - 6, count), F32)
    if is_target:
        rows = (high, low, high, norms, ones, rest)
    else:
        rows = (high, high, low, ones, norms, rest)
    return jnp.concatenate(rows, axis=0)


def pair_kernel(plan, *refs):
    refs = list(refs)
    place_ref = refs.pop(0)
    list_refs = [refs.pop(0) for _ in range(plan["parcels"])]
    x_refs = [refs.pop(0) for _ in range(plan["parcels"])]
    init_ref = refs.pop(0) if plan["init"] else None
    sides, (out_ref, y_buf, w_buf, xk_buf, sem) = (refs[:4], refs[4:8]), refs[8:]
    leaf = x_refs[0].shape[1]
    capacity = plan["capacity"]
    devices = plan["devices"]
    scale = plan["scale"]
    number = place_ref[0] * plan["per"] + plan["first"] + pl.program_id(0)
    row = number // plan["row_leaves"]

    def listed(n):
        value = sum(ref[n // 128, n % 128] for ref in list_refs)
        return value.astype(jnp.int32)

    skel_slot = 2 * capacity
    kept = leaf // 2
    copies = []
    for side, (pts, wts, _, _) in enumerate(sides):
        owner = place_ref[1 + side]
        for c in range(capacity):
            slot = side * capacity + c
            start = pl.multiple_of(listed((row * devices + owner) * capacity + c) * leaf, leaf)
            copies.append(pltpu.make_async_copy(
                pts.at[:, pl.ds(start, leaf)], y_buf.at[slot], sem.at[slot, 0]
            ))
            copies.append(pltpu.make_async_copy(
                wts.at[pl.ds(start, leaf), :], w_buf.at[slot], sem.at[slot, 1]
            ))
    for side, (_, _, pts, wts) in enumerate(sides):
        part = pl.ds(side * kept, kept)
        copies.append(pltpu.make_async_copy(
            pts, y_buf.at[skel_slot, :, part], sem.at[skel_slot, side]
        ))
        copies.append(pltpu.make_async_copy(
            wts, w_buf.at[skel_slot, part, :], sem.at[skel_slot, 2 + side]
        ))
    for copy in copies:
        copy.start()
    x = x_refs[0][...]
    for ref in x_refs[1:]:
        x = x + ref[...]
    xk_buf[...] = jnp.swapaxes(stacked(x, 2.0 * scale, scale, True), 0, 1).astype(BF16)
    if init_ref is None:
        out_ref[...] = jnp.zeros_like(out_ref)
    else:
        out_ref[...] = init_ref[...]

    def add(slot):
        y = y_buf[slot]
        w = w_buf[slot]
        yk = stacked(y, None, scale, False).astype(BF16)
        w_high, w_low = two_terms(w)
        wk = jnp.concatenate([w_high, w_low], axis=1).astype(BF16)
        wk = jnp.concatenate([wk, wk], axis=0)
        columns = w.shape[1]
        for t in range(0, leaf, plan["rows"]):
            part = slice(t, t + plan["rows"])
            exponent = jnp.dot(xk_buf[part, :], yk, preferred_element_type=F32)
            value = jnp.exp2(exponent)
            high = value.astype(BF16)
            low = (value - high.astype(F32)).astype(BF16)
            both = jnp.dot(
                jnp.concatenate([high, low], axis=1), wk, preferred_element_type=F32
            )
            out_ref[part, :] += both[:, :columns] + both[:, columns:]

    flags = None
    if not plan["dense"]:
        base = (plan["rows_listed"]) * devices * capacity
        near = [listed(base + number * plan["near"] + n) for n in range(plan["near"])]
        base += plan["targets"] * plan["near"]
        far = [listed(base + number * plan["far"] + n) for n in range(plan["far"])]

        def among(value, options):
            return sum((option == value).astype(jnp.int32) for option in options)

        flags = []
        for side in range(2):
            owner = place_ref[1 + side]
            flags += [among(owner * capacity + c, near) for c in range(capacity)]
        flags += [among(place_ref[1 + side], far) for side in range(2)]

    for copy in copies[-4:]:
        copy.wait()
    if flags is not None:
        for side in range(2):
            part = slice(side * kept, (side + 1) * kept)
            w_buf[skel_slot, part, :] = w_buf[skel_slot, part, :] * flags[
                2 * capacity + side
            ].astype(F32)

    def near_step(slot, carry):
        pts, wts = sides[0][0], sides[0][1]

        @pl.when(slot < skel_slot)
        def _():
            pltpu.make_async_copy(
                pts.at[:, pl.ds(0, leaf)], y_buf.at[slot], sem.at[slot, 0]
            ).wait()
            pltpu.make_async_copy(
                wts.at[pl.ds(0, leaf), :], w_buf.at[slot], sem.at[slot, 1]
            ).wait()

        add(slot)
        return carry

    if flags is None:
        lax.fori_loop(0, skel_slot + 1, near_step, 0)
    else:
        for n in range(skel_slot):
            copies[2 * n].wait()
            copies[2 * n + 1].wait()
            w_buf[n] = w_buf[n] * flags[n].astype(F32)
        lax.fori_loop(0, skel_slot + 1, lambda slot, carry: (add(slot), carry)[1], 0)


def pairs(sizes, place, parcels, init, sources, first, count):
    own = sources[0]
    features = own[0].shape[0]
    columns = own[1].shape[1]
    leaf = sizes["leaf"]
    slots = 2 * sizes["capacity"] + 1
    plan = dict(sizes, parcels=len(parcels), init=init is not None, first=first, rows=leaf // 2)
    in_specs = [pl.BlockSpec(memory_space=pltpu.SMEM)]
    in_specs += [
        pl.BlockSpec((8, 128), lambda i: (features // 8, 0), memory_space=pltpu.SMEM)
    ] * len(parcels)
    in_specs += [pl.BlockSpec((features, leaf), lambda i: (0, first + i))] * len(parcels)
    operands = [place, *parcels, *parcels]
    if init is not None:
        in_specs.append(pl.BlockSpec((leaf, columns), lambda i: (i, 0)))
        operands.append(init)
    in_specs += [pl.BlockSpec(memory_space=pl.ANY)] * 8
    operands += [array for side in sources for array in side]
    work = count * leaf * leaf * slots
    return pl.pallas_call(
        functools.partial(pair_kernel, plan),
        grid=(count,),
        in_specs=in_specs,
        out_specs=pl.BlockSpec((leaf, columns), lambda i: (i, 0)),
        out_shape=jax.ShapeDtypeStruct((count * leaf, columns), F32),
        scratch_shapes=[
            pltpu.VMEM((slots, features, leaf), F32),
            pltpu.VMEM((slots, leaf, columns), F32),
            pltpu.VMEM((leaf, 4 * features), BF16),
            pltpu.SemaphoreType.DMA((slots, 4)),
        ],
        compiler_params=pltpu.CompilerParams(vmem_limit_bytes=32 << 20),
        cost_estimate=pl.CostEstimate(
            flops=work * 2 * (4 * features + 4 * columns),
            bytes_accessed=count * slots * leaf * (features + columns) * 4,
            transcendentals=work,
        ),
        name="pairs",
    )(*operands)


def skeleton_kernel(idx_ref, points_ref, weights_ref, proj_ref, coords_ref, summed_ref):
    step = pl.program_id(0)
    count = points_ref.shape[1]

    @pl.when(step == 0)
    def _():
        coords_ref[...] = jnp.zeros_like(coords_ref)
        summed_ref[...] = jnp.zeros_like(summed_ref)

    place = lax.broadcasted_iota(jnp.int32, (count, idx_ref.shape[1]), 0) + step * count
    chosen = jnp.where(place == idx_ref[...], 1.0, 0.0).astype(BF16)
    features = points_ref.shape[0]
    terms = jnp.concatenate(three_terms(points_ref[...]), axis=0).astype(BF16)
    picked = jnp.dot(terms, chosen, preferred_element_type=F32)
    coords_ref[...] += (
        picked[:features] + picked[features : 2 * features] + picked[2 * features :]
    )
    w_high, w_low = two_terms(weights_ref[...])
    p_high, p_low = two_terms(proj_ref[...])
    columns = w_high.shape[1]
    both = jnp.dot(
        jnp.concatenate([p_high, p_low], axis=1).astype(BF16),
        jnp.concatenate([jnp.concatenate([w_high, w_low], axis=1)] * 2, axis=0).astype(BF16),
        preferred_element_type=F32,
    )
    summed_ref[...] += both[:, :columns] + both[:, columns:]


def skeleton(points, weights, proj, skel_idx, block):
    features, count = points.shape
    columns = weights.shape[1]
    kept = proj.shape[0]
    return pl.pallas_call(
        skeleton_kernel,
        grid=(count // block,),
        in_specs=[
            pl.BlockSpec((1, kept), lambda i: (0, 0)),
            pl.BlockSpec((features, block), lambda i: (0, i)),
            pl.BlockSpec((block, columns), lambda i: (i, 0)),
            pl.BlockSpec((kept, block), lambda i: (0, i)),
        ],
        out_specs=[
            pl.BlockSpec((features, kept), lambda i: (0, 0)),
            pl.BlockSpec((kept, columns), lambda i: (0, 0)),
        ],
        out_shape=[
            jax.ShapeDtypeStruct((features, kept), F32),
            jax.ShapeDtypeStruct((kept, columns), F32),
        ],
        cost_estimate=pl.CostEstimate(
            flops=2 * kept * count * columns * 4,
            bytes_accessed=4 * count * (features + columns + kept),
            transcendentals=0,
        ),
        name="skeleton",
    )(skel_idx, points, weights, proj)


def gather_kernel(groups, per, leaf, *refs):
    place_ref = refs[0]
    pieces = refs[1 : 1 + groups * per]
    out_ref = refs[1 + groups * per]
    buf, in_sem, out_sem = refs[2 + groups * per :]
    ins, outs = [], []
    for n, piece in enumerate(pieces):
        ins.append(pltpu.make_async_copy(piece, buf.at[n], in_sem.at[n]))
        m, i = divmod(n, per)
        start = pl.multiple_of((place_ref[m] * per + i) * leaf, leaf)
        outs.append(
            pltpu.make_async_copy(buf.at[n], out_ref.at[pl.ds(start, leaf), :], out_sem.at[n])
        )
    for c in ins:
        c.start()
    for c, d in zip(ins, outs):
        c.wait()
        d.start()
    for d in outs:
        d.wait()


def gathered(place, pieces, groups, per, leaf, columns):
    return pl.pallas_call(
        functools.partial(gather_kernel, groups, per, leaf),
        in_specs=[pl.BlockSpec(memory_space=pltpu.SMEM)]
        + [pl.BlockSpec(memory_space=pl.ANY)] * (groups * per),
        out_specs=pl.BlockSpec(memory_space=pl.ANY),
        out_shape=jax.ShapeDtypeStruct((groups * per * leaf, columns), F32),
        scratch_shapes=[
            pltpu.VMEM((groups * per, leaf, columns), F32),
            pltpu.SemaphoreType.DMA((groups * per,)),
            pltpu.SemaphoreType.DMA((groups * per,)),
        ],
        name="gathered",
    )(place, *pieces)


def on_device(points, weights, proj, fetch_table, near_list, far_list, skel_idx):
    features, column_points = points.shape
    columns = weights.shape[1]
    devices = lax.axis_size("dev")
    groups = lax.axis_size("grp")
    targets = near_list.shape[0]
    leaf = column_points // targets
    row_leaves = targets // (groups - 1)
    per = targets // groups
    capacity = fetch_table.shape[3]
    scale = 2.0 / features * math.log2(math.e)
    group = lax.axis_index("grp")
    device = lax.axis_index("dev")
    chips = devices // 2
    dense = near_list.shape[1] == devices * capacity and far_list.shape[1] == devices

    def along(moves):
        return [(2 * a + core, 2 * b + core) for a, b in moves for core in range(2)]

    def shift(array, moves):
        return lax.ppermute(array, "dev", along(moves))

    swap = [(d, d ^ 1) for d in range(devices)]

    width = per * leaf
    mine = lax.dynamic_slice_in_dim(points, group * width, width, 1)
    numbers = fetch_table.reshape(-1)
    if not dense:
        numbers = jnp.concatenate([numbers, near_list.reshape(-1), far_list.reshape(-1)])
    room = 8 * 128
    assert numbers.shape[0] <= room
    numbers = jnp.pad(numbers, (0, room - numbers.shape[0])).reshape(8, 128).astype(F32)
    numbers = jnp.pad(numbers, ((0, 0), (0, width - 128)))
    parcel = jnp.concatenate([mine, numbers], axis=0)
    place = jnp.stack([group, device, device ^ 1])
    sizes = {
        "leaf": leaf,
        "per": per,
        "row_leaves": row_leaves,
        "rows_listed": groups - 1,
        "capacity": capacity,
        "devices": devices,
        "targets": targets,
        "near": near_list.shape[1],
        "far": far_list.shape[1],
        "dense": dense,
        "scale": scale,
    }

    def with_partner(skel_block):
        skel, skel_w = skeleton(points, weights, proj, skel_idx, skel_block)
        own = (points, weights, skel, skel_w)
        return own, tuple(lax.ppermute(array, "dev", swap) for array in own)

    if chips == 4:
        chip = device // 2
        inner = (chip == 1) | (chip == 2)
        ends = [(0, 3), (3, 0), (1, 1), (2, 2)]
        sides = [(0, 1), (1, 0), (2, 3), (3, 2)]
        middle = [(1, 2), (2, 1), (0, 0), (3, 3)]
        inward = [(0, 1), (3, 2)]
        outward = [(1, 0), (2, 3)]
        cross = [(1, 2), (2, 1)]
        of_a, of_c, of_d = shift(parcel, ends), shift(parcel, sides), shift(parcel, middle)
        of_b = (shift(of_c, cross), shift(of_d, outward))
        sources = with_partner(width)
        work = lambda got, init, i: pairs(sizes, place, got, init, sources, i, 1)
        a = [work((of_a,), None, i) for i in range(per)]
        b = [work(of_b, shift(a[i], inward), i) for i in range(per)]
        done = []
        for i in range(per):
            from_b = (shift(b[i], cross), shift(b[i], inward))
            if i >= 2:
                (*from_b, done[i - 2]) = lax.optimization_barrier((*from_b, done[i - 2]))
            c = work((of_c,), from_b[0], i)
            d = work((of_d,), from_b[1], i)
            own = jnp.where(inner, a[i], 0.0)
            done.append(shift(c, sides) + shift(d, middle) + own)
    else:
        sources = with_partner(width)
        total = None
        for r in range(chips):
            got = shift(parcel, [(z, (z - r) % chips) for z in range(chips)])
            part = pairs(sizes, place, (got,), None, sources, 0, per)
            part = shift(part, [(z, (z + r) % chips) for z in range(chips)])
            total = part if total is None else total + part
        done = [total[i * leaf : (i + 1) * leaf] for i in range(per)]

    pieces = []
    for m in range(groups):
        for i in range(per):
            pieces.append(
                done[i]
                if m == 0
                else lax.ppermute(done[i], "grp", [(g, g ^ m) for g in range(groups)])
            )
    place = group ^ jnp.arange(groups, dtype=jnp.int32)
    return gathered(place, pieces, groups, per, leaf, columns)


def solution(mesh):
    placed = (
        P(None, "dev"),
        P("dev", None),
        P(None, "dev"),
        P(None, "dev", None, None),
        P("dev", None),
        P("dev", None),
        P("dev", None),
    )
    return jax.shard_map(
        on_device, mesh=mesh, in_specs=placed, out_specs=P("dev", None), check_vma=False
    )
```

profile of v0, /device:TPU:0, one launch (start us, length us, event | category | flops | bytes accessed | tf_op | source)
XLA Modules:
  0.0 162.7 jit_solution(16674004446330500960)
XLA Ops:
  0.0 0.5 collective-permute-start.6
  0.5 0.1 collective-permute-start.5
  0.6 6.9 %skeleton.1 = (f32[64,256]{1,0:T(8,128)}, f32[256,128]{1,0:T(8,128)}) custom-call(s32[1,256]{1,0:T(1,128)} %idx_ref.1, f32[64,6144]{1,0:T(8,128)} %refs_4_.17, f32[6144,128]{1,0:T(8,128)} %refs_5_.11, f32[256,6144]{1,0:T(8,128)} %proj_ref.1), custom_call_target="tpu_custom_call" | custom-call | flops 1610612736 | bytes 11010048 | tf_op jit(solution)/shard_map/skeleton/pallas_call | solution.py:233
  7.5 0.4 collective-permute-start.8
  8.0 0.1 copy.7
  8.1 0.1 reshape.5
  8.2 1.0 constant_dynamic-slice_fusion
  9.2 0.8 select_maximum_fusion
  10.0 3.0 %collective-permute-start = (f32[72,1536]{1,0:T(8,128)}, f32[72,1536]{1,0:T(8,128)}, u32[]{:S(2)}, u32[]{:S(2)}) collective-permute-start(f32[72,1536]{1,0:T(8,128)} %select_maximum_fusion), channel_id=1, source_target_pairs={{0,2},{1,3},{2,0},{3,1},{4,6},{5,7},{6,4},{7,5},{8,10},{9,11},{10,... | collective-permute-start | bytes 1327112 | tf_op jit(solution)/shard_map/ppermute | solution.py:317
  13.0 5.0 %collective-permute-start.2 = (f32[72,1536]{1,0:T(8,128)}, f32[72,1536]{1,0:T(8,128)}, u32[]{:S(2)}, u32[]{:S(2)}) collective-permute-start(f32[72,1536]{1,0:T(8,128)} %select_maximum_fusion), channel_id=1, source_target_pairs={{2,4},{3,5},{4,2},{5,3},{0,0},{1,1},{6,6},{7,7},{10,12},{11,13},{1... | collective-permute-start | bytes 1327112 | tf_op jit(solution)/shard_map/ppermute | solution.py:317
  18.0 4.4 %collective-permute-start.4 = (f32[72,1536]{1,0:T(8,128)}, f32[72,1536]{1,0:T(8,128)}, u32[]{:S(2)}, u32[]{:S(2)}) collective-permute-start(f32[72,1536]{1,0:T(8,128)} %select_maximum_fusion), channel_id=1, source_target_pairs={{0,6},{1,7},{6,0},{7,1},{2,2},{3,3},{4,4},{5,5},{8,14},{9,15},{14,... | collective-permute-start | bytes 1327112 | tf_op jit(solution)/shard_map/ppermute | solution.py:317
  22.4 0.1 pad_add_fusion.refs_0_
  22.5 1.2 collective-permute-done.refs_1_.refs_2_
  23.7 0.7 collective-permute-start.1
  24.4 1.3 collective-permute-start.3
  25.7 9.8 %collective-permute-done.4.refs_1_.refs_2_ = f32[72,1536]{1,0:T(8,128)} collective-permute-done((f32[72,1536]{1,0:T(8,128)}, f32[72,1536]{1,0:T(8,128)}, u32[]{:S(2)}, u32[]{:S(2)}) %collective-permute-start.4) | collective-permute-done | bytes 442400 | tf_op jit(solution)/shard_map/ppermute | solution.py:317
  35.5 1.4 copy-done.1
  36.9 0.9 copy-done.2
  37.8 0.8 copy-done.4
  38.7 4.6 %pairs.14 = f32[512,128]{1,0:T(8,128)S(1)} custom-call(s32[3]{0:T(128)S(1)} %pad_add_fusion.refs_0_, f32[72,1536]{1,0:T(8,128)} %collective-permute-done.4.refs_1_.refs_2_, f32[72,1536]{1,0:T(8,128)} %collective-permute-done.4.refs_1_.refs_2_, f32[64,6144]{1,0:T(8,128)S(1)} %copy-done.1, f32[6144,128]{1,0:T(8,128)S(1)} %copy-done, f32[64,256]{1,0:T(8,128)S(1)} %copy-done.4, ...), custom_call_target="tpu_custom_call" | custom-call | flops 2013265920 | bytes 1966080 | tf_op jit(solution)/shard_map/pairs/pallas_call | solution.py:179
  43.2 6.7 %collective-permute-start.12 = (f32[512,128]{1,0:T(8,128)S(1)}, f32[512,128]{1,0:T(8,128)S(1)}, u32[]{:S(2)}, u32[]{:S(2)}) collective-permute-start(f32[512,128]{1,0:T(8,128)S(1)} %pairs.14), channel_id=1, source_target_pairs={{0,2},{1,3},{6,4},{7,5},{8,10},{9,11},{14,12},{15,13},{16,18},{17,... | collective-permute-start | bytes 786440 | tf_op jit(solution)/shard_map/ppermute | solution.py:317
  49.9 4.6 %pairs.12 = f32[512,128]{1,0:T(8,128)S(1)} custom-call(s32[3]{0:T(128)S(1)} %pad_add_fusion.refs_0_, f32[72,1536]{1,0:T(8,128)} %collective-permute-done.4.refs_1_.refs_2_, f32[72,1536]{1,0:T(8,128)} %collective-permute-done.4.refs_1_.refs_2_, f32[64,6144]{1,0:T(8,128)S(1)} %copy-done.1, f32[6144,128]{1,0:T(8,128)S(1)} %copy-done, f32[64,256]{1,0:T(8,128)S(1)} %copy-done.4, ...), custom_call_target="tpu_custom_call" | custom-call | flops 2013265920 | bytes 1966080 | tf_op jit(solution)/shard_map/pairs/pallas_call | solution.py:179
  54.5 1.4 collective-permute-start.9
  55.9 4.6 %pairs.18 = f32[512,128]{1,0:T(8,128)S(1)} custom-call(s32[3]{0:T(128)S(1)} %pad_add_fusion.refs_0_, f32[72,1536]{1,0:T(8,128)} %collective-permute-done.4.refs_1_.refs_2_, f32[72,1536]{1,0:T(8,128)} %collective-permute-done.4.refs_1_.refs_2_, f32[64,6144]{1,0:T(8,128)S(1)} %copy-done.1, f32[6144,128]{1,0:T(8,128)S(1)} %copy-done, f32[64,256]{1,0:T(8,128)S(1)} %copy-done.4, ...), custom_call_target="tpu_custom_call" | custom-call | flops 2013265920 | bytes 1966080 | tf_op jit(solution)/shard_map/pairs/pallas_call | solution.py:179
  60.5 1.3 collective-permute-start.17
  61.9 4.3 %pairs.15 = f32[512,128]{1,0:T(8,128)S(1)} custom-call(s32[3]{0:T(128)S(1)} %pad_add_fusion.refs_0_, f32[72,1536]{1,0:T(8,128)S(1)} %collective-permute-done.1.refs_1_.refs_3_, f32[72,1536]{1,0:T(8,128)S(1)} %collective-permute-done.3.refs_2_.refs_4_, f32[72,1536]{1,0:T(8,128)S(1)} %collective-permute-done.1.refs_1_.refs_3_, ...), custom_call_target="tpu_custom_call" | custom-call | flops 2013265920 | bytes 1966080 | tf_op jit(solution)/shard_map/pairs/pallas_call | solution.py:179
  66.3 1.3 collective-permute-start.15
  67.6 0.7 collective-permute-start.13
  68.3 4.4 %pairs.13 = f32[512,128]{1,0:T(8,128)S(1)} custom-call(s32[3]{0:T(128)S(1)} %pad_add_fusion.refs_0_, f32[72,1536]{1,0:T(8,128)S(1)} %collective-permute-done.1.refs_1_.refs_3_, f32[72,1536]{1,0:T(8,128)S(1)} %collective-permute-done.3.refs_2_.refs_4_, f32[72,1536]{1,0:T(8,128)S(1)} %collective-permute-done.1.refs_1_.refs_3_, ...), custom_call_target="tpu_custom_call" | custom-call | flops 2013265920 | bytes 1966080 | tf_op jit(solution)/shard_map/pairs/pallas_call | solution.py:179
  72.6 0.7 collective-permute-start.10
  73.3 5.8 %collective-permute-start.11 = (f32[512,128]{1,0:T(8,128)S(1)}, f32[512,128]{1,0:T(8,128)S(1)}, u32[]{:S(2)}, u32[]{:S(2)}) collective-permute-start(f32[512,128]{1,0:T(8,128)S(1)} %pairs.13), channel_id=1, source_target_pairs={{0,2},{1,3},{6,4},{7,5},{8,10},{9,11},{14,12},{15,13},{16,18},{17,... | collective-permute-start | bytes 786440 | tf_op jit(solution)/shard_map/ppermute | solution.py:317
  79.1 4.3 %pairs.19 = f32[512,128]{1,0:T(8,128)S(1)} custom-call(s32[3]{0:T(128)S(1)} %pad_add_fusion.refs_0_, f32[72,1536]{1,0:T(8,128)S(1)} %collective-permute-done.1.refs_1_.refs_3_, f32[72,1536]{1,0:T(8,128)S(1)} %collective-permute-done.3.refs_2_.refs_4_, f32[72,1536]{1,0:T(8,128)S(1)} %collective-permute-done.1.refs_1_.refs_3_, ...), custom_call_target="tpu_custom_call" | custom-call | flops 2013265920 | bytes 1966080 | tf_op jit(solution)/shard_map/pairs/pallas_call | solution.py:179
  83.5 1.3 collective-permute-start.20
  84.8 0.7 collective-permute-start.18
  85.5 4.6 %pairs.17 = f32[512,128]{1,0:T(8,128)S(1)} custom-call(s32[3]{0:T(128)S(1)} %pad_add_fusion.refs_0_, f32[72,1536]{1,0:T(8,128)} %collective-permute-done.2.refs_1_.refs_2_, f32[72,1536]{1,0:T(8,128)} %collective-permute-done.2.refs_1_.refs_2_, f32[512,128]{1,0:T(8,128)S(1)} %collective-permute-done.15.refs_3_, f32[64,6144]{1,0:T(8,128)S(1)} %copy-done.1, ...), custom_call_target="tpu_custom_call" | custom-call | flops 2013265920 | bytes 1966080 | tf_op jit(solution)/shard_map/pairs/pallas_call | solution.py:179
  90.1 0.7 collective-permute-start.16
  90.8 4.6 %pairs.16 = f32[512,128]{1,0:T(8,128)S(1)} custom-call(s32[3]{0:T(128)S(1)} %pad_add_fusion.refs_0_, f32[72,1536]{1,0:T(8,128)} %collective-permute-done.refs_1_.refs_2_, f32[72,1536]{1,0:T(8,128)} %collective-permute-done.refs_1_.refs_2_, f32[512,128]{1,0:T(8,128)S(1)} %collective-permute-done.13.refs_3_, f32[64,6144]{1,0:T(8,128)S(1)} %copy-done.1, ...), custom_call_target="tpu_custom_call" | custom-call | flops 2013265920 | bytes 1966080 | tf_op jit(solution)/shard_map/pairs/pallas_call | solution.py:179
  95.4 3.9 %collective-permute-start.14 = (f32[512,128]{1,0:T(8,128)S(1)}, f32[512,128]{1,0:T(8,128)S(1)}, u32[]{:S(2)}, u32[]{:S(2)}) collective-permute-start(f32[512,128]{1,0:T(8,128)S(1)} %pairs.16), channel_id=1, source_target_pairs={{0,2},{1,3},{2,0},{3,1},{4,6},{5,7},{6,4},{7,5},{8,10},{9,11},{10,... | collective-permute-start | bytes 786440 | tf_op jit(solution)/shard_map/ppermute | solution.py:317
  99.3 4.6 %pairs.21 = f32[512,128]{1,0:T(8,128)S(1)} custom-call(s32[3]{0:T(128)S(1)} %pad_add_fusion.refs_0_, f32[72,1536]{1,0:T(8,128)} %collective-permute-done.2.refs_1_.refs_2_, f32[72,1536]{1,0:T(8,128)} %collective-permute-done.2.refs_1_.refs_2_, f32[512,128]{1,0:T(8,128)S(1)} %collective-permute-done.20.refs_3_, f32[64,6144]{1,0:T(8,128)S(1)} %copy-done.1, ...), custom_call_target="tpu_custom_call" | custom-call | flops 2013265920 | bytes 1966080 | tf_op jit(solution)/shard_map/pairs/pallas_call | solution.py:179
  103.9 0.7 collective-permute-start.21
  104.6 4.6 %pairs.20 = f32[512,128]{1,0:T(8,128)S(1)} custom-call(s32[3]{0:T(128)S(1)} %pad_add_fusion.refs_0_, f32[72,1536]{1,0:T(8,128)} %collective-permute-done.refs_1_.refs_2_, f32[72,1536]{1,0:T(8,128)} %collective-permute-done.refs_1_.refs_2_, f32[512,128]{1,0:T(8,128)S(1)} %collective-permute-done.18.refs_3_, f32[64,6144]{1,0:T(8,128)S(1)} %copy-done.1, ...), custom_call_target="tpu_custom_call" | custom-call | flops 2013265920 | bytes 1966080 | tf_op jit(solution)/shard_map/pairs/pallas_call | solution.py:179
  109.2 3.3 %collective-permute-start.19 = (f32[512,128]{1,0:T(8,128)S(1)}, f32[512,128]{1,0:T(8,128)S(1)}, u32[]{:S(2)}, u32[]{:S(2)}) collective-permute-start(f32[512,128]{1,0:T(8,128)S(1)} %pairs.20), channel_id=1, source_target_pairs={{0,2},{1,3},{2,0},{3,1},{4,6},{5,7},{6,4},{7,5},{8,10},{9,11},{10,... | collective-permute-start | bytes 786440 | tf_op jit(solution)/shard_map/ppermute | solution.py:317
  112.6 4.7 %pairs.23 = f32[512,128]{1,0:T(8,128)S(1)} custom-call(s32[3]{0:T(128)S(1)} %pad_add_fusion.refs_0_, f32[72,1536]{1,0:T(8,128)} %collective-permute-done.2.refs_1_.refs_2_, f32[72,1536]{1,0:T(8,128)} %collective-permute-done.2.refs_1_.refs_2_, f32[512,128]{1,0:T(8,128)S(1)} %collective-permute-done.11.refs_3_, f32[64,6144]{1,0:T(8,128)S(1)} %copy-done.1, ...), custom_call_target="tpu_custom_call" | custom-call | flops 2013265920 | bytes 1966080 | tf_op jit(solution)/shard_map/pairs/pallas_call | solution.py:179
  117.2 0.7 collective-permute-start.23
  117.9 4.6 %pairs.22 = f32[512,128]{1,0:T(8,128)S(1)} custom-call(s32[3]{0:T(128)S(1)} %pad_add_fusion.refs_0_, f32[72,1536]{1,0:T(8,128)} %collective-permute-done.refs_1_.refs_2_, f32[72,1536]{1,0:T(8,128)} %collective-permute-done.refs_1_.refs_2_, f32[512,128]{1,0:T(8,128)S(1)} %collective-permute-done.10.refs_3_, f32[64,6144]{1,0:T(8,128)S(1)} %copy-done.1, ...), custom_call_target="tpu_custom_call" | custom-call | flops 2013265920 | bytes 1966080 | tf_op jit(solution)/shard_map/pairs/pallas_call | solution.py:179
  122.5 2.1 %collective-permute-start.22 = (f32[512,128]{1,0:T(8,128)S(1)}, f32[512,128]{1,0:T(8,128)S(1)}, u32[]{:S(2)}, u32[]{:S(2)}) collective-permute-start(f32[512,128]{1,0:T(8,128)S(1)} %pairs.22), channel_id=1, source_target_pairs={{0,2},{1,3},{2,0},{3,1},{4,6},{5,7},{6,4},{7,5},{8,10},{9,11},{10,... | collective-permute-start | bytes 786440 | tf_op jit(solution)/shard_map/ppermute | solution.py:317
  124.6 1.6 collective-permute-start.25
  126.2 1.5 collective-permute-start.28
  127.7 0.5 collective-permute-start.31
  128.2 1.5 collective-permute-start.24
  129.7 1.5 collective-permute-start.27
  131.3 2.6 %collective-permute-done.25.refs_5_ = f32[512,128]{1,0:T(8,128)S(1)} collective-permute-done((f32[512,128]{1,0:T(8,128)S(1)}, f32[512,128]{1,0:T(8,128)S(1)}, u32[]{:S(2)}, u32[]{:S(2)}) %collective-permute-start.25) | collective-permute-done | bytes 262176 | tf_op jit(solution)/shard_map/ppermute | solution.py:391
  133.9 2.4 %collective-permute-start.30 = (f32[512,128]{1,0:T(8,128)S(1)}, f32[512,128]{1,0:T(8,128)S(1)}, u32[]{:S(2)}, u32[]{:S(2)}) collective-permute-start(f32[512,128]{1,0:T(8,128)S(1)} %select_add_fusion.2.refs_1_), channel_id=1, source_target_pairs={{0,24},{8,16},{16,8},{24,0},{1,25},{9,17},{17,9},{25,1},{2,26},{10... | collective-permute-start | bytes 786440 | tf_op jit(solution)/shard_map/ppermute | solution.py:391
  136.3 4.6 %collective-permute-done.28.refs_8_ = f32[512,128]{1,0:T(8,128)S(1)} collective-permute-done((f32[512,128]{1,0:T(8,128)S(1)}, f32[512,128]{1,0:T(8,128)S(1)}, u32[]{:S(2)}, u32[]{:S(2)}) %collective-permute-start.28) | collective-permute-done | bytes 262176 | tf_op jit(solution)/shard_map/ppermute | solution.py:391
  140.9 2.0 %collective-permute-start.29 = (f32[512,128]{1,0:T(8,128)S(1)}, f32[512,128]{1,0:T(8,128)S(1)}, u32[]{:S(2)}, u32[]{:S(2)}) collective-permute-start(f32[512,128]{1,0:T(8,128)S(1)} %select_add_fusion.refs_3_), channel_id=1, source_target_pairs={{0,16},{8,24},{16,0},{24,8},{1,17},{9,25},{17,1},{25,9},{2,18},{10... | collective-permute-start | bytes 786440 | tf_op jit(solution)/shard_map/ppermute | solution.py:391
  143.0 2.2 %collective-permute-done.24.refs_4_ = f32[512,128]{1,0:T(8,128)S(1)} collective-permute-done((f32[512,128]{1,0:T(8,128)S(1)}, f32[512,128]{1,0:T(8,128)S(1)}, u32[]{:S(2)}, u32[]{:S(2)}) %collective-permute-start.24) | collective-permute-done | bytes 262176 | tf_op jit(solution)/shard_map/ppermute | solution.py:391
  145.2 2.4 %collective-permute-start.32 = (f32[512,128]{1,0:T(8,128)S(1)}, f32[512,128]{1,0:T(8,128)S(1)}, u32[]{:S(2)}, u32[]{:S(2)}) collective-permute-start(f32[512,128]{1,0:T(8,128)S(1)} %select_add_fusion.refs_3_), channel_id=1, source_target_pairs={{0,24},{8,16},{16,8},{24,0},{1,25},{9,17},{17,9},{25,1},{2,26},{10... | collective-permute-start | bytes 786440 | tf_op jit(solution)/shard_map/ppermute | solution.py:391
  147.6 0.6 iota_xor_fusion.refs_0_
  148.2 3.8 %collective-permute-done.27.refs_7_ = f32[512,128]{1,0:T(8,128)S(1)} collective-permute-done((f32[512,128]{1,0:T(8,128)S(1)}, f32[512,128]{1,0:T(8,128)S(1)}, u32[]{:S(2)}, u32[]{:S(2)}) %collective-permute-start.27) | collective-permute-done | bytes 262176 | tf_op jit(solution)/shard_map/ppermute | solution.py:391
  152.0 1.9 %collective-permute-done.26.refs_6_ = f32[512,128]{1,0:T(8,128)S(1)} collective-permute-done((f32[512,128]{1,0:T(8,128)S(1)}, f32[512,128]{1,0:T(8,128)S(1)}, u32[]{:S(2)}, u32[]{:S(2)}) %collective-permute-start.26) | collective-permute-done | bytes 262176 | tf_op jit(solution)/shard_map/ppermute | solution.py:391
  154.0 3.9 %collective-permute-done.29.refs_9_ = f32[512,128]{1,0:T(8,128)S(1)} collective-permute-done((f32[512,128]{1,0:T(8,128)S(1)}, f32[512,128]{1,0:T(8,128)S(1)}, u32[]{:S(2)}, u32[]{:S(2)}) %collective-permute-start.29) | collective-permute-done | bytes 262176 | tf_op jit(solution)/shard_map/ppermute | solution.py:391
  157.9 0.6 copy-done.16
  158.6 0.7 copy-done.17
  159.3 3.5 %gathered.1 = f32[6144,128]{1,0:T(8,128)} custom-call(s32[4]{0:T(128)} %iota_xor_fusion.refs_0_, f32[512,128]{1,0:T(8,128)} %copy-done.6, f32[512,128]{1,0:T(8,128)} %copy-done.7, f32[512,128]{1,0:T(8,128)} %copy-done.8, f32[512,128]{1,0:T(8,128)} %copy-done.12, f32[512,128]{1,0:T(8,128)} %copy-done.9, f32[512,128]{1,0:T(8,128)} %copy-done.15, ...), custom_call_target="tpu_custom_call" | custom-call | tf_op jit(solution)/shard_map/gathered/pallas_call | solution.py:282
  (64 shorter events, 0.3 us)
Async XLA Ops:
  0.0 8.0 %copy-start.18 = (s32[3,1,8,2]{2,3,1,0:T(2,128)S(1)}, s32[3,1,8,2]{2,3,1,0:T(2,128)}, u32[]{:S(2)}) copy-start(s32[3,1,8,2]{2,3,1,0:T(2,128)} %param.10) | copy-start | bytes 580
  0.0 35.5 %collective-permute-start.6 = (f32[6144,128]{1,0:T(8,128)}, f32[6144,128]{1,0:T(8,128)}, u32[]{:S(2)}, u32[]{:S(2)}) collective-permute-start(f32[6144,128]{1,0:T(8,128)} %refs_5_.11), channel_id=1, source_target_pairs={{0,1},{1,0},{2,3},{3,2},{4,5},{5,4},{6,7},{7,6},{8,9},{9,8},{10,11... | collective-permute-start | bytes 9437192 | tf_op jit(solution)/shard_map/ppermute | solution.py:349
  0.5 35.0 %collective-permute-start.5 = (f32[64,6144]{1,0:T(8,128)}, f32[64,6144]{1,0:T(8,128)}, u32[]{:S(2)}, u32[]{:S(2)}) collective-permute-start(f32[64,6144]{1,0:T(8,128)} %refs_4_.17), channel_id=1, source_target_pairs={{0,1},{1,0},{2,3},{3,2},{4,5},{5,4},{6,7},{7,6},{8,9},{9,8},{10,11... | collective-permute-start | bytes 4718600 | tf_op jit(solution)/shard_map/ppermute | solution.py:349
  0.6 34.9 %copy-start = (f32[6144,128]{1,0:T(8,128)S(1)}, f32[6144,128]{1,0:T(8,128)}, u32[]{:S(2)}) copy-start(f32[6144,128]{1,0:T(8,128)} %refs_5_.11) | copy-start | bytes 9437188
  7.5 10.6 %collective-permute-start.8 = (f32[256,128]{1,0:T(8,128)}, f32[256,128]{1,0:T(8,128)S(1)}, u32[]{:S(2)}, u32[]{:S(2)}) collective-permute-start(f32[256,128]{1,0:T(8,128)} %get-tuple-element.11.refs_6_.refs_9_.refs_7_), channel_id=1, source_target_pairs={{0,1},{1,0},{2,3},{3,2},{4,5},{5,4},{6,7},{7,6},{8,9},{9,8},{10,11... | collective-permute-start | bytes 393224 | tf_op jit(solution)/shard_map/ppermute | solution.py:349
  7.9 5.1 %collective-permute-start.7 = (f32[64,256]{1,0:T(8,128)}, f32[64,256]{1,0:T(8,128)S(1)}, u32[]{:S(2)}, u32[]{:S(2)}) collective-permute-start(f32[64,256]{1,0:T(8,128)} %get-tuple-element.10.refs_5_.refs_8_.refs_6_), channel_id=1, source_target_pairs={{0,1},{1,0},{2,3},{3,2},{4,5},{5,4},{6,7},{7,6},{8,9},{9,8},{10,11... | collective-permute-start | bytes 196616 | tf_op jit(solution)/shard_map/ppermute | solution.py:349
  10.0 13.7 %collective-permute-start = (f32[72,1536]{1,0:T(8,128)}, f32[72,1536]{1,0:T(8,128)}, u32[]{:S(2)}, u32[]{:S(2)}) collective-permute-start(f32[72,1536]{1,0:T(8,128)} %select_maximum_fusion), channel_id=1, source_target_pairs={{0,2},{1,3},{2,0},{3,1},{4,6},{5,7},{6,4},{7,5},{8,10},{9,11},{10,... | collective-permute-start | bytes 1327112 | tf_op jit(solution)/shard_map/ppermute | solution.py:317
  13.0 11.4 %collective-permute-start.2 = (f32[72,1536]{1,0:T(8,128)}, f32[72,1536]{1,0:T(8,128)}, u32[]{:S(2)}, u32[]{:S(2)}) collective-permute-start(f32[72,1536]{1,0:T(8,128)} %select_maximum_fusion), channel_id=1, source_target_pairs={{2,4},{3,5},{4,2},{5,3},{0,0},{1,1},{6,6},{7,7},{10,12},{11,13},{1... | collective-permute-start | bytes 1327112 | tf_op jit(solution)/shard_map/ppermute | solution.py:317
  18.0 17.5 %collective-permute-start.4 = (f32[72,1536]{1,0:T(8,128)}, f32[72,1536]{1,0:T(8,128)}, u32[]{:S(2)}, u32[]{:S(2)}) collective-permute-start(f32[72,1536]{1,0:T(8,128)} %select_maximum_fusion), channel_id=1, source_target_pairs={{0,6},{1,7},{6,0},{7,1},{2,2},{3,3},{4,4},{5,5},{8,14},{9,15},{14,... | collective-permute-start | bytes 1327112 | tf_op jit(solution)/shard_map/ppermute | solution.py:317
  23.7 38.1 %collective-permute-start.1 = (f32[72,1536]{1,0:T(8,128)}, f32[72,1536]{1,0:T(8,128)S(1)}, u32[]{:S(2)}, u32[]{:S(2)}) collective-permute-start(f32[72,1536]{1,0:T(8,128)} %collective-permute-done.refs_1_.refs_2_), channel_id=1, source_target_pairs={{2,4},{3,5},{4,2},{5,3},{10,12},{11,13},{12,10},{13,11},{18,20},{1... | collective-permute-start | bytes 1327112 | tf_op jit(solution)/shard_map/ppermute | solution.py:317
  24.4 37.5 %collective-permute-start.3 = (f32[72,1536]{1,0:T(8,128)}, f32[72,1536]{1,0:T(8,128)S(1)}, u32[]{:S(2)}, u32[]{:S(2)}) collective-permute-start(f32[72,1536]{1,0:T(8,128)} %collective-permute-done.2.refs_1_.refs_2_), channel_id=1, source_target_pairs={{2,0},{3,1},{4,6},{5,7},{10,8},{11,9},{12,14},{13,15},{18,16},{19,... | collective-permute-start | bytes 1327112 | tf_op jit(solution)/shard_map/ppermute | solution.py:317
  35.5 1.4 copy-start.1
  36.9 0.9 copy-start.2
  37.8 0.8 copy-start.4
  43.2 18.6 %collective-permute-start.12 = (f32[512,128]{1,0:T(8,128)S(1)}, f32[512,128]{1,0:T(8,128)S(1)}, u32[]{:S(2)}, u32[]{:S(2)}) collective-permute-start(f32[512,128]{1,0:T(8,128)S(1)} %pairs.14), channel_id=1, source_target_pairs={{0,2},{1,3},{6,4},{7,5},{8,10},{9,11},{14,12},{15,13},{16,18},{17,... | collective-permute-start | bytes 786440 | tf_op jit(solution)/shard_map/ppermute | solution.py:317
  54.5 7.4 %copy-start.3 = (f32[256,128]{1,0:T(8,128)S(1)}, f32[256,128]{1,0:T(8,128)}, u32[]{:S(2)}) copy-start(f32[256,128]{1,0:T(8,128)} %get-tuple-element.11.refs_6_.refs_9_.refs_7_) | copy-start | bytes 393220
  54.5 7.4 %copy-start.5 = (f32[64,256]{1,0:T(8,128)S(1)}, f32[64,256]{1,0:T(8,128)}, u32[]{:S(2)}) copy-start(f32[64,256]{1,0:T(8,128)} %get-tuple-element.10.refs_5_.refs_8_.refs_6_) | copy-start | bytes 196612
  54.5 13.8 %collective-permute-start.9 = (f32[512,128]{1,0:T(8,128)S(1)}, f32[512,128]{1,0:T(8,128)S(1)}, u32[]{:S(2)}, u32[]{:S(2)}) collective-permute-start(f32[512,128]{1,0:T(8,128)S(1)} %pairs.12), channel_id=1, source_target_pairs={{0,2},{1,3},{6,4},{7,5},{8,10},{9,11},{14,12},{15,13},{16,18},{17,... | collective-permute-start | bytes 786440 | tf_op jit(solution)/shard_map/ppermute | solution.py:317
  60.5 18.5 %collective-permute-start.17 = (f32[512,128]{1,0:T(8,128)S(1)}, f32[512,128]{1,0:T(8,128)S(1)}, u32[]{:S(2)}, u32[]{:S(2)}) collective-permute-start(f32[512,128]{1,0:T(8,128)S(1)} %pairs.18), channel_id=1, source_target_pairs={{0,2},{1,3},{6,4},{7,5},{8,10},{9,11},{14,12},{15,13},{16,18},{17,... | collective-permute-start | bytes 786440 | tf_op jit(solution)/shard_map/ppermute | solution.py:317
  66.3 18.5 %collective-permute-start.15 = (f32[512,128]{1,0:T(8,128)S(1)}, f32[512,128]{1,0:T(8,128)S(1)}, u32[]{:S(2)}, u32[]{:S(2)}) collective-permute-start(f32[512,128]{1,0:T(8,128)S(1)} %pairs.15), channel_id=1, source_target_pairs={{0,2},{1,3},{6,4},{7,5},{8,10},{9,11},{14,12},{15,13},{16,18},{17,... | collective-permute-start | bytes 786440 | tf_op jit(solution)/shard_map/ppermute | solution.py:317
  67.6 22.5 %collective-permute-start.13 = (f32[512,128]{1,0:T(8,128)S(1)}, f32[512,128]{1,0:T(8,128)S(1)}, u32[]{:S(2)}, u32[]{:S(2)}) collective-permute-start(f32[512,128]{1,0:T(8,128)S(1)} %pairs.15), channel_id=1, source_target_pairs={{2,4},{3,5},{4,2},{5,3},{10,12},{11,13},{12,10},{13,11},{18,20},{1... | collective-permute-start | bytes 786440 | tf_op jit(solution)/shard_map/ppermute | solution.py:317
  72.6 39.9 %collective-permute-start.10 = (f32[512,128]{1,0:T(8,128)S(1)}, f32[512,128]{1,0:T(8,128)S(1)}, u32[]{:S(2)}, u32[]{:S(2)}) collective-permute-start(f32[512,128]{1,0:T(8,128)S(1)} %pairs.13), channel_id=1, source_target_pairs={{2,4},{3,5},{4,2},{5,3},{10,12},{11,13},{12,10},{13,11},{18,20},{1... | collective-permute-start | bytes 786440 | tf_op jit(solution)/shard_map/ppermute | solution.py:317
  73.3 39.2 %collective-permute-start.11 = (f32[512,128]{1,0:T(8,128)S(1)}, f32[512,128]{1,0:T(8,128)S(1)}, u32[]{:S(2)}, u32[]{:S(2)}) collective-permute-start(f32[512,128]{1,0:T(8,128)S(1)} %pairs.13), channel_id=1, source_target_pairs={{0,2},{1,3},{6,4},{7,5},{8,10},{9,11},{14,12},{15,13},{16,18},{17,... | collective-permute-start | bytes 786440 | tf_op jit(solution)/shard_map/ppermute | solution.py:317
  83.5 11.9 %collective-permute-start.20 = (f32[512,128]{1,0:T(8,128)S(1)}, f32[512,128]{1,0:T(8,128)S(1)}, u32[]{:S(2)}, u32[]{:S(2)}) collective-permute-start(f32[512,128]{1,0:T(8,128)S(1)} %pairs.19), channel_id=1, source_target_pairs={{0,2},{1,3},{6,4},{7,5},{8,10},{9,11},{14,12},{15,13},{16,18},{17,... | collective-permute-start | bytes 786440 | tf_op jit(solution)/shard_map/ppermute | solution.py:317
  84.8 19.1 %collective-permute-start.18 = (f32[512,128]{1,0:T(8,128)S(1)}, f32[512,128]{1,0:T(8,128)S(1)}, u32[]{:S(2)}, u32[]{:S(2)}) collective-permute-start(f32[512,128]{1,0:T(8,128)S(1)} %pairs.19), channel_id=1, source_target_pairs={{2,4},{3,5},{4,2},{5,3},{10,12},{11,13},{12,10},{13,11},{18,20},{1... | collective-permute-start | bytes 786440 | tf_op jit(solution)/shard_map/ppermute | solution.py:317
  90.1 19.1 %collective-permute-start.16 = (f32[512,128]{1,0:T(8,128)S(1)}, f32[512,128]{1,0:T(8,128)S(1)}, u32[]{:S(2)}, u32[]{:S(2)}) collective-permute-start(f32[512,128]{1,0:T(8,128)S(1)} %pairs.17), channel_id=1, source_target_pairs={{2,4},{3,5},{4,2},{5,3},{0,0},{1,1},{6,6},{7,7},{10,12},{11,13},{1... | collective-permute-start | bytes 786440 | tf_op jit(solution)/shard_map/ppermute | solution.py:317
  95.4 17.1 %collective-permute-start.14 = (f32[512,128]{1,0:T(8,128)S(1)}, f32[512,128]{1,0:T(8,128)S(1)}, u32[]{:S(2)}, u32[]{:S(2)}) collective-permute-start(f32[512,128]{1,0:T(8,128)S(1)} %pairs.16), channel_id=1, source_target_pairs={{0,2},{1,3},{2,0},{3,1},{4,6},{5,7},{6,4},{7,5},{8,10},{9,11},{10,... | collective-permute-start | bytes 786440 | tf_op jit(solution)/shard_map/ppermute | solution.py:317
  103.9 20.7 %collective-permute-start.21 = (f32[512,128]{1,0:T(8,128)S(1)}, f32[512,128]{1,0:T(8,128)S(1)}, u32[]{:S(2)}, u32[]{:S(2)}) collective-permute-start(f32[512,128]{1,0:T(8,128)S(1)} %pairs.21), channel_id=1, source_target_pairs={{2,4},{3,5},{4,2},{5,3},{0,0},{1,1},{6,6},{7,7},{10,12},{11,13},{1... | collective-permute-start | bytes 786440 | tf_op jit(solution)/shard_map/ppermute | solution.py:317
  109.2 15.4 %collective-permute-start.19 = (f32[512,128]{1,0:T(8,128)S(1)}, f32[512,128]{1,0:T(8,128)S(1)}, u32[]{:S(2)}, u32[]{:S(2)}) collective-permute-start(f32[512,128]{1,0:T(8,128)S(1)} %pairs.20), channel_id=1, source_target_pairs={{0,2},{1,3},{2,0},{3,1},{4,6},{5,7},{6,4},{7,5},{8,10},{9,11},{10,... | collective-permute-start | bytes 786440 | tf_op jit(solution)/shard_map/ppermute | solution.py:317
  112.5 21.4 %copy-start.6 = (f32[512,128]{1,0:T(8,128)}, f32[512,128]{1,0:T(8,128)S(1)}, u32[]{:S(2)}) copy-start(f32[512,128]{1,0:T(8,128)S(1)} %select_add_fusion.2.refs_1_) | copy-start | bytes 786436
  117.2 11.0 %collective-permute-start.23 = (f32[512,128]{1,0:T(8,128)S(1)}, f32[512,128]{1,0:T(8,128)S(1)}, u32[]{:S(2)}, u32[]{:S(2)}) collective-permute-start(f32[512,128]{1,0:T(8,128)S(1)} %pairs.23), channel_id=1, source_target_pairs={{2,4},{3,5},{4,2},{5,3},{0,0},{1,1},{6,6},{7,7},{10,12},{11,13},{1... | collective-permute-start | bytes 786440 | tf_op jit(solution)/shard_map/ppermute | solution.py:317
  122.5 7.2 %collective-permute-start.22 = (f32[512,128]{1,0:T(8,128)S(1)}, f32[512,128]{1,0:T(8,128)S(1)}, u32[]{:S(2)}, u32[]{:S(2)}) collective-permute-start(f32[512,128]{1,0:T(8,128)S(1)} %pairs.22), channel_id=1, source_target_pairs={{0,2},{1,3},{2,0},{3,1},{4,6},{5,7},{6,4},{7,5},{8,10},{9,11},{10,... | collective-permute-start | bytes 786440 | tf_op jit(solution)/shard_map/ppermute | solution.py:317
  124.6 33.2 %copy-start.7 = (f32[512,128]{1,0:T(8,128)}, f32[512,128]{1,0:T(8,128)S(1)}, u32[]{:S(2)}) copy-start(f32[512,128]{1,0:T(8,128)S(1)} %select_add_fusion.1.refs_2_) | copy-start | bytes 786436
  124.6 9.2 %collective-permute-start.25 = (f32[512,128]{1,0:T(8,128)S(1)}, f32[512,128]{1,0:T(8,128)S(1)}, u32[]{:S(2)}, u32[]{:S(2)}) collective-permute-start(f32[512,128]{1,0:T(8,128)S(1)} %select_add_fusion.1.refs_2_), channel_id=1, source_target_pairs={{0,8},{8,0},{16,24},{24,16},{1,9},{9,1},{17,25},{25,17},{2,10},{10... | collective-permute-start | bytes 786440 | tf_op jit(solution)/shard_map/ppermute | solution.py:391
  126.2 14.7 %collective-permute-start.28 = (f32[512,128]{1,0:T(8,128)S(1)}, f32[512,128]{1,0:T(8,128)S(1)}, u32[]{:S(2)}, u32[]{:S(2)}) collective-permute-start(f32[512,128]{1,0:T(8,128)S(1)} %select_add_fusion.1.refs_2_), channel_id=1, source_target_pairs={{0,16},{8,24},{16,0},{24,8},{1,17},{9,25},{17,1},{25,9},{2,18},{10... | collective-permute-start | bytes 786440 | tf_op jit(solution)/shard_map/ppermute | solution.py:391
  127.7 13.2 %collective-permute-start.31 = (f32[512,128]{1,0:T(8,128)S(1)}, f32[512,128]{1,0:T(8,128)S(1)}, u32[]{:S(2)}, u32[]{:S(2)}) collective-permute-start(f32[512,128]{1,0:T(8,128)S(1)} %select_add_fusion.1.refs_2_), channel_id=1, source_target_pairs={{0,24},{8,16},{16,8},{24,0},{1,25},{9,17},{17,9},{25,1},{2,26},{10... | collective-permute-start | bytes 786440 | tf_op jit(solution)/shard_map/ppermute | solution.py:391
  128.2 17.0 %collective-permute-start.24 = (f32[512,128]{1,0:T(8,128)S(1)}, f32[512,128]{1,0:T(8,128)S(1)}, u32[]{:S(2)}, u32[]{:S(2)}) collective-permute-start(f32[512,128]{1,0:T(8,128)S(1)} %select_add_fusion.2.refs_1_), channel_id=1, source_target_pairs={{0,8},{8,0},{16,24},{24,16},{1,9},{9,1},{17,25},{25,17},{2,10},{10... | collective-permute-start | bytes 786440 | tf_op jit(solution)/shard_map/ppermute | solution.py:391
  129.7 22.3 %collective-permute-start.27 = (f32[512,128]{1,0:T(8,128)S(1)}, f32[512,128]{1,0:T(8,128)S(1)}, u32[]{:S(2)}, u32[]{:S(2)}) collective-permute-start(f32[512,128]{1,0:T(8,128)S(1)} %select_add_fusion.2.refs_1_), channel_id=1, source_target_pairs={{0,16},{8,24},{16,0},{24,8},{1,17},{9,25},{17,1},{25,9},{2,18},{10... | collective-permute-start | bytes 786440 | tf_op jit(solution)/shard_map/ppermute | solution.py:391
  131.2 26.6 %copy-start.8 = (f32[512,128]{1,0:T(8,128)}, f32[512,128]{1,0:T(8,128)S(1)}, u32[]{:S(2)}) copy-start(f32[512,128]{1,0:T(8,128)S(1)} %select_add_fusion.refs_3_) | copy-start | bytes 786436
  133.9 24.0 %copy-start.9 = (f32[512,128]{1,0:T(8,128)}, f32[512,128]{1,0:T(8,128)S(1)}, u32[]{:S(2)}) copy-start(f32[512,128]{1,0:T(8,128)S(1)} %collective-permute-done.25.refs_5_) | copy-start | bytes 786436
  133.9 18.1 %collective-permute-start.30 = (f32[512,128]{1,0:T(8,128)S(1)}, f32[512,128]{1,0:T(8,128)S(1)}, u32[]{:S(2)}, u32[]{:S(2)}) collective-permute-start(f32[512,128]{1,0:T(8,128)S(1)} %select_add_fusion.2.refs_1_), channel_id=1, source_target_pairs={{0,24},{8,16},{16,8},{24,0},{1,25},{9,17},{17,9},{25,1},{2,26},{10... | collective-permute-start | bytes 786440 | tf_op jit(solution)/shard_map/ppermute | solution.py:391
  140.9 16.9 %copy-start.10 = (f32[512,128]{1,0:T(8,128)}, f32[512,128]{1,0:T(8,128)S(1)}, u32[]{:S(2)}) copy-start(f32[512,128]{1,0:T(8,128)S(1)} %collective-permute-done.28.refs_8_) | copy-start | bytes 786436
  140.9 13.0 %collective-permute-start.26 = (f32[512,128]{1,0:T(8,128)S(1)}, f32[512,128]{1,0:T(8,128)S(1)}, u32[]{:S(2)}, u32[]{:S(2)}) collective-permute-start(f32[512,128]{1,0:T(8,128)S(1)} %select_add_fusion.refs_3_), channel_id=1, source_target_pairs={{0,8},{8,0},{16,24},{24,16},{1,9},{9,1},{17,25},{25,17},{2,10},{10... | collective-permute-start | bytes 786440 | tf_op jit(solution)/shard_map/ppermute | solution.py:391
  140.9 16.9 %copy-start.11 = (f32[512,128]{1,0:T(8,128)}, f32[512,128]{1,0:T(8,128)S(1)}, u32[]{:S(2)}) copy-start(f32[512,128]{1,0:T(8,128)S(1)} %collective-permute-done.31.refs_11_) | copy-start | bytes 786436
  140.9 16.9 %collective-permute-start.29 = (f32[512,128]{1,0:T(8,128)S(1)}, f32[512,128]{1,0:T(8,128)S(1)}, u32[]{:S(2)}, u32[]{:S(2)}) collective-permute-start(f32[512,128]{1,0:T(8,128)S(1)} %select_add_fusion.refs_3_), channel_id=1, source_target_pairs={{0,16},{8,24},{16,0},{24,8},{1,17},{9,25},{17,1},{25,9},{2,18},{10... | collective-permute-start | bytes 786440 | tf_op jit(solution)/shard_map/ppermute | solution.py:391
  145.1 12.7 %copy-start.12 = (f32[512,128]{1,0:T(8,128)}, f32[512,128]{1,0:T(8,128)S(1)}, u32[]{:S(2)}) copy-start(f32[512,128]{1,0:T(8,128)S(1)} %collective-permute-done.24.refs_4_) | copy-start | bytes 786436
  145.2 12.7 %collective-permute-start.32 = (f32[512,128]{1,0:T(8,128)S(1)}, f32[512,128]{1,0:T(8,128)S(1)}, u32[]{:S(2)}, u32[]{:S(2)}) collective-permute-start(f32[512,128]{1,0:T(8,128)S(1)} %select_add_fusion.refs_3_), channel_id=1, source_target_pairs={{0,24},{8,16},{16,8},{24,0},{1,25},{9,17},{17,9},{25,1},{2,26},{10... | collective-permute-start | bytes 786440 | tf_op jit(solution)/shard_map/ppermute | solution.py:391
  152.0 5.9 %copy-start.13 = (f32[512,128]{1,0:T(8,128)}, f32[512,128]{1,0:T(8,128)S(1)}, u32[]{:S(2)}) copy-start(f32[512,128]{1,0:T(8,128)S(1)} %collective-permute-done.27.refs_7_) | copy-start | bytes 786436
  152.0 5.9 %copy-start.14 = (f32[512,128]{1,0:T(8,128)}, f32[512,128]{1,0:T(8,128)S(1)}, u32[]{:S(2)}) copy-start(f32[512,128]{1,0:T(8,128)S(1)} %collective-permute-done.30.refs_10_) | copy-start | bytes 786436
  153.9 4.0 %copy-start.15 = (f32[512,128]{1,0:T(8,128)}, f32[512,128]{1,0:T(8,128)S(1)}, u32[]{:S(2)}) copy-start(f32[512,128]{1,0:T(8,128)S(1)} %collective-permute-done.26.refs_6_) | copy-start | bytes 786436
  157.8 0.7 copy-start.16
  158.6 0.7 copy-start.17
where the time goes:
time: 164 us; the launch traced here: 163 us
  Pallas kernels  64.8 us (40%)
  starting transfers between devices  60 us (37%)
  waiting for transfers between devices  30.1 us (18%)
  local copies, waits for them, and re-layouts  5.75 us (4%)
    pallas_call x12, Pallas kernels, pairs(): pl.pallas_call(functools.partial(pair_kernel, plan), grid=(count,), in_sp...  54.4 us
    ppermute x20, starting transfers between devices, shift(): return lax.ppermute(array, 'dev', along(moves))  45.4 us
    ppermute x9, waiting for transfers between devices, on_device(): lax.ppermute(done[i], 'grp', [(g, g ^ m) for g in range(groups)])  19 us
    ppermute x9, starting transfers between devices, on_device(): lax.ppermute(done[i], 'grp', [(g, g ^ m) for g in range(groups)])  13.5 us
    ppermute x20, waiting for transfers between devices, shift(): return lax.ppermute(array, 'dev', along(moves))  11 us
    pallas_call x1, Pallas kernels, skeleton(): pl.pallas_call(skeleton_kernel, grid=(count // block,), in_specs=[pl.Bloc...  6.89 us
    unnamed x39, local copies, waits for them, and re-layouts  4.63 us
    pallas_call x1, Pallas kernels, gathered(): pl.pallas_call(functools.partial(gather_kernel, groups, per, leaf), in_sp...  3.47 us
  transfers between devices with their start and end apart: 33, of which 8 were waited for; matrix products, arithmetic and copies ran while one was open for 2% of the time, Pallas kernels for 38%

commit v1 on v0

--- a/solution.py
+++ b/solution.py
@@ -43,42 +43,72 @@
     list_refs = [refs.pop(0) for _ in range(plan["parcels"])]
     x_refs = [refs.pop(0) for _ in range(plan["parcels"])]
     init_ref = refs.pop(0) if plan["init"] else None
-    sides, (out_ref, y_buf, w_buf, xk_buf, sem) = (refs[:4], refs[4:8]), refs[8:]
+    sides, (out_ref, y_buf, w_buf, ys_buf, ws_buf, xk_buf, sem, skel_sem) = (
+        (refs[:4], refs[4:8]),
+        refs[8:],
+    )
     leaf = x_refs[0].shape[1]
     capacity = plan["capacity"]
     devices = plan["devices"]
     scale = plan["scale"]
-    number = place_ref[0] * plan["per"] + plan["first"] + pl.program_id(0)
-    row = number // plan["row_leaves"]
+    slots = 2 * capacity
+    kept = ys_buf.shape[1] // 2
+    step = pl.program_id(0)
+    half = step % 2
 
     def listed(n):
         value = sum(ref[n // 128, n % 128] for ref in list_refs)
         return value.astype(jnp.int32)
 
-    skel_slot = 2 * capacity
-    kept = leaf // 2
-    copies = []
-    for side, (pts, wts, _, _) in enumerate(sides):
-        owner = place_ref[1 + side]
-        for c in range(capacity):
-            slot = side * capacity + c
-            start = pl.multiple_of(listed((row * devices + owner) * capacity + c) * leaf, leaf)
-            copies.append(pltpu.make_async_copy(
-                pts.at[:, pl.ds(start, leaf)], y_buf.at[slot], sem.at[slot, 0]
-            ))
-            copies.append(pltpu.make_async_copy(
-                wts.at[pl.ds(start, leaf), :], w_buf.at[slot], sem.at[slot, 1]
-            ))
+    def leaf_number(at):
+        return place_ref[0] * plan["per"] + plan["first"] + at
+
+    def near_copies(at, buffer):
+        row = leaf_number(at) // plan["row_leaves"]
+        copies = []
+        for side, (pts, wts, _, _) in enumerate(sides):
+            for c in range(capacity):
+                slot = side * capacity + c
+                n = (row * devices + place_ref[1 + side]) * capacity + c
+                start = pl.multiple_of(listed(n) * leaf, leaf)
+                copies.append((
+                    pltpu.make_async_copy(
+                        pts.at[:, pl.ds(start, leaf)],
+                        y_buf.at[buffer, slot],
+                        sem.at[buffer, slot, 0],
+                    ),
+                    pltpu.make_async_copy(
+                        wts.at[pl.ds(start, leaf), :],
+                        w_buf.at[buffer, slot],
+                        sem.at[buffer, slot, 1],
+                    ),
+                ))
+        return copies
+
+    skel_copies = []
     for side, (_, _, pts, wts) in enumerate(sides):
         part = pl.ds(side * kept, kept)
-        copies.append(pltpu.make_async_copy(
-            pts, y_buf.at[skel_slot, :, part], sem.at[skel_slot, side]
-        ))
-        copies.append(pltpu.make_async_copy(
-            wts, w_buf.at[skel_slot, part, :], sem.at[skel_slot, 2 + side]
-        ))
-    for copy in copies:
-        copy.start()
+        skel_copies += [
+            pltpu.make_async_copy(pts, ys_buf.at[:, part], skel_sem.at[side, 0]),
+            pltpu.make_async_copy(wts, ws_buf.at[part, :], skel_sem.at[side, 1]),
+        ]
+
+    @pl.when(step == 0)
+    def _():
+        for copy in skel_copies:
+            copy.start()
+        for pair in near_copies(0, 0):
+            pair[0].start()
+            pair[1].start()
+
+    if plan["count"] > 1:
+
+        @pl.when(step + 1 < plan["count"])
+        def _():
+            for pair in near_copies(step + 1, 1 - half):
+                pair[0].start()
+                pair[1].start()
+
     x = x_refs[0][...]
     for ref in x_refs[1:]:
         x = x + ref[...]
@@ -88,9 +118,7 @@
     else:
         out_ref[...] = init_ref[...]
 
-    def add(slot):
-        y = y_buf[slot]
-        w = w_buf[slot]
+    def add(y, w):
         yk = stacked(y, None, scale, False).astype(BF16)
         w_high, w_low = two_terms(w)
         wk = jnp.concatenate([w_high, w_low], axis=1).astype(BF16)
@@ -109,13 +137,14 @@
 
     flags = None
     if not plan["dense"]:
-        base = (plan["rows_listed"]) * devices * capacity
+        number = leaf_number(step)
+        base = plan["rows_listed"] * devices * capacity
         near = [listed(base + number * plan["near"] + n) for n in range(plan["near"])]
         base += plan["targets"] * plan["near"]
         far = [listed(base + number * plan["far"] + n) for n in range(plan["far"])]
 
         def among(value, options):
-            return sum((option == value).astype(jnp.int32) for option in options)
+            return sum((option == value).astype(F32) for option in options)
 
         flags = []
         for side in range(2):
@@ -123,38 +152,24 @@
             flags += [among(owner * capacity + c, near) for c in range(capacity)]
         flags += [among(place_ref[1 + side], far) for side in range(2)]
 
-    for copy in copies[-4:]:
-        copy.wait()
+    def flagged(w, n):
+        return w if flags is None else w * flags[n]
+
+    @pl.when(step == 0)
+    def _():
+        for copy in skel_copies:
+            copy.wait()
+
+    ws = ws_buf[...]
     if flags is not None:
-        for side in range(2):
-            part = slice(side * kept, (side + 1) * kept)
-            w_buf[skel_slot, part, :] = w_buf[skel_slot, part, :] * flags[
-                2 * capacity + side
-            ].astype(F32)
-
-    def near_step(slot, carry):
-        pts, wts = sides[0][0], sides[0][1]
-
-        @pl.when(slot < skel_slot)
-        def _():
-            pltpu.make_async_copy(
-                pts.at[:, pl.ds(0, leaf)], y_buf.at[slot], sem.at[slot, 0]
-            ).wait()
-            pltpu.make_async_copy(
-                wts.at[pl.ds(0, leaf), :], w_buf.at[slot], sem.at[slot, 1]
-            ).wait()
-
-        add(slot)
-        return carry
-
-    if flags is None:
-        lax.fori_loop(0, skel_slot + 1, near_step, 0)
-    else:
-        for n in range(skel_slot):
-            copies[2 * n].wait()
-            copies[2 * n + 1].wait()
-            w_buf[n] = w_buf[n] * flags[n].astype(F32)
-        lax.fori_loop(0, skel_slot + 1, lambda slot, carry: (add(slot), carry)[1], 0)
+        ws = jnp.concatenate(
+            [flagged(ws[:kept], slots), flagged(ws[kept:], slots + 1)], axis=0
+        )
+    add(ys_buf[...], ws)
+    for slot, pair in enumerate(near_copies(step, half)):
+        pair[0].wait()
+        pair[1].wait()
+        add(y_buf[half, slot], flagged(w_buf[half, slot], slot))
 
 
 def pairs(sizes, place, parcels, init, sources, first, count):
@@ -162,8 +177,16 @@
     features = own[0].shape[0]
     columns = own[1].shape[1]
     leaf = sizes["leaf"]
-    slots = 2 * sizes["capacity"] + 1
-    plan = dict(sizes, parcels=len(parcels), init=init is not None, first=first, rows=leaf // 2)
+    slots = 2 * sizes["capacity"]
+    kept = own[2].shape[1]
+    plan = dict(
+        sizes,
+        parcels=len(parcels),
+        init=init is not None,
+        first=first,
+        count=count,
+        rows=leaf // 2,
+    )
     in_specs = [pl.BlockSpec(memory_space=pltpu.SMEM)]
     in_specs += [
         pl.BlockSpec((8, 128), lambda i: (features // 8, 0), memory_space=pltpu.SMEM)
@@ -175,7 +198,7 @@
         operands.append(init)
     in_specs += [pl.BlockSpec(memory_space=pl.ANY)] * 8
     operands += [array for side in sources for array in side]
-    work = count * leaf * leaf * slots
+    work = count * leaf * (leaf * slots + 2 * kept)
     return pl.pallas_call(
         functools.partial(pair_kernel, plan),
         grid=(count,),
@@ -183,10 +206,13 @@
         out_specs=pl.BlockSpec((leaf, columns), lambda i: (i, 0)),
         out_shape=jax.ShapeDtypeStruct((count * leaf, columns), F32),
         scratch_shapes=[
-            pltpu.VMEM((slots, features, leaf), F32),
-            pltpu.VMEM((slots, leaf, columns), F32),
+            pltpu.VMEM((2, slots, features, leaf), F32),
+            pltpu.VMEM((2, slots, leaf, columns), F32),
+            pltpu.VMEM((features, 2 * kept), F32),
+            pltpu.VMEM((2 * kept, columns), F32),
             pltpu.VMEM((leaf, 4 * features), BF16),
-            pltpu.SemaphoreType.DMA((slots, 4)),
+            pltpu.SemaphoreType.DMA((2, slots, 2)),
+            pltpu.SemaphoreType.DMA((2, 2)),
         ],
         compiler_params=pltpu.CompilerParams(vmem_limit_bytes=32 << 20),
         cost_estimate=pl.CostEstimate(
@@ -256,42 +282,38 @@
     )(skel_idx, points, weights, proj)
 
 
-def gather_kernel(groups, per, leaf, *refs):
+def spread_kernel(groups, per, first, leaf, aliased, *refs):
     place_ref = refs[0]
-    pieces = refs[1 : 1 + groups * per]
-    out_ref = refs[1 + groups * per]
-    buf, in_sem, out_sem = refs[2 + groups * per :]
-    ins, outs = [], []
-    for n, piece in enumerate(pieces):
-        ins.append(pltpu.make_async_copy(piece, buf.at[n], in_sem.at[n]))
-        m, i = divmod(n, per)
-        start = pl.multiple_of((place_ref[m] * per + i) * leaf, leaf)
-        outs.append(
-            pltpu.make_async_copy(buf.at[n], out_ref.at[pl.ds(start, leaf), :], out_sem.at[n])
+    pieces = refs[1 : 1 + groups]
+    out_ref, sem = refs[1 + groups + aliased :]
+    size = pieces[0].shape[0]
+    copies = []
+    for m, piece in enumerate(pieces):
+        start = pl.multiple_of((place_ref[m] * per + first) * leaf, leaf)
+        copies.append(
+            pltpu.make_async_copy(piece, out_ref.at[pl.ds(start, size), :], sem.at[m])
         )
-    for c in ins:
-        c.start()
-    for c, d in zip(ins, outs):
-        c.wait()
-        d.start()
-    for d in outs:
-        d.wait()
-
-
-def gathered(place, pieces, groups, per, leaf, columns):
+    for copy in copies:
+        copy.start()
+    for copy in copies:
+        copy.wait()
+
+
+def spread(place, pieces, out, per, first, leaf):
+    groups = len(pieces)
+    columns = pieces[0].shape[1]
+    aliased = [] if out is None else [out]
     return pl.pallas_call(
-        functools.partial(gather_kernel, groups, per, leaf),
+        functools.partial(spread_kernel, groups, per, first, leaf, len(aliased)),
         in_specs=[pl.BlockSpec(memory_space=pltpu.SMEM)]
-        + [pl.BlockSpec(memory_space=pl.ANY)] * (groups * per),
+        + [pl.BlockSpec(memory_space=pltpu.VMEM)] * groups
+        + [pl.BlockSpec(memory_space=pl.ANY)] * len(aliased),
         out_specs=pl.BlockSpec(memory_space=pl.ANY),
         out_shape=jax.ShapeDtypeStruct((groups * per * leaf, columns), F32),
-        scratch_shapes=[
-            pltpu.VMEM((groups * per, leaf, columns), F32),
-            pltpu.SemaphoreType.DMA((groups * per,)),
-            pltpu.SemaphoreType.DMA((groups * per,)),
-        ],
-        name="gathered",
-    )(place, *pieces)
+        scratch_shapes=[pltpu.SemaphoreType.DMA((groups,))],
+        input_output_aliases={1 + groups: 0} if aliased else {},
+        name="spread",
+    )(place, *pieces, *aliased)
 
 
 def on_device(points, weights, proj, fetch_table, near_list, far_list, skel_idx):
@@ -328,7 +350,10 @@
     numbers = jnp.pad(numbers, (0, room - numbers.shape[0])).reshape(8, 128).astype(F32)
     numbers = jnp.pad(numbers, ((0, 0), (0, width - 128)))
     parcel = jnp.concatenate([mine, numbers], axis=0)
+    proj, parcel = lax.optimization_barrier((proj, parcel))
     place = jnp.stack([group, device, device ^ 1])
+    late = per // 3
+    chunks = [(0, per - late)] + ([(per - late, late)] if late else [])
     sizes = {
         "leaf": leaf,
         "per": per,
@@ -360,17 +385,15 @@
         of_a, of_c, of_d = shift(parcel, ends), shift(parcel, sides), shift(parcel, middle)
         of_b = (shift(of_c, cross), shift(of_d, outward))
         sources = with_partner(width)
-        work = lambda got, init, i: pairs(sizes, place, got, init, sources, i, 1)
-        a = [work((of_a,), None, i) for i in range(per)]
-        b = [work(of_b, shift(a[i], inward), i) for i in range(per)]
+        work = lambda got, init, k: pairs(sizes, place, got, init, sources, *chunks[k])
+        every = range(len(chunks))
+        a = [work((of_a,), None, k) for k in every]
+        b = [work(of_b, shift(a[k], inward), k) for k in every]
         done = []
-        for i in range(per):
-            from_b = (shift(b[i], cross), shift(b[i], inward))
-            if i >= 2:
-                (*from_b, done[i - 2]) = lax.optimization_barrier((*from_b, done[i - 2]))
-            c = work((of_c,), from_b[0], i)
-            d = work((of_d,), from_b[1], i)
-            own = jnp.where(inner, a[i], 0.0)
+        for k in every:
+            c = work((of_c,), shift(b[k], cross), k)
+            d = work((of_d,), shift(b[k], inward), k)
+            own = jnp.where(inner, a[k], 0.0)
             done.append(shift(c, sides) + shift(d, middle) + own)
     else:
         sources = with_partner(width)
@@ -380,18 +403,17 @@
             part = pairs(sizes, place, (got,), None, sources, 0, per)
             part = shift(part, [(z, (z + r) % chips) for z in range(chips)])
             total = part if total is None else total + part
-        done = [total[i * leaf : (i + 1) * leaf] for i in range(per)]
-
-    pieces = []
-    for m in range(groups):
-        for i in range(per):
-            pieces.append(
-                done[i]
-                if m == 0
-                else lax.ppermute(done[i], "grp", [(g, g ^ m) for g in range(groups)])
-            )
-    place = group ^ jnp.arange(groups, dtype=jnp.int32)
-    return gathered(place, pieces, groups, per, leaf, columns)
+        done = [total[first * leaf : (first + count) * leaf] for first, count in chunks]
+
+    mask = group ^ jnp.arange(groups, dtype=jnp.int32)
+    out = None
+    for (first, _), piece in zip(chunks, done):
+        pieces = [
+            lax.ppermute(piece, "grp", [(g, g ^ m) for g in range(groups)]) if m else piece
+            for m in range(groups)
+        ]
+        out = spread(mask, pieces, out, per, first, leaf)
+    return out
 
 
 def solution(mesh):

time: 164 us -> 161 us (0.982)
  starting transfers between devices: 60 us -> 49.3 us
  local copies, waits for them, and re-layouts: 5.75 us -> 10.6 us
  waiting for transfers between devices: 30.1 us -> 33.1 us
  Pallas kernels: 64.8 us -> 62.8 us
    ppermute x20 -> x15, waiting for transfers between devices: 11 us -> 21.7 us  [shift(): return lax.ppermute(array, 'dev', along(moves))]
    ppermute x9 -> x6, waiting for transfers between devices: 19 us -> 10.4 us  [on_device(): lax.ppermute(piece, 'grp', [(g, g ^ m) for g in range(groups)])]
    ppermute x9 -> x6, starting transfers between devices: 13.5 us -> 7.13 us  [on_device(): lax.ppermute(piece, 'grp', [(g, g ^ m) for g in range(groups)])]
    unnamed x39 -> x47, local copies, waits for them, and re-layouts: 4.63 us -> 9.49 us
    ppermute x20 -> x15, starting transfers between devices: 45.4 us -> 41.2 us  [shift(): return lax.ppermute(array, 'dev', along(moves))]
    pallas_call x12 -> x8, Pallas kernels: 54.4 us -> 50.9 us  [pairs(): pl.pallas_call(functools.partial(pair_kernel, plan), grid=(count,), in_sp...]
    pallas_call x1 -> x2, Pallas kernels: 3.47 us -> 5.07 us  [spread(): pl.pallas_call(functools.partial(spread_kernel, groups, per, first, leaf,...]
  transfers between devices with their start and end apart: 33 -> 25, of which waited for: 8 -> 6; matrix products, arithmetic and copies ran while one was open for 2% -> 3% of each run, Pallas kernels for 38% -> 33%
where the time goes in v1:
time: 161 us; the launch traced here: 159 us
  Pallas kernels  62.8 us (39%)
  starting transfers between devices  49.3 us (31%)
  waiting for transfers between devices  33.1 us (21%)
  local copies, waits for them, and re-layouts  10.6 us (7%)
  other arithmetic  2.79 us (2%)
    pallas_call x8, Pallas kernels, pairs(): pl.pallas_call(functools.partial(pair_kernel, plan), grid=(count,), in_sp...  50.9 us
    ppermute x15, starting transfers between devices, shift(): return lax.ppermute(array, 'dev', along(moves))  41.2 us
    ppermute x15, waiting for transfers between devices, shift(): return lax.ppermute(array, 'dev', along(moves))  21.7 us
    ppermute x6, waiting for transfers between devices, on_device(): lax.ppermute(piece, 'grp', [(g, g ^ m) for g in range(groups)])  10.4 us
    unnamed x47, local copies, waits for them, and re-layouts  9.49 us
    ppermute x6, starting transfers between devices, on_device(): lax.ppermute(piece, 'grp', [(g, g ^ m) for g in range(groups)])  7.13 us
    pallas_call x1, Pallas kernels, skeleton(): pl.pallas_call(skeleton_kernel, grid=(count // block,), in_specs=[pl.Bloc...  6.76 us
    pallas_call x2, Pallas kernels, spread(): pl.pallas_call(functools.partial(spread_kernel, groups, per, first, leaf,...  5.07 us
  transfers between devices with their start and end apart: 25, of which 6 were waited for; matrix products, arithmetic and copies ran while one was open for 3% of the time, Pallas kernels for 33%

profile of v1, /device:TPU:0, one launch (start us, length us, event | category | flops | bytes accessed | tf_op | source)
XLA Modules:
  0.0 159.3 jit_solution(11840297088622446474)
XLA Ops:
  0.0 0.5 collective-permute-start.6
  0.5 0.0 collective-permute-start.5
  0.5 0.8 copy.8
  1.3 0.1 reshape.5
  1.4 1.0 constant_dynamic-slice_fusion
  2.4 0.8 select_maximum_fusion
  3.2 7.2 %collective-permute-start.4 = (f32[72,1536]{1,0:T(8,128)}, f32[72,1536]{1,0:T(8,128)}, u32[]{:S(2)}, u32[]{:S(2)}) collective-permute-start(f32[72,1536]{1,0:T(8,128)} %select_maximum_fusion), channel_id=1, source_target_pairs={{0,6},{1,7},{6,0},{7,1},{2,2},{3,3},{4,4},{5,5},{8,14},{9,15},{14,... | collective-permute-start | bytes 1327112 | tf_op jit(solution)/shard_map/ppermute | solution.py:339
  10.5 6.8 %skeleton.1 = (f32[64,256]{1,0:T(8,128)}, f32[256,128]{1,0:T(8,128)}) custom-call(s32[1,256]{1,0:T(1,128)} %idx_ref.1, f32[64,6144]{1,0:T(8,128)} %refs_4_.11, f32[6144,128]{1,0:T(8,128)} %refs_5_.7, f32[256,6144]{1,0:T(8,128)} %proj_ref), custom_call_target="tpu_custom_call" | custom-call | flops 1610612736 | bytes 11010048 | tf_op jit(solution)/shard_map/skeleton/pallas_call | solution.py:259
  17.2 0.5 collective-permute-start.7
  17.7 0.1 pad_add_fusion.refs_0_
  17.8 1.1 collective-permute-done.7.refs_9_.refs_12_.refs_10_
  18.9 1.7 %collective-permute-start.2 = (f32[72,1536]{1,0:T(8,128)}, f32[72,1536]{1,0:T(8,128)S(1)}, u32[]{:S(2)}, u32[]{:S(2)}) collective-permute-start(f32[72,1536]{1,0:T(8,128)} %select_maximum_fusion), channel_id=1, source_target_pairs={{2,4},{3,5},{4,2},{5,3},{0,0},{1,1},{6,6},{7,7},{10,12},{11,13},{1... | collective-permute-start | bytes 1327112 | tf_op jit(solution)/shard_map/ppermute | solution.py:339
  20.5 3.0 %collective-permute-start = (f32[72,1536]{1,0:T(8,128)}, f32[72,1536]{1,0:T(8,128)S(1)}, u32[]{:S(2)}, u32[]{:S(2)}) collective-permute-start(f32[72,1536]{1,0:T(8,128)} %select_maximum_fusion), channel_id=1, source_target_pairs={{0,2},{1,3},{2,0},{3,1},{4,6},{5,7},{6,4},{7,5},{8,10},{9,11},{10,... | collective-permute-start | bytes 1327112 | tf_op jit(solution)/shard_map/ppermute | solution.py:339
  23.6 0.0 copy-start.1
  23.6 1.4 copy-done.1
  25.0 0.9 copy-done.3
  25.9 0.8 copy-done.9
  26.7 7.9 %pairs.12 = f32[1024,128]{1,0:T(8,128)S(1)} custom-call(s32[3]{0:T(128)S(1)} %pad_add_fusion.refs_0_, f32[72,1536]{1,0:T(8,128)} %collective-permute-done.4.refs_1_.refs_2_, f32[72,1536]{1,0:T(8,128)} %collective-permute-done.4.refs_1_.refs_2_, f32[64,6144]{1,0:T(8,128)S(1)} %copy-done.1, f32[6144,128]{1,0:T(8,128)S(1)} %copy-done, f32[64,256]{1,0:T(8,128)S(1)} %copy-done.9, ...), custom_call_target="tpu_custom_call" | custom-call | flops 4026531840 | bytes 3145728 | tf_op jit(solution)/shard_map/pairs/pallas_call | solution.py:202
  34.6 0.0 copy-start.13
  34.6 2.0 %collective-permute-start.17 = (f32[1024,128]{1,0:T(8,128)S(1)}, f32[1024,128]{1,0:T(8,128)S(1)}, u32[]{:S(2)}, u32[]{:S(2)}) collective-permute-start(f32[1024,128]{1,0:T(8,128)S(1)} %pairs.12), channel_id=1, source_target_pairs={{0,2},{1,3},{6,4},{7,5},{8,10},{9,11},{14,12},{15,13},{16,18},{17,... | collective-permute-start | bytes 1572872 | tf_op jit(solution)/shard_map/ppermute | solution.py:339
  36.6 0.0 collective-permute-done.2.refs_1_.refs_2_
  36.6 1.3 collective-permute-start.3
  37.9 0.0 collective-permute-done.refs_1_.refs_2_
  38.0 0.7 collective-permute-start.1
  38.7 11.7 %collective-permute-done.3.refs_2_.refs_4_ = f32[72,1536]{1,0:T(8,128)S(1)} collective-permute-done((f32[72,1536]{1,0:T(8,128)S(1)}, f32[72,1536]{1,0:T(8,128)S(1)}, u32[]{:S(2)}, u32[]{:S(2)}) %collective-permute-start.3) | collective-permute-done | bytes 442400 | tf_op jit(solution)/shard_map/ppermute | solution.py:339
  50.4 0.0 collective-permute-done.1.refs_1_.refs_3_
  50.4 7.7 %pairs.13 = f32[1024,128]{1,0:T(8,128)S(1)} custom-call(s32[3]{0:T(128)S(1)} %pad_add_fusion.refs_0_, f32[72,1536]{1,0:T(8,128)S(1)} %collective-permute-done.1.refs_1_.refs_3_, f32[72,1536]{1,0:T(8,128)S(1)} %collective-permute-done.3.refs_2_.refs_4_, f32[72,1536]{1,0:T(8,128)S(1)} %collective-permute-done.1.refs_1_.refs_3_, ...), custom_call_target="tpu_custom_call" | custom-call | flops 4026531840 | bytes 3145728 | tf_op jit(solution)/shard_map/pairs/pallas_call | solution.py:202
  58.1 5.6 %collective-permute-start.20 = (f32[1024,128]{1,0:T(8,128)S(1)}, f32[1024,128]{1,0:T(8,128)S(1)}, u32[]{:S(2)}, u32[]{:S(2)}) collective-permute-start(f32[1024,128]{1,0:T(8,128)S(1)} %pairs.13), channel_id=1, source_target_pairs={{0,2},{1,3},{6,4},{7,5},{8,10},{9,11},{14,12},{15,13},{16,18},{17,... | collective-permute-start | bytes 1572872 | tf_op jit(solution)/shard_map/ppermute | solution.py:339
  63.8 0.7 collective-permute-start.18
  64.5 4.6 %pairs.8 = f32[512,128]{1,0:T(8,128)S(1)} custom-call(s32[3]{0:T(128)S(1)} %pad_add_fusion.refs_0_, f32[72,1536]{1,0:T(8,128)} %collective-permute-done.4.refs_1_.refs_2_, f32[72,1536]{1,0:T(8,128)} %collective-permute-done.4.refs_1_.refs_2_, f32[64,6144]{1,0:T(8,128)S(1)} %copy-done.1, f32[6144,128]{1,0:T(8,128)S(1)} %copy-done, f32[64,256]{1,0:T(8,128)S(1)} %copy-done.9, ...), custom_call_target="tpu_custom_call" | custom-call | flops 2013265920 | bytes 1572864 | tf_op jit(solution)/shard_map/pairs/pallas_call | solution.py:202
  69.1 3.1 %collective-permute-start.9 = (f32[512,128]{1,0:T(8,128)S(1)}, f32[512,128]{1,0:T(8,128)S(1)}, u32[]{:S(2)}, u32[]{:S(2)}) collective-permute-start(f32[512,128]{1,0:T(8,128)S(1)} %pairs.8), channel_id=1, source_target_pairs={{0,2},{1,3},{6,4},{7,5},{8,10},{9,11},{14,12},{15,13},{16,18},{17,... | collective-permute-start | bytes 786440 | tf_op jit(solution)/shard_map/ppermute | solution.py:339
  72.2 3.8 %collective-permute-done.20.refs_3_ = f32[1024,128]{1,0:T(8,128)S(1)} collective-permute-done((f32[1024,128]{1,0:T(8,128)S(1)}, f32[1024,128]{1,0:T(8,128)S(1)}, u32[]{:S(2)}, u32[]{:S(2)}) %collective-permute-start.20) | collective-permute-done | bytes 524320 | tf_op jit(solution)/shard_map/ppermute | solution.py:339
  76.0 8.3 %pairs.15 = f32[1024,128]{1,0:T(8,128)} custom-call(s32[3]{0:T(128)S(1)} %pad_add_fusion.refs_0_, f32[72,1536]{1,0:T(8,128)S(1)} %collective-permute-done.2.refs_1_.refs_2_, f32[72,1536]{1,0:T(8,128)S(1)} %collective-permute-done.2.refs_1_.refs_2_, f32[1024,128]{1,0:T(8,128)S(1)} %collective-permute-done.20.refs_3_, f32[64,6144]{1,0:T(8,128)S(1)} %copy-done.1, ...), custom_call_target="tpu_custom_call" | custom-call | flops 4026531840 | bytes 3145728 | tf_op jit(solution)/shard_map/pairs/pallas_call | solution.py:202
  84.4 5.4 %collective-permute-start.21 = (f32[1024,128]{1,0:T(8,128)}, f32[1024,128]{1,0:T(8,128)}, u32[]{:S(2)}, u32[]{:S(2)}) collective-permute-start(f32[1024,128]{1,0:T(8,128)} %pairs.15), channel_id=1, source_target_pairs={{2,4},{3,5},{4,2},{5,3},{0,0},{1,1},{6,6},{7,7},{10,12},{11,13},{1... | collective-permute-start | bytes 1572872 | tf_op jit(solution)/shard_map/ppermute | solution.py:339
  89.8 8.3 %pairs.14 = f32[1024,128]{1,0:T(8,128)} custom-call(s32[3]{0:T(128)S(1)} %pad_add_fusion.refs_0_, f32[72,1536]{1,0:T(8,128)S(1)} %collective-permute-done.refs_1_.refs_2_, f32[72,1536]{1,0:T(8,128)S(1)} %collective-permute-done.refs_1_.refs_2_, f32[1024,128]{1,0:T(8,128)S(1)} %collective-permute-done.18.refs_3_, f32[64,6144]{1,0:T(8,128)S(1)} %copy-done.1, ...), custom_call_target="tpu_custom_call" | custom-call | flops 4026531840 | bytes 3145728 | tf_op jit(solution)/shard_map/pairs/pallas_call | solution.py:202
  98.1 0.1 collective-permute-start.19
  98.2 5.1 %pairs.9 = f32[512,128]{1,0:T(8,128)} custom-call(s32[3]{0:T(128)S(1)} %pad_add_fusion.refs_0_, f32[72,1536]{1,0:T(8,128)S(1)} %collective-permute-done.1.refs_1_.refs_3_, f32[72,1536]{1,0:T(8,128)S(1)} %collective-permute-done.3.refs_2_.refs_4_, f32[72,1536]{1,0:T(8,128)S(1)} %collective-permute-done.1.refs_1_.refs_3_, ...), custom_call_target="tpu_custom_call" | custom-call | flops 2013265920 | bytes 1572864 | tf_op jit(solution)/shard_map/pairs/pallas_call | solution.py:202
  103.3 4.6 %collective-permute-start.12 = (f32[512,128]{1,0:T(8,128)}, f32[512,128]{1,0:T(8,128)}, u32[]{:S(2)}, u32[]{:S(2)}) collective-permute-start(f32[512,128]{1,0:T(8,128)} %pairs.9), channel_id=1, source_target_pairs={{0,2},{1,3},{6,4},{7,5},{8,10},{9,11},{14,12},{15,13},{16,18},{17,... | collective-permute-start | bytes 786440 | tf_op jit(solution)/shard_map/ppermute | solution.py:339
  107.9 0.7 collective-permute-start.10
  108.6 2.8 %collective-permute-done.12.refs_3_ = f32[512,128]{1,0:T(8,128)} collective-permute-done((f32[512,128]{1,0:T(8,128)}, f32[512,128]{1,0:T(8,128)}, u32[]{:S(2)}, u32[]{:S(2)}) %collective-permute-start.12) | collective-permute-done | bytes 262176 | tf_op jit(solution)/shard_map/ppermute | solution.py:339
  111.4 1.4 copy-done.2
  112.8 1.0 copy-done.8
  113.8 4.7 %pairs.11 = f32[512,128]{1,0:T(8,128)S(1)} custom-call(s32[3]{0:T(128)S(1)} %pad_add_fusion.refs_0_, f32[72,1536]{1,0:T(8,128)S(1)} %copy-done.8, f32[72,1536]{1,0:T(8,128)S(1)} %copy-done.8, f32[512,128]{1,0:T(8,128)} %collective-permute-done.12.refs_3_, f32[64,6144]{1,0:T(8,128)S(1)} %copy-done.2, f32[6144,128]{1,0:T(8,128)S(1)} %copy-done, ...), custom_call_target="tpu_custom_call" | custom-call | flops 2013265920 | bytes 1572864 | tf_op jit(solution)/shard_map/pairs/pallas_call | solution.py:202
  118.5 0.9 collective-permute-start.13
  119.5 1.3 select_add_fusion.refs_1_
  120.8 2.5 %collective-permute-start.24 = (f32[1024,128]{1,0:T(8,128)S(1)}, f32[1024,128]{1,0:T(8,128)S(1)}, u32[]{:S(2)}, u32[]{:S(2)}) collective-permute-start(f32[1024,128]{1,0:T(8,128)S(1)} %select_add_fusion.refs_1_), channel_id=1, source_target_pairs={{0,24},{8,16},{16,8},{24,0},{1,25},{9,17},{17,9},{25,1},{2,26},{10... | collective-permute-start | bytes 1572872 | tf_op jit(solution)/shard_map/ppermute | solution.py:412
  123.3 4.3 %pairs.10 = f32[512,128]{1,0:T(8,128)S(1)} custom-call(s32[3]{0:T(128)S(1)} %pad_add_fusion.refs_0_, f32[72,1536]{1,0:T(8,128)S(1)} %copy-done.6, f32[72,1536]{1,0:T(8,128)S(1)} %copy-done.6, f32[512,128]{1,0:T(8,128)S(1)} %collective-permute-done.10.refs_3_, f32[64,6144]{1,0:T(8,128)S(1)} %copy-done.2, f32[6144,128]{1,0:T(8,128)S(1)} %copy-done, ...), custom_call_target="tpu_custom_call" | custom-call | flops 2013265920 | bytes 1572864 | tf_op jit(solution)/shard_map/pairs/pallas_call | solution.py:202
  127.6 4.3 %collective-permute-start.11 = (f32[512,128]{1,0:T(8,128)S(1)}, f32[512,128]{1,0:T(8,128)S(1)}, u32[]{:S(2)}, u32[]{:S(2)}) collective-permute-start(f32[512,128]{1,0:T(8,128)S(1)} %pairs.10), channel_id=1, source_target_pairs={{0,2},{1,3},{2,0},{3,1},{4,6},{5,7},{6,4},{7,5},{8,10},{9,11},{10,... | collective-permute-start | bytes 786440 | tf_op jit(solution)/shard_map/ppermute | solution.py:339
  131.9 0.5 collective-permute-start.23
  132.4 0.5 collective-permute-start.22
  132.9 3.3 %collective-permute-done.11 = f32[512,128]{1,0:T(8,128)S(1)} collective-permute-done((f32[512,128]{1,0:T(8,128)S(1)}, f32[512,128]{1,0:T(8,128)S(1)}, u32[]{:S(2)}, u32[]{:S(2)}) %collective-permute-start.11) | collective-permute-done | bytes 262176 | tf_op jit(solution)/shard_map/ppermute | solution.py:339
  136.2 0.1 select_add_fusion.1.refs_1_
  136.3 0.5 collective-permute-start.16
  136.8 1.5 collective-permute-start.15
  138.4 1.5 collective-permute-start.14
  139.9 0.6 iota_xor_fusion.refs_0_
  140.4 10.4 %collective-permute-done.23.refs_3_ = f32[1024,128]{1,0:T(8,128)S(1)} collective-permute-done((f32[1024,128]{1,0:T(8,128)S(1)}, f32[1024,128]{1,0:T(8,128)S(1)}, u32[]{:S(2)}, u32[]{:S(2)}) %collective-permute-start.23) | collective-permute-done | bytes 524320 | tf_op jit(solution)/shard_map/ppermute | solution.py:412
  150.8 0.8 copy-done.18
  151.7 0.8 copy-done.19
  152.5 2.9 %spread.2.refs_5_ = f32[6144,128]{1,0:T(8,128)} custom-call(s32[4]{0:T(128)} %iota_xor_fusion.refs_0_, f32[1024,128]{1,0:T(8,128)} %copy-done.15, f32[1024,128]{1,0:T(8,128)} %copy-done.19, f32[1024,128]{1,0:T(8,128)} %copy-done.18, f32[1024,128]{1,0:T(8,128)} %copy-done.17), custom_call_target="tpu_custom_call" | custom-call | tf_op jit(solution)/shard_map/spread/pallas_call | solution.py:306
  155.4 0.7 copy-done.20
  156.1 0.1 copy-done.21
  156.2 0.7 copy-done.22
  156.9 2.2 %spread.3 = f32[6144,128]{1,0:T(8,128)} custom-call(s32[4]{0:T(128)} %iota_xor_fusion.refs_0_, f32[512,128]{1,0:T(8,128)} %copy-done.16, f32[512,128]{1,0:T(8,128)} %copy-done.22, f32[512,128]{1,0:T(8,128)} %copy-done.21, f32[512,128]{1,0:T(8,128)} %copy-done.20, f32[6144,128]{1,0:T(8,128)} %spread.2.refs_5_), custom_call_target="tpu_custom_call", output_to_operand_aliasing={{}: (5, {})} | custom-call | tf_op jit(solution)/shard_map/spread/pallas_call | solution.py:306
  (52 shorter events, 0.1 us)
Async XLA Ops:
  0.0 23.5 %collective-permute-start.6 = (f32[6144,128]{1,0:T(8,128)}, f32[6144,128]{1,0:T(8,128)}, u32[]{:S(2)}, u32[]{:S(2)}) collective-permute-start(f32[6144,128]{1,0:T(8,128)} %refs_5_.7), channel_id=1, source_target_pairs={{0,1},{1,0},{2,3},{3,2},{4,5},{5,4},{6,7},{7,6},{8,9},{9,8},{10,11... | collective-permute-start | bytes 9437192 | tf_op jit(solution)/shard_map/ppermute | solution.py:374
  0.5 23.0 %collective-permute-start.5 = (f32[64,6144]{1,0:T(8,128)}, f32[64,6144]{1,0:T(8,128)}, u32[]{:S(2)}, u32[]{:S(2)}) collective-permute-start(f32[64,6144]{1,0:T(8,128)} %refs_4_.11), channel_id=1, source_target_pairs={{0,1},{1,0},{2,3},{3,2},{4,5},{5,4},{6,7},{7,6},{8,9},{9,8},{10,11... | collective-permute-start | bytes 4718600 | tf_op jit(solution)/shard_map/ppermute | solution.py:374
  3.2 20.3 %copy-start = (f32[6144,128]{1,0:T(8,128)S(1)}, f32[6144,128]{1,0:T(8,128)}, u32[]{:S(2)}) copy-start(f32[6144,128]{1,0:T(8,128)} %refs_5_.7) | copy-start | bytes 9437188
  3.2 20.3 %collective-permute-start.4 = (f32[72,1536]{1,0:T(8,128)}, f32[72,1536]{1,0:T(8,128)}, u32[]{:S(2)}, u32[]{:S(2)}) collective-permute-start(f32[72,1536]{1,0:T(8,128)} %select_maximum_fusion), channel_id=1, source_target_pairs={{0,6},{1,7},{6,0},{7,1},{2,2},{3,3},{4,4},{5,5},{8,14},{9,15},{14,... | collective-permute-start | bytes 1327112 | tf_op jit(solution)/shard_map/ppermute | solution.py:339
  17.2 3.3 %collective-permute-start.8 = (f32[256,128]{1,0:T(8,128)}, f32[256,128]{1,0:T(8,128)S(1)}, u32[]{:S(2)}, u32[]{:S(2)}) collective-permute-start(f32[256,128]{1,0:T(8,128)} %get-tuple-element.12.refs_6_.refs_9_.refs_7_), channel_id=1, source_target_pairs={{0,1},{1,0},{2,3},{3,2},{4,5},{5,4},{6,7},{7,6},{8,9},{9,8},{10,11... | collective-permute-start | bytes 393224 | tf_op jit(solution)/shard_map/ppermute | solution.py:374
  17.2 1.6 %collective-permute-start.7 = (f32[64,256]{1,0:T(8,128)}, f32[64,256]{1,0:T(8,128)S(1)}, u32[]{:S(2)}, u32[]{:S(2)}) collective-permute-start(f32[64,256]{1,0:T(8,128)} %get-tuple-element.11.refs_5_.refs_8_.refs_6_), channel_id=1, source_target_pairs={{0,1},{1,0},{2,3},{3,2},{4,5},{5,4},{6,7},{7,6},{8,9},{9,8},{10,11... | collective-permute-start | bytes 196616 | tf_op jit(solution)/shard_map/ppermute | solution.py:374
  18.9 17.7 %collective-permute-start.2 = (f32[72,1536]{1,0:T(8,128)}, f32[72,1536]{1,0:T(8,128)S(1)}, u32[]{:S(2)}, u32[]{:S(2)}) collective-permute-start(f32[72,1536]{1,0:T(8,128)} %select_maximum_fusion), channel_id=1, source_target_pairs={{2,4},{3,5},{4,2},{5,3},{0,0},{1,1},{6,6},{7,7},{10,12},{11,13},{1... | collective-permute-start | bytes 1327112 | tf_op jit(solution)/shard_map/ppermute | solution.py:339
  20.5 17.4 %collective-permute-start = (f32[72,1536]{1,0:T(8,128)}, f32[72,1536]{1,0:T(8,128)S(1)}, u32[]{:S(2)}, u32[]{:S(2)}) collective-permute-start(f32[72,1536]{1,0:T(8,128)} %select_maximum_fusion), channel_id=1, source_target_pairs={{0,2},{1,3},{2,0},{3,1},{4,6},{5,7},{6,4},{7,5},{8,10},{9,11},{10,... | collective-permute-start | bytes 1327112 | tf_op jit(solution)/shard_map/ppermute | solution.py:339
  23.6 1.4 copy-start.1
  25.0 0.9 copy-start.3
  25.9 0.8 copy-start.9
  34.6 23.5 %copy-start.13 = (f32[1024,128]{1,0:T(8,128)}, f32[1024,128]{1,0:T(8,128)S(1)}, u32[]{:S(2)}) copy-start(f32[1024,128]{1,0:T(8,128)S(1)} %pairs.12) | copy-start | bytes 1572868
  34.6 15.7 %collective-permute-start.17 = (f32[1024,128]{1,0:T(8,128)S(1)}, f32[1024,128]{1,0:T(8,128)S(1)}, u32[]{:S(2)}, u32[]{:S(2)}) collective-permute-start(f32[1024,128]{1,0:T(8,128)S(1)} %pairs.12), channel_id=1, source_target_pairs={{0,2},{1,3},{6,4},{7,5},{8,10},{9,11},{14,12},{15,13},{16,18},{17,... | collective-permute-start | bytes 1572872 | tf_op jit(solution)/shard_map/ppermute | solution.py:339
  36.6 39.4 %copy-start.7 = (f32[72,1536]{1,0:T(8,128)}, f32[72,1536]{1,0:T(8,128)S(1)}, u32[]{:S(2)}) copy-start(f32[72,1536]{1,0:T(8,128)S(1)} %collective-permute-done.2.refs_1_.refs_2_) | copy-start | bytes 1327108
  36.6 13.7 %collective-permute-start.3 = (f32[72,1536]{1,0:T(8,128)S(1)}, f32[72,1536]{1,0:T(8,128)S(1)}, u32[]{:S(2)}, u32[]{:S(2)}) collective-permute-start(f32[72,1536]{1,0:T(8,128)S(1)} %collective-permute-done.2.refs_1_.refs_2_), channel_id=1, source_target_pairs={{2,0},{3,1},{4,6},{5,7},{10,8},{11,9},{12,14},{13,15},{18,16},{19,... | collective-permute-start | bytes 1327112 | tf_op jit(solution)/shard_map/ppermute | solution.py:339
  38.0 51.8 %copy-start.5 = (f32[72,1536]{1,0:T(8,128)}, f32[72,1536]{1,0:T(8,128)S(1)}, u32[]{:S(2)}) copy-start(f32[72,1536]{1,0:T(8,128)S(1)} %collective-permute-done.refs_1_.refs_2_) | copy-start | bytes 1327108
  38.0 12.4 %collective-permute-start.1 = (f32[72,1536]{1,0:T(8,128)S(1)}, f32[72,1536]{1,0:T(8,128)S(1)}, u32[]{:S(2)}, u32[]{:S(2)}) collective-permute-start(f32[72,1536]{1,0:T(8,128)S(1)} %collective-permute-done.refs_1_.refs_2_), channel_id=1, source_target_pairs={{2,4},{3,5},{4,2},{5,3},{10,12},{11,13},{12,10},{13,11},{18,20},{1... | collective-permute-start | bytes 1327112 | tf_op jit(solution)/shard_map/ppermute | solution.py:339
  58.1 17.9 %collective-permute-start.20 = (f32[1024,128]{1,0:T(8,128)S(1)}, f32[1024,128]{1,0:T(8,128)S(1)}, u32[]{:S(2)}, u32[]{:S(2)}) collective-permute-start(f32[1024,128]{1,0:T(8,128)S(1)} %pairs.13), channel_id=1, source_target_pairs={{0,2},{1,3},{6,4},{7,5},{8,10},{9,11},{14,12},{15,13},{16,18},{17,... | collective-permute-start | bytes 1572872 | tf_op jit(solution)/shard_map/ppermute | solution.py:339
  63.8 26.0 %collective-permute-start.18 = (f32[1024,128]{1,0:T(8,128)S(1)}, f32[1024,128]{1,0:T(8,128)S(1)}, u32[]{:S(2)}, u32[]{:S(2)}) collective-permute-start(f32[1024,128]{1,0:T(8,128)S(1)} %pairs.13), channel_id=1, source_target_pairs={{2,4},{3,5},{4,2},{5,3},{10,12},{11,13},{12,10},{13,11},{18,20},{1... | collective-permute-start | bytes 1572872 | tf_op jit(solution)/shard_map/ppermute | solution.py:339
  69.1 15.3 %copy-start.11 = (f32[512,128]{1,0:T(8,128)}, f32[512,128]{1,0:T(8,128)S(1)}, u32[]{:S(2)}) copy-start(f32[512,128]{1,0:T(8,128)S(1)} %pairs.8) | copy-start | bytes 786436
  69.1 29.1 %collective-permute-start.9 = (f32[512,128]{1,0:T(8,128)S(1)}, f32[512,128]{1,0:T(8,128)S(1)}, u32[]{:S(2)}, u32[]{:S(2)}) collective-permute-start(f32[512,128]{1,0:T(8,128)S(1)} %pairs.8), channel_id=1, source_target_pairs={{0,2},{1,3},{6,4},{7,5},{8,10},{9,11},{14,12},{15,13},{16,18},{17,... | collective-permute-start | bytes 786440 | tf_op jit(solution)/shard_map/ppermute | solution.py:339
  84.4 35.1 %collective-permute-start.21 = (f32[1024,128]{1,0:T(8,128)}, f32[1024,128]{1,0:T(8,128)}, u32[]{:S(2)}, u32[]{:S(2)}) collective-permute-start(f32[1024,128]{1,0:T(8,128)} %pairs.15), channel_id=1, source_target_pairs={{2,4},{3,5},{4,2},{5,3},{0,0},{1,1},{6,6},{7,7},{10,12},{11,13},{1... | collective-permute-start | bytes 1572872 | tf_op jit(solution)/shard_map/ppermute | solution.py:339
  98.1 13.3 %copy-start.4 = (f32[256,128]{1,0:T(8,128)S(1)}, f32[256,128]{1,0:T(8,128)}, u32[]{:S(2)}) copy-start(f32[256,128]{1,0:T(8,128)} %get-tuple-element.12.refs_6_.refs_9_.refs_7_) | copy-start | bytes 393220
  98.1 13.3 %copy-start.10 = (f32[64,256]{1,0:T(8,128)S(1)}, f32[64,256]{1,0:T(8,128)}, u32[]{:S(2)}) copy-start(f32[64,256]{1,0:T(8,128)} %get-tuple-element.11.refs_5_.refs_8_.refs_6_) | copy-start | bytes 196612
  98.1 21.3 %collective-permute-start.19 = (f32[1024,128]{1,0:T(8,128)}, f32[1024,128]{1,0:T(8,128)}, u32[]{:S(2)}, u32[]{:S(2)}) collective-permute-start(f32[1024,128]{1,0:T(8,128)} %pairs.14), channel_id=1, source_target_pairs={{0,2},{1,3},{2,0},{3,1},{4,6},{5,7},{6,4},{7,5},{8,10},{9,11},{10,... | collective-permute-start | bytes 1572872 | tf_op jit(solution)/shard_map/ppermute | solution.py:339
  103.3 8.1 %collective-permute-start.12 = (f32[512,128]{1,0:T(8,128)}, f32[512,128]{1,0:T(8,128)}, u32[]{:S(2)}, u32[]{:S(2)}) collective-permute-start(f32[512,128]{1,0:T(8,128)} %pairs.9), channel_id=1, source_target_pairs={{0,2},{1,3},{6,4},{7,5},{8,10},{9,11},{14,12},{15,13},{16,18},{17,... | collective-permute-start | bytes 786440 | tf_op jit(solution)/shard_map/ppermute | solution.py:339
  107.9 15.4 %collective-permute-start.10 = (f32[512,128]{1,0:T(8,128)}, f32[512,128]{1,0:T(8,128)S(1)}, u32[]{:S(2)}, u32[]{:S(2)}) collective-permute-start(f32[512,128]{1,0:T(8,128)} %pairs.9), channel_id=1, source_target_pairs={{2,4},{3,5},{4,2},{5,3},{10,12},{11,13},{12,10},{13,11},{18,20},{1... | collective-permute-start | bytes 786440 | tf_op jit(solution)/shard_map/ppermute | solution.py:339
  111.4 1.4 copy-start.2
  112.8 1.0 copy-start.8
  113.8 5.6 %copy-start.14 = (f32[1024,128]{1,0:T(8,128)S(1)}, f32[1024,128]{1,0:T(8,128)}, u32[]{:S(2)}) copy-start(f32[1024,128]{1,0:T(8,128)} %copy-done.13) | copy-start | bytes 1572868
  113.8 9.5 %copy-start.6 = (f32[72,1536]{1,0:T(8,128)S(1)}, f32[72,1536]{1,0:T(8,128)}, u32[]{:S(2)}) copy-start(f32[72,1536]{1,0:T(8,128)} %copy-done.5) | copy-start | bytes 1327108
  118.5 14.4 %collective-permute-start.13 = (f32[512,128]{1,0:T(8,128)S(1)}, f32[512,128]{1,0:T(8,128)S(1)}, u32[]{:S(2)}, u32[]{:S(2)}) collective-permute-start(f32[512,128]{1,0:T(8,128)S(1)} %pairs.11), channel_id=1, source_target_pairs={{2,4},{3,5},{4,2},{5,3},{0,0},{1,1},{6,6},{7,7},{10,12},{11,13},{1... | collective-permute-start | bytes 786440 | tf_op jit(solution)/shard_map/ppermute | solution.py:339
  120.8 11.6 %copy-start.15 = (f32[1024,128]{1,0:T(8,128)}, f32[1024,128]{1,0:T(8,128)S(1)}, u32[]{:S(2)}) copy-start(f32[1024,128]{1,0:T(8,128)S(1)} %select_add_fusion.refs_1_) | copy-start | bytes 1572868
  120.8 15.5 %copy-start.12 = (f32[512,128]{1,0:T(8,128)S(1)}, f32[512,128]{1,0:T(8,128)}, u32[]{:S(2)}) copy-start(f32[512,128]{1,0:T(8,128)} %copy-done.11) | copy-start | bytes 786436
  120.8 17.6 %collective-permute-start.24 = (f32[1024,128]{1,0:T(8,128)S(1)}, f32[1024,128]{1,0:T(8,128)S(1)}, u32[]{:S(2)}, u32[]{:S(2)}) collective-permute-start(f32[1024,128]{1,0:T(8,128)S(1)} %select_add_fusion.refs_1_), channel_id=1, source_target_pairs={{0,24},{8,16},{16,8},{24,0},{1,25},{9,17},{17,9},{25,1},{2,26},{10... | collective-permute-start | bytes 1572872 | tf_op jit(solution)/shard_map/ppermute | solution.py:412
  127.6 8.6 %collective-permute-start.11 = (f32[512,128]{1,0:T(8,128)S(1)}, f32[512,128]{1,0:T(8,128)S(1)}, u32[]{:S(2)}, u32[]{:S(2)}) collective-permute-start(f32[512,128]{1,0:T(8,128)S(1)} %pairs.10), channel_id=1, source_target_pairs={{0,2},{1,3},{2,0},{3,1},{4,6},{5,7},{6,4},{7,5},{8,10},{9,11},{10,... | collective-permute-start | bytes 786440 | tf_op jit(solution)/shard_map/ppermute | solution.py:339
  131.9 18.9 %collective-permute-start.23 = (f32[1024,128]{1,0:T(8,128)S(1)}, f32[1024,128]{1,0:T(8,128)S(1)}, u32[]{:S(2)}, u32[]{:S(2)}) collective-permute-start(f32[1024,128]{1,0:T(8,128)S(1)} %select_add_fusion.refs_1_), channel_id=1, source_target_pairs={{0,16},{8,24},{16,0},{24,8},{1,17},{9,25},{17,1},{25,9},{2,18},{10... | collective-permute-start | bytes 1572872 | tf_op jit(solution)/shard_map/ppermute | solution.py:412
  132.4 18.5 %collective-permute-start.22 = (f32[1024,128]{1,0:T(8,128)S(1)}, f32[1024,128]{1,0:T(8,128)S(1)}, u32[]{:S(2)}, u32[]{:S(2)}) collective-permute-start(f32[1024,128]{1,0:T(8,128)S(1)} %select_add_fusion.refs_1_), channel_id=1, source_target_pairs={{0,8},{8,0},{16,24},{24,16},{1,9},{9,1},{17,25},{25,17},{2,10},{10... | collective-permute-start | bytes 1572872 | tf_op jit(solution)/shard_map/ppermute | solution.py:412
  136.3 19.1 %copy-start.16 = (f32[512,128]{1,0:T(8,128)}, f32[512,128]{1,0:T(8,128)S(1)}, u32[]{:S(2)}) copy-start(f32[512,128]{1,0:T(8,128)S(1)} %select_add_fusion.1.refs_1_) | copy-start | bytes 786436
  136.3 19.1 %collective-permute-start.16 = (f32[512,128]{1,0:T(8,128)S(1)}, f32[512,128]{1,0:T(8,128)S(1)}, u32[]{:S(2)}, u32[]{:S(2)}) collective-permute-start(f32[512,128]{1,0:T(8,128)S(1)} %select_add_fusion.1.refs_1_), channel_id=1, source_target_pairs={{0,24},{8,16},{16,8},{24,0},{1,25},{9,17},{17,9},{25,1},{2,26},{10... | collective-permute-start | bytes 786440 | tf_op jit(solution)/shard_map/ppermute | solution.py:412
  136.8 18.5 %collective-permute-start.15 = (f32[512,128]{1,0:T(8,128)S(1)}, f32[512,128]{1,0:T(8,128)S(1)}, u32[]{:S(2)}, u32[]{:S(2)}) collective-permute-start(f32[512,128]{1,0:T(8,128)S(1)} %select_add_fusion.1.refs_1_), channel_id=1, source_target_pairs={{0,16},{8,24},{16,0},{24,8},{1,17},{9,25},{17,1},{25,9},{2,18},{10... | collective-permute-start | bytes 786440 | tf_op jit(solution)/shard_map/ppermute | solution.py:412
  138.3 12.5 %copy-start.17 = (f32[1024,128]{1,0:T(8,128)}, f32[1024,128]{1,0:T(8,128)S(1)}, u32[]{:S(2)}) copy-start(f32[1024,128]{1,0:T(8,128)S(1)} %collective-permute-done.24.refs_4_) | copy-start | bytes 1572868
  138.4 17.0 %collective-permute-start.14 = (f32[512,128]{1,0:T(8,128)S(1)}, f32[512,128]{1,0:T(8,128)S(1)}, u32[]{:S(2)}, u32[]{:S(2)}) collective-permute-start(f32[512,128]{1,0:T(8,128)S(1)} %select_add_fusion.1.refs_1_), channel_id=1, source_target_pairs={{0,8},{8,0},{16,24},{24,16},{1,9},{9,1},{17,25},{25,17},{2,10},{10... | collective-permute-start | bytes 786440 | tf_op jit(solution)/shard_map/ppermute | solution.py:412
  150.8 0.8 copy-start.18
  151.7 0.8 copy-start.19
  155.4 0.7 copy-start.20
  155.4 0.8 copy-start.21
  156.2 0.7 copy-start.22

commit v2 on v1

--- a/solution.py
+++ b/solution.py
@@ -7,6 +7,7 @@
 from jax.experimental import pallas as pl
 from jax.experimental.pallas import tpu as pltpu
 from jax.sharding import PartitionSpec as P
+
 
 F32 = jnp.float32
 BF16 = jnp.bfloat16
@@ -69,18 +70,13 @@
         for side, (pts, wts, _, _) in enumerate(sides):
             for c in range(capacity):
                 slot = side * capacity + c
-                n = (row * devices + place_ref[1 + side]) * capacity + c
-                start = pl.multiple_of(listed(n) * leaf, leaf)
+                source = listed((row * devices + place_ref[1 + side]) * capacity + c)
                 copies.append((
                     pltpu.make_async_copy(
-                        pts.at[:, pl.ds(start, leaf)],
-                        y_buf.at[buffer, slot],
-                        sem.at[buffer, slot, 0],
+                        pts.at[source], y_buf.at[buffer, slot], sem.at[buffer, slot, 0]
                     ),
                     pltpu.make_async_copy(
-                        wts.at[pl.ds(start, leaf), :],
-                        w_buf.at[buffer, slot],
-                        sem.at[buffer, slot, 1],
+                        wts.at[source], w_buf.at[buffer, slot], sem.at[buffer, slot, 1]
                     ),
                 ))
         return copies
@@ -118,16 +114,15 @@
     else:
         out_ref[...] = init_ref[...]
 
-    def add(y, w):
-        yk = stacked(y, None, scale, False).astype(BF16)
-        w_high, w_low = two_terms(w)
-        wk = jnp.concatenate([w_high, w_low], axis=1).astype(BF16)
+    def add(yk, wk, gain):
         wk = jnp.concatenate([wk, wk], axis=0)
-        columns = w.shape[1]
+        columns = out_ref.shape[1]
         for t in range(0, leaf, plan["rows"]):
             part = slice(t, t + plan["rows"])
             exponent = jnp.dot(xk_buf[part, :], yk, preferred_element_type=F32)
             value = jnp.exp2(exponent)
+            if gain is not None:
+                value = value * gain
             high = value.astype(BF16)
             low = (value - high.astype(F32)).astype(BF16)
             both = jnp.dot(
@@ -135,7 +130,7 @@
             )
             out_ref[part, :] += both[:, :columns] + both[:, columns:]
 
-    flags = None
+    gains = [None] * (slots + 1)
     if not plan["dense"]:
         number = leaf_number(step)
         base = plan["rows_listed"] * devices * capacity
@@ -146,37 +141,31 @@
         def among(value, options):
             return sum((option == value).astype(F32) for option in options)
 
-        flags = []
+        gains = []
         for side in range(2):
             owner = place_ref[1 + side]
-            flags += [among(owner * capacity + c, near) for c in range(capacity)]
-        flags += [among(place_ref[1 + side], far) for side in range(2)]
-
-    def flagged(w, n):
-        return w if flags is None else w * flags[n]
+            gains += [among(owner * capacity + c, near) for c in range(capacity)]
+        own, partner = (among(place_ref[1 + side], far) for side in range(2))
+        first_half = lax.broadcasted_iota(jnp.int32, (1, 2 * kept), 1) < kept
+        gains.append(jnp.where(first_half, own, partner))
 
     @pl.when(step == 0)
     def _():
         for copy in skel_copies:
             copy.wait()
 
-    ws = ws_buf[...]
-    if flags is not None:
-        ws = jnp.concatenate(
-            [flagged(ws[:kept], slots), flagged(ws[kept:], slots + 1)], axis=0
-        )
-    add(ys_buf[...], ws)
+    add(ys_buf[...], ws_buf[...], gains[slots])
     for slot, pair in enumerate(near_copies(step, half)):
         pair[0].wait()
         pair[1].wait()
-        add(y_buf[half, slot], flagged(w_buf[half, slot], slot))
+        add(y_buf[half, slot], w_buf[half, slot], gains[slot])
 
 
 def pairs(sizes, place, parcels, init, sources, first, count):
     own = sources[0]
-    features = own[0].shape[0]
-    columns = own[1].shape[1]
-    leaf = sizes["leaf"]
+    rows, leaf = own[0].shape[1:]
+    features = rows // 4
+    columns = own[1].shape[2] // 2
     slots = 2 * sizes["capacity"]
     kept = own[2].shape[1]
     plan = dict(
@@ -196,7 +185,7 @@
     if init is not None:
         in_specs.append(pl.BlockSpec((leaf, columns), lambda i: (i, 0)))
         operands.append(init)
-    in_specs += [pl.BlockSpec(memory_space=pl.ANY)] * 8
+    in_specs += [pl.BlockSpec(memory_space=pltpu.HBM)] * 8
     operands += [array for side in sources for array in side]
     work = count * leaf * (leaf * slots + 2 * kept)
     return pl.pallas_call(
@@ -206,15 +195,15 @@
         out_specs=pl.BlockSpec((leaf, columns), lambda i: (i, 0)),
         out_shape=jax.ShapeDtypeStruct((count * leaf, columns), F32),
         scratch_shapes=[
-            pltpu.VMEM((2, slots, features, leaf), F32),
-            pltpu.VMEM((2, slots, leaf, columns), F32),
-            pltpu.VMEM((features, 2 * kept), F32),
-            pltpu.VMEM((2 * kept, columns), F32),
-            pltpu.VMEM((leaf, 4 * features), BF16),
+            pltpu.VMEM((2, slots, rows, leaf), BF16),
+            pltpu.VMEM((2, slots, leaf, 2 * columns), BF16),
+            pltpu.VMEM((rows, 2 * kept), BF16),
+            pltpu.VMEM((2 * kept, 2 * columns), BF16),
+            pltpu.VMEM((leaf, rows), BF16),
             pltpu.SemaphoreType.DMA((2, slots, 2)),
             pltpu.SemaphoreType.DMA((2, 2)),
         ],
-        compiler_params=pltpu.CompilerParams(vmem_limit_bytes=32 << 20),
+        compiler_params=pltpu.CompilerParams(vmem_limit_bytes=58 << 20),
         cost_estimate=pl.CostEstimate(
             flops=work * 2 * (4 * features + 4 * columns),
             bytes_accessed=count * slots * leaf * (features + columns) * 4,
@@ -224,62 +213,113 @@
     )(*operands)
 
 
-def skeleton_kernel(idx_ref, points_ref, weights_ref, proj_ref, coords_ref, summed_ref):
+def source_rows(coords, scale):
+    return stacked(coords, None, scale, False).astype(BF16)
+
+
+def value_columns(values):
+    return jnp.concatenate(two_terms(values), axis=1).astype(BF16)
+
+
+def write_sources(points_ref, weights_ref, y_ref, w_ref, scale):
+    leaves, _, leaf = y_ref.shape
+    for n in range(leaves):
+        part = slice(n * leaf, (n + 1) * leaf)
+        y_ref[n] = source_rows(points_ref[:, part], scale)
+        w_ref[n] = value_columns(weights_ref[part, :])
+
+
+def own_kernel(scale, idx_ref, points_ref, weights_ref, proj_ref, y_ref, w_ref, ys_ref, ws_ref,
+               coords_ref, summed_ref):
     step = pl.program_id(0)
-    count = points_ref.shape[1]
+    features, count = points_ref.shape
 
     @pl.when(step == 0)
     def _():
         coords_ref[...] = jnp.zeros_like(coords_ref)
         summed_ref[...] = jnp.zeros_like(summed_ref)
 
+    write_sources(points_ref, weights_ref, y_ref, w_ref, scale)
     place = lax.broadcasted_iota(jnp.int32, (count, idx_ref.shape[1]), 0) + step * count
     chosen = jnp.where(place == idx_ref[...], 1.0, 0.0).astype(BF16)
-    features = points_ref.shape[0]
     terms = jnp.concatenate(three_terms(points_ref[...]), axis=0).astype(BF16)
     picked = jnp.dot(terms, chosen, preferred_element_type=F32)
     coords_ref[...] += (
         picked[:features] + picked[features : 2 * features] + picked[2 * features :]
     )
-    w_high, w_low = two_terms(weights_ref[...])
     p_high, p_low = two_terms(proj_ref[...])
-    columns = w_high.shape[1]
+    columns = weights_ref.shape[1]
+    values = jnp.concatenate([w_ref[n] for n in range(w_ref.shape[0])], axis=0)
     both = jnp.dot(
         jnp.concatenate([p_high, p_low], axis=1).astype(BF16),
-        jnp.concatenate([jnp.concatenate([w_high, w_low], axis=1)] * 2, axis=0).astype(BF16),
+        jnp.concatenate([values, values], axis=0),
         preferred_element_type=F32,
     )
     summed_ref[...] += both[:, :columns] + both[:, columns:]
 
-
-def skeleton(points, weights, proj, skel_idx, block):
+    @pl.when(step == pl.num_programs(0) - 1)
+    def _():
+        ys_ref[...] = source_rows(coords_ref[...], scale)
+        ws_ref[...] = value_columns(summed_ref[...])
+
+
+def other_kernel(scale, points_ref, weights_ref, coords_ref, summed_ref, y_ref, w_ref, ys_ref, ws_ref):
+    write_sources(points_ref, weights_ref, y_ref, w_ref, scale)
+
+    @pl.when(pl.program_id(0) == 0)
+    def _():
+        ys_ref[...] = source_rows(coords_ref[...], scale)
+        ws_ref[...] = value_columns(summed_ref[...])
+
+
+def prepared(points, weights, leaf, scale, proj=None, skel_idx=None, skel=None):
     features, count = points.shape
     columns = weights.shape[1]
-    kept = proj.shape[0]
-    return pl.pallas_call(
-        skeleton_kernel,
-        grid=(count // block,),
-        in_specs=[
-            pl.BlockSpec((1, kept), lambda i: (0, 0)),
-            pl.BlockSpec((features, block), lambda i: (0, i)),
-            pl.BlockSpec((block, columns), lambda i: (i, 0)),
-            pl.BlockSpec((kept, block), lambda i: (0, i)),
-        ],
-        out_specs=[
-            pl.BlockSpec((features, kept), lambda i: (0, 0)),
-            pl.BlockSpec((kept, columns), lambda i: (0, 0)),
-        ],
-        out_shape=[
+    kept = (proj if skel is None else skel[1]).shape[0]
+    leaves = math.gcd(count // leaf, 2)
+    block = leaves * leaf
+    whole = lambda *shape: pl.BlockSpec(shape, lambda i: (0,) * len(shape))
+    in_specs = [
+        pl.BlockSpec((features, block), lambda i: (0, i)),
+        pl.BlockSpec((block, columns), lambda i: (i, 0)),
+    ]
+    out_specs = [
+        pl.BlockSpec((leaves, 4 * features, leaf), lambda i: (i, 0, 0)),
+        pl.BlockSpec((leaves, leaf, 2 * columns), lambda i: (i, 0, 0)),
+        whole(4 * features, kept),
+        whole(kept, 2 * columns),
+    ]
+    out_shape = [
+        pltpu.HBM((count // leaf, 4 * features, leaf), BF16),
+        pltpu.HBM((count // leaf, leaf, 2 * columns), BF16),
+        pltpu.HBM((4 * features, kept), BF16),
+        pltpu.HBM((kept, 2 * columns), BF16),
+    ]
+    moved = 12 * count * (features + columns)
+    if skel is None:
+        in_specs = [whole(1, kept), *in_specs, pl.BlockSpec((kept, block), lambda i: (0, i))]
+        out_specs += [whole(features, kept), whole(kept, columns)]
+        out_shape += [
             jax.ShapeDtypeStruct((features, kept), F32),
             jax.ShapeDtypeStruct((kept, columns), F32),
-        ],
+        ]
+        operands = (skel_idx, points, weights, proj)
+        body, moved = own_kernel, moved + 4 * count * kept
+    else:
+        in_specs += [whole(features, kept), whole(kept, columns)]
+        operands = (points, weights, *skel)
+        body = other_kernel
+    return pl.pallas_call(
+        functools.partial(body, scale),
+        grid=(count // block,),
+        in_specs=in_specs,
+        out_specs=out_specs,
+        out_shape=out_shape,
         cost_estimate=pl.CostEstimate(
-            flops=2 * kept * count * columns * 4,
-            bytes_accessed=4 * count * (features + columns + kept),
-            transcendentals=0,
+            flops=8 * kept * count * columns, bytes_accessed=moved, transcendentals=0
         ),
-        name="skeleton",
-    )(skel_idx, points, weights, proj)
+        name="prepared",
+    )(*operands)
 
 
 def spread_kernel(groups, per, first, leaf, aliased, *refs):
@@ -318,7 +358,6 @@
 
 def on_device(points, weights, proj, fetch_table, near_list, far_list, skel_idx):
     features, column_points = points.shape
-    columns = weights.shape[1]
     devices = lax.axis_size("dev")
     groups = lax.axis_size("grp")
     targets = near_list.shape[0]
@@ -368,10 +407,15 @@
         "scale": scale,
     }
 
-    def with_partner(skel_block):
-        skel, skel_w = skeleton(points, weights, proj, skel_idx, skel_block)
-        own = (points, weights, skel, skel_w)
-        return own, tuple(lax.ppermute(array, "dev", swap) for array in own)
+    def to_partner(array):
+        return lax.ppermute(array, "dev", swap)
+
+    def make_sources():
+        other_points, other_weights = to_partner(points), to_partner(weights)
+        *own, skel, skel_w = prepared(points, weights, leaf, scale, proj, skel_idx)
+        skel = (to_partner(skel), to_partner(skel_w))
+        other = prepared(other_points, other_weights, leaf, scale, skel=skel)
+        return tuple(own), tuple(other)
 
     if chips == 4:
         chip = device // 2
@@ -384,8 +428,17 @@
         cross = [(1, 2), (2, 1)]
         of_a, of_c, of_d = shift(parcel, ends), shift(parcel, sides), shift(parcel, middle)
         of_b = (shift(of_c, cross), shift(of_d, outward))
-        sources = with_partner(width)
-        work = lambda got, init, k: pairs(sizes, place, got, init, sources, *chunks[k])
+        sources = make_sources()
+        before = None
+
+        def work(got, init, k):
+            nonlocal before
+            spot = place
+            if before is not None:
+                spot, _ = lax.optimization_barrier((place, before))
+            before = pairs(sizes, spot, got, init, sources, *chunks[k])
+            return before
+
         every = range(len(chunks))
         a = [work((of_a,), None, k) for k in every]
         b = [work(of_b, shift(a[k], inward), k) for k in every]
@@ -396,7 +449,7 @@
             own = jnp.where(inner, a[k], 0.0)
             done.append(shift(c, sides) + shift(d, middle) + own)
     else:
-        sources = with_partner(width)
+        sources = make_sources()
         total = None
         for r in range(chips):
             got = shift(parcel, [(z, (z - r) % chips) for z in range(chips)])

time: 161 us -> 182 us (1.13)
  Pallas kernels: 62.8 us -> 84.4 us
    pallas_call x8, Pallas kernels: 50.9 us -> 63 us  [pairs(): pl.pallas_call(functools.partial(pair_kernel, plan), grid=(count,), in_sp...]
    ppermute x6, waiting for transfers between devices: 10.4 us -> 20.8 us  [on_device(): lax.ppermute(piece, 'grp', [(g, g ^ m) for g in range(groups)])]
    ppermute x15, waiting for transfers between devices: 21.7 us -> 11.3 us  [shift(): return lax.ppermute(array, 'dev', along(moves))]
    pallas_call x1 -> x2, Pallas kernels: 6.76 us -> 16.4 us  [prepared(): pl.pallas_call(functools.partial(body, scale), grid=(count // block,), in...]
    unnamed x47 -> x51, local copies, waits for them, and re-layouts: 9.49 us -> 11 us
  transfers between devices with their start and end apart: 25 -> 25, of which waited for: 6 -> 4; matrix products, arithmetic and copies ran while one was open for 3% -> 2% of each run, Pallas kernels for 33% -> 40%
where the time goes in v2:
time: 182 us; the launch traced here: 181 us
  Pallas kernels  84.4 us (46%)
  starting transfers between devices  50.2 us (28%)
  waiting for transfers between devices  32.7 us (18%)
  local copies, waits for them, and re-layouts  12.1 us (7%)
    pallas_call x8, Pallas kernels, pairs(): pl.pallas_call(functools.partial(pair_kernel, plan), grid=(count,), in_sp...  63 us
    ppermute x15, starting transfers between devices, shift(): return lax.ppermute(array, 'dev', along(moves))  42 us
    ppermute x6, waiting for transfers between devices, on_device(): lax.ppermute(piece, 'grp', [(g, g ^ m) for g in range(groups)])  20.8 us
    pallas_call x2, Pallas kernels, prepared(): pl.pallas_call(functools.partial(body, scale), grid=(count // block,), in...  16.4 us
    ppermute x15, waiting for transfers between devices, shift(): return lax.ppermute(array, 'dev', along(moves))  11.3 us
    unnamed x51, local copies, waits for them, and re-layouts  11 us
    ppermute x6, starting transfers between devices, on_device(): lax.ppermute(piece, 'grp', [(g, g ^ m) for g in range(groups)])  7.11 us
    pallas_call x2, Pallas kernels, spread(): pl.pallas_call(functools.partial(spread_kernel, groups, per, first, leaf,...  5.07 us
  transfers between devices with their start and end apart: 25, of which 4 were waited for; matrix products, arithmetic and copies ran while one was open for 2% of the time, Pallas kernels for 40%

profile of v2, /device:TPU:0, one launch (start us, length us, event | category | flops | bytes accessed | tf_op | source)
XLA Modules:
  0.0 181.5 jit_solution(3351329643083856815)
XLA Ops:
  0.0 0.5 collective-permute-start.2
  0.5 0.0 collective-permute-start.1
  0.5 0.8 copy.8
  1.3 0.1 reshape.5
  1.4 1.0 constant_dynamic-slice_fusion
  2.5 7.0 %collective-permute-start = (f32[72,1536]{1,0:T(8,128)S(1)}, f32[72,1536]{1,0:T(8,128)S(1)}, u32[]{:S(2)}, u32[]{:S(2)}) collective-permute-start(f32[72,1536]{1,0:T(8,128)S(1)} %select_maximum_fusion), channel_id=1, source_target_pairs={{0,6},{1,7},{6,0},{7,1},{2,2},{3,3},{4,4},{5,5},{8,14},{9,15},{14,... | collective-permute-start | bytes 1327112 | tf_op jit(solution)/shard_map/ppermute | solution.py:378
  9.5 9.8 %prepared.2 = (bf16[12,256,512]{2,1,0:T(8,128)(2,1)}, bf16[12,512,256]{2,1,0:T(8,128)(2,1)}, bf16[256,256]{1,0:T(8,128)(2,1)}, bf16[256,256]{1,0:T(8,128)(2,1)}, f32[64,256]{1,0:T(8,128)}, /*index=5*/f32[256,128]{1,0:T(8,128)}) custom-call(s32[1,256]{1,0:T(1,128)} %idx_ref.1, f32[64,6144]{1,0:T(8,128)} %points_ref.1, f32[6144,128]{1,0:T(8,128)} %weights_ref.1, ...), custom_call_target="tpu_custom_call" | custom-call | flops 1610612736 | bytes 20447232 | tf_op jit(solution)/shard_map/prepared/pallas_call | solution.py:312
  19.2 0.1 collective-permute-start.4
  19.3 0.5 collective-permute-start.3
  19.8 0.7 pad_add_fusion.refs_0_
  20.5 0.5 collective-permute-done.3.coords_ref
  21.0 0.0 collective-permute-start.5
  21.0 0.0 collective-permute-done.4.summed_ref
  21.0 0.7 collective-permute-start.7
  21.7 0.0 collective-permute-done.2.weights_ref
  21.7 1.1 copy-done.22
  22.8 6.6 %prepared.3 = (bf16[12,256,512]{2,1,0:T(8,128)(2,1)}, bf16[12,512,256]{2,1,0:T(8,128)(2,1)}, bf16[256,256]{1,0:T(8,128)(2,1)}, bf16[256,256]{1,0:T(8,128)(2,1)}) custom-call(f32[64,6144]{1,0:T(8,128)} %copy-done.22, f32[6144,128]{1,0:T(8,128)} %collective-permute-done.2.weights_ref, f32[64,256]{1,0:T(8,128)} %copy-done.24, f32[256,128]{1,0:T(8,128)} %copy-done.23), custom_call_target="tpu_custom_call" | custom-call | flops 1610612736 | bytes 14155776 | tf_op jit(solution)/shard_map/prepared/pallas_call | solution.py:312
  29.4 0.0 collective-permute-done.refs_1_.refs_2_
  29.4 0.8 copy-done.5
  30.2 9.3 %pairs.8 = f32[1024,128]{1,0:T(8,128)} custom-call(s32[3]{0:T(128)} %pad_add_fusion.refs_0_, f32[72,1536]{1,0:T(8,128)} %copy-done.5, f32[72,1536]{1,0:T(8,128)} %copy-done.5, bf16[12,256,512]{2,1,0:T(8,128)(2,1)} %get-tuple-element.26.refs_3_.refs_6_.refs_4_, bf16[12,512,256]{2,1,0:T(8,128)(2,1)} %get-tuple-element.27.refs_4_.refs_7_.refs_5_, ...), custom_call_target="tpu_custom_call" | custom-call | flops 4026531840 | bytes 3145728 | tf_op jit(solution)/shard_map/pairs/pallas_call | solution.py:191
  39.5 5.2 %collective-permute-start.9 = (f32[1024,128]{1,0:T(8,128)}, f32[1024,128]{1,0:T(8,128)S(1)}, u32[]{:S(2)}, u32[]{:S(2)}) collective-permute-start(f32[1024,128]{1,0:T(8,128)} %pairs.8), channel_id=1, source_target_pairs={{0,2},{1,3},{6,4},{7,5},{8,10},{9,11},{14,12},{15,13},{16,18},{17,... | collective-permute-start | bytes 1572872 | tf_op jit(solution)/shard_map/ppermute | solution.py:378
  44.7 0.7 collective-permute-start.6
  45.5 1.3 collective-permute-start.8
  46.8 6.2 %pairs.9 = f32[512,128]{1,0:T(8,128)} custom-call(s32[3]{0:T(128)} %pad_add_fusion.refs_0_, f32[72,1536]{1,0:T(8,128)} %copy-done.5, f32[72,1536]{1,0:T(8,128)} %copy-done.5, bf16[12,256,512]{2,1,0:T(8,128)(2,1)} %get-tuple-element.26.refs_3_.refs_6_.refs_4_, bf16[12,512,256]{2,1,0:T(8,128)(2,1)} %get-tuple-element.27.refs_4_.refs_7_.refs_5_, ...), custom_call_target="tpu_custom_call" | custom-call | flops 2013265920 | bytes 1572864 | tf_op jit(solution)/shard_map/pairs/pallas_call | solution.py:191
  53.0 6.2 %collective-permute-done.8.refs_2_.refs_4_ = f32[72,1536]{1,0:T(8,128)S(1)} collective-permute-done((f32[72,1536]{1,0:T(8,128)S(1)}, f32[72,1536]{1,0:T(8,128)S(1)}, u32[]{:S(2)}, u32[]{:S(2)}) %collective-permute-start.8) | collective-permute-done | bytes 442400 | tf_op jit(solution)/shard_map/ppermute | solution.py:378
  59.2 0.8 copy-done.1
  60.0 0.8 copy-done.9
  60.8 9.5 %pairs.10 = f32[1024,128]{1,0:T(8,128)} custom-call(s32[3]{0:T(128)} %pad_add_fusion.refs_0_, f32[72,1536]{1,0:T(8,128)} %copy-done, f32[72,1536]{1,0:T(8,128)} %copy-done.1, f32[72,1536]{1,0:T(8,128)} %copy-done, f32[72,1536]{1,0:T(8,128)} %copy-done.1, f32[1024,128]{1,0:T(8,128)} %copy-done.9, ...), custom_call_target="tpu_custom_call" | custom-call | flops 4026531840 | bytes 3145728 | tf_op jit(solution)/shard_map/pairs/pallas_call | solution.py:191
  70.3 0.7 collective-permute-start.11
  71.0 4.4 %collective-permute-start.10 = (f32[512,128]{1,0:T(8,128)S(1)}, f32[512,128]{1,0:T(8,128)S(1)}, u32[]{:S(2)}, u32[]{:S(2)}) collective-permute-start(f32[512,128]{1,0:T(8,128)S(1)} %copy-done.6), channel_id=1, source_target_pairs={{0,2},{1,3},{6,4},{7,5},{8,10},{9,11},{14,12},{15,13},{16,18},{17,... | collective-permute-start | bytes 786440 | tf_op jit(solution)/shard_map/ppermute | solution.py:378
  75.4 1.5 collective-permute-start.12
  76.9 5.2 %collective-permute-done.10.refs_5_ = f32[512,128]{1,0:T(8,128)S(1)} collective-permute-done((f32[512,128]{1,0:T(8,128)S(1)}, f32[512,128]{1,0:T(8,128)S(1)}, u32[]{:S(2)}, u32[]{:S(2)}) %collective-permute-start.10) | collective-permute-done | bytes 262176 | tf_op jit(solution)/shard_map/ppermute | solution.py:378
  82.1 0.7 copy-done.18
  82.8 6.4 %pairs.11 = f32[512,128]{1,0:T(8,128)} custom-call(s32[3]{0:T(128)} %pad_add_fusion.refs_0_, f32[72,1536]{1,0:T(8,128)} %copy-done, f32[72,1536]{1,0:T(8,128)} %copy-done.1, f32[72,1536]{1,0:T(8,128)} %copy-done, f32[72,1536]{1,0:T(8,128)} %copy-done.1, f32[512,128]{1,0:T(8,128)} %copy-done.18, ...), custom_call_target="tpu_custom_call" | custom-call | flops 2013265920 | bytes 1572864 | tf_op jit(solution)/shard_map/pairs/pallas_call | solution.py:191
  89.2 0.8 copy-done.11
  90.0 9.5 %pairs.12 = f32[1024,128]{1,0:T(8,128)} custom-call(s32[3]{0:T(128)} %pad_add_fusion.refs_0_, f32[72,1536]{1,0:T(8,128)} %copy-done.3, f32[72,1536]{1,0:T(8,128)} %copy-done.3, f32[1024,128]{1,0:T(8,128)} %copy-done.11, bf16[12,256,512]{2,1,0:T(8,128)(2,1)} %get-tuple-element.26.refs_3_.refs_6_.refs_4_, ...), custom_call_target="tpu_custom_call" | custom-call | flops 4026531840 | bytes 3145728 | tf_op jit(solution)/shard_map/pairs/pallas_call | solution.py:191
  99.4 2.5 %collective-permute-start.20 = (f32[1024,128]{1,0:T(8,128)}, f32[1024,128]{1,0:T(8,128)S(1)}, u32[]{:S(2)}, u32[]{:S(2)}) collective-permute-start(f32[1024,128]{1,0:T(8,128)} %pairs.12), channel_id=1, source_target_pairs={{0,2},{1,3},{2,0},{3,1},{4,6},{5,7},{6,4},{7,5},{8,10},{9,11},{10,... | collective-permute-start | bytes 1572872 | tf_op jit(solution)/shard_map/ppermute | solution.py:378
  102.0 0.8 copy-done.10
  102.8 9.4 %pairs.13 = f32[1024,128]{1,0:T(8,128)} custom-call(s32[3]{0:T(128)} %pad_add_fusion.refs_0_, f32[72,1536]{1,0:T(8,128)} %copy-done.2, f32[72,1536]{1,0:T(8,128)} %copy-done.2, f32[1024,128]{1,0:T(8,128)} %copy-done.10, bf16[12,256,512]{2,1,0:T(8,128)(2,1)} %get-tuple-element.26.refs_3_.refs_6_.refs_4_, ...), custom_call_target="tpu_custom_call" | custom-call | flops 4026531840 | bytes 3145728 | tf_op jit(solution)/shard_map/pairs/pallas_call | solution.py:191
  112.2 1.7 collective-permute-start.21
  113.9 0.7 collective-permute-start.13
  114.6 5.8 %collective-permute-start.15 = (f32[512,128]{1,0:T(8,128)S(1)}, f32[512,128]{1,0:T(8,128)S(1)}, u32[]{:S(2)}, u32[]{:S(2)}) collective-permute-start(f32[512,128]{1,0:T(8,128)S(1)} %copy-done.15), channel_id=1, source_target_pairs={{0,2},{1,3},{6,4},{7,5},{8,10},{9,11},{14,12},{15,13},{16,18},{17,... | collective-permute-start | bytes 786440 | tf_op jit(solution)/shard_map/ppermute | solution.py:378
  120.4 0.7 copy-done.16
  121.1 6.3 %pairs.14 = f32[512,128]{1,0:T(8,128)} custom-call(s32[3]{0:T(128)} %pad_add_fusion.refs_0_, f32[72,1536]{1,0:T(8,128)} %copy-done.3, f32[72,1536]{1,0:T(8,128)} %copy-done.3, f32[512,128]{1,0:T(8,128)} %copy-done.16, bf16[12,256,512]{2,1,0:T(8,128)(2,1)} %get-tuple-element.26.refs_3_.refs_6_.refs_4_, ...), custom_call_target="tpu_custom_call" | custom-call | flops 2013265920 | bytes 1572864 | tf_op jit(solution)/shard_map/pairs/pallas_call | solution.py:191
  127.5 8.3 %collective-permute-start.14 = (f32[512,128]{1,0:T(8,128)}, f32[512,128]{1,0:T(8,128)S(1)}, u32[]{:S(2)}, u32[]{:S(2)}) collective-permute-start(f32[512,128]{1,0:T(8,128)} %pairs.14), channel_id=1, source_target_pairs={{0,2},{1,3},{2,0},{3,1},{4,6},{5,7},{6,4},{7,5},{8,10},{9,11},{10,... | collective-permute-start | bytes 786440 | tf_op jit(solution)/shard_map/ppermute | solution.py:378
  135.8 0.1 select_add_fusion.refs_1_
  135.9 1.6 collective-permute-start.22
  137.5 0.7 copy-done.17
  138.1 6.3 %pairs.15 = f32[512,128]{1,0:T(8,128)} custom-call(s32[3]{0:T(128)} %pad_add_fusion.refs_0_, f32[72,1536]{1,0:T(8,128)} %copy-done.2, f32[72,1536]{1,0:T(8,128)} %copy-done.2, f32[512,128]{1,0:T(8,128)} %copy-done.17, bf16[12,256,512]{2,1,0:T(8,128)(2,1)} %get-tuple-element.26.refs_3_.refs_6_.refs_4_, ...), custom_call_target="tpu_custom_call" | custom-call | flops 2013265920 | bytes 1572864 | tf_op jit(solution)/shard_map/pairs/pallas_call | solution.py:191
  144.5 1.6 collective-permute-start.16
  146.1 1.5 collective-permute-start.23
  147.6 0.5 collective-permute-start.24
  148.2 1.6 collective-permute-start.17
  149.7 1.5 collective-permute-start.18
  151.2 0.5 collective-permute-start.19
  151.7 0.5 iota_xor_fusion.refs_0_
  152.2 20.8 %collective-permute-done.23.refs_3_ = f32[1024,128]{1,0:T(8,128)S(1)} collective-permute-done((f32[1024,128]{1,0:T(8,128)S(1)}, f32[1024,128]{1,0:T(8,128)S(1)}, u32[]{:S(2)}, u32[]{:S(2)}) %collective-permute-start.23) | collective-permute-done | bytes 524320 | tf_op jit(solution)/shard_map/ppermute | solution.py:465
  173.0 0.8 copy-done.13
  173.9 0.8 copy-done.14
  174.7 2.9 %spread.2.refs_5_ = f32[6144,128]{1,0:T(8,128)} custom-call(s32[4]{0:T(128)} %iota_xor_fusion.refs_0_, f32[1024,128]{1,0:T(8,128)} %copy-done.4, f32[1024,128]{1,0:T(8,128)} %copy-done.12, f32[1024,128]{1,0:T(8,128)} %copy-done.13, f32[1024,128]{1,0:T(8,128)} %copy-done.14), custom_call_target="tpu_custom_call" | custom-call | tf_op jit(solution)/shard_map/spread/pallas_call | solution.py:346
  177.6 0.6 copy-done.19
  178.3 0.1 copy-done.20
  178.4 0.7 copy-done.21
  179.1 2.2 %spread.3 = f32[6144,128]{1,0:T(8,128)} custom-call(s32[4]{0:T(128)} %iota_xor_fusion.refs_0_, f32[512,128]{1,0:T(8,128)} %copy-done.7, f32[512,128]{1,0:T(8,128)} %copy-done.19, f32[512,128]{1,0:T(8,128)} %copy-done.20, f32[512,128]{1,0:T(8,128)} %copy-done.21, f32[6144,128]{1,0:T(8,128)} %spread.2.refs_5_), custom_call_target="tpu_custom_call", output_to_operand_aliasing={{}: (5, {})} | custom-call | tf_op jit(solution)/shard_map/spread/pallas_call | solution.py:346
  (57 shorter events, 0.2 us)
Async XLA Ops:
  0.0 21.7 %collective-permute-start.2 = (f32[6144,128]{1,0:T(8,128)}, f32[6144,128]{1,0:T(8,128)}, u32[]{:S(2)}, u32[]{:S(2)}) collective-permute-start(f32[6144,128]{1,0:T(8,128)} %weights_ref.1), channel_id=1, source_target_pairs={{0,1},{1,0},{2,3},{3,2},{4,5},{5,4},{6,7},{7,6},{8,9},{9,8},{10,11... | collective-permute-start | bytes 9437192 | tf_op jit(solution)/shard_map/ppermute | solution.py:411
  0.5 21.2 %collective-permute-start.1 = (f32[64,6144]{1,0:T(8,128)}, f32[64,6144]{1,0:T(8,128)S(1)}, u32[]{:S(2)}, u32[]{:S(2)}) collective-permute-start(f32[64,6144]{1,0:T(8,128)} %points_ref.1), channel_id=1, source_target_pairs={{0,1},{1,0},{2,3},{3,2},{4,5},{5,4},{6,7},{7,6},{8,9},{9,8},{10,11... | collective-permute-start | bytes 4718600 | tf_op jit(solution)/shard_map/ppermute | solution.py:411
  2.5 27.0 %collective-permute-start = (f32[72,1536]{1,0:T(8,128)S(1)}, f32[72,1536]{1,0:T(8,128)S(1)}, u32[]{:S(2)}, u32[]{:S(2)}) collective-permute-start(f32[72,1536]{1,0:T(8,128)S(1)} %select_maximum_fusion), channel_id=1, source_target_pairs={{0,6},{1,7},{6,0},{7,1},{2,2},{3,3},{4,4},{5,5},{8,14},{9,15},{14,... | collective-permute-start | bytes 1327112 | tf_op jit(solution)/shard_map/ppermute | solution.py:378
  19.2 1.7 collective-permute-start.4
  19.3 1.6 collective-permute-start.3
  21.0 0.8 copy-start.24
  21.0 23.8 %collective-permute-start.5 = (f32[72,1536]{1,0:T(8,128)S(1)}, f32[72,1536]{1,0:T(8,128)S(1)}, u32[]{:S(2)}, u32[]{:S(2)}) collective-permute-start(f32[72,1536]{1,0:T(8,128)S(1)} %select_maximum_fusion), channel_id=1, source_target_pairs={{0,2},{1,3},{2,0},{3,1},{4,6},{5,7},{6,4},{7,5},{8,10},{9,11},{10,... | collective-permute-start | bytes 1327112 | tf_op jit(solution)/shard_map/ppermute | solution.py:378
  21.0 0.8 copy-start.23
  21.0 24.5 %collective-permute-start.7 = (f32[72,1536]{1,0:T(8,128)S(1)}, f32[72,1536]{1,0:T(8,128)S(1)}, u32[]{:S(2)}, u32[]{:S(2)}) collective-permute-start(f32[72,1536]{1,0:T(8,128)S(1)} %select_maximum_fusion), channel_id=1, source_target_pairs={{2,4},{3,5},{4,2},{5,3},{0,0},{1,1},{6,6},{7,7},{10,12},{11,13},{1... | collective-permute-start | bytes 1327112 | tf_op jit(solution)/shard_map/ppermute | solution.py:378
  21.7 1.1 copy-start.22
  29.4 0.8 copy-start.5
  39.5 19.7 %collective-permute-start.9 = (f32[1024,128]{1,0:T(8,128)}, f32[1024,128]{1,0:T(8,128)S(1)}, u32[]{:S(2)}, u32[]{:S(2)}) collective-permute-start(f32[1024,128]{1,0:T(8,128)} %pairs.8), channel_id=1, source_target_pairs={{0,2},{1,3},{6,4},{7,5},{8,10},{9,11},{14,12},{15,13},{16,18},{17,... | collective-permute-start | bytes 1572872 | tf_op jit(solution)/shard_map/ppermute | solution.py:378
  44.7 8.3 %copy-start.3 = (f32[72,1536]{1,0:T(8,128)}, f32[72,1536]{1,0:T(8,128)S(1)}, u32[]{:S(2)}) copy-start(f32[72,1536]{1,0:T(8,128)S(1)} %collective-permute-done.5.refs_1_.refs_2_) | copy-start | bytes 1327108
  44.7 8.3 %collective-permute-start.6 = (f32[72,1536]{1,0:T(8,128)S(1)}, f32[72,1536]{1,0:T(8,128)S(1)}, u32[]{:S(2)}, u32[]{:S(2)}) collective-permute-start(f32[72,1536]{1,0:T(8,128)S(1)} %collective-permute-done.5.refs_1_.refs_2_), channel_id=1, source_target_pairs={{2,4},{3,5},{4,2},{5,3},{10,12},{11,13},{12,10},{13,11},{18,20},{1... | collective-permute-start | bytes 1327112 | tf_op jit(solution)/shard_map/ppermute | solution.py:378
  45.4 7.5 %copy-start.2 = (f32[72,1536]{1,0:T(8,128)}, f32[72,1536]{1,0:T(8,128)S(1)}, u32[]{:S(2)}) copy-start(f32[72,1536]{1,0:T(8,128)S(1)} %collective-permute-done.7.refs_1_.refs_2_) | copy-start | bytes 1327108
  45.5 13.7 %collective-permute-start.8 = (f32[72,1536]{1,0:T(8,128)S(1)}, f32[72,1536]{1,0:T(8,128)S(1)}, u32[]{:S(2)}, u32[]{:S(2)}) collective-permute-start(f32[72,1536]{1,0:T(8,128)S(1)} %collective-permute-done.7.refs_1_.refs_2_), channel_id=1, source_target_pairs={{2,0},{3,1},{4,6},{5,7},{10,8},{11,9},{12,14},{13,15},{18,16},{19,... | collective-permute-start | bytes 1327112 | tf_op jit(solution)/shard_map/ppermute | solution.py:378
  53.0 18.0 %copy-start.6 = (f32[512,128]{1,0:T(8,128)S(1)}, f32[512,128]{1,0:T(8,128)}, u32[]{:S(2)}) copy-start(f32[512,128]{1,0:T(8,128)} %pairs.9) | copy-start | bytes 786436
  53.0 6.2 %copy-start = (f32[72,1536]{1,0:T(8,128)}, f32[72,1536]{1,0:T(8,128)S(1)}, u32[]{:S(2)}) copy-start(f32[72,1536]{1,0:T(8,128)S(1)} %collective-permute-done.6.refs_1_.refs_3_) | copy-start | bytes 1327108
  59.2 0.8 copy-start.1
  60.0 0.8 copy-start.9
  70.3 18.9 %collective-permute-start.11 = (f32[1024,128]{1,0:T(8,128)}, f32[1024,128]{1,0:T(8,128)S(1)}, u32[]{:S(2)}, u32[]{:S(2)}) collective-permute-start(f32[1024,128]{1,0:T(8,128)} %pairs.10), channel_id=1, source_target_pairs={{2,4},{3,5},{4,2},{5,3},{10,12},{11,13},{12,10},{13,11},{18,20},{1... | collective-permute-start | bytes 1572872 | tf_op jit(solution)/shard_map/ppermute | solution.py:378
  71.0 11.1 %collective-permute-start.10 = (f32[512,128]{1,0:T(8,128)S(1)}, f32[512,128]{1,0:T(8,128)S(1)}, u32[]{:S(2)}, u32[]{:S(2)}) collective-permute-start(f32[512,128]{1,0:T(8,128)S(1)} %copy-done.6), channel_id=1, source_target_pairs={{0,2},{1,3},{6,4},{7,5},{8,10},{9,11},{14,12},{15,13},{16,18},{17,... | collective-permute-start | bytes 786440 | tf_op jit(solution)/shard_map/ppermute | solution.py:378
  75.4 26.6 %collective-permute-start.12 = (f32[1024,128]{1,0:T(8,128)}, f32[1024,128]{1,0:T(8,128)S(1)}, u32[]{:S(2)}, u32[]{:S(2)}) collective-permute-start(f32[1024,128]{1,0:T(8,128)} %pairs.10), channel_id=1, source_target_pairs={{0,2},{1,3},{6,4},{7,5},{8,10},{9,11},{14,12},{15,13},{16,18},{17,... | collective-permute-start | bytes 1572872 | tf_op jit(solution)/shard_map/ppermute | solution.py:378
  82.1 0.7 copy-start.18
  89.2 0.8 copy-start.11
  99.4 14.5 %copy-start.15 = (f32[512,128]{1,0:T(8,128)S(1)}, f32[512,128]{1,0:T(8,128)}, u32[]{:S(2)}) copy-start(f32[512,128]{1,0:T(8,128)} %pairs.11) | copy-start | bytes 786436
  99.4 36.3 %collective-permute-start.20 = (f32[1024,128]{1,0:T(8,128)}, f32[1024,128]{1,0:T(8,128)S(1)}, u32[]{:S(2)}, u32[]{:S(2)}) collective-permute-start(f32[1024,128]{1,0:T(8,128)} %pairs.12), channel_id=1, source_target_pairs={{0,2},{1,3},{2,0},{3,1},{4,6},{5,7},{6,4},{7,5},{8,10},{9,11},{10,... | collective-permute-start | bytes 1572872 | tf_op jit(solution)/shard_map/ppermute | solution.py:378
  102.0 0.8 copy-start.10
  112.2 23.6 %collective-permute-start.21 = (f32[1024,128]{1,0:T(8,128)}, f32[1024,128]{1,0:T(8,128)S(1)}, u32[]{:S(2)}, u32[]{:S(2)}) collective-permute-start(f32[1024,128]{1,0:T(8,128)} %pairs.13), channel_id=1, source_target_pairs={{2,4},{3,5},{4,2},{5,3},{0,0},{1,1},{6,6},{7,7},{10,12},{11,13},{1... | collective-permute-start | bytes 1572872 | tf_op jit(solution)/shard_map/ppermute | solution.py:378
  113.9 6.5 %collective-permute-start.13 = (f32[512,128]{1,0:T(8,128)S(1)}, f32[512,128]{1,0:T(8,128)S(1)}, u32[]{:S(2)}, u32[]{:S(2)}) collective-permute-start(f32[512,128]{1,0:T(8,128)S(1)} %copy-done.15), channel_id=1, source_target_pairs={{2,4},{3,5},{4,2},{5,3},{10,12},{11,13},{12,10},{13,11},{18,20},{1... | collective-permute-start | bytes 786440 | tf_op jit(solution)/shard_map/ppermute | solution.py:378
  114.6 21.2 %copy-start.8 = (f32[1024,128]{1,0:T(8,128)S(1)}, f32[1024,128]{1,0:T(8,128)}, u32[]{:S(2)}) copy-start(f32[1024,128]{1,0:T(8,128)} %pairs.8) | copy-start | bytes 1572868
  114.6 22.8 %collective-permute-start.15 = (f32[512,128]{1,0:T(8,128)S(1)}, f32[512,128]{1,0:T(8,128)S(1)}, u32[]{:S(2)}, u32[]{:S(2)}) collective-permute-start(f32[512,128]{1,0:T(8,128)S(1)} %copy-done.15), channel_id=1, source_target_pairs={{0,2},{1,3},{6,4},{7,5},{8,10},{9,11},{14,12},{15,13},{16,18},{17,... | collective-permute-start | bytes 786440 | tf_op jit(solution)/shard_map/ppermute | solution.py:378
  120.4 0.7 copy-start.16
  127.5 20.6 %collective-permute-start.14 = (f32[512,128]{1,0:T(8,128)}, f32[512,128]{1,0:T(8,128)S(1)}, u32[]{:S(2)}, u32[]{:S(2)}) collective-permute-start(f32[512,128]{1,0:T(8,128)} %pairs.14), channel_id=1, source_target_pairs={{0,2},{1,3},{2,0},{3,1},{4,6},{5,7},{6,4},{7,5},{8,10},{9,11},{10,... | collective-permute-start | bytes 786440 | tf_op jit(solution)/shard_map/ppermute | solution.py:378
  135.9 11.7 %copy-start.4 = (f32[1024,128]{1,0:T(8,128)}, f32[1024,128]{1,0:T(8,128)S(1)}, u32[]{:S(2)}) copy-start(f32[1024,128]{1,0:T(8,128)S(1)} %select_add_fusion.refs_1_) | copy-start | bytes 1572868
  135.9 15.3 %collective-permute-start.22 = (f32[1024,128]{1,0:T(8,128)S(1)}, f32[1024,128]{1,0:T(8,128)S(1)}, u32[]{:S(2)}, u32[]{:S(2)}) collective-permute-start(f32[1024,128]{1,0:T(8,128)S(1)} %select_add_fusion.refs_1_), channel_id=1, source_target_pairs={{0,8},{8,0},{16,24},{24,16},{1,9},{9,1},{17,25},{25,17},{2,10},{10... | collective-permute-start | bytes 1572872 | tf_op jit(solution)/shard_map/ppermute | solution.py:465
  137.4 0.7 copy-start.17
  144.5 3.6 %collective-permute-start.16 = (f32[512,128]{1,0:T(8,128)}, f32[512,128]{1,0:T(8,128)S(1)}, u32[]{:S(2)}, u32[]{:S(2)}) collective-permute-start(f32[512,128]{1,0:T(8,128)} %pairs.15), channel_id=1, source_target_pairs={{2,4},{3,5},{4,2},{5,3},{0,0},{1,1},{6,6},{7,7},{10,12},{11,13},{1... | collective-permute-start | bytes 786440 | tf_op jit(solution)/shard_map/ppermute | solution.py:378
  146.1 26.9 %collective-permute-start.23 = (f32[1024,128]{1,0:T(8,128)S(1)}, f32[1024,128]{1,0:T(8,128)S(1)}, u32[]{:S(2)}, u32[]{:S(2)}) collective-permute-start(f32[1024,128]{1,0:T(8,128)S(1)} %select_add_fusion.refs_1_), channel_id=1, source_target_pairs={{0,16},{8,24},{16,0},{24,8},{1,17},{9,25},{17,1},{25,9},{2,18},{10... | collective-permute-start | bytes 1572872 | tf_op jit(solution)/shard_map/ppermute | solution.py:465
  147.6 25.4 %collective-permute-start.24 = (f32[1024,128]{1,0:T(8,128)S(1)}, f32[1024,128]{1,0:T(8,128)S(1)}, u32[]{:S(2)}, u32[]{:S(2)}) collective-permute-start(f32[1024,128]{1,0:T(8,128)S(1)} %select_add_fusion.refs_1_), channel_id=1, source_target_pairs={{0,24},{8,16},{16,8},{24,0},{1,25},{9,17},{17,9},{25,1},{2,26},{10... | collective-permute-start | bytes 1572872 | tf_op jit(solution)/shard_map/ppermute | solution.py:465
  148.2 29.5 %copy-start.7 = (f32[512,128]{1,0:T(8,128)}, f32[512,128]{1,0:T(8,128)S(1)}, u32[]{:S(2)}) copy-start(f32[512,128]{1,0:T(8,128)S(1)} %select_add_fusion.1.refs_1_) | copy-start | bytes 786436
  148.2 29.4 %collective-permute-start.17 = (f32[512,128]{1,0:T(8,128)S(1)}, f32[512,128]{1,0:T(8,128)S(1)}, u32[]{:S(2)}, u32[]{:S(2)}) collective-permute-start(f32[512,128]{1,0:T(8,128)S(1)} %select_add_fusion.1.refs_1_), channel_id=1, source_target_pairs={{0,8},{8,0},{16,24},{24,16},{1,9},{9,1},{17,25},{25,17},{2,10},{10... | collective-permute-start | bytes 786440 | tf_op jit(solution)/shard_map/ppermute | solution.py:465
  149.7 27.9 %collective-permute-start.18 = (f32[512,128]{1,0:T(8,128)S(1)}, f32[512,128]{1,0:T(8,128)S(1)}, u32[]{:S(2)}, u32[]{:S(2)}) collective-permute-start(f32[512,128]{1,0:T(8,128)S(1)} %select_add_fusion.1.refs_1_), channel_id=1, source_target_pairs={{0,16},{8,24},{16,0},{24,8},{1,17},{9,25},{17,1},{25,9},{2,18},{10... | collective-permute-start | bytes 786440 | tf_op jit(solution)/shard_map/ppermute | solution.py:465
  151.2 21.8 %copy-start.12 = (f32[1024,128]{1,0:T(8,128)}, f32[1024,128]{1,0:T(8,128)S(1)}, u32[]{:S(2)}) copy-start(f32[1024,128]{1,0:T(8,128)S(1)} %collective-permute-done.22.refs_2_) | copy-start | bytes 1572868
  151.2 26.4 %collective-permute-start.19 = (f32[512,128]{1,0:T(8,128)S(1)}, f32[512,128]{1,0:T(8,128)S(1)}, u32[]{:S(2)}, u32[]{:S(2)}) collective-permute-start(f32[512,128]{1,0:T(8,128)S(1)} %select_add_fusion.1.refs_1_), channel_id=1, source_target_pairs={{0,24},{8,16},{16,8},{24,0},{1,25},{9,17},{17,9},{25,1},{2,26},{10... | collective-permute-start | bytes 786440 | tf_op jit(solution)/shard_map/ppermute | solution.py:465
  173.0 0.8 copy-start.13
  173.9 0.8 copy-start.14
  177.6 0.7 copy-start.19
  177.6 0.8 copy-start.20
  178.4 0.7 copy-start.21

commit v3 on v2

--- a/solution.py
+++ b/solution.py
@@ -44,67 +44,21 @@
     list_refs = [refs.pop(0) for _ in range(plan["parcels"])]
     x_refs = [refs.pop(0) for _ in range(plan["parcels"])]
     init_ref = refs.pop(0) if plan["init"] else None
-    sides, (out_ref, y_buf, w_buf, ys_buf, ws_buf, xk_buf, sem, skel_sem) = (
-        (refs[:4], refs[4:8]),
-        refs[8:],
-    )
+    sides, (out_ref, xk_buf) = (refs[:4], refs[4:8]), refs[8:]
     leaf = x_refs[0].shape[1]
     capacity = plan["capacity"]
     devices = plan["devices"]
     scale = plan["scale"]
     slots = 2 * capacity
-    kept = ys_buf.shape[1] // 2
+    kept = sides[0][2].shape[1]
     step = pl.program_id(0)
-    half = step % 2
 
     def listed(n):
         value = sum(ref[n // 128, n % 128] for ref in list_refs)
         return value.astype(jnp.int32)
 
-    def leaf_number(at):
-        return place_ref[0] * plan["per"] + plan["first"] + at
-
-    def near_copies(at, buffer):
-        row = leaf_number(at) // plan["row_leaves"]
-        copies = []
-        for side, (pts, wts, _, _) in enumerate(sides):
-            for c in range(capacity):
-                slot = side * capacity + c
-                source = listed((row * devices + place_ref[1 + side]) * capacity + c)
-                copies.append((
-                    pltpu.make_async_copy(
-                        pts.at[source], y_buf.at[buffer, slot], sem.at[buffer, slot, 0]
-                    ),
-                    pltpu.make_async_copy(
-                        wts.at[source], w_buf.at[buffer, slot], sem.at[buffer, slot, 1]
-                    ),
-                ))
-        return copies
-
-    skel_copies = []
-    for side, (_, _, pts, wts) in enumerate(sides):
-        part = pl.ds(side * kept, kept)
-        skel_copies += [
-            pltpu.make_async_copy(pts, ys_buf.at[:, part], skel_sem.at[side, 0]),
-            pltpu.make_async_copy(wts, ws_buf.at[part, :], skel_sem.at[side, 1]),
-        ]
-
-    @pl.when(step == 0)
-    def _():
-        for copy in skel_copies:
-            copy.start()
-        for pair in near_copies(0, 0):
-            pair[0].start()
-            pair[1].start()
-
-    if plan["count"] > 1:
-
-        @pl.when(step + 1 < plan["count"])
-        def _():
-            for pair in near_copies(step + 1, 1 - half):
-                pair[0].start()
-                pair[1].start()
-
+    number = place_ref[0] * plan["per"] + plan["first"] + step
+    row = number // plan["row_leaves"]
     x = x_refs[0][...]
     for ref in x_refs[1:]:
         x = x + ref[...]
@@ -132,7 +86,6 @@
 
     gains = [None] * (slots + 1)
     if not plan["dense"]:
-        number = leaf_number(step)
         base = plan["rows_listed"] * devices * capacity
         near = [listed(base + number * plan["near"] + n) for n in range(plan["near"])]
         base += plan["targets"] * plan["near"]
@@ -149,16 +102,15 @@
         first_half = lax.broadcasted_iota(jnp.int32, (1, 2 * kept), 1) < kept
         gains.append(jnp.where(first_half, own, partner))
 
-    @pl.when(step == 0)
-    def _():
-        for copy in skel_copies:
-            copy.wait()
-
-    add(ys_buf[...], ws_buf[...], gains[slots])
-    for slot, pair in enumerate(near_copies(step, half)):
-        pair[0].wait()
-        pair[1].wait()
-        add(y_buf[half, slot], w_buf[half, slot], gains[slot])
+    add(
+        jnp.concatenate([side[2][...] for side in sides], axis=1),
+        jnp.concatenate([side[3][...] for side in sides], axis=0),
+        gains[slots],
+    )
+    for n, (pts, wts, _, _) in enumerate(sides):
+        for c in range(capacity):
+            source = listed((row * devices + place_ref[1 + n]) * capacity + c)
+            add(pts[source], wts[source], gains[n * capacity + c])
 
 
 def pairs(sizes, place, parcels, init, sources, first, count):
@@ -185,7 +137,7 @@
     if init is not None:
         in_specs.append(pl.BlockSpec((leaf, columns), lambda i: (i, 0)))
         operands.append(init)
-    in_specs += [pl.BlockSpec(memory_space=pltpu.HBM)] * 8
+    in_specs += [pl.BlockSpec(memory_space=pltpu.VMEM)] * 8
     operands += [array for side in sources for array in side]
     work = count * leaf * (leaf * slots + 2 * kept)
     return pl.pallas_call(
@@ -195,15 +147,9 @@
         out_specs=pl.BlockSpec((leaf, columns), lambda i: (i, 0)),
         out_shape=jax.ShapeDtypeStruct((count * leaf, columns), F32),
         scratch_shapes=[
-            pltpu.VMEM((2, slots, rows, leaf), BF16),
-            pltpu.VMEM((2, slots, leaf, 2 * columns), BF16),
-            pltpu.VMEM((rows, 2 * kept), BF16),
-            pltpu.VMEM((2 * kept, 2 * columns), BF16),
             pltpu.VMEM((leaf, rows), BF16),
-            pltpu.SemaphoreType.DMA((2, slots, 2)),
-            pltpu.SemaphoreType.DMA((2, 2)),
         ],
-        compiler_params=pltpu.CompilerParams(vmem_limit_bytes=58 << 20),
+        compiler_params=pltpu.CompilerParams(vmem_limit_bytes=16 << 20),
         cost_estimate=pl.CostEstimate(
             flops=work * 2 * (4 * features + 4 * columns),
             bytes_accessed=count * slots * leaf * (features + columns) * 4,
@@ -222,11 +168,16 @@
 
 
 def write_sources(points_ref, weights_ref, y_ref, w_ref, scale):
-    leaves, _, leaf = y_ref.shape
+    leaf = y_ref.shape[2]
+    leaves = points_ref.shape[1] // leaf
+    values = []
     for n in range(leaves):
         part = slice(n * leaf, (n + 1) * leaf)
-        y_ref[n] = source_rows(points_ref[:, part], scale)
-        w_ref[n] = value_columns(weights_ref[part, :])
+        here = pl.program_id(0) * leaves + n
+        y_ref[here] = source_rows(points_ref[:, part], scale)
+        values.append(value_columns(weights_ref[part, :]))
+        w_ref[here] = values[-1]
+    return values
 
 
 def own_kernel(scale, idx_ref, points_ref, weights_ref, proj_ref, y_ref, w_ref, ys_ref, ws_ref,
@@ -239,7 +190,7 @@
         coords_ref[...] = jnp.zeros_like(coords_ref)
         summed_ref[...] = jnp.zeros_like(summed_ref)
 
-    write_sources(points_ref, weights_ref, y_ref, w_ref, scale)
+    values = write_sources(points_ref, weights_ref, y_ref, w_ref, scale)
     place = lax.broadcasted_iota(jnp.int32, (count, idx_ref.shape[1]), 0) + step * count
     chosen = jnp.where(place == idx_ref[...], 1.0, 0.0).astype(BF16)
     terms = jnp.concatenate(three_terms(points_ref[...]), axis=0).astype(BF16)
@@ -249,7 +200,7 @@
     )
     p_high, p_low = two_terms(proj_ref[...])
     columns = weights_ref.shape[1]
-    values = jnp.concatenate([w_ref[n] for n in range(w_ref.shape[0])], axis=0)
+    values = jnp.concatenate(values, axis=0)
     both = jnp.dot(
         jnp.concatenate([p_high, p_low], axis=1).astype(BF16),
         jnp.concatenate([values, values], axis=0),
@@ -283,17 +234,12 @@
         pl.BlockSpec((features, block), lambda i: (0, i)),
         pl.BlockSpec((block, columns), lambda i: (i, 0)),
     ]
-    out_specs = [
-        pl.BlockSpec((leaves, 4 * features, leaf), lambda i: (i, 0, 0)),
-        pl.BlockSpec((leaves, leaf, 2 * columns), lambda i: (i, 0, 0)),
-        whole(4 * features, kept),
-        whole(kept, 2 * columns),
-    ]
+    out_specs = [pl.BlockSpec(memory_space=pltpu.VMEM)] * 4
     out_shape = [
-        pltpu.HBM((count // leaf, 4 * features, leaf), BF16),
-        pltpu.HBM((count // leaf, leaf, 2 * columns), BF16),
-        pltpu.HBM((4 * features, kept), BF16),
-        pltpu.HBM((kept, 2 * columns), BF16),
+        pltpu.VMEM((count // leaf, 4 * features, leaf), BF16),
+        pltpu.VMEM((count // leaf, leaf, 2 * columns), BF16),
+        pltpu.VMEM((4 * features, kept), BF16),
+        pltpu.VMEM((kept, 2 * columns), BF16),
     ]
     moved = 12 * count * (features + columns)
     if skel is None:
@@ -304,11 +250,11 @@
             jax.ShapeDtypeStruct((kept, columns), F32),
         ]
         operands = (skel_idx, points, weights, proj)
-        body, moved = own_kernel, moved + 4 * count * kept
+        body, moved, limit = own_kernel, moved + 4 * count * kept, 52
     else:
         in_specs += [whole(features, kept), whole(kept, columns)]
         operands = (points, weights, *skel)
-        body = other_kernel
+        body, limit = other_kernel, 44
     return pl.pallas_call(
         functools.partial(body, scale),
         grid=(count // block,),
@@ -318,6 +264,7 @@
         cost_estimate=pl.CostEstimate(
             flops=8 * kept * count * columns, bytes_accessed=moved, transcendentals=0
         ),
+        compiler_params=pltpu.CompilerParams(vmem_limit_bytes=limit << 20),
         name="prepared",
     )(*operands)
 
@@ -358,6 +305,7 @@
 
 def on_device(points, weights, proj, fetch_table, near_list, far_list, skel_idx):
     features, column_points = points.shape
+    columns = weights.shape[1]
     devices = lax.axis_size("dev")
     groups = lax.axis_size("grp")
     targets = near_list.shape[0]
@@ -389,8 +337,13 @@
     numbers = jnp.pad(numbers, (0, room - numbers.shape[0])).reshape(8, 128).astype(F32)
     numbers = jnp.pad(numbers, ((0, 0), (0, width - 128)))
     parcel = jnp.concatenate([mine, numbers], axis=0)
-    proj, parcel = lax.optimization_barrier((proj, parcel))
+    chip = device // 2
     place = jnp.stack([group, device, device ^ 1])
+    mask = group ^ jnp.arange(groups, dtype=jnp.int32)
+    inner = jnp.full((1, columns), (chip > 0) & (chip < chips - 1), F32)
+    proj, parcel, place, mask, inner = lax.optimization_barrier(
+        (proj, parcel, place, mask, inner)
+    )
     late = per // 3
     chunks = [(0, per - late)] + ([(per - late, late)] if late else [])
     sizes = {
@@ -418,8 +371,6 @@
         return tuple(own), tuple(other)
 
     if chips == 4:
-        chip = device // 2
-        inner = (chip == 1) | (chip == 2)
         ends = [(0, 3), (3, 0), (1, 1), (2, 2)]
         sides = [(0, 1), (1, 0), (2, 3), (3, 2)]
         middle = [(1, 2), (2, 1), (0, 0), (3, 3)]
@@ -446,8 +397,7 @@
         for k in every:
             c = work((of_c,), shift(b[k], cross), k)
             d = work((of_d,), shift(b[k], inward), k)
-            own = jnp.where(inner, a[k], 0.0)
-            done.append(shift(c, sides) + shift(d, middle) + own)
+            done.append(shift(c, sides) + shift(d, middle) + a[k] * inner)
     else:
         sources = make_sources()
         total = None
@@ -458,7 +408,6 @@
             total = part if total is None else total + part
         done = [total[first * leaf : (first + count) * leaf] for first, count in chunks]
 
-    mask = group ^ jnp.arange(groups, dtype=jnp.int32)
     out = None
     for (first, _), piece in zip(chunks, done):
         pieces = [

time: 182 us -> 146 us (0.80)
  Pallas kernels: 84.4 us -> 49.6 us
  local copies, waits for them, and re-layouts: 12.1 us -> 4.93 us
  starting transfers between devices: 50.2 us -> 53.8 us
  waiting for transfers between devices: 32.7 us -> 35.9 us
    pallas_call x8, Pallas kernels: 63 us -> 32.5 us  [pairs(): pl.pallas_call(functools.partial(pair_kernel, plan), grid=(count,), in_sp...]
    unnamed x51 -> x17, local copies, waits for them, and re-layouts: 11 us -> 3.81 us
    pallas_call x2, Pallas kernels: 16.4 us -> 12 us  [prepared(): pl.pallas_call(functools.partial(body, scale), grid=(count // block,), in...]
    ppermute x15, waiting for transfers between devices: 11.3 us -> 15.2 us  [shift(): return lax.ppermute(array, 'dev', along(moves))]
    ppermute x6, starting transfers between devices: 7.11 us -> 9.15 us  [on_device(): lax.ppermute(piece, 'grp', [(g, g ^ m) for g in range(groups)])]
  transfers between devices with their start and end apart: 25 -> 25, of which waited for: 4 -> 6; matrix products, arithmetic and copies ran while one was open for 2% -> 2% of each run, Pallas kernels for 40% -> 29%
where the time goes in v3:
time: 146 us
  starting transfers between devices  53.8 us (37%)
  Pallas kernels  49.6 us (34%)
  waiting for transfers between devices  35.9 us (25%)
  local copies, waits for them, and re-layouts  4.93 us (3%)
    ppermute x15, starting transfers between devices, shift(): return lax.ppermute(array, 'dev', along(moves))  43.6 us
    pallas_call x8, Pallas kernels, pairs(): pl.pallas_call(functools.partial(pair_kernel, plan), grid=(count,), in_sp...  32.5 us
    ppermute x6, waiting for transfers between devices, on_device(): lax.ppermute(piece, 'grp', [(g, g ^ m) for g in range(groups)])  19.5 us
    ppermute x15, waiting for transfers between devices, shift(): return lax.ppermute(array, 'dev', along(moves))  15.2 us
    pallas_call x2, Pallas kernels, prepared(): pl.pallas_call(functools.partial(body, scale), grid=(count // block,), in...  12 us
    ppermute x6, starting transfers between devices, on_device(): lax.ppermute(piece, 'grp', [(g, g ^ m) for g in range(groups)])  9.15 us
    pallas_call x2, Pallas kernels, spread(): pl.pallas_call(functools.partial(spread_kernel, groups, per, first, leaf,...  5.07 us
    unnamed x17, local copies, waits for them, and re-layouts  3.81 us
  transfers between devices with their start and end apart: 25, of which 6 were waited for; matrix products, arithmetic and copies ran while one was open for 2% of the time, Pallas kernels for 29%

profile of v3, /device:TPU:0, one launch (start us, length us, event | category | flops | bytes accessed | tf_op | source)
XLA Modules:
  0.0 145.5 jit_solution(15508378843055168213)
XLA Ops:
  0.0 0.5 collective-permute-start.2
  0.5 0.0 collective-permute-start.1
  0.5 0.8 copy.8
  1.3 0.1 reshape.5
  1.4 0.5 iota_xor_fusion.refs_0_
  1.9 0.1 pad_add_fusion.refs_0_
  2.0 1.0 constant_dynamic-slice_fusion
  3.1 7.0 %collective-permute-start = (f32[72,1536]{1,0:T(8,128)S(1)}, f32[72,1536]{1,0:T(8,128)S(1)}, u32[]{:S(2)}, u32[]{:S(2)}) collective-permute-start(f32[72,1536]{1,0:T(8,128)S(1)} %select_maximum_fusion), channel_id=1, source_target_pairs={{0,6},{1,7},{6,0},{7,1},{2,2},{3,3},{4,4},{5,5},{8,14},{9,15},{14,... | collective-permute-start | bytes 1327112 | tf_op jit(solution)/shard_map/ppermute | solution.py:326
  10.1 8.1 %prepared.2 = (bf16[12,256,512]{2,1,0:T(8,128)(2,1)S(1)}, bf16[12,512,256]{2,1,0:T(8,128)(2,1)S(1)}, bf16[256,256]{1,0:T(8,128)(2,1)S(1)}, bf16[256,256]{1,0:T(8...) custom-call(s32[1,256]{1,0:T(1,128)} %idx_ref.1, f32[64,6144]{1,0:T(8,128)} %points_ref.1, ...), custom_call_target="tpu_custom_call" | custom-call | flops 1610612736 | bytes 20447232 | tf_op jit(solution)/shard_map/prepared/pallas_call | solution.py:258
  18.2 0.0 collective-permute-start.4
  18.2 0.5 collective-permute-start.3
  18.7 1.1 collective-permute-done.3.coords_ref
  19.9 0.0 collective-permute-start.5
  19.9 0.0 collective-permute-done.4.summed_ref
  19.9 0.7 collective-permute-start.7
  20.5 0.0 collective-permute-done.1.points_ref
  20.6 0.0 collective-permute-done.2.weights_ref
  20.6 3.9 %prepared.3 = (bf16[12,256,512]{2,1,0:T(8,128)(2,1)S(1)}, bf16[12,512,256]{2,1,0:T(8,128)(2,1)S(1)}, bf16[256,256]{1,0:T(8,128)(2,1)S(1)}, bf16[256,256]{1,0:T(8,128)(2,1)S(1)}) custom-call(f32[64,6144]{1,0:T(8,128)S(1)} %collective-permute-done.1.points_ref, f32[6144,128]{1,0:T(8,128)} %collective-permute-done.2.weights_ref, ...), custom_call_target="tpu_custom_call" | custom-call | flops 1610612736 | bytes 14155776 | tf_op jit(solution)/shard_map/prepared/pallas_call | solution.py:258
  24.5 0.0 collective-permute-done.refs_1_.refs_2_
  24.5 5.2 %pairs.8 = f32[1024,128]{1,0:T(8,128)S(1)} custom-call(s32[3]{0:T(128)S(1)} %pad_add_fusion.refs_0_, f32[72,1536]{1,0:T(8,128)S(1)} %collective-permute-done.refs_1_.refs_2_, f32[72,1536]{1,0:T(8,128)S(1)} %collective-permute-done.refs_1_.refs_2_, bf16[12,256,512]{2,1,0:T(8,128)(2,1)S(1)} %get-tuple-element.31.refs_3_.refs_6_.refs_4_, ...), custom_call_target="tpu_custom_call" | custom-call | flops 4026531840 | bytes 3145728 | tf_op jit(solution)/shard_map/pairs/pallas_call | solution.py:143
  29.7 5.2 %collective-permute-start.9 = (f32[1024,128]{1,0:T(8,128)S(1)}, f32[1024,128]{1,0:T(8,128)S(1)}, u32[]{:S(2)}, u32[]{:S(2)}) collective-permute-start(f32[1024,128]{1,0:T(8,128)S(1)} %pairs.8), channel_id=1, source_target_pairs={{0,2},{1,3},{6,4},{7,5},{8,10},{9,11},{14,12},{15,13},{16,18},{17,... | collective-permute-start | bytes 1572872 | tf_op jit(solution)/shard_map/ppermute | solution.py:326
  34.9 0.7 collective-permute-start.6
  35.6 0.0 collective-permute-done.7.refs_1_.refs_2_
  35.6 1.3 collective-permute-start.8
  36.9 2.9 %pairs.9 = f32[512,128]{1,0:T(8,128)S(1)} custom-call(s32[3]{0:T(128)S(1)} %pad_add_fusion.refs_0_, f32[72,1536]{1,0:T(8,128)S(1)} %collective-permute-done.refs_1_.refs_2_, f32[72,1536]{1,0:T(8,128)S(1)} %collective-permute-done.refs_1_.refs_2_, bf16[12,256,512]{2,1,0:T(8,128)(2,1)S(1)} %get-tuple-element.31.refs_3_.refs_6_.refs_4_, ...), custom_call_target="tpu_custom_call" | custom-call | flops 2013265920 | bytes 1572864 | tf_op jit(solution)/shard_map/pairs/pallas_call | solution.py:143
  39.8 9.5 %collective-permute-done.8.refs_2_.refs_4_ = f32[72,1536]{1,0:T(8,128)S(1)} collective-permute-done((f32[72,1536]{1,0:T(8,128)S(1)}, f32[72,1536]{1,0:T(8,128)S(1)}, u32[]{:S(2)}, u32[]{:S(2)}) %collective-permute-start.8) | collective-permute-done | bytes 442400 | tf_op jit(solution)/shard_map/ppermute | solution.py:326
  49.4 5.3 %pairs.10 = f32[1024,128]{1,0:T(8,128)S(1)} custom-call(s32[3]{0:T(128)S(1)} %pad_add_fusion.refs_0_, f32[72,1536]{1,0:T(8,128)S(1)} %collective-permute-done.6.refs_1_.refs_3_, f32[72,1536]{1,0:T(8,128)S(1)} %collective-permute-done.8.refs_2_.refs_4_, f32[72,1536]{1,0:T(8,128)S(1)} %collective-permute-done.6.refs_1_.refs_3_, ...), custom_call_target="tpu_custom_call" | custom-call | flops 4026531840 | bytes 3145728 | tf_op jit(solution)/shard_map/pairs/pallas_call | solution.py:143
  54.7 0.7 collective-permute-start.11
  55.4 4.4 %collective-permute-start.10 = (f32[512,128]{1,0:T(8,128)S(1)}, f32[512,128]{1,0:T(8,128)S(1)}, u32[]{:S(2)}, u32[]{:S(2)}) collective-permute-start(f32[512,128]{1,0:T(8,128)S(1)} %pairs.9), channel_id=1, source_target_pairs={{0,2},{1,3},{6,4},{7,5},{8,10},{9,11},{14,12},{15,13},{16,18},{17,... | collective-permute-start | bytes 786440 | tf_op jit(solution)/shard_map/ppermute | solution.py:326
  59.8 1.5 %collective-permute-start.12 = (f32[1024,128]{1,0:T(8,128)S(1)}, f32[1024,128]{1,0:T(8,128)S(1)}, u32[]{:S(2)}, u32[]{:S(2)}) collective-permute-start(f32[1024,128]{1,0:T(8,128)S(1)} %pairs.10), channel_id=1, source_target_pairs={{0,2},{1,3},{6,4},{7,5},{8,10},{9,11},{14,12},{15,13},{16,18},{17,... | collective-permute-start | bytes 1572872 | tf_op jit(solution)/shard_map/ppermute | solution.py:326
  61.3 5.2 %collective-permute-done.10.refs_5_ = f32[512,128]{1,0:T(8,128)S(1)} collective-permute-done((f32[512,128]{1,0:T(8,128)S(1)}, f32[512,128]{1,0:T(8,128)S(1)}, u32[]{:S(2)}, u32[]{:S(2)}) %collective-permute-start.10) | collective-permute-done | bytes 262176 | tf_op jit(solution)/shard_map/ppermute | solution.py:326
  66.5 2.9 %pairs.11 = f32[512,128]{1,0:T(8,128)S(1)} custom-call(s32[3]{0:T(128)S(1)} %pad_add_fusion.refs_0_, f32[72,1536]{1,0:T(8,128)S(1)} %collective-permute-done.6.refs_1_.refs_3_, f32[72,1536]{1,0:T(8,128)S(1)} %collective-permute-done.8.refs_2_.refs_4_, f32[72,1536]{1,0:T(8,128)S(1)} %collective-permute-done.6.refs_1_.refs_3_, ...), custom_call_target="tpu_custom_call" | custom-call | flops 2013265920 | bytes 1572864 | tf_op jit(solution)/shard_map/pairs/pallas_call | solution.py:143
  69.4 0.0 collective-permute-done.11.refs_3_
  69.4 5.2 %pairs.12 = f32[1024,128]{1,0:T(8,128)S(1)} custom-call(s32[3]{0:T(128)S(1)} %pad_add_fusion.refs_0_, f32[72,1536]{1,0:T(8,128)S(1)} %collective-permute-done.5.refs_1_.refs_2_, f32[72,1536]{1,0:T(8,128)S(1)} %collective-permute-done.5.refs_1_.refs_2_, f32[1024,128]{1,0:T(8,128)S(1)} %collective-permute-done.11.refs_3_, ...), custom_call_target="tpu_custom_call" | custom-call | flops 4026531840 | bytes 3145728 | tf_op jit(solution)/shard_map/pairs/pallas_call | solution.py:143
  74.6 2.5 %collective-permute-start.20 = (f32[1024,128]{1,0:T(8,128)S(1)}, f32[1024,128]{1,0:T(8,128)S(1)}, u32[]{:S(2)}, u32[]{:S(2)}) collective-permute-start(f32[1024,128]{1,0:T(8,128)S(1)} %pairs.12), channel_id=1, source_target_pairs={{0,2},{1,3},{2,0},{3,1},{4,6},{5,7},{6,4},{7,5},{8,10},{9,11},{10,... | collective-permute-start | bytes 1572872 | tf_op jit(solution)/shard_map/ppermute | solution.py:326
  77.2 0.5 collective-permute-done.12.refs_3_
  77.7 5.2 %pairs.13 = f32[1024,128]{1,0:T(8,128)S(1)} custom-call(s32[3]{0:T(128)S(1)} %pad_add_fusion.refs_0_, f32[72,1536]{1,0:T(8,128)S(1)} %collective-permute-done.7.refs_1_.refs_2_, f32[72,1536]{1,0:T(8,128)S(1)} %collective-permute-done.7.refs_1_.refs_2_, f32[1024,128]{1,0:T(8,128)S(1)} %collective-permute-done.12.refs_3_, ...), custom_call_target="tpu_custom_call" | custom-call | flops 4026531840 | bytes 3145728 | tf_op jit(solution)/shard_map/pairs/pallas_call | solution.py:143
  82.9 0.7 collective-permute-start.21
  83.6 0.7 collective-permute-start.13
  84.3 8.9 %collective-permute-start.15 = (f32[512,128]{1,0:T(8,128)S(1)}, f32[512,128]{1,0:T(8,128)S(1)}, u32[]{:S(2)}, u32[]{:S(2)}) collective-permute-start(f32[512,128]{1,0:T(8,128)S(1)} %pairs.11), channel_id=1, source_target_pairs={{0,2},{1,3},{6,4},{7,5},{8,10},{9,11},{14,12},{15,13},{16,18},{17,... | collective-permute-start | bytes 786440 | tf_op jit(solution)/shard_map/ppermute | solution.py:326
  93.2 0.0 collective-permute-done.13.refs_3_
  93.2 2.9 %pairs.14 = f32[512,128]{1,0:T(8,128)S(1)} custom-call(s32[3]{0:T(128)S(1)} %pad_add_fusion.refs_0_, f32[72,1536]{1,0:T(8,128)S(1)} %collective-permute-done.5.refs_1_.refs_2_, f32[72,1536]{1,0:T(8,128)S(1)} %collective-permute-done.5.refs_1_.refs_2_, f32[512,128]{1,0:T(8,128)S(1)} %collective-permute-done.13.refs_3_, ...), custom_call_target="tpu_custom_call" | custom-call | flops 2013265920 | bytes 1572864 | tf_op jit(solution)/shard_map/pairs/pallas_call | solution.py:143
  96.0 8.7 %collective-permute-start.14 = (f32[512,128]{1,0:T(8,128)S(1)}, f32[512,128]{1,0:T(8,128)S(1)}, u32[]{:S(2)}, u32[]{:S(2)}) collective-permute-start(f32[512,128]{1,0:T(8,128)S(1)} %pairs.14), channel_id=1, source_target_pairs={{0,2},{1,3},{2,0},{3,1},{4,6},{5,7},{6,4},{7,5},{8,10},{9,11},{10,... | collective-permute-start | bytes 786440 | tf_op jit(solution)/shard_map/ppermute | solution.py:326
  104.7 0.0 collective-permute-done.20
  104.7 0.1 multiply_add_fusion.refs_1_
  104.9 1.6 %collective-permute-start.22 = (f32[1024,128]{1,0:T(8,128)S(1)}, f32[1024,128]{1,0:T(8,128)S(1)}, u32[]{:S(2)}, u32[]{:S(2)}) collective-permute-start(f32[1024,128]{1,0:T(8,128)S(1)} %multiply_add_fusion.refs_1_), channel_id=1, source_target_pairs={{0,8},{8,0},{16,24},{24,16},{1,9},{9,1},{17,25},{25,17},{2,10},{10... | collective-permute-start | bytes 1572872 | tf_op jit(solution)/shard_map/ppermute | solution.py:414
  106.4 0.0 collective-permute-done.15.refs_3_
  106.4 2.9 %pairs.15 = f32[512,128]{1,0:T(8,128)S(1)} custom-call(s32[3]{0:T(128)S(1)} %pad_add_fusion.refs_0_, f32[72,1536]{1,0:T(8,128)S(1)} %collective-permute-done.7.refs_1_.refs_2_, f32[72,1536]{1,0:T(8,128)S(1)} %collective-permute-done.7.refs_1_.refs_2_, f32[512,128]{1,0:T(8,128)S(1)} %collective-permute-done.15.refs_3_, ...), custom_call_target="tpu_custom_call" | custom-call | flops 2013265920 | bytes 1572864 | tf_op jit(solution)/shard_map/pairs/pallas_call | solution.py:143
  109.3 0.7 collective-permute-start.16
  110.0 1.6 %collective-permute-start.23 = (f32[1024,128]{1,0:T(8,128)S(1)}, f32[1024,128]{1,0:T(8,128)S(1)}, u32[]{:S(2)}, u32[]{:S(2)}) collective-permute-start(f32[1024,128]{1,0:T(8,128)S(1)} %multiply_add_fusion.refs_1_), channel_id=1, source_target_pairs={{0,16},{8,24},{16,0},{24,8},{1,17},{9,25},{17,1},{25,9},{2,18},{10... | collective-permute-start | bytes 1572872 | tf_op jit(solution)/shard_map/ppermute | solution.py:414
  111.6 0.5 collective-permute-start.24
  112.0 0.1 multiply_add_fusion.1.refs_1_
  112.1 1.6 %collective-permute-start.17 = (f32[512,128]{1,0:T(8,128)S(1)}, f32[512,128]{1,0:T(8,128)S(1)}, u32[]{:S(2)}, u32[]{:S(2)}) collective-permute-start(f32[512,128]{1,0:T(8,128)S(1)} %multiply_add_fusion.1.refs_1_), channel_id=1, source_target_pairs={{0,8},{8,0},{16,24},{24,16},{1,9},{9,1},{17,25},{25,17},{2,10},{10... | collective-permute-start | bytes 786440 | tf_op jit(solution)/shard_map/ppermute | solution.py:414
  113.7 1.5 %collective-permute-start.18 = (f32[512,128]{1,0:T(8,128)S(1)}, f32[512,128]{1,0:T(8,128)S(1)}, u32[]{:S(2)}, u32[]{:S(2)}) collective-permute-start(f32[512,128]{1,0:T(8,128)S(1)} %multiply_add_fusion.1.refs_1_), channel_id=1, source_target_pairs={{0,16},{8,24},{16,0},{24,8},{1,17},{9,25},{17,1},{25,9},{2,18},{10... | collective-permute-start | bytes 786440 | tf_op jit(solution)/shard_map/ppermute | solution.py:414
  115.2 4.5 %collective-permute-done.22.refs_2_ = f32[1024,128]{1,0:T(8,128)S(1)} collective-permute-done((f32[1024,128]{1,0:T(8,128)S(1)}, f32[1024,128]{1,0:T(8,128)S(1)}, u32[]{:S(2)}, u32[]{:S(2)}) %collective-permute-start.22) | collective-permute-done | bytes 524320 | tf_op jit(solution)/shard_map/ppermute | solution.py:414
  119.7 2.5 %collective-permute-start.19 = (f32[512,128]{1,0:T(8,128)S(1)}, f32[512,128]{1,0:T(8,128)S(1)}, u32[]{:S(2)}, u32[]{:S(2)}) collective-permute-start(f32[512,128]{1,0:T(8,128)S(1)} %multiply_add_fusion.1.refs_1_), channel_id=1, source_target_pairs={{0,24},{8,16},{16,8},{24,0},{1,25},{9,17},{17,9},{25,1},{2,26},{10... | collective-permute-start | bytes 786440 | tf_op jit(solution)/shard_map/ppermute | solution.py:414
  122.2 15.0 %collective-permute-done.23.refs_3_ = f32[1024,128]{1,0:T(8,128)S(1)} collective-permute-done((f32[1024,128]{1,0:T(8,128)S(1)}, f32[1024,128]{1,0:T(8,128)S(1)}, u32[]{:S(2)}, u32[]{:S(2)}) %collective-permute-start.23) | collective-permute-done | bytes 524320 | tf_op jit(solution)/shard_map/ppermute | solution.py:414
  137.2 0.8 copy-done.3
  138.0 0.8 copy-done.4
  138.8 2.9 %spread.2.refs_5_ = f32[6144,128]{1,0:T(8,128)} custom-call(s32[4]{0:T(128)} %iota_xor_fusion.refs_0_, f32[1024,128]{1,0:T(8,128)} %copy-done, f32[1024,128]{1,0:T(8,128)} %copy-done.2, f32[1024,128]{1,0:T(8,128)} %copy-done.3, f32[1024,128]{1,0:T(8,128)} %copy-done.4), custom_call_target="tpu_custom_call" | custom-call | tf_op jit(solution)/shard_map/spread/pallas_call | solution.py:293
  141.7 0.6 copy-done.5
  142.4 0.1 copy-done.6
  142.5 0.7 copy-done.7
  143.2 2.2 %spread.3 = f32[6144,128]{1,0:T(8,128)} custom-call(s32[4]{0:T(128)} %iota_xor_fusion.refs_0_, f32[512,128]{1,0:T(8,128)} %copy-done.1, f32[512,128]{1,0:T(8,128)} %copy-done.5, f32[512,128]{1,0:T(8,128)} %copy-done.6, f32[512,128]{1,0:T(8,128)} %copy-done.7, f32[6144,128]{1,0:T(8,128)} %spread.2.refs_5_), custom_call_target="tpu_custom_call", output_to_operand_aliasing={{}: (5, {})} | custom-call | tf_op jit(solution)/shard_map/spread/pallas_call | solution.py:293
  (24 shorter events, 0.1 us)
Async XLA Ops:
  0.0 20.6 %collective-permute-start.2 = (f32[6144,128]{1,0:T(8,128)}, f32[6144,128]{1,0:T(8,128)}, u32[]{:S(2)}, u32[]{:S(2)}) collective-permute-start(f32[6144,128]{1,0:T(8,128)} %weights_ref.1), channel_id=1, source_target_pairs={{0,1},{1,0},{2,3},{3,2},{4,5},{5,4},{6,7},{7,6},{8,9},{9,8},{10,11... | collective-permute-start | bytes 9437192 | tf_op jit(solution)/shard_map/ppermute | solution.py:364
  0.5 20.1 %collective-permute-start.1 = (f32[64,6144]{1,0:T(8,128)}, f32[64,6144]{1,0:T(8,128)S(1)}, u32[]{:S(2)}, u32[]{:S(2)}) collective-permute-start(f32[64,6144]{1,0:T(8,128)} %points_ref.1), channel_id=1, source_target_pairs={{0,1},{1,0},{2,3},{3,2},{4,5},{5,4},{6,7},{7,6},{8,9},{9,8},{10,11... | collective-permute-start | bytes 4718600 | tf_op jit(solution)/shard_map/ppermute | solution.py:364
  3.1 21.4 %collective-permute-start = (f32[72,1536]{1,0:T(8,128)S(1)}, f32[72,1536]{1,0:T(8,128)S(1)}, u32[]{:S(2)}, u32[]{:S(2)}) collective-permute-start(f32[72,1536]{1,0:T(8,128)S(1)} %select_maximum_fusion), channel_id=1, source_target_pairs={{0,6},{1,7},{6,0},{7,1},{2,2},{3,3},{4,4},{5,5},{8,14},{9,15},{14,... | collective-permute-start | bytes 1327112 | tf_op jit(solution)/shard_map/ppermute | solution.py:326
  18.2 1.7 %collective-permute-start.4 = (f32[256,128]{1,0:T(8,128)}, f32[256,128]{1,0:T(8,128)S(1)}, u32[]{:S(2)}, u32[]{:S(2)}) collective-permute-start(f32[256,128]{1,0:T(8,128)} %get-tuple-element.36), channel_id=1, source_target_pairs={{0,1},{1,0},{2,3},{3,2},{4,5},{5,4},{6,7},{7,6},{8,9},{9,8},{10,11... | collective-permute-start | bytes 393224 | tf_op jit(solution)/shard_map/ppermute | solution.py:364
  18.2 1.6 %collective-permute-start.3 = (f32[64,256]{1,0:T(8,128)}, f32[64,256]{1,0:T(8,128)S(1)}, u32[]{:S(2)}, u32[]{:S(2)}) collective-permute-start(f32[64,256]{1,0:T(8,128)} %get-tuple-element.35), channel_id=1, source_target_pairs={{0,1},{1,0},{2,3},{3,2},{4,5},{5,4},{6,7},{7,6},{8,9},{9,8},{10,11... | collective-permute-start | bytes 196616 | tf_op jit(solution)/shard_map/ppermute | solution.py:364
  19.9 15.1 %collective-permute-start.5 = (f32[72,1536]{1,0:T(8,128)S(1)}, f32[72,1536]{1,0:T(8,128)S(1)}, u32[]{:S(2)}, u32[]{:S(2)}) collective-permute-start(f32[72,1536]{1,0:T(8,128)S(1)} %select_maximum_fusion), channel_id=1, source_target_pairs={{0,2},{1,3},{2,0},{3,1},{4,6},{5,7},{6,4},{7,5},{8,10},{9,11},{10,... | collective-permute-start | bytes 1327112 | tf_op jit(solution)/shard_map/ppermute | solution.py:326
  19.9 15.8 %collective-permute-start.7 = (f32[72,1536]{1,0:T(8,128)S(1)}, f32[72,1536]{1,0:T(8,128)S(1)}, u32[]{:S(2)}, u32[]{:S(2)}) collective-permute-start(f32[72,1536]{1,0:T(8,128)S(1)} %select_maximum_fusion), channel_id=1, source_target_pairs={{2,4},{3,5},{4,2},{5,3},{0,0},{1,1},{6,6},{7,7},{10,12},{11,13},{1... | collective-permute-start | bytes 1327112 | tf_op jit(solution)/shard_map/ppermute | solution.py:326
  29.7 19.7 %collective-permute-start.9 = (f32[1024,128]{1,0:T(8,128)S(1)}, f32[1024,128]{1,0:T(8,128)S(1)}, u32[]{:S(2)}, u32[]{:S(2)}) collective-permute-start(f32[1024,128]{1,0:T(8,128)S(1)} %pairs.8), channel_id=1, source_target_pairs={{0,2},{1,3},{6,4},{7,5},{8,10},{9,11},{14,12},{15,13},{16,18},{17,... | collective-permute-start | bytes 1572872 | tf_op jit(solution)/shard_map/ppermute | solution.py:326
  34.9 4.9 %collective-permute-start.6 = (f32[72,1536]{1,0:T(8,128)S(1)}, f32[72,1536]{1,0:T(8,128)S(1)}, u32[]{:S(2)}, u32[]{:S(2)}) collective-permute-start(f32[72,1536]{1,0:T(8,128)S(1)} %collective-permute-done.5.refs_1_.refs_2_), channel_id=1, source_target_pairs={{2,4},{3,5},{4,2},{5,3},{10,12},{11,13},{12,10},{13,11},{18,20},{1... | collective-permute-start | bytes 1327112 | tf_op jit(solution)/shard_map/ppermute | solution.py:326
  35.6 13.7 %collective-permute-start.8 = (f32[72,1536]{1,0:T(8,128)S(1)}, f32[72,1536]{1,0:T(8,128)S(1)}, u32[]{:S(2)}, u32[]{:S(2)}) collective-permute-start(f32[72,1536]{1,0:T(8,128)S(1)} %collective-permute-done.7.refs_1_.refs_2_), channel_id=1, source_target_pairs={{2,0},{3,1},{4,6},{5,7},{10,8},{11,9},{12,14},{13,15},{18,16},{19,... | collective-permute-start | bytes 1327112 | tf_op jit(solution)/shard_map/ppermute | solution.py:326
  54.7 14.7 %collective-permute-start.11 = (f32[1024,128]{1,0:T(8,128)S(1)}, f32[1024,128]{1,0:T(8,128)S(1)}, u32[]{:S(2)}, u32[]{:S(2)}) collective-permute-start(f32[1024,128]{1,0:T(8,128)S(1)} %pairs.10), channel_id=1, source_target_pairs={{2,4},{3,5},{4,2},{5,3},{10,12},{11,13},{12,10},{13,11},{18,20},{1... | collective-permute-start | bytes 1572872 | tf_op jit(solution)/shard_map/ppermute | solution.py:326
  55.4 11.1 %collective-permute-start.10 = (f32[512,128]{1,0:T(8,128)S(1)}, f32[512,128]{1,0:T(8,128)S(1)}, u32[]{:S(2)}, u32[]{:S(2)}) collective-permute-start(f32[512,128]{1,0:T(8,128)S(1)} %pairs.9), channel_id=1, source_target_pairs={{0,2},{1,3},{6,4},{7,5},{8,10},{9,11},{14,12},{15,13},{16,18},{17,... | collective-permute-start | bytes 786440 | tf_op jit(solution)/shard_map/ppermute | solution.py:326
  59.8 17.9 %collective-permute-start.12 = (f32[1024,128]{1,0:T(8,128)S(1)}, f32[1024,128]{1,0:T(8,128)S(1)}, u32[]{:S(2)}, u32[]{:S(2)}) collective-permute-start(f32[1024,128]{1,0:T(8,128)S(1)} %pairs.10), channel_id=1, source_target_pairs={{0,2},{1,3},{6,4},{7,5},{8,10},{9,11},{14,12},{15,13},{16,18},{17,... | collective-permute-start | bytes 1572872 | tf_op jit(solution)/shard_map/ppermute | solution.py:326
  74.6 30.1 %collective-permute-start.20 = (f32[1024,128]{1,0:T(8,128)S(1)}, f32[1024,128]{1,0:T(8,128)S(1)}, u32[]{:S(2)}, u32[]{:S(2)}) collective-permute-start(f32[1024,128]{1,0:T(8,128)S(1)} %pairs.12), channel_id=1, source_target_pairs={{0,2},{1,3},{2,0},{3,1},{4,6},{5,7},{6,4},{7,5},{8,10},{9,11},{10,... | collective-permute-start | bytes 1572872 | tf_op jit(solution)/shard_map/ppermute | solution.py:326
  82.9 21.8 %collective-permute-start.21 = (f32[1024,128]{1,0:T(8,128)S(1)}, f32[1024,128]{1,0:T(8,128)S(1)}, u32[]{:S(2)}, u32[]{:S(2)}) collective-permute-start(f32[1024,128]{1,0:T(8,128)S(1)} %pairs.13), channel_id=1, source_target_pairs={{2,4},{3,5},{4,2},{5,3},{0,0},{1,1},{6,6},{7,7},{10,12},{11,13},{1... | collective-permute-start | bytes 1572872 | tf_op jit(solution)/shard_map/ppermute | solution.py:326
  83.6 9.6 %collective-permute-start.13 = (f32[512,128]{1,0:T(8,128)S(1)}, f32[512,128]{1,0:T(8,128)S(1)}, u32[]{:S(2)}, u32[]{:S(2)}) collective-permute-start(f32[512,128]{1,0:T(8,128)S(1)} %pairs.11), channel_id=1, source_target_pairs={{2,4},{3,5},{4,2},{5,3},{10,12},{11,13},{12,10},{13,11},{18,20},{1... | collective-permute-start | bytes 786440 | tf_op jit(solution)/shard_map/ppermute | solution.py:326
  84.3 22.1 %collective-permute-start.15 = (f32[512,128]{1,0:T(8,128)S(1)}, f32[512,128]{1,0:T(8,128)S(1)}, u32[]{:S(2)}, u32[]{:S(2)}) collective-permute-start(f32[512,128]{1,0:T(8,128)S(1)} %pairs.11), channel_id=1, source_target_pairs={{0,2},{1,3},{6,4},{7,5},{8,10},{9,11},{14,12},{15,13},{16,18},{17,... | collective-permute-start | bytes 786440 | tf_op jit(solution)/shard_map/ppermute | solution.py:326
  96.0 16.0 %collective-permute-start.14 = (f32[512,128]{1,0:T(8,128)S(1)}, f32[512,128]{1,0:T(8,128)S(1)}, u32[]{:S(2)}, u32[]{:S(2)}) collective-permute-start(f32[512,128]{1,0:T(8,128)S(1)} %pairs.14), channel_id=1, source_target_pairs={{0,2},{1,3},{2,0},{3,1},{4,6},{5,7},{6,4},{7,5},{8,10},{9,11},{10,... | collective-permute-start | bytes 786440 | tf_op jit(solution)/shard_map/ppermute | solution.py:326
  104.8 6.7 %copy-start = (f32[1024,128]{1,0:T(8,128)}, f32[1024,128]{1,0:T(8,128)S(1)}, u32[]{:S(2)}) copy-start(f32[1024,128]{1,0:T(8,128)S(1)} %multiply_add_fusion.refs_1_) | copy-start | bytes 1572868
  104.9 14.9 %collective-permute-start.22 = (f32[1024,128]{1,0:T(8,128)S(1)}, f32[1024,128]{1,0:T(8,128)S(1)}, u32[]{:S(2)}, u32[]{:S(2)}) collective-permute-start(f32[1024,128]{1,0:T(8,128)S(1)} %multiply_add_fusion.refs_1_), channel_id=1, source_target_pairs={{0,8},{8,0},{16,24},{24,16},{1,9},{9,1},{17,25},{25,17},{2,10},{10... | collective-permute-start | bytes 1572872 | tf_op jit(solution)/shard_map/ppermute | solution.py:414
  109.3 2.8 %collective-permute-start.16 = (f32[512,128]{1,0:T(8,128)S(1)}, f32[512,128]{1,0:T(8,128)S(1)}, u32[]{:S(2)}, u32[]{:S(2)}) collective-permute-start(f32[512,128]{1,0:T(8,128)S(1)} %pairs.15), channel_id=1, source_target_pairs={{2,4},{3,5},{4,2},{5,3},{0,0},{1,1},{6,6},{7,7},{10,12},{11,13},{1... | collective-permute-start | bytes 786440 | tf_op jit(solution)/shard_map/ppermute | solution.py:326
  110.0 27.2 %collective-permute-start.23 = (f32[1024,128]{1,0:T(8,128)S(1)}, f32[1024,128]{1,0:T(8,128)S(1)}, u32[]{:S(2)}, u32[]{:S(2)}) collective-permute-start(f32[1024,128]{1,0:T(8,128)S(1)} %multiply_add_fusion.refs_1_), channel_id=1, source_target_pairs={{0,16},{8,24},{16,0},{24,8},{1,17},{9,25},{17,1},{25,9},{2,18},{10... | collective-permute-start | bytes 1572872 | tf_op jit(solution)/shard_map/ppermute | solution.py:414
  111.6 25.6 %collective-permute-start.24 = (f32[1024,128]{1,0:T(8,128)S(1)}, f32[1024,128]{1,0:T(8,128)S(1)}, u32[]{:S(2)}, u32[]{:S(2)}) collective-permute-start(f32[1024,128]{1,0:T(8,128)S(1)} %multiply_add_fusion.refs_1_), channel_id=1, source_target_pairs={{0,24},{8,16},{16,8},{24,0},{1,25},{9,17},{17,9},{25,1},{2,26},{10... | collective-permute-start | bytes 1572872 | tf_op jit(solution)/shard_map/ppermute | solution.py:414
  112.1 29.6 %copy-start.1 = (f32[512,128]{1,0:T(8,128)}, f32[512,128]{1,0:T(8,128)S(1)}, u32[]{:S(2)}) copy-start(f32[512,128]{1,0:T(8,128)S(1)} %multiply_add_fusion.1.refs_1_) | copy-start | bytes 786436
  112.1 29.5 %collective-permute-start.17 = (f32[512,128]{1,0:T(8,128)S(1)}, f32[512,128]{1,0:T(8,128)S(1)}, u32[]{:S(2)}, u32[]{:S(2)}) collective-permute-start(f32[512,128]{1,0:T(8,128)S(1)} %multiply_add_fusion.1.refs_1_), channel_id=1, source_target_pairs={{0,8},{8,0},{16,24},{24,16},{1,9},{9,1},{17,25},{25,17},{2,10},{10... | collective-permute-start | bytes 786440 | tf_op jit(solution)/shard_map/ppermute | solution.py:414
  113.7 28.0 %collective-permute-start.18 = (f32[512,128]{1,0:T(8,128)S(1)}, f32[512,128]{1,0:T(8,128)S(1)}, u32[]{:S(2)}, u32[]{:S(2)}) collective-permute-start(f32[512,128]{1,0:T(8,128)S(1)} %multiply_add_fusion.1.refs_1_), channel_id=1, source_target_pairs={{0,16},{8,24},{16,0},{24,8},{1,17},{9,25},{17,1},{25,9},{2,18},{10... | collective-permute-start | bytes 786440 | tf_op jit(solution)/shard_map/ppermute | solution.py:414
  119.7 17.5 %copy-start.2 = (f32[1024,128]{1,0:T(8,128)}, f32[1024,128]{1,0:T(8,128)S(1)}, u32[]{:S(2)}) copy-start(f32[1024,128]{1,0:T(8,128)S(1)} %collective-permute-done.22.refs_2_) | copy-start | bytes 1572868
  119.7 22.0 %collective-permute-start.19 = (f32[512,128]{1,0:T(8,128)S(1)}, f32[512,128]{1,0:T(8,128)S(1)}, u32[]{:S(2)}, u32[]{:S(2)}) collective-permute-start(f32[512,128]{1,0:T(8,128)S(1)} %multiply_add_fusion.1.refs_1_), channel_id=1, source_target_pairs={{0,24},{8,16},{16,8},{24,0},{1,25},{9,17},{17,9},{25,1},{2,26},{10... | collective-permute-start | bytes 786440 | tf_op jit(solution)/shard_map/ppermute | solution.py:414
  137.2 0.8 copy-start.3
  138.0 0.8 copy-start.4
  141.7 0.7 copy-start.5
  141.7 0.8 copy-start.6
  142.5 0.7 copy-start.7

commit v4 on v3

--- a/solution.py
+++ b/solution.py
@@ -298,6 +298,7 @@
         out_specs=pl.BlockSpec(memory_space=pl.ANY),
         out_shape=jax.ShapeDtypeStruct((groups * per * leaf, columns), F32),
         scratch_shapes=[pltpu.SemaphoreType.DMA((groups,))],
+        compiler_params=pltpu.CompilerParams(vmem_limit_bytes=8 << 20),
         input_output_aliases={1 + groups: 0} if aliased else {},
         name="spread",
     )(place, *pieces, *aliased)
@@ -344,8 +345,7 @@
     proj, parcel, place, mask, inner = lax.optimization_barrier(
         (proj, parcel, place, mask, inner)
     )
-    late = per // 3
-    chunks = [(0, per - late)] + ([(per - late, late)] if late else [])
+    chunks = [(first, 1) for first in range(per)]
     sizes = {
         "leaf": leaf,
         "per": per,
@@ -377,7 +377,9 @@
         inward = [(0, 1), (3, 2)]
         outward = [(1, 0), (2, 3)]
         cross = [(1, 2), (2, 1)]
-        of_a, of_c, of_d = shift(parcel, ends), shift(parcel, sides), shift(parcel, middle)
+
+        of_a = shift(parcel, ends)
+        of_c, of_d = shift(parcel, sides), shift(parcel, middle)
         of_b = (shift(of_c, cross), shift(of_d, outward))
         sources = make_sources()
         before = None
@@ -397,7 +399,10 @@
         for k in every:
             c = work((of_c,), shift(b[k], cross), k)
             d = work((of_d,), shift(b[k], inward), k)
-            done.append(shift(c, sides) + shift(d, middle) + a[k] * inner)
+            from_c, from_d = shift(c, sides), shift(d, middle)
+            if done:
+                from_c, _ = lax.optimization_barrier((from_c, done[-1]))
+            done.append(from_c + from_d + a[k] * inner)
     else:
         sources = make_sources()
         total = None
@@ -410,10 +415,11 @@
 
     out = None
     for (first, _), piece in zip(chunks, done):
-        pieces = [
-            lax.ppermute(piece, "grp", [(g, g ^ m) for g in range(groups)]) if m else piece
-            for m in range(groups)
-        ]
+        pieces = [piece]
+        for m in range(1, groups):
+            pieces.append(
+                lax.ppermute(piece, "grp", [(g, g ^ m) for g in range(groups)])
+            )
         out = spread(mask, pieces, out, per, first, leaf)
     return out
 

time: 146 us -> 144 us (0.986)
  the two profiles are of different devices: /device:TPU:0 before, /device:TPU:18 now
where the time goes in v4:
time: 144 us
  Pallas kernels  51.3 us (36%)
  starting transfers between devices  46.7 us (32%)
  waiting for transfers between devices  42.9 us (30%)
  local copies, waits for them, and re-layouts  1.89 us (1%)
    ppermute x20, starting transfers between devices, shift(): return lax.ppermute(array, 'dev', along(moves))  36.4 us
    pallas_call x12, Pallas kernels, pairs(): pl.pallas_call(functools.partial(pair_kernel, plan), grid=(count,), in_sp...  34.7 us
    ppermute x9, waiting for transfers between devices, on_device(): lax.ppermute(piece, 'grp', [(g, g ^ m) for g in range(groups)])  21.6 us
    ppermute x20, waiting for transfers between devices, shift(): return lax.ppermute(array, 'dev', along(moves))  20 us
    pallas_call x2, Pallas kernels, prepared(): pl.pallas_call(functools.partial(body, scale), grid=(count // block,), in...  12 us
    ppermute x9, starting transfers between devices, on_device(): lax.ppermute(piece, 'grp', [(g, g ^ m) for g in range(groups)])  9.55 us
    pallas_call x3, Pallas kernels, spread(): pl.pallas_call(functools.partial(spread_kernel, groups, per, first, leaf,...  4.62 us
  transfers between devices with their start and end apart: 33, of which 10 were waited for; matrix products, arithmetic and copies ran while one was open for 2% of the time, Pallas kernels for 35%

profile of v4, /device:TPU:18, one launch (start us, length us, event | category | flops | bytes accessed | tf_op | source)
XLA Modules:
  0.0 143.7 jit_solution(3632608221217061550)
XLA Ops:
  0.0 0.0 collective-permute-start.2
  0.0 0.5 collective-permute-start.1
  0.5 0.8 copy.9
  1.3 0.1 reshape.5
  1.4 0.1 pad_add_fusion.refs_0_
  1.5 1.0 constant_dynamic-slice_fusion
  2.6 8.1 %prepared.2 = (bf16[12,256,512]{2,1,0:T(8,128)(2,1)S(1)}, bf16[12,512,256]{2,1,0:T(8,128)(2,1)S(1)}, bf16[256,256]{1,0:T(8,128)(2,1)S(1)}, bf16[256,256]{1,0:T(8...) custom-call(s32[1,256]{1,0:T(1,128)} %idx_ref.1, f32[64,6144]{1,0:T(8,128)} %points_ref.1, ...), custom_call_target="tpu_custom_call" | custom-call | flops 1610612736 | bytes 20447232 | tf_op jit(solution)/shard_map/prepared/pallas_call | solution.py:258
  10.7 1.6 %collective-permute-start.5 = (f32[72,1536]{1,0:T(8,128)S(1)}, f32[72,1536]{1,0:T(8,128)S(1)}, u32[]{:S(2)}, u32[]{:S(2)}) collective-permute-start(f32[72,1536]{1,0:T(8,128)S(1)} %select_maximum_fusion), channel_id=1, source_target_pairs={{0,2},{1,3},{2,0},{3,1},{4,6},{5,7},{6,4},{7,5},{8,10},{9,11},{10,... | collective-permute-start | bytes 1327112 | tf_op jit(solution)/shard_map/ppermute | solution.py:327
  12.3 1.9 %collective-permute-start.7 = (f32[72,1536]{1,0:T(8,128)S(1)}, f32[72,1536]{1,0:T(8,128)S(1)}, u32[]{:S(2)}, u32[]{:S(2)}) collective-permute-start(f32[72,1536]{1,0:T(8,128)S(1)} %select_maximum_fusion), channel_id=1, source_target_pairs={{2,4},{3,5},{4,2},{5,3},{0,0},{1,1},{6,6},{7,7},{10,12},{11,13},{1... | collective-permute-start | bytes 1327112 | tf_op jit(solution)/shard_map/ppermute | solution.py:327
  14.2 0.3 collective-permute-start.4
  14.5 1.3 collective-permute-done.4.summed_ref
  15.8 0.7 collective-permute-start
  16.5 7.2 %collective-permute-done.5.refs_1_.refs_2_ = f32[72,1536]{1,0:T(8,128)S(1)} collective-permute-done((f32[72,1536]{1,0:T(8,128)S(1)}, f32[72,1536]{1,0:T(8,128)S(1)}, u32[]{:S(2)}, u32[]{:S(2)}) %collective-permute-start.5) | collective-permute-done | bytes 442400 | tf_op jit(solution)/shard_map/ppermute | solution.py:327
  23.8 2.3 %collective-permute-start.6 = (f32[72,1536]{1,0:T(8,128)S(1)}, f32[72,1536]{1,0:T(8,128)S(1)}, u32[]{:S(2)}, u32[]{:S(2)}) collective-permute-start(f32[72,1536]{1,0:T(8,128)S(1)} %collective-permute-done.5.refs_1_.refs_2_), channel_id=1, source_target_pairs={{2,4},{3,5},{4,2},{5,3},{10,12},{11,13},{12,10},{13,11},{18,20},{1... | collective-permute-start | bytes 1327112 | tf_op jit(solution)/shard_map/ppermute | solution.py:327
  26.1 10.6 %collective-permute-done.7.refs_1_.refs_2_ = f32[72,1536]{1,0:T(8,128)S(1)} collective-permute-done((f32[72,1536]{1,0:T(8,128)S(1)}, f32[72,1536]{1,0:T(8,128)S(1)}, u32[]{:S(2)}, u32[]{:S(2)}) %collective-permute-start.7) | collective-permute-done | bytes 442400 | tf_op jit(solution)/shard_map/ppermute | solution.py:327
  36.7 1.3 collective-permute-start.8
  38.0 3.9 %prepared.3 = (bf16[12,256,512]{2,1,0:T(8,128)(2,1)S(1)}, bf16[12,512,256]{2,1,0:T(8,128)(2,1)S(1)}, bf16[256,256]{1,0:T(8,128)(2,1)S(1)}, bf16[256,256]{1,0:T(8,128)(2,1)S(1)}) custom-call(f32[64,6144]{1,0:T(8,128)S(1)} %collective-permute-done.1.points_ref, f32[6144,128]{1,0:T(8,128)} %collective-permute-done.2.weights_ref, ...), custom_call_target="tpu_custom_call" | custom-call | flops 1610612736 | bytes 14155776 | tf_op jit(solution)/shard_map/prepared/pallas_call | solution.py:258
  42.0 2.9 %pairs.12 = f32[512,128]{1,0:T(8,128)S(1)} custom-call(s32[3]{0:T(128)S(1)} %pad_add_fusion.refs_0_, f32[72,1536]{1,0:T(8,128)S(1)} %collective-permute-done.refs_1_.refs_2_, f32[72,1536]{1,0:T(8,128)S(1)} %collective-permute-done.refs_1_.refs_2_, bf16[12,256,512]{2,1,0:T(8,128)(2,1)S(1)} %get-tuple-element.37.refs_3_.refs_6_.refs_4_, ...), custom_call_target="tpu_custom_call" | custom-call | flops 2013265920 | bytes 1572864 | tf_op jit(solution)/shard_map/pairs/pallas_call | solution.py:143
  44.8 1.3 collective-permute-start.9
  46.1 2.9 %pairs.13 = f32[512,128]{1,0:T(8,128)S(1)} custom-call(s32[3]{0:T(128)S(1)} %pad_add_fusion.refs_0_, f32[72,1536]{1,0:T(8,128)S(1)} %collective-permute-done.refs_1_.refs_2_, f32[72,1536]{1,0:T(8,128)S(1)} %collective-permute-done.refs_1_.refs_2_, bf16[12,256,512]{2,1,0:T(8,128)(2,1)S(1)} %get-tuple-element.37.refs_3_.refs_6_.refs_4_, ...), custom_call_target="tpu_custom_call" | custom-call | flops 2013265920 | bytes 1572864 | tf_op jit(solution)/shard_map/pairs/pallas_call | solution.py:143
  49.0 1.3 collective-permute-start.10
  50.3 2.9 %pairs.14 = f32[512,128]{1,0:T(8,128)S(1)} custom-call(s32[3]{0:T(128)S(1)} %pad_add_fusion.refs_0_, f32[72,1536]{1,0:T(8,128)S(1)} %collective-permute-done.refs_1_.refs_2_, f32[72,1536]{1,0:T(8,128)S(1)} %collective-permute-done.refs_1_.refs_2_, bf16[12,256,512]{2,1,0:T(8,128)(2,1)S(1)} %get-tuple-element.37.refs_3_.refs_6_.refs_4_, ...), custom_call_target="tpu_custom_call" | custom-call | flops 2013265920 | bytes 1572864 | tf_op jit(solution)/shard_map/pairs/pallas_call | solution.py:143
  53.2 1.3 collective-permute-start.11
  54.5 0.5 collective-permute-done.9.refs_5_
  55.0 2.9 %pairs.15 = f32[512,128]{1,0:T(8,128)S(1)} custom-call(s32[3]{0:T(128)S(1)} %pad_add_fusion.refs_0_, f32[72,1536]{1,0:T(8,128)S(1)} %collective-permute-done.6.refs_1_.refs_3_, f32[72,1536]{1,0:T(8,128)S(1)} %collective-permute-done.8.refs_2_.refs_4_, f32[72,1536]{1,0:T(8,128)S(1)} %collective-permute-done.6.refs_1_.refs_3_, ...), custom_call_target="tpu_custom_call" | custom-call | flops 2013265920 | bytes 1572864 | tf_op jit(solution)/shard_map/pairs/pallas_call | solution.py:143
  57.9 2.5 %collective-permute-start.12 = (f32[512,128]{1,0:T(8,128)S(1)}, f32[512,128]{1,0:T(8,128)S(1)}, u32[]{:S(2)}, u32[]{:S(2)}) collective-permute-start(f32[512,128]{1,0:T(8,128)S(1)} %pairs.15), channel_id=1, source_target_pairs={{2,4},{3,5},{4,2},{5,3},{10,12},{11,13},{12,10},{13,11},{18,20},{1... | collective-permute-start | bytes 786440 | tf_op jit(solution)/shard_map/ppermute | solution.py:327
  60.4 1.5 %collective-permute-start.13 = (f32[512,128]{1,0:T(8,128)S(1)}, f32[512,128]{1,0:T(8,128)S(1)}, u32[]{:S(2)}, u32[]{:S(2)}) collective-permute-start(f32[512,128]{1,0:T(8,128)S(1)} %pairs.15), channel_id=1, source_target_pairs={{0,2},{1,3},{6,4},{7,5},{8,10},{9,11},{14,12},{15,13},{16,18},{17,... | collective-permute-start | bytes 786440 | tf_op jit(solution)/shard_map/ppermute | solution.py:327
  61.9 2.9 %pairs.16 = f32[512,128]{1,0:T(8,128)S(1)} custom-call(s32[3]{0:T(128)S(1)} %pad_add_fusion.refs_0_, f32[72,1536]{1,0:T(8,128)S(1)} %collective-permute-done.6.refs_1_.refs_3_, f32[72,1536]{1,0:T(8,128)S(1)} %collective-permute-done.8.refs_2_.refs_4_, f32[72,1536]{1,0:T(8,128)S(1)} %collective-permute-done.6.refs_1_.refs_3_, ...), custom_call_target="tpu_custom_call" | custom-call | flops 2013265920 | bytes 1572864 | tf_op jit(solution)/shard_map/pairs/pallas_call | solution.py:143
  64.9 3.3 %collective-permute-start.14 = (f32[512,128]{1,0:T(8,128)S(1)}, f32[512,128]{1,0:T(8,128)S(1)}, u32[]{:S(2)}, u32[]{:S(2)}) collective-permute-start(f32[512,128]{1,0:T(8,128)S(1)} %pairs.16), channel_id=1, source_target_pairs={{2,4},{3,5},{4,2},{5,3},{10,12},{11,13},{12,10},{13,11},{18,20},{1... | collective-permute-start | bytes 786440 | tf_op jit(solution)/shard_map/ppermute | solution.py:327
  68.2 1.3 collective-permute-start.15
  69.5 2.9 %pairs.17 = f32[512,128]{1,0:T(8,128)S(1)} custom-call(s32[3]{0:T(128)S(1)} %pad_add_fusion.refs_0_, f32[72,1536]{1,0:T(8,128)S(1)} %collective-permute-done.6.refs_1_.refs_3_, f32[72,1536]{1,0:T(8,128)S(1)} %collective-permute-done.8.refs_2_.refs_4_, f32[72,1536]{1,0:T(8,128)S(1)} %collective-permute-done.6.refs_1_.refs_3_, ...), custom_call_target="tpu_custom_call" | custom-call | flops 2013265920 | bytes 1572864 | tf_op jit(solution)/shard_map/pairs/pallas_call | solution.py:143
  72.5 2.5 %collective-permute-start.16 = (f32[512,128]{1,0:T(8,128)S(1)}, f32[512,128]{1,0:T(8,128)S(1)}, u32[]{:S(2)}, u32[]{:S(2)}) collective-permute-start(f32[512,128]{1,0:T(8,128)S(1)} %pairs.17), channel_id=1, source_target_pairs={{2,4},{3,5},{4,2},{5,3},{10,12},{11,13},{12,10},{13,11},{18,20},{1... | collective-permute-start | bytes 786440 | tf_op jit(solution)/shard_map/ppermute | solution.py:327
  75.0 1.3 collective-permute-start.22
  76.3 2.9 %pairs.18 = f32[512,128]{1,0:T(8,128)S(1)} custom-call(s32[3]{0:T(128)S(1)} %pad_add_fusion.refs_0_, f32[72,1536]{1,0:T(8,128)S(1)} %collective-permute-done.5.refs_1_.refs_2_, f32[72,1536]{1,0:T(8,128)S(1)} %collective-permute-done.5.refs_1_.refs_2_, f32[512,128]{1,0:T(8,128)S(1)} %collective-permute-done.12.refs_3_, ...), custom_call_target="tpu_custom_call" | custom-call | flops 2013265920 | bytes 1572864 | tf_op jit(solution)/shard_map/pairs/pallas_call | solution.py:143
  79.2 2.9 %pairs.19 = f32[512,128]{1,0:T(8,128)S(1)} custom-call(s32[3]{0:T(128)S(1)} %pad_add_fusion.refs_0_, f32[72,1536]{1,0:T(8,128)S(1)} %collective-permute-done.7.refs_1_.refs_2_, f32[72,1536]{1,0:T(8,128)S(1)} %collective-permute-done.7.refs_1_.refs_2_, f32[512,128]{1,0:T(8,128)S(1)} %collective-permute-done.13.refs_3_, ...), custom_call_target="tpu_custom_call" | custom-call | flops 2013265920 | bytes 1572864 | tf_op jit(solution)/shard_map/pairs/pallas_call | solution.py:143
  82.1 2.9 %pairs.20 = f32[512,128]{1,0:T(8,128)S(1)} custom-call(s32[3]{0:T(128)S(1)} %pad_add_fusion.refs_0_, f32[72,1536]{1,0:T(8,128)S(1)} %collective-permute-done.5.refs_1_.refs_2_, f32[72,1536]{1,0:T(8,128)S(1)} %collective-permute-done.5.refs_1_.refs_2_, f32[512,128]{1,0:T(8,128)S(1)} %collective-permute-done.14.refs_3_, ...), custom_call_target="tpu_custom_call" | custom-call | flops 2013265920 | bytes 1572864 | tf_op jit(solution)/shard_map/pairs/pallas_call | solution.py:143
  84.9 2.7 %collective-permute-start.18 = (f32[512,128]{1,0:T(8,128)S(1)}, f32[512,128]{1,0:T(8,128)S(1)}, u32[]{:S(2)}, u32[]{:S(2)}) collective-permute-start(f32[512,128]{1,0:T(8,128)S(1)} %pairs.20), channel_id=1, source_target_pairs={{0,2},{1,3},{2,0},{3,1},{4,6},{5,7},{6,4},{7,5},{8,10},{9,11},{10,... | collective-permute-start | bytes 786440 | tf_op jit(solution)/shard_map/ppermute | solution.py:327
  87.7 0.1 collective-permute-start.19
  87.7 3.6 %collective-permute-start.20 = (f32[512,128]{1,0:T(8,128)S(1)}, f32[512,128]{1,0:T(8,128)S(1)}, u32[]{:S(2)}, u32[]{:S(2)}) collective-permute-start(f32[512,128]{1,0:T(8,128)S(1)} %pairs.19), channel_id=1, source_target_pairs={{2,4},{3,5},{4,2},{5,3},{0,0},{1,1},{6,6},{7,7},{10,12},{11,13},{1... | collective-permute-start | bytes 786440 | tf_op jit(solution)/shard_map/ppermute | solution.py:327
  91.3 2.9 %pairs.21 = f32[512,128]{1,0:T(8,128)S(1)} custom-call(s32[3]{0:T(128)S(1)} %pad_add_fusion.refs_0_, f32[72,1536]{1,0:T(8,128)S(1)} %collective-permute-done.7.refs_1_.refs_2_, f32[72,1536]{1,0:T(8,128)S(1)} %collective-permute-done.7.refs_1_.refs_2_, f32[512,128]{1,0:T(8,128)S(1)} %collective-permute-done.15.refs_3_, ...), custom_call_target="tpu_custom_call" | custom-call | flops 2013265920 | bytes 1572864 | tf_op jit(solution)/shard_map/pairs/pallas_call | solution.py:143
  94.2 2.9 %pairs.22 = f32[512,128]{1,0:T(8,128)S(1)} custom-call(s32[3]{0:T(128)S(1)} %pad_add_fusion.refs_0_, f32[72,1536]{1,0:T(8,128)S(1)} %collective-permute-done.5.refs_1_.refs_2_, f32[72,1536]{1,0:T(8,128)S(1)} %collective-permute-done.5.refs_1_.refs_2_, f32[512,128]{1,0:T(8,128)S(1)} %collective-permute-done.16.refs_3_, ...), custom_call_target="tpu_custom_call" | custom-call | flops 2013265920 | bytes 1572864 | tf_op jit(solution)/shard_map/pairs/pallas_call | solution.py:143
  97.1 0.1 collective-permute-start.17
  97.2 2.6 %collective-permute-start.21 = (f32[512,128]{1,0:T(8,128)S(1)}, f32[512,128]{1,0:T(8,128)S(1)}, u32[]{:S(2)}, u32[]{:S(2)}) collective-permute-start(f32[512,128]{1,0:T(8,128)S(1)} %pairs.21), channel_id=1, source_target_pairs={{2,4},{3,5},{4,2},{5,3},{0,0},{1,1},{6,6},{7,7},{10,12},{11,13},{1... | collective-permute-start | bytes 786440 | tf_op jit(solution)/shard_map/ppermute | solution.py:327
  99.8 2.9 %pairs.23 = f32[512,128]{1,0:T(8,128)S(1)} custom-call(s32[3]{0:T(128)S(1)} %pad_add_fusion.refs_0_, f32[72,1536]{1,0:T(8,128)S(1)} %collective-permute-done.7.refs_1_.refs_2_, f32[72,1536]{1,0:T(8,128)S(1)} %collective-permute-done.7.refs_1_.refs_2_, f32[512,128]{1,0:T(8,128)S(1)} %collective-permute-done.22.refs_3_, ...), custom_call_target="tpu_custom_call" | custom-call | flops 2013265920 | bytes 1572864 | tf_op jit(solution)/shard_map/pairs/pallas_call | solution.py:143
  102.7 3.2 %collective-permute-start.23 = (f32[512,128]{1,0:T(8,128)S(1)}, f32[512,128]{1,0:T(8,128)S(1)}, u32[]{:S(2)}, u32[]{:S(2)}) collective-permute-start(f32[512,128]{1,0:T(8,128)S(1)} %pairs.23), channel_id=1, source_target_pairs={{2,4},{3,5},{4,2},{5,3},{0,0},{1,1},{6,6},{7,7},{10,12},{11,13},{1... | collective-permute-start | bytes 786440 | tf_op jit(solution)/shard_map/ppermute | solution.py:327
  106.0 1.6 %collective-permute-done.21 = f32[512,128]{1,0:T(8,128)S(1)} collective-permute-done((f32[512,128]{1,0:T(8,128)S(1)}, f32[512,128]{1,0:T(8,128)S(1)}, u32[]{:S(2)}, u32[]{:S(2)}) %collective-permute-start.21) | collective-permute-done | bytes 262176 | tf_op jit(solution)/shard_map/ppermute | solution.py:327
  107.7 0.6 collective-permute-start.27
  108.2 1.5 %collective-permute-start.30 = (f32[512,128]{1,0:T(8,128)S(1)}, f32[512,128]{1,0:T(8,128)S(1)}, u32[]{:S(2)}, u32[]{:S(2)}) collective-permute-start(f32[512,128]{1,0:T(8,128)S(1)} %multiply_add_fusion.2.refs_1_), channel_id=1, source_target_pairs={{0,8},{8,0},{16,24},{24,16},{1,9},{9,1},{17,25},{25,17},{2,10},{10... | collective-permute-start | bytes 786440 | tf_op jit(solution)/shard_map/ppermute | solution.py:421
  109.8 1.5 %collective-permute-start.31 = (f32[512,128]{1,0:T(8,128)S(1)}, f32[512,128]{1,0:T(8,128)S(1)}, u32[]{:S(2)}, u32[]{:S(2)}) collective-permute-start(f32[512,128]{1,0:T(8,128)S(1)} %multiply_add_fusion.2.refs_1_), channel_id=1, source_target_pairs={{0,16},{8,24},{16,0},{24,8},{1,17},{9,25},{17,1},{25,9},{2,18},{10... | collective-permute-start | bytes 786440 | tf_op jit(solution)/shard_map/ppermute | solution.py:421
  111.3 0.5 collective-permute-start.32
  111.7 1.5 %collective-permute-start.28 = (f32[512,128]{1,0:T(8,128)S(1)}, f32[512,128]{1,0:T(8,128)S(1)}, u32[]{:S(2)}, u32[]{:S(2)}) collective-permute-start(f32[512,128]{1,0:T(8,128)S(1)} %multiply_add_fusion.1.refs_1_), channel_id=1, source_target_pairs={{0,16},{8,24},{16,0},{24,8},{1,17},{9,25},{17,1},{25,9},{2,18},{10... | collective-permute-start | bytes 786440 | tf_op jit(solution)/shard_map/ppermute | solution.py:421
  113.3 0.1 multiply_add_fusion.refs_1_
  113.3 3.6 %collective-permute-done.27.refs_2_ = f32[512,128]{1,0:T(8,128)S(1)} collective-permute-done((f32[512,128]{1,0:T(8,128)S(1)}, f32[512,128]{1,0:T(8,128)S(1)}, u32[]{:S(2)}, u32[]{:S(2)}) %collective-permute-start.27) | collective-permute-done | bytes 262176 | tf_op jit(solution)/shard_map/ppermute | solution.py:421
  116.9 1.5 %collective-permute-start.29 = (f32[512,128]{1,0:T(8,128)S(1)}, f32[512,128]{1,0:T(8,128)S(1)}, u32[]{:S(2)}, u32[]{:S(2)}) collective-permute-start(f32[512,128]{1,0:T(8,128)S(1)} %multiply_add_fusion.1.refs_1_), channel_id=1, source_target_pairs={{0,24},{8,16},{16,8},{24,0},{1,25},{9,17},{17,9},{25,1},{2,26},{10... | collective-permute-start | bytes 786440 | tf_op jit(solution)/shard_map/ppermute | solution.py:421
  118.4 4.1 %collective-permute-done.30.refs_2_ = f32[512,128]{1,0:T(8,128)S(1)} collective-permute-done((f32[512,128]{1,0:T(8,128)S(1)}, f32[512,128]{1,0:T(8,128)S(1)}, u32[]{:S(2)}, u32[]{:S(2)}) %collective-permute-start.30) | collective-permute-done | bytes 262176 | tf_op jit(solution)/shard_map/ppermute | solution.py:421
  122.5 0.5 collective-permute-start.24
  123.0 1.5 %collective-permute-start.25 = (f32[512,128]{1,0:T(8,128)S(1)}, f32[512,128]{1,0:T(8,128)S(1)}, u32[]{:S(2)}, u32[]{:S(2)}) collective-permute-start(f32[512,128]{1,0:T(8,128)S(1)} %multiply_add_fusion.refs_1_), channel_id=1, source_target_pairs={{0,16},{8,24},{16,0},{24,8},{1,17},{9,25},{17,1},{25,9},{2,18},{10... | collective-permute-start | bytes 786440 | tf_op jit(solution)/shard_map/ppermute | solution.py:421
  124.6 4.6 %collective-permute-done.32.refs_4_ = f32[512,128]{1,0:T(8,128)S(1)} collective-permute-done((f32[512,128]{1,0:T(8,128)S(1)}, f32[512,128]{1,0:T(8,128)S(1)}, u32[]{:S(2)}, u32[]{:S(2)}) %collective-permute-start.32) | collective-permute-done | bytes 262176 | tf_op jit(solution)/shard_map/ppermute | solution.py:421
  129.2 0.5 collective-permute-start.26
  129.7 1.5 %spread.3.refs_5_ = f32[6144,128]{1,0:T(8,128)} custom-call(s32[4]{0:T(128)S(1)} %iota_xor_fusion.refs_0_, f32[512,128]{1,0:T(8,128)S(1)} %multiply_add_fusion.2.refs_1_, f32[512,128]{1,0:T(8,128)S(1)} %collective-permute-done.30.refs_2_, f32[512,128]{1,0:T(8,128)S(1)} %collective-permute-done.31.refs_3_, f32[512,128]{1,0:T(8,128)S(1)} %collective-permute-done.32.refs_4_), custom_call_target="tpu_custom_call" | custom-call | tf_op jit(solution)/shard_map/spread/pallas_call | solution.py:293
  131.2 5.1 %collective-permute-done.28.refs_3_ = f32[512,128]{1,0:T(8,128)S(1)} collective-permute-done((f32[512,128]{1,0:T(8,128)S(1)}, f32[512,128]{1,0:T(8,128)S(1)}, u32[]{:S(2)}, u32[]{:S(2)}) %collective-permute-start.28) | collective-permute-done | bytes 262176 | tf_op jit(solution)/shard_map/ppermute | solution.py:421
  136.4 1.5 %spread.4.refs_5_ = f32[6144,128]{1,0:T(8,128)} custom-call(s32[4]{0:T(128)S(1)} %iota_xor_fusion.refs_0_, f32[512,128]{1,0:T(8,128)S(1)} %multiply_add_fusion.1.refs_1_, f32[512,128]{1,0:T(8,128)S(1)} %collective-permute-done.27.refs_2_, f32[512,128]{1,0:T(8,128)S(1)} %collective-permute-done.28.refs_3_, ...), custom_call_target="tpu_custom_call", output_to_operand_aliasing={{}: (5, {})} | custom-call | tf_op jit(solution)/shard_map/spread/pallas_call | solution.py:293
  137.9 4.1 %collective-permute-done.25.refs_3_ = f32[512,128]{1,0:T(8,128)S(1)} collective-permute-done((f32[512,128]{1,0:T(8,128)S(1)}, f32[512,128]{1,0:T(8,128)S(1)}, u32[]{:S(2)}, u32[]{:S(2)}) %collective-permute-start.25) | collective-permute-done | bytes 262176 | tf_op jit(solution)/shard_map/ppermute | solution.py:421
  142.0 1.5 %spread.5 = f32[6144,128]{1,0:T(8,128)} custom-call(s32[4]{0:T(128)S(1)} %iota_xor_fusion.refs_0_, f32[512,128]{1,0:T(8,128)S(1)} %multiply_add_fusion.refs_1_, f32[512,128]{1,0:T(8,128)S(1)} %collective-permute-done.24.refs_2_, f32[512,128]{1,0:T(8,128)S(1)} %collective-permute-done.25.refs_3_, ...), custom_call_target="tpu_custom_call", output_to_operand_aliasing={{}: (5, {})} | custom-call | tf_op jit(solution)/shard_map/spread/pallas_call | solution.py:293
  (30 shorter events, 0.2 us)
Async XLA Ops:
  0.0 38.0 %collective-permute-start.2 = (f32[6144,128]{1,0:T(8,128)}, f32[6144,128]{1,0:T(8,128)}, u32[]{:S(2)}, u32[]{:S(2)}) collective-permute-start(f32[6144,128]{1,0:T(8,128)} %weights_ref.1), channel_id=1, source_target_pairs={{0,1},{1,0},{2,3},{3,2},{4,5},{5,4},{6,7},{7,6},{8,9},{9,8},{10,11... | collective-permute-start | bytes 9437192 | tf_op jit(solution)/shard_map/ppermute | solution.py:364
  0.0 38.0 %collective-permute-start.1 = (f32[64,6144]{1,0:T(8,128)}, f32[64,6144]{1,0:T(8,128)S(1)}, u32[]{:S(2)}, u32[]{:S(2)}) collective-permute-start(f32[64,6144]{1,0:T(8,128)} %points_ref.1), channel_id=1, source_target_pairs={{0,1},{1,0},{2,3},{3,2},{4,5},{5,4},{6,7},{7,6},{8,9},{9,8},{10,11... | collective-permute-start | bytes 4718600 | tf_op jit(solution)/shard_map/ppermute | solution.py:364
  10.7 3.5 %collective-permute-start.3 = (f32[64,256]{1,0:T(8,128)}, f32[64,256]{1,0:T(8,128)S(1)}, u32[]{:S(2)}, u32[]{:S(2)}) collective-permute-start(f32[64,256]{1,0:T(8,128)} %get-tuple-element.41), channel_id=1, source_target_pairs={{0,1},{1,0},{2,3},{3,2},{4,5},{5,4},{6,7},{7,6},{8,9},{9,8},{10,11... | collective-permute-start | bytes 196616 | tf_op jit(solution)/shard_map/ppermute | solution.py:364
  10.7 13.0 %collective-permute-start.5 = (f32[72,1536]{1,0:T(8,128)S(1)}, f32[72,1536]{1,0:T(8,128)S(1)}, u32[]{:S(2)}, u32[]{:S(2)}) collective-permute-start(f32[72,1536]{1,0:T(8,128)S(1)} %select_maximum_fusion), channel_id=1, source_target_pairs={{0,2},{1,3},{2,0},{3,1},{4,6},{5,7},{6,4},{7,5},{8,10},{9,11},{10,... | collective-permute-start | bytes 1327112 | tf_op jit(solution)/shard_map/ppermute | solution.py:327
  12.3 24.4 %collective-permute-start.7 = (f32[72,1536]{1,0:T(8,128)S(1)}, f32[72,1536]{1,0:T(8,128)S(1)}, u32[]{:S(2)}, u32[]{:S(2)}) collective-permute-start(f32[72,1536]{1,0:T(8,128)S(1)} %select_maximum_fusion), channel_id=1, source_target_pairs={{2,4},{3,5},{4,2},{5,3},{0,0},{1,1},{6,6},{7,7},{10,12},{11,13},{1... | collective-permute-start | bytes 1327112 | tf_op jit(solution)/shard_map/ppermute | solution.py:327
  14.2 1.6 %collective-permute-start.4 = (f32[256,128]{1,0:T(8,128)}, f32[256,128]{1,0:T(8,128)S(1)}, u32[]{:S(2)}, u32[]{:S(2)}) collective-permute-start(f32[256,128]{1,0:T(8,128)} %get-tuple-element.42), channel_id=1, source_target_pairs={{0,1},{1,0},{2,3},{3,2},{4,5},{5,4},{6,7},{7,6},{8,9},{9,8},{10,11... | collective-permute-start | bytes 393224 | tf_op jit(solution)/shard_map/ppermute | solution.py:364
  15.8 26.1 %collective-permute-start = (f32[72,1536]{1,0:T(8,128)S(1)}, f32[72,1536]{1,0:T(8,128)S(1)}, u32[]{:S(2)}, u32[]{:S(2)}) collective-permute-start(f32[72,1536]{1,0:T(8,128)S(1)} %select_maximum_fusion), channel_id=1, source_target_pairs={{0,6},{1,7},{6,0},{7,1},{2,2},{3,3},{4,4},{5,5},{8,14},{9,15},{14,... | collective-permute-start | bytes 1327112 | tf_op jit(solution)/shard_map/ppermute | solution.py:327
  23.8 30.8 %collective-permute-start.6 = (f32[72,1536]{1,0:T(8,128)S(1)}, f32[72,1536]{1,0:T(8,128)S(1)}, u32[]{:S(2)}, u32[]{:S(2)}) collective-permute-start(f32[72,1536]{1,0:T(8,128)S(1)} %collective-permute-done.5.refs_1_.refs_2_), channel_id=1, source_target_pairs={{2,4},{3,5},{4,2},{5,3},{10,12},{11,13},{12,10},{13,11},{18,20},{1... | collective-permute-start | bytes 1327112 | tf_op jit(solution)/shard_map/ppermute | solution.py:327
  36.7 17.8 %collective-permute-start.8 = (f32[72,1536]{1,0:T(8,128)S(1)}, f32[72,1536]{1,0:T(8,128)S(1)}, u32[]{:S(2)}, u32[]{:S(2)}) collective-permute-start(f32[72,1536]{1,0:T(8,128)S(1)} %collective-permute-done.7.refs_1_.refs_2_), channel_id=1, source_target_pairs={{2,0},{3,1},{4,6},{5,7},{10,8},{11,9},{12,14},{13,15},{18,16},{19,... | collective-permute-start | bytes 1327112 | tf_op jit(solution)/shard_map/ppermute | solution.py:327
  44.8 10.2 %collective-permute-start.9 = (f32[512,128]{1,0:T(8,128)S(1)}, f32[512,128]{1,0:T(8,128)S(1)}, u32[]{:S(2)}, u32[]{:S(2)}) collective-permute-start(f32[512,128]{1,0:T(8,128)S(1)} %pairs.12), channel_id=1, source_target_pairs={{0,2},{1,3},{6,4},{7,5},{8,10},{9,11},{14,12},{15,13},{16,18},{17,... | collective-permute-start | bytes 786440 | tf_op jit(solution)/shard_map/ppermute | solution.py:327
  49.0 12.9 %collective-permute-start.10 = (f32[512,128]{1,0:T(8,128)S(1)}, f32[512,128]{1,0:T(8,128)S(1)}, u32[]{:S(2)}, u32[]{:S(2)}) collective-permute-start(f32[512,128]{1,0:T(8,128)S(1)} %pairs.13), channel_id=1, source_target_pairs={{0,2},{1,3},{6,4},{7,5},{8,10},{9,11},{14,12},{15,13},{16,18},{17,... | collective-permute-start | bytes 786440 | tf_op jit(solution)/shard_map/ppermute | solution.py:327
  53.2 16.3 %collective-permute-start.11 = (f32[512,128]{1,0:T(8,128)S(1)}, f32[512,128]{1,0:T(8,128)S(1)}, u32[]{:S(2)}, u32[]{:S(2)}) collective-permute-start(f32[512,128]{1,0:T(8,128)S(1)} %pairs.14), channel_id=1, source_target_pairs={{0,2},{1,3},{6,4},{7,5},{8,10},{9,11},{14,12},{15,13},{16,18},{17,... | collective-permute-start | bytes 786440 | tf_op jit(solution)/shard_map/ppermute | solution.py:327
  57.9 17.0 %collective-permute-start.12 = (f32[512,128]{1,0:T(8,128)S(1)}, f32[512,128]{1,0:T(8,128)S(1)}, u32[]{:S(2)}, u32[]{:S(2)}) collective-permute-start(f32[512,128]{1,0:T(8,128)S(1)} %pairs.15), channel_id=1, source_target_pairs={{2,4},{3,5},{4,2},{5,3},{10,12},{11,13},{12,10},{13,11},{18,20},{1... | collective-permute-start | bytes 786440 | tf_op jit(solution)/shard_map/ppermute | solution.py:327
  60.4 18.7 %collective-permute-start.13 = (f32[512,128]{1,0:T(8,128)S(1)}, f32[512,128]{1,0:T(8,128)S(1)}, u32[]{:S(2)}, u32[]{:S(2)}) collective-permute-start(f32[512,128]{1,0:T(8,128)S(1)} %pairs.15), channel_id=1, source_target_pairs={{0,2},{1,3},{6,4},{7,5},{8,10},{9,11},{14,12},{15,13},{16,18},{17,... | collective-permute-start | bytes 786440 | tf_op jit(solution)/shard_map/ppermute | solution.py:327
  64.9 17.2 %collective-permute-start.14 = (f32[512,128]{1,0:T(8,128)S(1)}, f32[512,128]{1,0:T(8,128)S(1)}, u32[]{:S(2)}, u32[]{:S(2)}) collective-permute-start(f32[512,128]{1,0:T(8,128)S(1)} %pairs.16), channel_id=1, source_target_pairs={{2,4},{3,5},{4,2},{5,3},{10,12},{11,13},{12,10},{13,11},{18,20},{1... | collective-permute-start | bytes 786440 | tf_op jit(solution)/shard_map/ppermute | solution.py:327
  68.2 19.5 %collective-permute-start.15 = (f32[512,128]{1,0:T(8,128)S(1)}, f32[512,128]{1,0:T(8,128)S(1)}, u32[]{:S(2)}, u32[]{:S(2)}) collective-permute-start(f32[512,128]{1,0:T(8,128)S(1)} %pairs.16), channel_id=1, source_target_pairs={{0,2},{1,3},{6,4},{7,5},{8,10},{9,11},{14,12},{15,13},{16,18},{17,... | collective-permute-start | bytes 786440 | tf_op jit(solution)/shard_map/ppermute | solution.py:327
  72.5 21.7 %collective-permute-start.16 = (f32[512,128]{1,0:T(8,128)S(1)}, f32[512,128]{1,0:T(8,128)S(1)}, u32[]{:S(2)}, u32[]{:S(2)}) collective-permute-start(f32[512,128]{1,0:T(8,128)S(1)} %pairs.17), channel_id=1, source_target_pairs={{2,4},{3,5},{4,2},{5,3},{10,12},{11,13},{12,10},{13,11},{18,20},{1... | collective-permute-start | bytes 786440 | tf_op jit(solution)/shard_map/ppermute | solution.py:327
  75.0 22.2 %collective-permute-start.22 = (f32[512,128]{1,0:T(8,128)S(1)}, f32[512,128]{1,0:T(8,128)S(1)}, u32[]{:S(2)}, u32[]{:S(2)}) collective-permute-start(f32[512,128]{1,0:T(8,128)S(1)} %pairs.17), channel_id=1, source_target_pairs={{0,2},{1,3},{6,4},{7,5},{8,10},{9,11},{14,12},{15,13},{16,18},{17,... | collective-permute-start | bytes 786440 | tf_op jit(solution)/shard_map/ppermute | solution.py:327
  84.9 21.0 %collective-permute-start.18 = (f32[512,128]{1,0:T(8,128)S(1)}, f32[512,128]{1,0:T(8,128)S(1)}, u32[]{:S(2)}, u32[]{:S(2)}) collective-permute-start(f32[512,128]{1,0:T(8,128)S(1)} %pairs.20), channel_id=1, source_target_pairs={{0,2},{1,3},{2,0},{3,1},{4,6},{5,7},{6,4},{7,5},{8,10},{9,11},{10,... | collective-permute-start | bytes 786440 | tf_op jit(solution)/shard_map/ppermute | solution.py:327
  87.7 15.0 %collective-permute-start.19 = (f32[512,128]{1,0:T(8,128)S(1)}, f32[512,128]{1,0:T(8,128)S(1)}, u32[]{:S(2)}, u32[]{:S(2)}) collective-permute-start(f32[512,128]{1,0:T(8,128)S(1)} %pairs.18), channel_id=1, source_target_pairs={{0,2},{1,3},{2,0},{3,1},{4,6},{5,7},{6,4},{7,5},{8,10},{9,11},{10,... | collective-permute-start | bytes 786440 | tf_op jit(solution)/shard_map/ppermute | solution.py:327
  87.7 18.2 %collective-permute-start.20 = (f32[512,128]{1,0:T(8,128)S(1)}, f32[512,128]{1,0:T(8,128)S(1)}, u32[]{:S(2)}, u32[]{:S(2)}) collective-permute-start(f32[512,128]{1,0:T(8,128)S(1)} %pairs.19), channel_id=1, source_target_pairs={{2,4},{3,5},{4,2},{5,3},{0,0},{1,1},{6,6},{7,7},{10,12},{11,13},{1... | collective-permute-start | bytes 786440 | tf_op jit(solution)/shard_map/ppermute | solution.py:327
  97.1 14.2 %collective-permute-start.17 = (f32[512,128]{1,0:T(8,128)S(1)}, f32[512,128]{1,0:T(8,128)S(1)}, u32[]{:S(2)}, u32[]{:S(2)}) collective-permute-start(f32[512,128]{1,0:T(8,128)S(1)} %pairs.22), channel_id=1, source_target_pairs={{0,2},{1,3},{2,0},{3,1},{4,6},{5,7},{6,4},{7,5},{8,10},{9,11},{10,... | collective-permute-start | bytes 786440 | tf_op jit(solution)/shard_map/ppermute | solution.py:327
  97.2 10.5 %collective-permute-start.21 = (f32[512,128]{1,0:T(8,128)S(1)}, f32[512,128]{1,0:T(8,128)S(1)}, u32[]{:S(2)}, u32[]{:S(2)}) collective-permute-start(f32[512,128]{1,0:T(8,128)S(1)} %pairs.21), channel_id=1, source_target_pairs={{2,4},{3,5},{4,2},{5,3},{0,0},{1,1},{6,6},{7,7},{10,12},{11,13},{1... | collective-permute-start | bytes 786440 | tf_op jit(solution)/shard_map/ppermute | solution.py:327
  102.7 9.1 %collective-permute-start.23 = (f32[512,128]{1,0:T(8,128)S(1)}, f32[512,128]{1,0:T(8,128)S(1)}, u32[]{:S(2)}, u32[]{:S(2)}) collective-permute-start(f32[512,128]{1,0:T(8,128)S(1)} %pairs.23), channel_id=1, source_target_pairs={{2,4},{3,5},{4,2},{5,3},{0,0},{1,1},{6,6},{7,7},{10,12},{11,13},{1... | collective-permute-start | bytes 786440 | tf_op jit(solution)/shard_map/ppermute | solution.py:327
  107.7 9.2 %collective-permute-start.27 = (f32[512,128]{1,0:T(8,128)S(1)}, f32[512,128]{1,0:T(8,128)S(1)}, u32[]{:S(2)}, u32[]{:S(2)}) collective-permute-start(f32[512,128]{1,0:T(8,128)S(1)} %multiply_add_fusion.1.refs_1_), channel_id=1, source_target_pairs={{0,8},{8,0},{16,24},{24,16},{1,9},{9,1},{17,25},{25,17},{2,10},{10... | collective-permute-start | bytes 786440 | tf_op jit(solution)/shard_map/ppermute | solution.py:421
  108.2 14.3 %collective-permute-start.30 = (f32[512,128]{1,0:T(8,128)S(1)}, f32[512,128]{1,0:T(8,128)S(1)}, u32[]{:S(2)}, u32[]{:S(2)}) collective-permute-start(f32[512,128]{1,0:T(8,128)S(1)} %multiply_add_fusion.2.refs_1_), channel_id=1, source_target_pairs={{0,8},{8,0},{16,24},{24,16},{1,9},{9,1},{17,25},{25,17},{2,10},{10... | collective-permute-start | bytes 786440 | tf_op jit(solution)/shard_map/ppermute | solution.py:421
  109.8 13.3 %collective-permute-start.31 = (f32[512,128]{1,0:T(8,128)S(1)}, f32[512,128]{1,0:T(8,128)S(1)}, u32[]{:S(2)}, u32[]{:S(2)}) collective-permute-start(f32[512,128]{1,0:T(8,128)S(1)} %multiply_add_fusion.2.refs_1_), channel_id=1, source_target_pairs={{0,16},{8,24},{16,0},{24,8},{1,17},{9,25},{17,1},{25,9},{2,18},{10... | collective-permute-start | bytes 786440 | tf_op jit(solution)/shard_map/ppermute | solution.py:421
  111.3 17.9 %collective-permute-start.32 = (f32[512,128]{1,0:T(8,128)S(1)}, f32[512,128]{1,0:T(8,128)S(1)}, u32[]{:S(2)}, u32[]{:S(2)}) collective-permute-start(f32[512,128]{1,0:T(8,128)S(1)} %multiply_add_fusion.2.refs_1_), channel_id=1, source_target_pairs={{0,24},{8,16},{16,8},{24,0},{1,25},{9,17},{17,9},{25,1},{2,26},{10... | collective-permute-start | bytes 786440 | tf_op jit(solution)/shard_map/ppermute | solution.py:421
  111.7 24.6 %collective-permute-start.28 = (f32[512,128]{1,0:T(8,128)S(1)}, f32[512,128]{1,0:T(8,128)S(1)}, u32[]{:S(2)}, u32[]{:S(2)}) collective-permute-start(f32[512,128]{1,0:T(8,128)S(1)} %multiply_add_fusion.1.refs_1_), channel_id=1, source_target_pairs={{0,16},{8,24},{16,0},{24,8},{1,17},{9,25},{17,1},{25,9},{2,18},{10... | collective-permute-start | bytes 786440 | tf_op jit(solution)/shard_map/ppermute | solution.py:421
  116.9 19.4 %collective-permute-start.29 = (f32[512,128]{1,0:T(8,128)S(1)}, f32[512,128]{1,0:T(8,128)S(1)}, u32[]{:S(2)}, u32[]{:S(2)}) collective-permute-start(f32[512,128]{1,0:T(8,128)S(1)} %multiply_add_fusion.1.refs_1_), channel_id=1, source_target_pairs={{0,24},{8,16},{16,8},{24,0},{1,25},{9,17},{17,9},{25,1},{2,26},{10... | collective-permute-start | bytes 786440 | tf_op jit(solution)/shard_map/ppermute | solution.py:421
  122.5 15.4 %collective-permute-start.24 = (f32[512,128]{1,0:T(8,128)S(1)}, f32[512,128]{1,0:T(8,128)S(1)}, u32[]{:S(2)}, u32[]{:S(2)}) collective-permute-start(f32[512,128]{1,0:T(8,128)S(1)} %multiply_add_fusion.refs_1_), channel_id=1, source_target_pairs={{0,8},{8,0},{16,24},{24,16},{1,9},{9,1},{17,25},{25,17},{2,10},{10... | collective-permute-start | bytes 786440 | tf_op jit(solution)/shard_map/ppermute | solution.py:421
  123.0 18.9 %collective-permute-start.25 = (f32[512,128]{1,0:T(8,128)S(1)}, f32[512,128]{1,0:T(8,128)S(1)}, u32[]{:S(2)}, u32[]{:S(2)}) collective-permute-start(f32[512,128]{1,0:T(8,128)S(1)} %multiply_add_fusion.refs_1_), channel_id=1, source_target_pairs={{0,16},{8,24},{16,0},{24,8},{1,17},{9,25},{17,1},{25,9},{2,18},{10... | collective-permute-start | bytes 786440 | tf_op jit(solution)/shard_map/ppermute | solution.py:421
  129.2 12.8 %collective-permute-start.26 = (f32[512,128]{1,0:T(8,128)S(1)}, f32[512,128]{1,0:T(8,128)S(1)}, u32[]{:S(2)}, u32[]{:S(2)}) collective-permute-start(f32[512,128]{1,0:T(8,128)S(1)} %multiply_add_fusion.refs_1_), channel_id=1, source_target_pairs={{0,24},{8,16},{16,8},{24,0},{1,25},{9,17},{17,9},{25,1},{2,26},{10... | collective-permute-start | bytes 786440 | tf_op jit(solution)/shard_map/ppermute | solution.py:421

commit v5 on v4

--- a/solution.py
+++ b/solution.py
@@ -8,6 +8,8 @@
 from jax.experimental.pallas import tpu as pltpu
 from jax.sharding import PartitionSpec as P
 
+
+ROUNDS = ("a0", "a1", "d0", "b0", "c0", "b1", "d1", "c1")
 
 F32 = jnp.float32
 BF16 = jnp.bfloat16
@@ -45,7 +47,6 @@
     x_refs = [refs.pop(0) for _ in range(plan["parcels"])]
     init_ref = refs.pop(0) if plan["init"] else None
     sides, (out_ref, xk_buf) = (refs[:4], refs[4:8]), refs[8:]
-    leaf = x_refs[0].shape[1]
     capacity = plan["capacity"]
     devices = plan["devices"]
     scale = plan["scale"]
@@ -57,7 +58,7 @@
         value = sum(ref[n // 128, n % 128] for ref in list_refs)
         return value.astype(jnp.int32)
 
-    number = place_ref[0] * plan["per"] + plan["first"] + step
+    number = place_ref[0] * plan["per"] + (plan["first"] + step) // plan["units"]
     row = number // plan["row_leaves"]
     x = x_refs[0][...]
     for ref in x_refs[1:]:
@@ -71,18 +72,14 @@
     def add(yk, wk, gain):
         wk = jnp.concatenate([wk, wk], axis=0)
         columns = out_ref.shape[1]
-        for t in range(0, leaf, plan["rows"]):
-            part = slice(t, t + plan["rows"])
-            exponent = jnp.dot(xk_buf[part, :], yk, preferred_element_type=F32)
-            value = jnp.exp2(exponent)
-            if gain is not None:
-                value = value * gain
-            high = value.astype(BF16)
-            low = (value - high.astype(F32)).astype(BF16)
-            both = jnp.dot(
-                jnp.concatenate([high, low], axis=1), wk, preferred_element_type=F32
-            )
-            out_ref[part, :] += both[:, :columns] + both[:, columns:]
+        exponent = jnp.dot(xk_buf[...], yk, preferred_element_type=F32)
+        value = jnp.exp2(exponent)
+        if gain is not None:
+            value = value * gain
+        high = value.astype(BF16)
+        low = (value - high.astype(F32)).astype(BF16)
+        both = jnp.dot(jnp.concatenate([high, low], axis=1), wk, preferred_element_type=F32)
+        out_ref[...] += both[:, :columns] + both[:, columns:]
 
     gains = [None] * (slots + 1)
     if not plan["dense"]:
@@ -126,33 +123,33 @@
         init=init is not None,
         first=first,
         count=count,
-        rows=leaf // 2,
-    )
+    )
+    unit = leaf // sizes["units"]
     in_specs = [pl.BlockSpec(memory_space=pltpu.SMEM)]
     in_specs += [
         pl.BlockSpec((8, 128), lambda i: (features // 8, 0), memory_space=pltpu.SMEM)
     ] * len(parcels)
-    in_specs += [pl.BlockSpec((features, leaf), lambda i: (0, first + i))] * len(parcels)
+    in_specs += [pl.BlockSpec((features, unit), lambda i: (0, first + i))] * len(parcels)
     operands = [place, *parcels, *parcels]
     if init is not None:
-        in_specs.append(pl.BlockSpec((leaf, columns), lambda i: (i, 0)))
+        in_specs.append(pl.BlockSpec((unit, columns), lambda i: (i, 0)))
         operands.append(init)
     in_specs += [pl.BlockSpec(memory_space=pltpu.VMEM)] * 8
     operands += [array for side in sources for array in side]
-    work = count * leaf * (leaf * slots + 2 * kept)
+    work = count * unit * (leaf * slots + 2 * kept)
     return pl.pallas_call(
         functools.partial(pair_kernel, plan),
         grid=(count,),
         in_specs=in_specs,
-        out_specs=pl.BlockSpec((leaf, columns), lambda i: (i, 0)),
-        out_shape=jax.ShapeDtypeStruct((count * leaf, columns), F32),
+        out_specs=pl.BlockSpec((unit, columns), lambda i: (i, 0)),
+        out_shape=jax.ShapeDtypeStruct((count * unit, columns), F32),
         scratch_shapes=[
-            pltpu.VMEM((leaf, rows), BF16),
+            pltpu.VMEM((unit, rows), BF16),
         ],
         compiler_params=pltpu.CompilerParams(vmem_limit_bytes=16 << 20),
         cost_estimate=pl.CostEstimate(
             flops=work * 2 * (4 * features + 4 * columns),
-            bytes_accessed=count * slots * leaf * (features + columns) * 4,
+            bytes_accessed=count * slots * unit * (features + columns) * 4,
             transcendentals=work,
         ),
         name="pairs",
@@ -269,14 +266,14 @@
     )(*operands)
 
 
-def spread_kernel(groups, per, first, leaf, aliased, *refs):
+def spread_kernel(groups, per, first, unit, aliased, *refs):
     place_ref = refs[0]
     pieces = refs[1 : 1 + groups]
     out_ref, sem = refs[1 + groups + aliased :]
     size = pieces[0].shape[0]
     copies = []
     for m, piece in enumerate(pieces):
-        start = pl.multiple_of((place_ref[m] * per + first) * leaf, leaf)
+        start = pl.multiple_of((place_ref[m] * per + first) * unit, unit)
         copies.append(
             pltpu.make_async_copy(piece, out_ref.at[pl.ds(start, size), :], sem.at[m])
         )
@@ -286,17 +283,17 @@
         copy.wait()
 
 
-def spread(place, pieces, out, per, first, leaf):
+def spread(place, pieces, out, per, first, unit):
     groups = len(pieces)
     columns = pieces[0].shape[1]
     aliased = [] if out is None else [out]
     return pl.pallas_call(
-        functools.partial(spread_kernel, groups, per, first, leaf, len(aliased)),
+        functools.partial(spread_kernel, groups, per, first, unit, len(aliased)),
         in_specs=[pl.BlockSpec(memory_space=pltpu.SMEM)]
         + [pl.BlockSpec(memory_space=pltpu.VMEM)] * groups
         + [pl.BlockSpec(memory_space=pl.ANY)] * len(aliased),
         out_specs=pl.BlockSpec(memory_space=pl.ANY),
-        out_shape=jax.ShapeDtypeStruct((groups * per * leaf, columns), F32),
+        out_shape=jax.ShapeDtypeStruct((groups * per * unit, columns), F32),
         scratch_shapes=[pltpu.SemaphoreType.DMA((groups,))],
         compiler_params=pltpu.CompilerParams(vmem_limit_bytes=8 << 20),
         input_output_aliases={1 + groups: 0} if aliased else {},
@@ -345,10 +342,14 @@
     proj, parcel, place, mask, inner = lax.optimization_barrier(
         (proj, parcel, place, mask, inner)
     )
-    chunks = [(first, 1) for first in range(per)]
+    units = 2
+    unit = leaf // units
+    size = -(-per * units // 2)
+    chunks = [(0, size), (size, per * units - size)]
     sizes = {
         "leaf": leaf,
         "per": per,
+        "units": units,
         "row_leaves": row_leaves,
         "rows_listed": groups - 1,
         "capacity": capacity,
@@ -376,6 +377,7 @@
         middle = [(1, 2), (2, 1), (0, 0), (3, 3)]
         inward = [(0, 1), (3, 2)]
         outward = [(1, 0), (2, 3)]
+        across = [(0, 2), (2, 0), (1, 3), (3, 1)]
         cross = [(1, 2), (2, 1)]
 
         of_a = shift(parcel, ends)
@@ -392,35 +394,43 @@
             before = pairs(sizes, spot, got, init, sources, *chunks[k])
             return before
 
-        every = range(len(chunks))
-        a = [work((of_a,), None, k) for k in every]
-        b = [work(of_b, shift(a[k], inward), k) for k in every]
+        rounds = {}
+        for label in ROUNDS:
+            k = int(label[1])
+            if label[0] == "a":
+                rounds[label] = work((of_a,), None, k)
+            elif label[0] == "b":
+                arrived = shift(rounds[f"a{k}"], inward)
+                rounds[label] = work(of_b, arrived, k)
+            else:
+                rounds[label] = work((of_c if label[0] == "c" else of_d,), None, k)
         done = []
-        for k in every:
-            c = work((of_c,), shift(b[k], cross), k)
-            d = work((of_d,), shift(b[k], inward), k)
-            from_c, from_d = shift(c, sides), shift(d, middle)
+        for k in range(len(chunks)):
+            from_b = shift(rounds[f"b{k}"], across)
+            from_c = shift(rounds[f"c{k}"], sides)
+            from_d = shift(rounds[f"d{k}"], middle)
             if done:
                 from_c, _ = lax.optimization_barrier((from_c, done[-1]))
-            done.append(from_c + from_d + a[k] * inner)
+            own = rounds[f"a{k}"] * inner
+            done.append(from_b + from_c + from_d + own)
     else:
         sources = make_sources()
         total = None
         for r in range(chips):
             got = shift(parcel, [(z, (z - r) % chips) for z in range(chips)])
-            part = pairs(sizes, place, (got,), None, sources, 0, per)
+            part = pairs(sizes, place, (got,), None, sources, 0, per * units)
             part = shift(part, [(z, (z + r) % chips) for z in range(chips)])
             total = part if total is None else total + part
-        done = [total[first * leaf : (first + count) * leaf] for first, count in chunks]
+        done = [total[first * unit : (first + count) * unit] for first, count in chunks]
 
     out = None
-    for (first, _), piece in zip(chunks, done):
+    for k, ((first, _), piece) in enumerate(zip(chunks, done)):
         pieces = [piece]
         for m in range(1, groups):
             pieces.append(
                 lax.ppermute(piece, "grp", [(g, g ^ m) for g in range(groups)])
             )
-        out = spread(mask, pieces, out, per, first, leaf)
+        out = spread(mask, pieces, out, per * units, first, unit)
     return out
 
 

time: 144 us -> 141 us (0.979)
  the two profiles are of different devices: /device:TPU:18 before, /device:TPU:0 now
where the time goes in v5:
time: 141 us; the launch traced here: 140 us
  Pallas kernels  55.1 us (39%)
  starting transfers between devices  41.7 us (30%)
  waiting for transfers between devices  40.8 us (29%)
  local copies, waits for them, and re-layouts  1.89 us (1%)
    pallas_call x8, Pallas kernels, pairs(): pl.pallas_call(functools.partial(pair_kernel, plan), grid=(count,), in_sp...  39.6 us
    ppermute x13, starting transfers between devices, shift(): return lax.ppermute(array, 'dev', along(moves))  31.3 us
    ppermute x13, waiting for transfers between devices, shift(): return lax.ppermute(array, 'dev', along(moves))  27.4 us
    ppermute x6, waiting for transfers between devices, on_device(): lax.ppermute(piece, 'grp', [(g, g ^ m) for g in range(groups)])  12.1 us
    pallas_call x2, Pallas kernels, prepared(): pl.pallas_call(functools.partial(body, scale), grid=(count // block,), in...  12 us
    ppermute x6, starting transfers between devices, on_device(): lax.ppermute(piece, 'grp', [(g, g ^ m) for g in range(groups)])  9.08 us
    pallas_call x2, Pallas kernels, spread(): pl.pallas_call(functools.partial(spread_kernel, groups, per, first, unit,...  3.43 us
  transfers between devices with their start and end apart: 23, of which 7 were waited for; matrix products, arithmetic and copies ran while one was open for 2% of the time, Pallas kernels for 38%

profile of v5, /device:TPU:0, one launch (start us, length us, event | category | flops | bytes accessed | tf_op | source)
XLA Modules:
  0.0 140.2 jit_solution(12492412392020511783)
XLA Ops:
  0.0 0.5 collective-permute-start.2
  0.5 0.0 collective-permute-start.1
  0.5 0.8 copy.8
  1.3 0.1 reshape.5
  1.4 0.1 pad_add_fusion.refs_0_
  1.5 1.0 constant_dynamic-slice_fusion
  2.6 8.1 %prepared.2 = (bf16[12,256,512]{2,1,0:T(8,128)(2,1)S(1)}, bf16[12,512,256]{2,1,0:T(8,128)(2,1)S(1)}, bf16[256,256]{1,0:T(8,128)(2,1)S(1)}, bf16[256,256]{1,0:T(8...) custom-call(s32[1,256]{1,0:T(1,128)} %idx_ref.1, f32[64,6144]{1,0:T(8,128)} %points_ref.1, ...), custom_call_target="tpu_custom_call" | custom-call | flops 1610612736 | bytes 20447232 | tf_op jit(solution)/shard_map/prepared/pallas_call | solution.py:255
  10.7 0.5 collective-permute-start.3
  11.2 2.6 %collective-permute-start.6 = (f32[72,1536]{1,0:T(8,128)S(1)}, f32[72,1536]{1,0:T(8,128)S(1)}, u32[]{:S(2)}, u32[]{:S(2)}) collective-permute-start(f32[72,1536]{1,0:T(8,128)S(1)} %select_maximum_fusion), channel_id=1, source_target_pairs={{0,2},{1,3},{2,0},{3,1},{4,6},{5,7},{6,4},{7,5},{8,10},{9,11},{10,... | collective-permute-start | bytes 1327112 | tf_op jit(solution)/shard_map/ppermute | solution.py:324
  13.8 0.7 collective-permute-start.5
  14.5 0.0 collective-permute-done.3.coords_ref
  14.5 0.3 collective-permute-start.4
  14.8 1.3 collective-permute-done.4.summed_ref
  16.1 4.6 %collective-permute-start = (f32[72,1536]{1,0:T(8,128)S(1)}, f32[72,1536]{1,0:T(8,128)S(1)}, u32[]{:S(2)}, u32[]{:S(2)}) collective-permute-start(f32[72,1536]{1,0:T(8,128)S(1)} %select_maximum_fusion), channel_id=1, source_target_pairs={{0,6},{1,7},{6,0},{7,1},{2,2},{3,3},{4,4},{5,5},{8,14},{9,15},{14,... | collective-permute-start | bytes 1327112 | tf_op jit(solution)/shard_map/ppermute | solution.py:324
  20.7 3.9 %collective-permute-done.6.refs_1_.refs_2_ = f32[72,1536]{1,0:T(8,128)S(1)} collective-permute-done((f32[72,1536]{1,0:T(8,128)S(1)}, f32[72,1536]{1,0:T(8,128)S(1)}, u32[]{:S(2)}, u32[]{:S(2)}) %collective-permute-start.6) | collective-permute-done | bytes 442400 | tf_op jit(solution)/shard_map/ppermute | solution.py:324
  24.6 0.7 collective-permute-start.7
  25.3 0.0 collective-permute-done.5.refs_1_.refs_2_
  25.3 1.3 collective-permute-start.8
  26.6 0.0 collective-permute-done.1.points_ref
  26.6 0.0 collective-permute-done.2.weights_ref
  26.6 3.9 %prepared.3 = (bf16[12,256,512]{2,1,0:T(8,128)(2,1)S(1)}, bf16[12,512,256]{2,1,0:T(8,128)(2,1)S(1)}, bf16[256,256]{1,0:T(8,128)(2,1)S(1)}, bf16[256,256]{1,0:T(8,128)(2,1)S(1)}) custom-call(f32[64,6144]{1,0:T(8,128)S(1)} %collective-permute-done.1.points_ref, f32[6144,128]{1,0:T(8,128)} %collective-permute-done.2.weights_ref, ...), custom_call_target="tpu_custom_call" | custom-call | flops 1610612736 | bytes 14155776 | tf_op jit(solution)/shard_map/prepared/pallas_call | solution.py:255
  30.5 5.8 %collective-permute-done.refs_1_.refs_2_ = f32[72,1536]{1,0:T(8,128)S(1)} collective-permute-done((f32[72,1536]{1,0:T(8,128)S(1)}, f32[72,1536]{1,0:T(8,128)S(1)}, u32[]{:S(2)}, u32[]{:S(2)}) %collective-permute-start) | collective-permute-done | bytes 442400 | tf_op jit(solution)/shard_map/ppermute | solution.py:324
  36.4 4.9 %pairs.8 = f32[768,128]{1,0:T(8,128)S(1)} custom-call(s32[3]{0:T(128)S(1)} %pad_add_fusion.refs_0_, f32[72,1536]{1,0:T(8,128)S(1)} %collective-permute-done.refs_1_.refs_2_, f32[72,1536]{1,0:T(8,128)S(1)} %collective-permute-done.refs_1_.refs_2_, bf16[12,256,512]{2,1,0:T(8,128)(2,1)S(1)} %get-tuple-element.32.refs_3_.refs_6_, ...), custom_call_target="tpu_custom_call" | custom-call | flops 3019898880 | bytes 2359296 | tf_op jit(solution)/shard_map/pairs/pallas_call | solution.py:140
  41.3 10.2 %collective-permute-start.9 = (f32[768,128]{1,0:T(8,128)S(1)}, f32[768,128]{1,0:T(8,128)S(1)}, u32[]{:S(2)}, u32[]{:S(2)}) collective-permute-start(f32[768,128]{1,0:T(8,128)S(1)} %pairs.8), channel_id=1, source_target_pairs={{0,2},{1,3},{6,4},{7,5},{8,10},{9,11},{14,12},{15,13},{16,18},{17,... | collective-permute-start | bytes 1179656 | tf_op jit(solution)/shard_map/ppermute | solution.py:324
  51.4 4.9 %pairs.9 = f32[768,128]{1,0:T(8,128)S(1)} custom-call(s32[3]{0:T(128)S(1)} %pad_add_fusion.refs_0_, f32[72,1536]{1,0:T(8,128)S(1)} %collective-permute-done.refs_1_.refs_2_, f32[72,1536]{1,0:T(8,128)S(1)} %collective-permute-done.refs_1_.refs_2_, bf16[12,256,512]{2,1,0:T(8,128)(2,1)S(1)} %get-tuple-element.32.refs_3_.refs_6_, ...), custom_call_target="tpu_custom_call" | custom-call | flops 3019898880 | bytes 2359296 | tf_op jit(solution)/shard_map/pairs/pallas_call | solution.py:140
  56.4 1.3 collective-permute-start.10
  57.7 4.9 %pairs.10 = f32[768,128]{1,0:T(8,128)S(1)} custom-call(s32[3]{0:T(128)S(1)} %pad_add_fusion.refs_0_, f32[72,1536]{1,0:T(8,128)S(1)} %collective-permute-done.5.refs_1_.refs_2_, f32[72,1536]{1,0:T(8,128)S(1)} %collective-permute-done.5.refs_1_.refs_2_, bf16[12,256,512]{2,1,0:T(8,128)(2,1)S(1)} %get-tuple-element.32.refs_3_.refs_6_, ...), custom_call_target="tpu_custom_call" | custom-call | flops 3019898880 | bytes 2359296 | tf_op jit(solution)/shard_map/pairs/pallas_call | solution.py:140
  62.7 0.9 collective-permute-start.15
  63.5 0.0 collective-permute-done.7.refs_1_.refs_3_
  63.5 0.0 collective-permute-done.8.refs_2_.refs_4_
  63.5 0.0 collective-permute-done.9.refs_5_
  63.6 5.0 %pairs.11 = f32[768,128]{1,0:T(8,128)S(1)} custom-call(s32[3]{0:T(128)S(1)} %pad_add_fusion.refs_0_, f32[72,1536]{1,0:T(8,128)S(1)} %collective-permute-done.7.refs_1_.refs_3_, f32[72,1536]{1,0:T(8,128)S(1)} %collective-permute-done.8.refs_2_.refs_4_, f32[72,1536]{1,0:T(8,128)S(1)} %collective-permute-done.7.refs_1_.refs_3_, ...), custom_call_target="tpu_custom_call" | custom-call | flops 3019898880 | bytes 2359296 | tf_op jit(solution)/shard_map/pairs/pallas_call | solution.py:140
  68.6 2.1 %collective-permute-start.13 = (f32[768,128]{1,0:T(8,128)S(1)}, f32[768,128]{1,0:T(8,128)S(1)}, u32[]{:S(2)}, u32[]{:S(2)}) collective-permute-start(f32[768,128]{1,0:T(8,128)S(1)} %pairs.11), channel_id=1, source_target_pairs={{0,4},{1,5},{4,0},{5,1},{2,6},{3,7},{6,2},{7,3},{8,12},{9,13},{12,... | collective-permute-start | bytes 1179656 | tf_op jit(solution)/shard_map/ppermute | solution.py:324
  70.7 4.9 %pairs.12 = f32[768,128]{1,0:T(8,128)S(1)} custom-call(s32[3]{0:T(128)S(1)} %pad_add_fusion.refs_0_, f32[72,1536]{1,0:T(8,128)S(1)} %collective-permute-done.6.refs_1_.refs_2_, f32[72,1536]{1,0:T(8,128)S(1)} %collective-permute-done.6.refs_1_.refs_2_, bf16[12,256,512]{2,1,0:T(8,128)(2,1)S(1)} %get-tuple-element.32.refs_3_.refs_6_, ...), custom_call_target="tpu_custom_call" | custom-call | flops 3019898880 | bytes 2359296 | tf_op jit(solution)/shard_map/pairs/pallas_call | solution.py:140
  75.6 1.5 %collective-permute-start.14 = (f32[768,128]{1,0:T(8,128)S(1)}, f32[768,128]{1,0:T(8,128)S(1)}, u32[]{:S(2)}, u32[]{:S(2)}) collective-permute-start(f32[768,128]{1,0:T(8,128)S(1)} %pairs.12), channel_id=1, source_target_pairs={{0,2},{1,3},{2,0},{3,1},{4,6},{5,7},{6,4},{7,5},{8,10},{9,11},{10,... | collective-permute-start | bytes 1179656 | tf_op jit(solution)/shard_map/ppermute | solution.py:324
  77.1 0.0 collective-permute-done.10.refs_5_
  77.2 5.0 %pairs.13 = f32[768,128]{1,0:T(8,128)S(1)} custom-call(s32[3]{0:T(128)S(1)} %pad_add_fusion.refs_0_, f32[72,1536]{1,0:T(8,128)S(1)} %collective-permute-done.7.refs_1_.refs_3_, f32[72,1536]{1,0:T(8,128)S(1)} %collective-permute-done.8.refs_2_.refs_4_, f32[72,1536]{1,0:T(8,128)S(1)} %collective-permute-done.7.refs_1_.refs_3_, ...), custom_call_target="tpu_custom_call" | custom-call | flops 3019898880 | bytes 2359296 | tf_op jit(solution)/shard_map/pairs/pallas_call | solution.py:140
  82.2 4.9 %pairs.14 = f32[768,128]{1,0:T(8,128)S(1)} custom-call(s32[3]{0:T(128)S(1)} %pad_add_fusion.refs_0_, f32[72,1536]{1,0:T(8,128)S(1)} %collective-permute-done.5.refs_1_.refs_2_, f32[72,1536]{1,0:T(8,128)S(1)} %collective-permute-done.5.refs_1_.refs_2_, bf16[12,256,512]{2,1,0:T(8,128)(2,1)S(1)} %get-tuple-element.32.refs_3_.refs_6_, ...), custom_call_target="tpu_custom_call" | custom-call | flops 3019898880 | bytes 2359296 | tf_op jit(solution)/shard_map/pairs/pallas_call | solution.py:140
  87.1 4.9 %pairs.15 = f32[768,128]{1,0:T(8,128)S(1)} custom-call(s32[3]{0:T(128)S(1)} %pad_add_fusion.refs_0_, f32[72,1536]{1,0:T(8,128)S(1)} %collective-permute-done.6.refs_1_.refs_2_, f32[72,1536]{1,0:T(8,128)S(1)} %collective-permute-done.6.refs_1_.refs_2_, bf16[12,256,512]{2,1,0:T(8,128)(2,1)S(1)} %get-tuple-element.32.refs_3_.refs_6_, ...), custom_call_target="tpu_custom_call" | custom-call | flops 3019898880 | bytes 2359296 | tf_op jit(solution)/shard_map/pairs/pallas_call | solution.py:140
  92.1 0.6 collective-permute-start.12
  92.7 0.7 collective-permute-start.16
  93.4 0.0 collective-permute-done.15
  93.4 4.2 %collective-permute-start.11 = (f32[768,128]{1,0:T(8,128)S(1)}, f32[768,128]{1,0:T(8,128)S(1)}, u32[]{:S(2)}, u32[]{:S(2)}) collective-permute-start(f32[768,128]{1,0:T(8,128)S(1)} %pairs.13), channel_id=1, source_target_pairs={{0,4},{1,5},{4,0},{5,1},{2,6},{3,7},{6,2},{7,3},{8,12},{9,13},{12,... | collective-permute-start | bytes 1179656 | tf_op jit(solution)/shard_map/ppermute | solution.py:324
  97.6 0.0 collective-permute-done.13
  97.6 0.0 collective-permute-done.14
  97.6 0.1 multiply_add_fusion.1.refs_1_
  97.7 1.6 %collective-permute-start.20 = (f32[768,128]{1,0:T(8,128)S(1)}, f32[768,128]{1,0:T(8,128)S(1)}, u32[]{:S(2)}, u32[]{:S(2)}) collective-permute-start(f32[768,128]{1,0:T(8,128)S(1)} %multiply_add_fusion.1.refs_1_), channel_id=1, source_target_pairs={{0,8},{8,0},{16,24},{24,16},{1,9},{9,1},{17,25},{25,17},{2,10},{10... | collective-permute-start | bytes 1179656 | tf_op jit(solution)/shard_map/ppermute | solution.py:431
  99.2 1.5 %collective-permute-start.21 = (f32[768,128]{1,0:T(8,128)S(1)}, f32[768,128]{1,0:T(8,128)S(1)}, u32[]{:S(2)}, u32[]{:S(2)}) collective-permute-start(f32[768,128]{1,0:T(8,128)S(1)} %multiply_add_fusion.1.refs_1_), channel_id=1, source_target_pairs={{0,16},{8,24},{16,0},{24,8},{1,17},{9,25},{17,1},{25,9},{2,18},{10... | collective-permute-start | bytes 1179656 | tf_op jit(solution)/shard_map/ppermute | solution.py:431
  100.8 1.5 %collective-permute-done.12 = f32[768,128]{1,0:T(8,128)S(1)} collective-permute-done((f32[768,128]{1,0:T(8,128)S(1)}, f32[768,128]{1,0:T(8,128)S(1)}, u32[]{:S(2)}, u32[]{:S(2)}) %collective-permute-start.12) | collective-permute-done | bytes 393248 | tf_op jit(solution)/shard_map/ppermute | solution.py:324
  102.2 2.4 %collective-permute-start.22 = (f32[768,128]{1,0:T(8,128)S(1)}, f32[768,128]{1,0:T(8,128)S(1)}, u32[]{:S(2)}, u32[]{:S(2)}) collective-permute-start(f32[768,128]{1,0:T(8,128)S(1)} %multiply_add_fusion.1.refs_1_), channel_id=1, source_target_pairs={{0,24},{8,16},{16,8},{24,0},{1,25},{9,17},{17,9},{25,1},{2,26},{10... | collective-permute-start | bytes 1179656 | tf_op jit(solution)/shard_map/ppermute | solution.py:431
  104.7 0.0 collective-permute-done.16
  104.7 16.2 %collective-permute-done.11 = f32[768,128]{1,0:T(8,128)S(1)} collective-permute-done((f32[768,128]{1,0:T(8,128)S(1)}, f32[768,128]{1,0:T(8,128)S(1)}, u32[]{:S(2)}, u32[]{:S(2)}) %collective-permute-start.11) | collective-permute-done | bytes 393248 | tf_op jit(solution)/shard_map/ppermute | solution.py:324
  120.8 0.1 multiply_add_fusion.refs_1_
  121.0 1.6 %collective-permute-start.17 = (f32[768,128]{1,0:T(8,128)S(1)}, f32[768,128]{1,0:T(8,128)S(1)}, u32[]{:S(2)}, u32[]{:S(2)}) collective-permute-start(f32[768,128]{1,0:T(8,128)S(1)} %multiply_add_fusion.refs_1_), channel_id=1, source_target_pairs={{0,8},{8,0},{16,24},{24,16},{1,9},{9,1},{17,25},{25,17},{2,10},{10... | collective-permute-start | bytes 1179656 | tf_op jit(solution)/shard_map/ppermute | solution.py:431
  122.5 1.5 %collective-permute-start.18 = (f32[768,128]{1,0:T(8,128)S(1)}, f32[768,128]{1,0:T(8,128)S(1)}, u32[]{:S(2)}, u32[]{:S(2)}) collective-permute-start(f32[768,128]{1,0:T(8,128)S(1)} %multiply_add_fusion.refs_1_), channel_id=1, source_target_pairs={{0,16},{8,24},{16,0},{24,8},{1,17},{9,25},{17,1},{25,9},{2,18},{10... | collective-permute-start | bytes 1179656 | tf_op jit(solution)/shard_map/ppermute | solution.py:431
  124.1 0.0 collective-permute-done.20.refs_2_
  124.1 0.5 collective-permute-start.19
  124.5 0.0 collective-permute-done.21.refs_3_
  124.5 0.0 collective-permute-done.22.refs_4_
  124.5 1.7 %spread.2.refs_5_ = f32[6144,128]{1,0:T(8,128)} custom-call(s32[4]{0:T(128)S(1)} %iota_xor_fusion.refs_0_, f32[768,128]{1,0:T(8,128)S(1)} %multiply_add_fusion.1.refs_1_, f32[768,128]{1,0:T(8,128)S(1)} %collective-permute-done.20.refs_2_, f32[768,128]{1,0:T(8,128)S(1)} %collective-permute-done.21.refs_3_, f32[768,128]{1,0:T(8,128)S(1)} %collective-permute-done.22.refs_4_), custom_call_target="tpu_custom_call" | custom-call | tf_op jit(solution)/shard_map/spread/pallas_call | solution.py:290
  126.2 6.7 %collective-permute-done.17.refs_2_ = f32[768,128]{1,0:T(8,128)S(1)} collective-permute-done((f32[768,128]{1,0:T(8,128)S(1)}, f32[768,128]{1,0:T(8,128)S(1)}, u32[]{:S(2)}, u32[]{:S(2)}) %collective-permute-start.17) | collective-permute-done | bytes 393248 | tf_op jit(solution)/shard_map/ppermute | solution.py:431
  132.9 5.5 %collective-permute-done.18.refs_3_ = f32[768,128]{1,0:T(8,128)S(1)} collective-permute-done((f32[768,128]{1,0:T(8,128)S(1)}, f32[768,128]{1,0:T(8,128)S(1)}, u32[]{:S(2)}, u32[]{:S(2)}) %collective-permute-start.18) | collective-permute-done | bytes 393248 | tf_op jit(solution)/shard_map/ppermute | solution.py:431
  138.4 0.0 collective-permute-done.19.refs_4_
  138.4 1.7 %spread.3 = f32[6144,128]{1,0:T(8,128)} custom-call(s32[4]{0:T(128)S(1)} %iota_xor_fusion.refs_0_, f32[768,128]{1,0:T(8,128)S(1)} %multiply_add_fusion.refs_1_, f32[768,128]{1,0:T(8,128)S(1)} %collective-permute-done.17.refs_2_, f32[768,128]{1,0:T(8,128)S(1)} %collective-permute-done.18.refs_3_, ...), custom_call_target="tpu_custom_call", output_to_operand_aliasing={{}: (5, {})} | custom-call | tf_op jit(solution)/shard_map/spread/pallas_call | solution.py:290
  (4 shorter events, 0.0 us)
Async XLA Ops:
  0.0 26.6 %collective-permute-start.2 = (f32[6144,128]{1,0:T(8,128)}, f32[6144,128]{1,0:T(8,128)}, u32[]{:S(2)}, u32[]{:S(2)}) collective-permute-start(f32[6144,128]{1,0:T(8,128)} %weights_ref.1), channel_id=1, source_target_pairs={{0,1},{1,0},{2,3},{3,2},{4,5},{5,4},{6,7},{7,6},{8,9},{9,8},{10,11... | collective-permute-start | bytes 9437192 | tf_op jit(solution)/shard_map/ppermute | solution.py:365
  0.5 26.1 %collective-permute-start.1 = (f32[64,6144]{1,0:T(8,128)}, f32[64,6144]{1,0:T(8,128)S(1)}, u32[]{:S(2)}, u32[]{:S(2)}) collective-permute-start(f32[64,6144]{1,0:T(8,128)} %points_ref.1), channel_id=1, source_target_pairs={{0,1},{1,0},{2,3},{3,2},{4,5},{5,4},{6,7},{7,6},{8,9},{9,8},{10,11... | collective-permute-start | bytes 4718600 | tf_op jit(solution)/shard_map/ppermute | solution.py:365
  10.7 3.8 %collective-permute-start.3 = (f32[64,256]{1,0:T(8,128)}, f32[64,256]{1,0:T(8,128)S(1)}, u32[]{:S(2)}, u32[]{:S(2)}) collective-permute-start(f32[64,256]{1,0:T(8,128)} %get-tuple-element.36), channel_id=1, source_target_pairs={{0,1},{1,0},{2,3},{3,2},{4,5},{5,4},{6,7},{7,6},{8,9},{9,8},{10,11... | collective-permute-start | bytes 196616 | tf_op jit(solution)/shard_map/ppermute | solution.py:365
  11.2 13.4 %collective-permute-start.6 = (f32[72,1536]{1,0:T(8,128)S(1)}, f32[72,1536]{1,0:T(8,128)S(1)}, u32[]{:S(2)}, u32[]{:S(2)}) collective-permute-start(f32[72,1536]{1,0:T(8,128)S(1)} %select_maximum_fusion), channel_id=1, source_target_pairs={{0,2},{1,3},{2,0},{3,1},{4,6},{5,7},{6,4},{7,5},{8,10},{9,11},{10,... | collective-permute-start | bytes 1327112 | tf_op jit(solution)/shard_map/ppermute | solution.py:324
  13.8 11.5 %collective-permute-start.5 = (f32[72,1536]{1,0:T(8,128)S(1)}, f32[72,1536]{1,0:T(8,128)S(1)}, u32[]{:S(2)}, u32[]{:S(2)}) collective-permute-start(f32[72,1536]{1,0:T(8,128)S(1)} %select_maximum_fusion), channel_id=1, source_target_pairs={{2,4},{3,5},{4,2},{5,3},{0,0},{1,1},{6,6},{7,7},{10,12},{11,13},{1... | collective-permute-start | bytes 1327112 | tf_op jit(solution)/shard_map/ppermute | solution.py:324
  14.5 1.6 %collective-permute-start.4 = (f32[256,128]{1,0:T(8,128)}, f32[256,128]{1,0:T(8,128)S(1)}, u32[]{:S(2)}, u32[]{:S(2)}) collective-permute-start(f32[256,128]{1,0:T(8,128)} %get-tuple-element.37), channel_id=1, source_target_pairs={{0,1},{1,0},{2,3},{3,2},{4,5},{5,4},{6,7},{7,6},{8,9},{9,8},{10,11... | collective-permute-start | bytes 393224 | tf_op jit(solution)/shard_map/ppermute | solution.py:365
  16.1 20.3 %collective-permute-start = (f32[72,1536]{1,0:T(8,128)S(1)}, f32[72,1536]{1,0:T(8,128)S(1)}, u32[]{:S(2)}, u32[]{:S(2)}) collective-permute-start(f32[72,1536]{1,0:T(8,128)S(1)} %select_maximum_fusion), channel_id=1, source_target_pairs={{0,6},{1,7},{6,0},{7,1},{2,2},{3,3},{4,4},{5,5},{8,14},{9,15},{14,... | collective-permute-start | bytes 1327112 | tf_op jit(solution)/shard_map/ppermute | solution.py:324
  24.6 38.9 %collective-permute-start.7 = (f32[72,1536]{1,0:T(8,128)S(1)}, f32[72,1536]{1,0:T(8,128)S(1)}, u32[]{:S(2)}, u32[]{:S(2)}) collective-permute-start(f32[72,1536]{1,0:T(8,128)S(1)} %collective-permute-done.6.refs_1_.refs_2_), channel_id=1, source_target_pairs={{2,4},{3,5},{4,2},{5,3},{10,12},{11,13},{12,10},{13,11},{18,20},{1... | collective-permute-start | bytes 1327112 | tf_op jit(solution)/shard_map/ppermute | solution.py:324
  25.3 38.2 %collective-permute-start.8 = (f32[72,1536]{1,0:T(8,128)S(1)}, f32[72,1536]{1,0:T(8,128)S(1)}, u32[]{:S(2)}, u32[]{:S(2)}) collective-permute-start(f32[72,1536]{1,0:T(8,128)S(1)} %collective-permute-done.5.refs_1_.refs_2_), channel_id=1, source_target_pairs={{2,0},{3,1},{4,6},{5,7},{10,8},{11,9},{12,14},{13,15},{18,16},{19,... | collective-permute-start | bytes 1327112 | tf_op jit(solution)/shard_map/ppermute | solution.py:324
  41.3 22.3 %collective-permute-start.9 = (f32[768,128]{1,0:T(8,128)S(1)}, f32[768,128]{1,0:T(8,128)S(1)}, u32[]{:S(2)}, u32[]{:S(2)}) collective-permute-start(f32[768,128]{1,0:T(8,128)S(1)} %pairs.8), channel_id=1, source_target_pairs={{0,2},{1,3},{6,4},{7,5},{8,10},{9,11},{14,12},{15,13},{16,18},{17,... | collective-permute-start | bytes 1179656 | tf_op jit(solution)/shard_map/ppermute | solution.py:324
  56.4 20.8 %collective-permute-start.10 = (f32[768,128]{1,0:T(8,128)S(1)}, f32[768,128]{1,0:T(8,128)S(1)}, u32[]{:S(2)}, u32[]{:S(2)}) collective-permute-start(f32[768,128]{1,0:T(8,128)S(1)} %pairs.9), channel_id=1, source_target_pairs={{0,2},{1,3},{6,4},{7,5},{8,10},{9,11},{14,12},{15,13},{16,18},{17,... | collective-permute-start | bytes 1179656 | tf_op jit(solution)/shard_map/ppermute | solution.py:324
  62.7 30.7 %collective-permute-start.15 = (f32[768,128]{1,0:T(8,128)S(1)}, f32[768,128]{1,0:T(8,128)S(1)}, u32[]{:S(2)}, u32[]{:S(2)}) collective-permute-start(f32[768,128]{1,0:T(8,128)S(1)} %pairs.10), channel_id=1, source_target_pairs={{2,4},{3,5},{4,2},{5,3},{0,0},{1,1},{6,6},{7,7},{10,12},{11,13},{1... | collective-permute-start | bytes 1179656 | tf_op jit(solution)/shard_map/ppermute | solution.py:324
  68.6 29.0 %collective-permute-start.13 = (f32[768,128]{1,0:T(8,128)S(1)}, f32[768,128]{1,0:T(8,128)S(1)}, u32[]{:S(2)}, u32[]{:S(2)}) collective-permute-start(f32[768,128]{1,0:T(8,128)S(1)} %pairs.11), channel_id=1, source_target_pairs={{0,4},{1,5},{4,0},{5,1},{2,6},{3,7},{6,2},{7,3},{8,12},{9,13},{12,... | collective-permute-start | bytes 1179656 | tf_op jit(solution)/shard_map/ppermute | solution.py:324
  75.6 22.0 %collective-permute-start.14 = (f32[768,128]{1,0:T(8,128)S(1)}, f32[768,128]{1,0:T(8,128)S(1)}, u32[]{:S(2)}, u32[]{:S(2)}) collective-permute-start(f32[768,128]{1,0:T(8,128)S(1)} %pairs.12), channel_id=1, source_target_pairs={{0,2},{1,3},{2,0},{3,1},{4,6},{5,7},{6,4},{7,5},{8,10},{9,11},{10,... | collective-permute-start | bytes 1179656 | tf_op jit(solution)/shard_map/ppermute | solution.py:324
  92.1 10.2 %collective-permute-start.12 = (f32[768,128]{1,0:T(8,128)S(1)}, f32[768,128]{1,0:T(8,128)S(1)}, u32[]{:S(2)}, u32[]{:S(2)}) collective-permute-start(f32[768,128]{1,0:T(8,128)S(1)} %pairs.15), channel_id=1, source_target_pairs={{0,2},{1,3},{2,0},{3,1},{4,6},{5,7},{6,4},{7,5},{8,10},{9,11},{10,... | collective-permute-start | bytes 1179656 | tf_op jit(solution)/shard_map/ppermute | solution.py:324
  92.7 12.0 %collective-permute-start.16 = (f32[768,128]{1,0:T(8,128)S(1)}, f32[768,128]{1,0:T(8,128)S(1)}, u32[]{:S(2)}, u32[]{:S(2)}) collective-permute-start(f32[768,128]{1,0:T(8,128)S(1)} %pairs.14), channel_id=1, source_target_pairs={{2,4},{3,5},{4,2},{5,3},{0,0},{1,1},{6,6},{7,7},{10,12},{11,13},{1... | collective-permute-start | bytes 1179656 | tf_op jit(solution)/shard_map/ppermute | solution.py:324
  93.4 27.4 %collective-permute-start.11 = (f32[768,128]{1,0:T(8,128)S(1)}, f32[768,128]{1,0:T(8,128)S(1)}, u32[]{:S(2)}, u32[]{:S(2)}) collective-permute-start(f32[768,128]{1,0:T(8,128)S(1)} %pairs.13), channel_id=1, source_target_pairs={{0,4},{1,5},{4,0},{5,1},{2,6},{3,7},{6,2},{7,3},{8,12},{9,13},{12,... | collective-permute-start | bytes 1179656 | tf_op jit(solution)/shard_map/ppermute | solution.py:324
  97.7 26.4 %collective-permute-start.20 = (f32[768,128]{1,0:T(8,128)S(1)}, f32[768,128]{1,0:T(8,128)S(1)}, u32[]{:S(2)}, u32[]{:S(2)}) collective-permute-start(f32[768,128]{1,0:T(8,128)S(1)} %multiply_add_fusion.1.refs_1_), channel_id=1, source_target_pairs={{0,8},{8,0},{16,24},{24,16},{1,9},{9,1},{17,25},{25,17},{2,10},{10... | collective-permute-start | bytes 1179656 | tf_op jit(solution)/shard_map/ppermute | solution.py:431
  99.2 25.3 %collective-permute-start.21 = (f32[768,128]{1,0:T(8,128)S(1)}, f32[768,128]{1,0:T(8,128)S(1)}, u32[]{:S(2)}, u32[]{:S(2)}) collective-permute-start(f32[768,128]{1,0:T(8,128)S(1)} %multiply_add_fusion.1.refs_1_), channel_id=1, source_target_pairs={{0,16},{8,24},{16,0},{24,8},{1,17},{9,25},{17,1},{25,9},{2,18},{10... | collective-permute-start | bytes 1179656 | tf_op jit(solution)/shard_map/ppermute | solution.py:431
  102.2 22.3 %collective-permute-start.22 = (f32[768,128]{1,0:T(8,128)S(1)}, f32[768,128]{1,0:T(8,128)S(1)}, u32[]{:S(2)}, u32[]{:S(2)}) collective-permute-start(f32[768,128]{1,0:T(8,128)S(1)} %multiply_add_fusion.1.refs_1_), channel_id=1, source_target_pairs={{0,24},{8,16},{16,8},{24,0},{1,25},{9,17},{17,9},{25,1},{2,26},{10... | collective-permute-start | bytes 1179656 | tf_op jit(solution)/shard_map/ppermute | solution.py:431
  121.0 11.9 %collective-permute-start.17 = (f32[768,128]{1,0:T(8,128)S(1)}, f32[768,128]{1,0:T(8,128)S(1)}, u32[]{:S(2)}, u32[]{:S(2)}) collective-permute-start(f32[768,128]{1,0:T(8,128)S(1)} %multiply_add_fusion.refs_1_), channel_id=1, source_target_pairs={{0,8},{8,0},{16,24},{24,16},{1,9},{9,1},{17,25},{25,17},{2,10},{10... | collective-permute-start | bytes 1179656 | tf_op jit(solution)/shard_map/ppermute | solution.py:431
  122.5 15.8 %collective-permute-start.18 = (f32[768,128]{1,0:T(8,128)S(1)}, f32[768,128]{1,0:T(8,128)S(1)}, u32[]{:S(2)}, u32[]{:S(2)}) collective-permute-start(f32[768,128]{1,0:T(8,128)S(1)} %multiply_add_fusion.refs_1_), channel_id=1, source_target_pairs={{0,16},{8,24},{16,0},{24,8},{1,17},{9,25},{17,1},{25,9},{2,18},{10... | collective-permute-start | bytes 1179656 | tf_op jit(solution)/shard_map/ppermute | solution.py:431
  124.1 14.3 %collective-permute-start.19 = (f32[768,128]{1,0:T(8,128)S(1)}, f32[768,128]{1,0:T(8,128)S(1)}, u32[]{:S(2)}, u32[]{:S(2)}) collective-permute-start(f32[768,128]{1,0:T(8,128)S(1)} %multiply_add_fusion.refs_1_), channel_id=1, source_target_pairs={{0,24},{8,16},{16,8},{24,0},{1,25},{9,17},{17,9},{25,1},{2,26},{10... | collective-permute-start | bytes 1179656 | tf_op jit(solution)/shard_map/ppermute | solution.py:431

commit v6 on v5

--- a/solution.py
+++ b/solution.py
@@ -9,7 +9,7 @@
 from jax.sharding import PartitionSpec as P
 
 
-ROUNDS = ("a0", "a1", "d0", "b0", "c0", "b1", "d1", "c1")
+ROUNDS = ("d0", "a0", "d1", "a1", "b0", "c0", "b1", "c1")
 
 F32 = jnp.float32
 BF16 = jnp.bfloat16
@@ -125,9 +125,10 @@
         count=count,
     )
     unit = leaf // sizes["units"]
+    width = parcels[0].shape[1] - 128
     in_specs = [pl.BlockSpec(memory_space=pltpu.SMEM)]
     in_specs += [
-        pl.BlockSpec((8, 128), lambda i: (features // 8, 0), memory_space=pltpu.SMEM)
+        pl.BlockSpec((8, 128), lambda i: (0, width // 128), memory_space=pltpu.SMEM)
     ] * len(parcels)
     in_specs += [pl.BlockSpec((features, unit), lambda i: (0, first + i))] * len(parcels)
     operands = [place, *parcels, *parcels]
@@ -333,8 +334,8 @@
     room = 8 * 128
     assert numbers.shape[0] <= room
     numbers = jnp.pad(numbers, (0, room - numbers.shape[0])).reshape(8, 128).astype(F32)
-    numbers = jnp.pad(numbers, ((0, 0), (0, width - 128)))
-    parcel = jnp.concatenate([mine, numbers], axis=0)
+    numbers = jnp.pad(numbers, ((0, features - 8), (0, 0)))
+    parcel = jnp.concatenate([mine, numbers], axis=1)
     chip = device // 2
     place = jnp.stack([group, device, device ^ 1])
     mask = group ^ jnp.arange(groups, dtype=jnp.int32)

time: 141 us -> 129 us (0.915)
  starting transfers between devices: 41.7 us -> 34.7 us
  waiting for transfers between devices: 40.8 us -> 35.5 us
    ppermute x13, waiting for transfers between devices: 27.4 us -> 19.3 us  [shift(): return lax.ppermute(array, 'dev', along(moves))]
    ppermute x13, starting transfers between devices: 31.3 us -> 25 us  [shift(): return lax.ppermute(array, 'dev', along(moves))]
    ppermute x4, waiting for transfers between devices: 1.34 us -> 2.87 us  [to_partner(): return lax.ppermute(array, 'dev', swap)]
  transfers between devices with their start and end apart: 23 -> 23, of which waited for: 7 -> 8; matrix products, arithmetic and copies ran while one was open for 2% -> 2% of each run, Pallas kernels for 38% -> 42%
where the time goes in v6:
time: 129 us
  Pallas kernels  55.7 us (43%)
  waiting for transfers between devices  35.5 us (28%)
  starting transfers between devices  34.7 us (27%)
  local copies, waits for them, and re-layouts  1.89 us (1%)
    pallas_call x8, Pallas kernels, pairs(): pl.pallas_call(functools.partial(pair_kernel, plan), grid=(count,), in_sp...  40.3 us
    ppermute x13, starting transfers between devices, shift(): return lax.ppermute(array, 'dev', along(moves))  25 us
    ppermute x13, waiting for transfers between devices, shift(): return lax.ppermute(array, 'dev', along(moves))  19.3 us
    ppermute x6, waiting for transfers between devices, on_device(): lax.ppermute(piece, 'grp', [(g, g ^ m) for g in range(groups)])  13.4 us
    pallas_call x2, Pallas kernels, prepared(): pl.pallas_call(functools.partial(body, scale), grid=(count // block,), in...  12 us
    ppermute x6, starting transfers between devices, on_device(): lax.ppermute(piece, 'grp', [(g, g ^ m) for g in range(groups)])  9.02 us
    pallas_call x2, Pallas kernels, spread(): pl.pallas_call(functools.partial(spread_kernel, groups, per, first, unit,...  3.43 us
    ppermute x4, waiting for transfers between devices, to_partner(): return lax.ppermute(array, 'dev', swap)  2.87 us
  transfers between devices with their start and end apart: 23, of which 8 were waited for; matrix products, arithmetic and copies ran while one was open for 2% of the time, Pallas kernels for 42%

profile of v6, /device:TPU:0, one launch (start us, length us, event | category | flops | bytes accessed | tf_op | source)
XLA Modules:
  0.0 128.6 jit_solution(876467962559579750)
XLA Ops:
  0.0 0.5 collective-permute-start.2
  0.5 0.0 collective-permute-start.1
  0.5 0.8 copy.8
  1.3 0.1 reshape.5
  1.4 0.1 pad_add_fusion.refs_0_
  1.5 1.0 constant_dynamic-slice_fusion
  2.6 3.1 %collective-permute-start.6 = (f32[64,1664]{1,0:T(8,128)S(1)}, f32[64,1664]{1,0:T(8,128)S(1)}, u32[]{:S(2)}, u32[]{:S(2)}) collective-permute-start(f32[64,1664]{1,0:T(8,128)S(1)} %select_maximum_fusion), channel_id=1, source_target_pairs={{0,2},{1,3},{2,0},{3,1},{4,6},{5,7},{6,4},{7,5},{8,10},{9,11},{10,... | collective-permute-start | bytes 1277960 | tf_op jit(solution)/shard_map/ppermute | solution.py:325
  5.7 0.7 collective-permute-start
  6.4 8.1 %prepared.2 = (bf16[12,256,512]{2,1,0:T(8,128)(2,1)S(1)}, bf16[12,512,256]{2,1,0:T(8,128)(2,1)S(1)}, bf16[256,256]{1,0:T(8,128)(2,1)S(1)}, bf16[256,256]{1,0:T(8...) custom-call(s32[1,256]{1,0:T(1,128)} %idx_ref.1, f32[64,6144]{1,0:T(8,128)} %points_ref.1, ...), custom_call_target="tpu_custom_call" | custom-call | flops 1610612736 | bytes 20447232 | tf_op jit(solution)/shard_map/prepared/pallas_call | solution.py:256
  14.5 0.0 collective-permute-start.3
  14.5 1.5 %collective-permute-done.3.coords_ref = f32[64,256]{1,0:T(8,128)S(1)} collective-permute-done((f32[64,256]{1,0:T(8,128)}, f32[64,256]{1,0:T(8,128)S(1)}, u32[]{:S(2)}, u32[]{:S(2)}) %collective-permute-start.3) | collective-permute-done | bytes 65568 | tf_op jit(solution)/shard_map/ppermute | solution.py:366
  16.0 0.2 collective-permute-start.4
  16.1 1.4 %collective-permute-done.4.summed_ref = f32[256,128]{1,0:T(8,128)S(1)} collective-permute-done((f32[256,128]{1,0:T(8,128)}, f32[256,128]{1,0:T(8,128)S(1)}, u32[]{:S(2)}, u32[]{:S(2)}) %collective-permute-start.4) | collective-permute-done | bytes 131104 | tf_op jit(solution)/shard_map/ppermute | solution.py:366
  17.5 4.4 %collective-permute-start.5 = (f32[64,1664]{1,0:T(8,128)S(1)}, f32[64,1664]{1,0:T(8,128)S(1)}, u32[]{:S(2)}, u32[]{:S(2)}) collective-permute-start(f32[64,1664]{1,0:T(8,128)S(1)} %select_maximum_fusion), channel_id=1, source_target_pairs={{0,6},{1,7},{6,0},{7,1},{2,2},{3,3},{4,4},{5,5},{8,14},{9,15},{14,... | collective-permute-start | bytes 1277960 | tf_op jit(solution)/shard_map/ppermute | solution.py:325
  21.9 0.0 collective-permute-done.6.refs_1_.refs_2_
  21.9 0.7 collective-permute-start.7
  22.6 0.0 collective-permute-done.refs_1_.refs_2_
  22.6 1.3 %collective-permute-start.8 = (f32[64,1664]{1,0:T(8,128)S(1)}, f32[64,1664]{1,0:T(8,128)S(1)}, u32[]{:S(2)}, u32[]{:S(2)}) collective-permute-start(f32[64,1664]{1,0:T(8,128)S(1)} %collective-permute-done.refs_1_.refs_2_), channel_id=1, source_target_pairs={{2,0},{3,1},{4,6},{5,7},{10,8},{11,9},{12,14},{13,15},{18,16},{19,... | collective-permute-start | bytes 1277960 | tf_op jit(solution)/shard_map/ppermute | solution.py:325
  23.9 0.0 collective-permute-done.1.points_ref
  23.9 0.0 collective-permute-done.2.weights_ref
  24.0 3.9 %prepared.3 = (bf16[12,256,512]{2,1,0:T(8,128)(2,1)S(1)}, bf16[12,512,256]{2,1,0:T(8,128)(2,1)S(1)}, bf16[256,256]{1,0:T(8,128)(2,1)S(1)}, bf16[256,256]{1,0:T(8,128)(2,1)S(1)}) custom-call(f32[64,6144]{1,0:T(8,128)S(1)} %collective-permute-done.1.points_ref, f32[6144,128]{1,0:T(8,128)} %collective-permute-done.2.weights_ref, ...), custom_call_target="tpu_custom_call" | custom-call | flops 1610612736 | bytes 14155776 | tf_op jit(solution)/shard_map/prepared/pallas_call | solution.py:256
  27.9 5.0 %pairs.8 = f32[768,128]{1,0:T(8,128)S(1)} custom-call(s32[3]{0:T(128)S(1)} %pad_add_fusion.refs_0_, f32[64,1664]{1,0:T(8,128)S(1)} %collective-permute-done.refs_1_.refs_2_, f32[64,1664]{1,0:T(8,128)S(1)} %collective-permute-done.refs_1_.refs_2_, bf16[12,256,512]{2,1,0:T(8,128)(2,1)S(1)} %get-tuple-element.32.refs_3_.refs_6_, ...), custom_call_target="tpu_custom_call" | custom-call | flops 3019898880 | bytes 2359296 | tf_op jit(solution)/shard_map/pairs/pallas_call | solution.py:141
  32.9 0.3 collective-permute-done.5.refs_1_.refs_2_
  33.2 4.9 %pairs.9 = f32[768,128]{1,0:T(8,128)S(1)} custom-call(s32[3]{0:T(128)S(1)} %pad_add_fusion.refs_0_, f32[64,1664]{1,0:T(8,128)S(1)} %collective-permute-done.5.refs_1_.refs_2_, f32[64,1664]{1,0:T(8,128)S(1)} %collective-permute-done.5.refs_1_.refs_2_, bf16[12,256,512]{2,1,0:T(8,128)(2,1)S(1)} %get-tuple-element.32.refs_3_.refs_6_, ...), custom_call_target="tpu_custom_call" | custom-call | flops 3019898880 | bytes 2359296 | tf_op jit(solution)/shard_map/pairs/pallas_call | solution.py:141
  38.2 4.3 %collective-permute-start.9 = (f32[768,128]{1,0:T(8,128)S(1)}, f32[768,128]{1,0:T(8,128)S(1)}, u32[]{:S(2)}, u32[]{:S(2)}) collective-permute-start(f32[768,128]{1,0:T(8,128)S(1)} %pairs.9), channel_id=1, source_target_pairs={{0,2},{1,3},{6,4},{7,5},{8,10},{9,11},{14,12},{15,13},{16,18},{17,... | collective-permute-start | bytes 1179656 | tf_op jit(solution)/shard_map/ppermute | solution.py:325
  42.5 5.0 %pairs.10 = f32[768,128]{1,0:T(8,128)S(1)} custom-call(s32[3]{0:T(128)S(1)} %pad_add_fusion.refs_0_, f32[64,1664]{1,0:T(8,128)S(1)} %collective-permute-done.refs_1_.refs_2_, f32[64,1664]{1,0:T(8,128)S(1)} %collective-permute-done.refs_1_.refs_2_, bf16[12,256,512]{2,1,0:T(8,128)(2,1)S(1)} %get-tuple-element.32.refs_3_.refs_6_, ...), custom_call_target="tpu_custom_call" | custom-call | flops 3019898880 | bytes 2359296 | tf_op jit(solution)/shard_map/pairs/pallas_call | solution.py:141
  47.5 5.0 %pairs.11 = f32[768,128]{1,0:T(8,128)S(1)} custom-call(s32[3]{0:T(128)S(1)} %pad_add_fusion.refs_0_, f32[64,1664]{1,0:T(8,128)S(1)} %collective-permute-done.5.refs_1_.refs_2_, f32[64,1664]{1,0:T(8,128)S(1)} %collective-permute-done.5.refs_1_.refs_2_, bf16[12,256,512]{2,1,0:T(8,128)(2,1)S(1)} %get-tuple-element.32.refs_3_.refs_6_, ...), custom_call_target="tpu_custom_call" | custom-call | flops 3019898880 | bytes 2359296 | tf_op jit(solution)/shard_map/pairs/pallas_call | solution.py:141
  52.6 1.3 %collective-permute-start.10 = (f32[768,128]{1,0:T(8,128)S(1)}, f32[768,128]{1,0:T(8,128)S(1)}, u32[]{:S(2)}, u32[]{:S(2)}) collective-permute-start(f32[768,128]{1,0:T(8,128)S(1)} %pairs.11), channel_id=1, source_target_pairs={{0,2},{1,3},{6,4},{7,5},{8,10},{9,11},{14,12},{15,13},{16,18},{17,... | collective-permute-start | bytes 1179656 | tf_op jit(solution)/shard_map/ppermute | solution.py:325
  53.9 0.9 collective-permute-start.15
  54.8 0.0 collective-permute-done.7.refs_1_.refs_3_
  54.8 0.0 collective-permute-done.8.refs_2_.refs_4_
  54.8 0.0 collective-permute-done.9.refs_5_
  54.8 5.2 %pairs.12 = f32[768,128]{1,0:T(8,128)S(1)} custom-call(s32[3]{0:T(128)S(1)} %pad_add_fusion.refs_0_, f32[64,1664]{1,0:T(8,128)S(1)} %collective-permute-done.7.refs_1_.refs_3_, f32[64,1664]{1,0:T(8,128)S(1)} %collective-permute-done.8.refs_2_.refs_4_, f32[64,1664]{1,0:T(8,128)S(1)} %collective-permute-done.7.refs_1_.refs_3_, ...), custom_call_target="tpu_custom_call" | custom-call | flops 3019898880 | bytes 2359296 | tf_op jit(solution)/shard_map/pairs/pallas_call | solution.py:141
  60.0 2.1 %collective-permute-start.13 = (f32[768,128]{1,0:T(8,128)S(1)}, f32[768,128]{1,0:T(8,128)S(1)}, u32[]{:S(2)}, u32[]{:S(2)}) collective-permute-start(f32[768,128]{1,0:T(8,128)S(1)} %pairs.12), channel_id=1, source_target_pairs={{0,4},{1,5},{4,0},{5,1},{2,6},{3,7},{6,2},{7,3},{8,12},{9,13},{12,... | collective-permute-start | bytes 1179656 | tf_op jit(solution)/shard_map/ppermute | solution.py:325
  62.1 5.0 %pairs.13 = f32[768,128]{1,0:T(8,128)S(1)} custom-call(s32[3]{0:T(128)S(1)} %pad_add_fusion.refs_0_, f32[64,1664]{1,0:T(8,128)S(1)} %collective-permute-done.6.refs_1_.refs_2_, f32[64,1664]{1,0:T(8,128)S(1)} %collective-permute-done.6.refs_1_.refs_2_, bf16[12,256,512]{2,1,0:T(8,128)(2,1)S(1)} %get-tuple-element.32.refs_3_.refs_6_, ...), custom_call_target="tpu_custom_call" | custom-call | flops 3019898880 | bytes 2359296 | tf_op jit(solution)/shard_map/pairs/pallas_call | solution.py:141
  67.0 0.8 collective-permute-start.14
  67.8 0.0 collective-permute-done.10.refs_5_
  67.8 5.1 %pairs.14 = f32[768,128]{1,0:T(8,128)S(1)} custom-call(s32[3]{0:T(128)S(1)} %pad_add_fusion.refs_0_, f32[64,1664]{1,0:T(8,128)S(1)} %collective-permute-done.7.refs_1_.refs_3_, f32[64,1664]{1,0:T(8,128)S(1)} %collective-permute-done.8.refs_2_.refs_4_, f32[64,1664]{1,0:T(8,128)S(1)} %collective-permute-done.7.refs_1_.refs_3_, ...), custom_call_target="tpu_custom_call" | custom-call | flops 3019898880 | bytes 2359296 | tf_op jit(solution)/shard_map/pairs/pallas_call | solution.py:141
  72.9 5.0 %pairs.15 = f32[768,128]{1,0:T(8,128)S(1)} custom-call(s32[3]{0:T(128)S(1)} %pad_add_fusion.refs_0_, f32[64,1664]{1,0:T(8,128)S(1)} %collective-permute-done.6.refs_1_.refs_2_, f32[64,1664]{1,0:T(8,128)S(1)} %collective-permute-done.6.refs_1_.refs_2_, bf16[12,256,512]{2,1,0:T(8,128)(2,1)S(1)} %get-tuple-element.32.refs_3_.refs_6_, ...), custom_call_target="tpu_custom_call" | custom-call | flops 3019898880 | bytes 2359296 | tf_op jit(solution)/shard_map/pairs/pallas_call | solution.py:141
  78.0 1.4 %collective-permute-start.12 = (f32[768,128]{1,0:T(8,128)S(1)}, f32[768,128]{1,0:T(8,128)S(1)}, u32[]{:S(2)}, u32[]{:S(2)}) collective-permute-start(f32[768,128]{1,0:T(8,128)S(1)} %pairs.15), channel_id=1, source_target_pairs={{0,2},{1,3},{2,0},{3,1},{4,6},{5,7},{6,4},{7,5},{8,10},{9,11},{10,... | collective-permute-start | bytes 1179656 | tf_op jit(solution)/shard_map/ppermute | solution.py:325
  79.4 0.7 collective-permute-start.16
  80.0 0.0 collective-permute-done.15
  80.0 3.4 %collective-permute-start.11 = (f32[768,128]{1,0:T(8,128)S(1)}, f32[768,128]{1,0:T(8,128)S(1)}, u32[]{:S(2)}, u32[]{:S(2)}) collective-permute-start(f32[768,128]{1,0:T(8,128)S(1)} %pairs.14), channel_id=1, source_target_pairs={{0,4},{1,5},{4,0},{5,1},{2,6},{3,7},{6,2},{7,3},{8,12},{9,13},{12,... | collective-permute-start | bytes 1179656 | tf_op jit(solution)/shard_map/ppermute | solution.py:325
  83.5 0.0 collective-permute-done.13
  83.5 3.4 %collective-permute-done.14 = f32[768,128]{1,0:T(8,128)S(1)} collective-permute-done((f32[768,128]{1,0:T(8,128)S(1)}, f32[768,128]{1,0:T(8,128)S(1)}, u32[]{:S(2)}, u32[]{:S(2)}) %collective-permute-start.14) | collective-permute-done | bytes 393248 | tf_op jit(solution)/shard_map/ppermute | solution.py:325
  86.9 0.1 multiply_add_fusion.1.refs_1_
  87.0 1.5 %collective-permute-start.20 = (f32[768,128]{1,0:T(8,128)S(1)}, f32[768,128]{1,0:T(8,128)S(1)}, u32[]{:S(2)}, u32[]{:S(2)}) collective-permute-start(f32[768,128]{1,0:T(8,128)S(1)} %multiply_add_fusion.1.refs_1_), channel_id=1, source_target_pairs={{0,8},{8,0},{16,24},{24,16},{1,9},{9,1},{17,25},{25,17},{2,10},{10... | collective-permute-start | bytes 1179656 | tf_op jit(solution)/shard_map/ppermute | solution.py:432
  88.5 1.5 %collective-permute-start.21 = (f32[768,128]{1,0:T(8,128)S(1)}, f32[768,128]{1,0:T(8,128)S(1)}, u32[]{:S(2)}, u32[]{:S(2)}) collective-permute-start(f32[768,128]{1,0:T(8,128)S(1)} %multiply_add_fusion.1.refs_1_), channel_id=1, source_target_pairs={{0,16},{8,24},{16,0},{24,8},{1,17},{9,25},{17,1},{25,9},{2,18},{10... | collective-permute-start | bytes 1179656 | tf_op jit(solution)/shard_map/ppermute | solution.py:432
  90.1 4.1 %collective-permute-done.12 = f32[768,128]{1,0:T(8,128)S(1)} collective-permute-done((f32[768,128]{1,0:T(8,128)S(1)}, f32[768,128]{1,0:T(8,128)S(1)}, u32[]{:S(2)}, u32[]{:S(2)}) %collective-permute-start.12) | collective-permute-done | bytes 393248 | tf_op jit(solution)/shard_map/ppermute | solution.py:325
  94.1 2.4 %collective-permute-start.22 = (f32[768,128]{1,0:T(8,128)S(1)}, f32[768,128]{1,0:T(8,128)S(1)}, u32[]{:S(2)}, u32[]{:S(2)}) collective-permute-start(f32[768,128]{1,0:T(8,128)S(1)} %multiply_add_fusion.1.refs_1_), channel_id=1, source_target_pairs={{0,24},{8,16},{16,8},{24,0},{1,25},{9,17},{17,9},{25,1},{2,26},{10... | collective-permute-start | bytes 1179656 | tf_op jit(solution)/shard_map/ppermute | solution.py:432
  96.5 0.0 collective-permute-done.16
  96.5 11.5 %collective-permute-done.11 = f32[768,128]{1,0:T(8,128)S(1)} collective-permute-done((f32[768,128]{1,0:T(8,128)S(1)}, f32[768,128]{1,0:T(8,128)S(1)}, u32[]{:S(2)}, u32[]{:S(2)}) %collective-permute-start.11) | collective-permute-done | bytes 393248 | tf_op jit(solution)/shard_map/ppermute | solution.py:325
  108.0 0.1 multiply_add_fusion.refs_1_
  108.1 1.6 %collective-permute-start.17 = (f32[768,128]{1,0:T(8,128)S(1)}, f32[768,128]{1,0:T(8,128)S(1)}, u32[]{:S(2)}, u32[]{:S(2)}) collective-permute-start(f32[768,128]{1,0:T(8,128)S(1)} %multiply_add_fusion.refs_1_), channel_id=1, source_target_pairs={{0,8},{8,0},{16,24},{24,16},{1,9},{9,1},{17,25},{25,17},{2,10},{10... | collective-permute-start | bytes 1179656 | tf_op jit(solution)/shard_map/ppermute | solution.py:432
  109.7 1.5 %collective-permute-start.18 = (f32[768,128]{1,0:T(8,128)S(1)}, f32[768,128]{1,0:T(8,128)S(1)}, u32[]{:S(2)}, u32[]{:S(2)}) collective-permute-start(f32[768,128]{1,0:T(8,128)S(1)} %multiply_add_fusion.refs_1_), channel_id=1, source_target_pairs={{0,16},{8,24},{16,0},{24,8},{1,17},{9,25},{17,1},{25,9},{2,18},{10... | collective-permute-start | bytes 1179656 | tf_op jit(solution)/shard_map/ppermute | solution.py:432
  111.2 0.0 collective-permute-done.20.refs_2_
  111.2 0.5 collective-permute-start.19
  111.7 0.0 collective-permute-done.21.refs_3_
  111.7 0.0 collective-permute-done.22.refs_4_
  111.7 1.7 %spread.2.refs_5_ = f32[6144,128]{1,0:T(8,128)} custom-call(s32[4]{0:T(128)S(1)} %iota_xor_fusion.refs_0_, f32[768,128]{1,0:T(8,128)S(1)} %multiply_add_fusion.1.refs_1_, f32[768,128]{1,0:T(8,128)S(1)} %collective-permute-done.20.refs_2_, f32[768,128]{1,0:T(8,128)S(1)} %collective-permute-done.21.refs_3_, f32[768,128]{1,0:T(8,128)S(1)} %collective-permute-done.22.refs_4_), custom_call_target="tpu_custom_call" | custom-call | tf_op jit(solution)/shard_map/spread/pallas_call | solution.py:291
  113.4 6.8 %collective-permute-done.17.refs_2_ = f32[768,128]{1,0:T(8,128)S(1)} collective-permute-done((f32[768,128]{1,0:T(8,128)S(1)}, f32[768,128]{1,0:T(8,128)S(1)}, u32[]{:S(2)}, u32[]{:S(2)}) %collective-permute-start.17) | collective-permute-done | bytes 393248 | tf_op jit(solution)/shard_map/ppermute | solution.py:432
  120.2 6.6 %collective-permute-done.18.refs_3_ = f32[768,128]{1,0:T(8,128)S(1)} collective-permute-done((f32[768,128]{1,0:T(8,128)S(1)}, f32[768,128]{1,0:T(8,128)S(1)}, u32[]{:S(2)}, u32[]{:S(2)}) %collective-permute-start.18) | collective-permute-done | bytes 393248 | tf_op jit(solution)/shard_map/ppermute | solution.py:432
  126.8 0.0 collective-permute-done.19.refs_4_
  126.8 1.7 %spread.3 = f32[6144,128]{1,0:T(8,128)} custom-call(s32[4]{0:T(128)S(1)} %iota_xor_fusion.refs_0_, f32[768,128]{1,0:T(8,128)S(1)} %multiply_add_fusion.refs_1_, f32[768,128]{1,0:T(8,128)S(1)} %collective-permute-done.17.refs_2_, f32[768,128]{1,0:T(8,128)S(1)} %collective-permute-done.18.refs_3_, ...), custom_call_target="tpu_custom_call", output_to_operand_aliasing={{}: (5, {})} | custom-call | tf_op jit(solution)/shard_map/spread/pallas_call | solution.py:291
  (4 shorter events, 0.0 us)
Async XLA Ops:
  0.0 23.9 %collective-permute-start.2 = (f32[6144,128]{1,0:T(8,128)}, f32[6144,128]{1,0:T(8,128)}, u32[]{:S(2)}, u32[]{:S(2)}) collective-permute-start(f32[6144,128]{1,0:T(8,128)} %weights_ref.1), channel_id=1, source_target_pairs={{0,1},{1,0},{2,3},{3,2},{4,5},{5,4},{6,7},{7,6},{8,9},{9,8},{10,11... | collective-permute-start | bytes 9437192 | tf_op jit(solution)/shard_map/ppermute | solution.py:366
  0.5 23.4 %collective-permute-start.1 = (f32[64,6144]{1,0:T(8,128)}, f32[64,6144]{1,0:T(8,128)S(1)}, u32[]{:S(2)}, u32[]{:S(2)}) collective-permute-start(f32[64,6144]{1,0:T(8,128)} %points_ref.1), channel_id=1, source_target_pairs={{0,1},{1,0},{2,3},{3,2},{4,5},{5,4},{6,7},{7,6},{8,9},{9,8},{10,11... | collective-permute-start | bytes 4718600 | tf_op jit(solution)/shard_map/ppermute | solution.py:366
  2.6 19.3 %collective-permute-start.6 = (f32[64,1664]{1,0:T(8,128)S(1)}, f32[64,1664]{1,0:T(8,128)S(1)}, u32[]{:S(2)}, u32[]{:S(2)}) collective-permute-start(f32[64,1664]{1,0:T(8,128)S(1)} %select_maximum_fusion), channel_id=1, source_target_pairs={{0,2},{1,3},{2,0},{3,1},{4,6},{5,7},{6,4},{7,5},{8,10},{9,11},{10,... | collective-permute-start | bytes 1277960 | tf_op jit(solution)/shard_map/ppermute | solution.py:325
  5.7 16.9 %collective-permute-start = (f32[64,1664]{1,0:T(8,128)S(1)}, f32[64,1664]{1,0:T(8,128)S(1)}, u32[]{:S(2)}, u32[]{:S(2)}) collective-permute-start(f32[64,1664]{1,0:T(8,128)S(1)} %select_maximum_fusion), channel_id=1, source_target_pairs={{2,4},{3,5},{4,2},{5,3},{0,0},{1,1},{6,6},{7,7},{10,12},{11,13},{1... | collective-permute-start | bytes 1277960 | tf_op jit(solution)/shard_map/ppermute | solution.py:325
  14.5 1.5 %collective-permute-start.3 = (f32[64,256]{1,0:T(8,128)}, f32[64,256]{1,0:T(8,128)S(1)}, u32[]{:S(2)}, u32[]{:S(2)}) collective-permute-start(f32[64,256]{1,0:T(8,128)} %get-tuple-element.36), channel_id=1, source_target_pairs={{0,1},{1,0},{2,3},{3,2},{4,5},{5,4},{6,7},{7,6},{8,9},{9,8},{10,11... | collective-permute-start | bytes 196616 | tf_op jit(solution)/shard_map/ppermute | solution.py:366
  16.0 1.6 %collective-permute-start.4 = (f32[256,128]{1,0:T(8,128)}, f32[256,128]{1,0:T(8,128)S(1)}, u32[]{:S(2)}, u32[]{:S(2)}) collective-permute-start(f32[256,128]{1,0:T(8,128)} %get-tuple-element.37), channel_id=1, source_target_pairs={{0,1},{1,0},{2,3},{3,2},{4,5},{5,4},{6,7},{7,6},{8,9},{9,8},{10,11... | collective-permute-start | bytes 393224 | tf_op jit(solution)/shard_map/ppermute | solution.py:366
  17.5 15.7 %collective-permute-start.5 = (f32[64,1664]{1,0:T(8,128)S(1)}, f32[64,1664]{1,0:T(8,128)S(1)}, u32[]{:S(2)}, u32[]{:S(2)}) collective-permute-start(f32[64,1664]{1,0:T(8,128)S(1)} %select_maximum_fusion), channel_id=1, source_target_pairs={{0,6},{1,7},{6,0},{7,1},{2,2},{3,3},{4,4},{5,5},{8,14},{9,15},{14,... | collective-permute-start | bytes 1277960 | tf_op jit(solution)/shard_map/ppermute | solution.py:325
  21.9 32.8 %collective-permute-start.7 = (f32[64,1664]{1,0:T(8,128)S(1)}, f32[64,1664]{1,0:T(8,128)S(1)}, u32[]{:S(2)}, u32[]{:S(2)}) collective-permute-start(f32[64,1664]{1,0:T(8,128)S(1)} %collective-permute-done.6.refs_1_.refs_2_), channel_id=1, source_target_pairs={{2,4},{3,5},{4,2},{5,3},{10,12},{11,13},{12,10},{13,11},{18,20},{1... | collective-permute-start | bytes 1277960 | tf_op jit(solution)/shard_map/ppermute | solution.py:325
  22.6 32.1 %collective-permute-start.8 = (f32[64,1664]{1,0:T(8,128)S(1)}, f32[64,1664]{1,0:T(8,128)S(1)}, u32[]{:S(2)}, u32[]{:S(2)}) collective-permute-start(f32[64,1664]{1,0:T(8,128)S(1)} %collective-permute-done.refs_1_.refs_2_), channel_id=1, source_target_pairs={{2,0},{3,1},{4,6},{5,7},{10,8},{11,9},{12,14},{13,15},{18,16},{19,... | collective-permute-start | bytes 1277960 | tf_op jit(solution)/shard_map/ppermute | solution.py:325
  38.2 16.6 %collective-permute-start.9 = (f32[768,128]{1,0:T(8,128)S(1)}, f32[768,128]{1,0:T(8,128)S(1)}, u32[]{:S(2)}, u32[]{:S(2)}) collective-permute-start(f32[768,128]{1,0:T(8,128)S(1)} %pairs.9), channel_id=1, source_target_pairs={{0,2},{1,3},{6,4},{7,5},{8,10},{9,11},{14,12},{15,13},{16,18},{17,... | collective-permute-start | bytes 1179656 | tf_op jit(solution)/shard_map/ppermute | solution.py:325
  52.6 15.2 %collective-permute-start.10 = (f32[768,128]{1,0:T(8,128)S(1)}, f32[768,128]{1,0:T(8,128)S(1)}, u32[]{:S(2)}, u32[]{:S(2)}) collective-permute-start(f32[768,128]{1,0:T(8,128)S(1)} %pairs.11), channel_id=1, source_target_pairs={{0,2},{1,3},{6,4},{7,5},{8,10},{9,11},{14,12},{15,13},{16,18},{17,... | collective-permute-start | bytes 1179656 | tf_op jit(solution)/shard_map/ppermute | solution.py:325
  53.9 26.2 %collective-permute-start.15 = (f32[768,128]{1,0:T(8,128)S(1)}, f32[768,128]{1,0:T(8,128)S(1)}, u32[]{:S(2)}, u32[]{:S(2)}) collective-permute-start(f32[768,128]{1,0:T(8,128)S(1)} %pairs.8), channel_id=1, source_target_pairs={{2,4},{3,5},{4,2},{5,3},{0,0},{1,1},{6,6},{7,7},{10,12},{11,13},{1... | collective-permute-start | bytes 1179656 | tf_op jit(solution)/shard_map/ppermute | solution.py:325
  60.0 23.5 %collective-permute-start.13 = (f32[768,128]{1,0:T(8,128)S(1)}, f32[768,128]{1,0:T(8,128)S(1)}, u32[]{:S(2)}, u32[]{:S(2)}) collective-permute-start(f32[768,128]{1,0:T(8,128)S(1)} %pairs.12), channel_id=1, source_target_pairs={{0,4},{1,5},{4,0},{5,1},{2,6},{3,7},{6,2},{7,3},{8,12},{9,13},{12,... | collective-permute-start | bytes 1179656 | tf_op jit(solution)/shard_map/ppermute | solution.py:325
  67.0 19.9 %collective-permute-start.14 = (f32[768,128]{1,0:T(8,128)S(1)}, f32[768,128]{1,0:T(8,128)S(1)}, u32[]{:S(2)}, u32[]{:S(2)}) collective-permute-start(f32[768,128]{1,0:T(8,128)S(1)} %pairs.13), channel_id=1, source_target_pairs={{0,2},{1,3},{2,0},{3,1},{4,6},{5,7},{6,4},{7,5},{8,10},{9,11},{10,... | collective-permute-start | bytes 1179656 | tf_op jit(solution)/shard_map/ppermute | solution.py:325
  78.0 16.1 %collective-permute-start.12 = (f32[768,128]{1,0:T(8,128)S(1)}, f32[768,128]{1,0:T(8,128)S(1)}, u32[]{:S(2)}, u32[]{:S(2)}) collective-permute-start(f32[768,128]{1,0:T(8,128)S(1)} %pairs.15), channel_id=1, source_target_pairs={{0,2},{1,3},{2,0},{3,1},{4,6},{5,7},{6,4},{7,5},{8,10},{9,11},{10,... | collective-permute-start | bytes 1179656 | tf_op jit(solution)/shard_map/ppermute | solution.py:325
  79.4 17.2 %collective-permute-start.16 = (f32[768,128]{1,0:T(8,128)S(1)}, f32[768,128]{1,0:T(8,128)S(1)}, u32[]{:S(2)}, u32[]{:S(2)}) collective-permute-start(f32[768,128]{1,0:T(8,128)S(1)} %pairs.10), channel_id=1, source_target_pairs={{2,4},{3,5},{4,2},{5,3},{0,0},{1,1},{6,6},{7,7},{10,12},{11,13},{1... | collective-permute-start | bytes 1179656 | tf_op jit(solution)/shard_map/ppermute | solution.py:325
  80.0 28.0 %collective-permute-start.11 = (f32[768,128]{1,0:T(8,128)S(1)}, f32[768,128]{1,0:T(8,128)S(1)}, u32[]{:S(2)}, u32[]{:S(2)}) collective-permute-start(f32[768,128]{1,0:T(8,128)S(1)} %pairs.14), channel_id=1, source_target_pairs={{0,4},{1,5},{4,0},{5,1},{2,6},{3,7},{6,2},{7,3},{8,12},{9,13},{12,... | collective-permute-start | bytes 1179656 | tf_op jit(solution)/shard_map/ppermute | solution.py:325
  87.0 24.2 %collective-permute-start.20 = (f32[768,128]{1,0:T(8,128)S(1)}, f32[768,128]{1,0:T(8,128)S(1)}, u32[]{:S(2)}, u32[]{:S(2)}) collective-permute-start(f32[768,128]{1,0:T(8,128)S(1)} %multiply_add_fusion.1.refs_1_), channel_id=1, source_target_pairs={{0,8},{8,0},{16,24},{24,16},{1,9},{9,1},{17,25},{25,17},{2,10},{10... | collective-permute-start | bytes 1179656 | tf_op jit(solution)/shard_map/ppermute | solution.py:432
  88.5 23.2 %collective-permute-start.21 = (f32[768,128]{1,0:T(8,128)S(1)}, f32[768,128]{1,0:T(8,128)S(1)}, u32[]{:S(2)}, u32[]{:S(2)}) collective-permute-start(f32[768,128]{1,0:T(8,128)S(1)} %multiply_add_fusion.1.refs_1_), channel_id=1, source_target_pairs={{0,16},{8,24},{16,0},{24,8},{1,17},{9,25},{17,1},{25,9},{2,18},{10... | collective-permute-start | bytes 1179656 | tf_op jit(solution)/shard_map/ppermute | solution.py:432
  94.1 17.6 %collective-permute-start.22 = (f32[768,128]{1,0:T(8,128)S(1)}, f32[768,128]{1,0:T(8,128)S(1)}, u32[]{:S(2)}, u32[]{:S(2)}) collective-permute-start(f32[768,128]{1,0:T(8,128)S(1)} %multiply_add_fusion.1.refs_1_), channel_id=1, source_target_pairs={{0,24},{8,16},{16,8},{24,0},{1,25},{9,17},{17,9},{25,1},{2,26},{10... | collective-permute-start | bytes 1179656 | tf_op jit(solution)/shard_map/ppermute | solution.py:432
  108.1 12.0 %collective-permute-start.17 = (f32[768,128]{1,0:T(8,128)S(1)}, f32[768,128]{1,0:T(8,128)S(1)}, u32[]{:S(2)}, u32[]{:S(2)}) collective-permute-start(f32[768,128]{1,0:T(8,128)S(1)} %multiply_add_fusion.refs_1_), channel_id=1, source_target_pairs={{0,8},{8,0},{16,24},{24,16},{1,9},{9,1},{17,25},{25,17},{2,10},{10... | collective-permute-start | bytes 1179656 | tf_op jit(solution)/shard_map/ppermute | solution.py:432
  109.7 17.1 %collective-permute-start.18 = (f32[768,128]{1,0:T(8,128)S(1)}, f32[768,128]{1,0:T(8,128)S(1)}, u32[]{:S(2)}, u32[]{:S(2)}) collective-permute-start(f32[768,128]{1,0:T(8,128)S(1)} %multiply_add_fusion.refs_1_), channel_id=1, source_target_pairs={{0,16},{8,24},{16,0},{24,8},{1,17},{9,25},{17,1},{25,9},{2,18},{10... | collective-permute-start | bytes 1179656 | tf_op jit(solution)/shard_map/ppermute | solution.py:432
  111.2 15.5 %collective-permute-start.19 = (f32[768,128]{1,0:T(8,128)S(1)}, f32[768,128]{1,0:T(8,128)S(1)}, u32[]{:S(2)}, u32[]{:S(2)}) collective-permute-start(f32[768,128]{1,0:T(8,128)S(1)} %multiply_add_fusion.refs_1_), channel_id=1, source_target_pairs={{0,24},{8,16},{16,8},{24,0},{1,25},{9,17},{17,9},{25,1},{2,26},{10... | collective-permute-start | bytes 1179656 | tf_op jit(solution)/shard_map/ppermute | solution.py:432

commit v7 on v6

--- a/solution.py
+++ b/solution.py
@@ -9,7 +9,7 @@
 from jax.sharding import PartitionSpec as P
 
 
-ROUNDS = ("d0", "a0", "d1", "a1", "b0", "c0", "b1", "c1")
+ROUNDS = ("a0", "d0", "a1", "d1", "b0", "c0", "b1", "c1")
 
 F32 = jnp.float32
 BF16 = jnp.bfloat16
@@ -47,6 +47,7 @@
     x_refs = [refs.pop(0) for _ in range(plan["parcels"])]
     init_ref = refs.pop(0) if plan["init"] else None
     sides, (out_ref, xk_buf) = (refs[:4], refs[4:8]), refs[8:]
+    unit = plan["unit"]
     capacity = plan["capacity"]
     devices = plan["devices"]
     scale = plan["scale"]
@@ -58,31 +59,22 @@
         value = sum(ref[n // 128, n % 128] for ref in list_refs)
         return value.astype(jnp.int32)
 
-    number = place_ref[0] * plan["per"] + (plan["first"] + step) // plan["units"]
-    row = number // plan["row_leaves"]
-    x = x_refs[0][...]
-    for ref in x_refs[1:]:
-        x = x + ref[...]
-    xk_buf[...] = jnp.swapaxes(stacked(x, 2.0 * scale, scale, True), 0, 1).astype(BF16)
-    if init_ref is None:
-        out_ref[...] = jnp.zeros_like(out_ref)
-    else:
-        out_ref[...] = init_ref[...]
-
-    def add(yk, wk, gain):
+    columns = out_ref.shape[1]
+
+    def add(part, yk, wk, gain):
         wk = jnp.concatenate([wk, wk], axis=0)
-        columns = out_ref.shape[1]
-        exponent = jnp.dot(xk_buf[...], yk, preferred_element_type=F32)
+        exponent = jnp.dot(xk_buf[part, :], yk, preferred_element_type=F32)
         value = jnp.exp2(exponent)
         if gain is not None:
             value = value * gain
         high = value.astype(BF16)
         low = (value - high.astype(F32)).astype(BF16)
         both = jnp.dot(jnp.concatenate([high, low], axis=1), wk, preferred_element_type=F32)
-        out_ref[...] += both[:, :columns] + both[:, columns:]
-
-    gains = [None] * (slots + 1)
-    if not plan["dense"]:
+        out_ref[part, :] += both[:, :columns] + both[:, columns:]
+
+    def gains_of(number):
+        if plan["dense"]:
+            return [None] * (slots + 1)
         base = plan["rows_listed"] * devices * capacity
         near = [listed(base + number * plan["near"] + n) for n in range(plan["near"])]
         base += plan["targets"] * plan["near"]
@@ -97,17 +89,33 @@
             gains += [among(owner * capacity + c, near) for c in range(capacity)]
         own, partner = (among(place_ref[1 + side], far) for side in range(2))
         first_half = lax.broadcasted_iota(jnp.int32, (1, 2 * kept), 1) < kept
-        gains.append(jnp.where(first_half, own, partner))
-
-    add(
-        jnp.concatenate([side[2][...] for side in sides], axis=1),
-        jnp.concatenate([side[3][...] for side in sides], axis=0),
-        gains[slots],
-    )
-    for n, (pts, wts, _, _) in enumerate(sides):
-        for c in range(capacity):
-            source = listed((row * devices + place_ref[1 + n]) * capacity + c)
-            add(pts[source], wts[source], gains[n * capacity + c])
+        return gains + [jnp.where(first_half, own, partner)]
+
+    for u in range(plan["group"]):
+        part = slice(u * unit, (u + 1) * unit)
+        at = plan["first"] + step * plan["group"] + u
+        number = place_ref[0] * plan["per"] + at // plan["units"]
+        row = number // plan["row_leaves"]
+        x = x_refs[0][:, part]
+        for ref in x_refs[1:]:
+            x = x + ref[:, part]
+        rows = stacked(x, 2.0 * scale, scale, True)
+        xk_buf[part, :] = jnp.swapaxes(rows, 0, 1).astype(BF16)
+        if init_ref is None:
+            out_ref[part, :] = jnp.zeros_like(out_ref[part, :])
+        else:
+            out_ref[part, :] = init_ref[part, :]
+        gains = gains_of(number)
+        add(
+            part,
+            jnp.concatenate([side[2][...] for side in sides], axis=1),
+            jnp.concatenate([side[3][...] for side in sides], axis=0),
+            gains[slots],
+        )
+        for n, (pts, wts, _, _) in enumerate(sides):
+            for c in range(capacity):
+                source = listed((row * devices + place_ref[1 + n]) * capacity + c)
+                add(part, pts[source], wts[source], gains[n * capacity + c])
 
 
 def pairs(sizes, place, parcels, init, sources, first, count):
@@ -117,35 +125,39 @@
     columns = own[1].shape[2] // 2
     slots = 2 * sizes["capacity"]
     kept = own[2].shape[1]
+    unit = leaf // sizes["units"]
+    width = parcels[0].shape[1] - 128
+    group = math.gcd(count, 3)
+    assert first % group == 0
+    block = group * unit
     plan = dict(
         sizes,
         parcels=len(parcels),
         init=init is not None,
         first=first,
-        count=count,
-    )
-    unit = leaf // sizes["units"]
-    width = parcels[0].shape[1] - 128
+        group=group,
+        unit=unit,
+    )
     in_specs = [pl.BlockSpec(memory_space=pltpu.SMEM)]
     in_specs += [
         pl.BlockSpec((8, 128), lambda i: (0, width // 128), memory_space=pltpu.SMEM)
     ] * len(parcels)
-    in_specs += [pl.BlockSpec((features, unit), lambda i: (0, first + i))] * len(parcels)
+    in_specs += [pl.BlockSpec((features, block), lambda i: (0, first // group + i))] * len(parcels)
     operands = [place, *parcels, *parcels]
     if init is not None:
-        in_specs.append(pl.BlockSpec((unit, columns), lambda i: (i, 0)))
+        in_specs.append(pl.BlockSpec((block, columns), lambda i: (i, 0)))
         operands.append(init)
     in_specs += [pl.BlockSpec(memory_space=pltpu.VMEM)] * 8
     operands += [array for side in sources for array in side]
     work = count * unit * (leaf * slots + 2 * kept)
     return pl.pallas_call(
         functools.partial(pair_kernel, plan),
-        grid=(count,),
+        grid=(count // group,),
         in_specs=in_specs,
-        out_specs=pl.BlockSpec((unit, columns), lambda i: (i, 0)),
+        out_specs=pl.BlockSpec((block, columns), lambda i: (i, 0)),
         out_shape=jax.ShapeDtypeStruct((count * unit, columns), F32),
         scratch_shapes=[
-            pltpu.VMEM((unit, rows), BF16),
+            pltpu.VMEM((block, rows), BF16),
         ],
         compiler_params=pltpu.CompilerParams(vmem_limit_bytes=16 << 20),
         cost_estimate=pl.CostEstimate(

time: 129 us -> 133 us (1.031)
  Pallas kernels: 55.7 us -> 48.2 us
  starting transfers between devices: 34.7 us -> 41.9 us
  waiting for transfers between devices: 35.5 us -> 40.1 us
    pallas_call x8, Pallas kernels: 40.3 us -> 32.7 us  [pairs(): pl.pallas_call(functools.partial(pair_kernel, plan), grid=(count // group...]
    ppermute x13, waiting for transfers between devices: 19.3 us -> 26.7 us  [shift(): return lax.ppermute(array, 'dev', along(moves))]
    ppermute x13, starting transfers between devices: 25 us -> 31.5 us  [shift(): return lax.ppermute(array, 'dev', along(moves))]
    ppermute x4, waiting for transfers between devices: 2.87 us -> 1.34 us  [to_partner(): return lax.ppermute(array, 'dev', swap)]
  transfers between devices with their start and end apart: 23 -> 23, of which waited for: 8 -> 8; matrix products, arithmetic and copies ran while one was open for 2% -> 2% of each run, Pallas kernels for 42% -> 35%
where the time goes in v7:
time: 133 us
  Pallas kernels  48.2 us (36%)
  starting transfers between devices  41.9 us (32%)
  waiting for transfers between devices  40.1 us (30%)
  local copies, waits for them, and re-layouts  1.89 us (1%)
    pallas_call x8, Pallas kernels, pairs(): pl.pallas_call(functools.partial(pair_kernel, plan), grid=(count // group...  32.7 us
    ppermute x13, starting transfers between devices, shift(): return lax.ppermute(array, 'dev', along(moves))  31.5 us
    ppermute x13, waiting for transfers between devices, shift(): return lax.ppermute(array, 'dev', along(moves))  26.7 us
    ppermute x6, waiting for transfers between devices, on_device(): lax.ppermute(piece, 'grp', [(g, g ^ m) for g in range(groups)])  12.1 us
    pallas_call x2, Pallas kernels, prepared(): pl.pallas_call(functools.partial(body, scale), grid=(count // block,), in...  12 us
    ppermute x6, starting transfers between devices, on_device(): lax.ppermute(piece, 'grp', [(g, g ^ m) for g in range(groups)])  9.09 us
    pallas_call x2, Pallas kernels, spread(): pl.pallas_call(functools.partial(spread_kernel, groups, per, first, unit,...  3.43 us
  transfers between devices with their start and end apart: 23, of which 8 were waited for; matrix products, arithmetic and copies ran while one was open for 2% of the time, Pallas kernels for 35%

profile of v7, /device:TPU:0, one launch (start us, length us, event | category | flops | bytes accessed | tf_op | source)
XLA Modules:
  0.0 132.8 jit_solution(3282511105951949434)
XLA Ops:
  0.0 0.5 collective-permute-start.2
  0.5 0.0 collective-permute-start.1
  0.5 0.8 copy.8
  1.3 0.1 reshape.5
  1.4 0.1 pad_add_fusion.refs_0_
  1.5 1.0 constant_dynamic-slice_fusion
  2.6 8.1 %prepared.2 = (bf16[12,256,512]{2,1,0:T(8,128)(2,1)S(1)}, bf16[12,512,256]{2,1,0:T(8,128)(2,1)S(1)}, bf16[256,256]{1,0:T(8,128)(2,1)S(1)}, bf16[256,256]{1,0:T(8...) custom-call(s32[1,256]{1,0:T(1,128)} %idx_ref.1, f32[64,6144]{1,0:T(8,128)} %points_ref.1, ...), custom_call_target="tpu_custom_call" | custom-call | flops 1610612736 | bytes 20447232 | tf_op jit(solution)/shard_map/prepared/pallas_call | solution.py:268
  10.7 0.5 collective-permute-start.3
  11.2 2.6 %collective-permute-start.6 = (f32[64,1664]{1,0:T(8,128)S(1)}, f32[64,1664]{1,0:T(8,128)S(1)}, u32[]{:S(2)}, u32[]{:S(2)}) collective-permute-start(f32[64,1664]{1,0:T(8,128)S(1)} %select_maximum_fusion), channel_id=1, source_target_pairs={{0,2},{1,3},{2,0},{3,1},{4,6},{5,7},{6,4},{7,5},{8,10},{9,11},{10,... | collective-permute-start | bytes 1277960 | tf_op jit(solution)/shard_map/ppermute | solution.py:337
  13.8 0.7 collective-permute-start.5
  14.4 0.0 collective-permute-done.3.coords_ref
  14.4 0.3 collective-permute-start.4
  14.7 1.3 %collective-permute-done.4.summed_ref = f32[256,128]{1,0:T(8,128)S(1)} collective-permute-done((f32[256,128]{1,0:T(8,128)}, f32[256,128]{1,0:T(8,128)S(1)}, u32[]{:S(2)}, u32[]{:S(2)}) %collective-permute-start.4) | collective-permute-done | bytes 131104 | tf_op jit(solution)/shard_map/ppermute | solution.py:378
  16.1 4.6 %collective-permute-start = (f32[64,1664]{1,0:T(8,128)S(1)}, f32[64,1664]{1,0:T(8,128)S(1)}, u32[]{:S(2)}, u32[]{:S(2)}) collective-permute-start(f32[64,1664]{1,0:T(8,128)S(1)} %select_maximum_fusion), channel_id=1, source_target_pairs={{0,6},{1,7},{6,0},{7,1},{2,2},{3,3},{4,4},{5,5},{8,14},{9,15},{14,... | collective-permute-start | bytes 1277960 | tf_op jit(solution)/shard_map/ppermute | solution.py:337
  20.7 3.5 %collective-permute-done.6.refs_1_.refs_2_ = f32[64,1664]{1,0:T(8,128)S(1)} collective-permute-done((f32[64,1664]{1,0:T(8,128)S(1)}, f32[64,1664]{1,0:T(8,128)S(1)}, u32[]{:S(2)}, u32[]{:S(2)}) %collective-permute-start.6) | collective-permute-done | bytes 426016 | tf_op jit(solution)/shard_map/ppermute | solution.py:337
  24.2 0.7 collective-permute-start.7
  24.9 0.0 collective-permute-done.5.refs_1_.refs_2_
  24.9 1.3 collective-permute-start.8
  26.2 0.0 collective-permute-done.1.points_ref
  26.2 0.0 collective-permute-done.2.weights_ref
  26.3 3.9 %prepared.3 = (bf16[12,256,512]{2,1,0:T(8,128)(2,1)S(1)}, bf16[12,512,256]{2,1,0:T(8,128)(2,1)S(1)}, bf16[256,256]{1,0:T(8,128)(2,1)S(1)}, bf16[256,256]{1,0:T(8,128)(2,1)S(1)}) custom-call(f32[64,6144]{1,0:T(8,128)S(1)} %collective-permute-done.1.points_ref, f32[6144,128]{1,0:T(8,128)} %collective-permute-done.2.weights_ref, ...), custom_call_target="tpu_custom_call" | custom-call | flops 1610612736 | bytes 14155776 | tf_op jit(solution)/shard_map/prepared/pallas_call | solution.py:268
  30.2 5.5 %collective-permute-done.refs_1_.refs_2_ = f32[64,1664]{1,0:T(8,128)S(1)} collective-permute-done((f32[64,1664]{1,0:T(8,128)S(1)}, f32[64,1664]{1,0:T(8,128)S(1)}, u32[]{:S(2)}, u32[]{:S(2)}) %collective-permute-start) | collective-permute-done | bytes 426016 | tf_op jit(solution)/shard_map/ppermute | solution.py:337
  35.7 4.1 %pairs.8 = f32[768,128]{1,0:T(8,128)S(1)} custom-call(s32[3]{0:T(128)S(1)} %pad_add_fusion.refs_0_, f32[64,1664]{1,0:T(8,128)S(1)} %collective-permute-done.refs_1_.refs_2_, f32[64,1664]{1,0:T(8,128)S(1)} %collective-permute-done.refs_1_.refs_2_, bf16[12,256,512]{2,1,0:T(8,128)(2,1)S(1)} %get-tuple-element.32.refs_3_.refs_6_, ...), custom_call_target="tpu_custom_call" | custom-call | flops 3019898880 | bytes 2359296 | tf_op jit(solution)/shard_map/pairs/pallas_call | solution.py:153
  39.7 10.3 %collective-permute-start.9 = (f32[768,128]{1,0:T(8,128)S(1)}, f32[768,128]{1,0:T(8,128)S(1)}, u32[]{:S(2)}, u32[]{:S(2)}) collective-permute-start(f32[768,128]{1,0:T(8,128)S(1)} %pairs.8), channel_id=1, source_target_pairs={{0,2},{1,3},{6,4},{7,5},{8,10},{9,11},{14,12},{15,13},{16,18},{17,... | collective-permute-start | bytes 1179656 | tf_op jit(solution)/shard_map/ppermute | solution.py:337
  50.1 4.1 %pairs.9 = f32[768,128]{1,0:T(8,128)S(1)} custom-call(s32[3]{0:T(128)S(1)} %pad_add_fusion.refs_0_, f32[64,1664]{1,0:T(8,128)S(1)} %collective-permute-done.5.refs_1_.refs_2_, f32[64,1664]{1,0:T(8,128)S(1)} %collective-permute-done.5.refs_1_.refs_2_, bf16[12,256,512]{2,1,0:T(8,128)(2,1)S(1)} %get-tuple-element.32.refs_3_.refs_6_, ...), custom_call_target="tpu_custom_call" | custom-call | flops 3019898880 | bytes 2359296 | tf_op jit(solution)/shard_map/pairs/pallas_call | solution.py:153
  54.1 4.1 %pairs.10 = f32[768,128]{1,0:T(8,128)S(1)} custom-call(s32[3]{0:T(128)S(1)} %pad_add_fusion.refs_0_, f32[64,1664]{1,0:T(8,128)S(1)} %collective-permute-done.refs_1_.refs_2_, f32[64,1664]{1,0:T(8,128)S(1)} %collective-permute-done.refs_1_.refs_2_, bf16[12,256,512]{2,1,0:T(8,128)(2,1)S(1)} %get-tuple-element.32.refs_3_.refs_6_, ...), custom_call_target="tpu_custom_call" | custom-call | flops 3019898880 | bytes 2359296 | tf_op jit(solution)/shard_map/pairs/pallas_call | solution.py:153
  58.2 1.3 collective-permute-start.10
  59.5 0.9 collective-permute-start.15
  60.5 4.1 %pairs.11 = f32[768,128]{1,0:T(8,128)S(1)} custom-call(s32[3]{0:T(128)S(1)} %pad_add_fusion.refs_0_, f32[64,1664]{1,0:T(8,128)S(1)} %collective-permute-done.5.refs_1_.refs_2_, f32[64,1664]{1,0:T(8,128)S(1)} %collective-permute-done.5.refs_1_.refs_2_, bf16[12,256,512]{2,1,0:T(8,128)(2,1)S(1)} %get-tuple-element.32.refs_3_.refs_6_, ...), custom_call_target="tpu_custom_call" | custom-call | flops 3019898880 | bytes 2359296 | tf_op jit(solution)/shard_map/pairs/pallas_call | solution.py:153
  64.5 0.0 collective-permute-done.7.refs_1_.refs_3_
  64.5 0.0 collective-permute-done.8.refs_2_.refs_4_
  64.5 0.0 collective-permute-done.9.refs_5_
  64.6 4.1 %pairs.12 = f32[768,128]{1,0:T(8,128)S(1)} custom-call(s32[3]{0:T(128)S(1)} %pad_add_fusion.refs_0_, f32[64,1664]{1,0:T(8,128)S(1)} %collective-permute-done.7.refs_1_.refs_3_, f32[64,1664]{1,0:T(8,128)S(1)} %collective-permute-done.8.refs_2_.refs_4_, f32[64,1664]{1,0:T(8,128)S(1)} %collective-permute-done.7.refs_1_.refs_3_, ...), custom_call_target="tpu_custom_call" | custom-call | flops 3019898880 | bytes 2359296 | tf_op jit(solution)/shard_map/pairs/pallas_call | solution.py:153
  68.7 2.1 %collective-permute-start.13 = (f32[768,128]{1,0:T(8,128)S(1)}, f32[768,128]{1,0:T(8,128)S(1)}, u32[]{:S(2)}, u32[]{:S(2)}) collective-permute-start(f32[768,128]{1,0:T(8,128)S(1)} %pairs.12), channel_id=1, source_target_pairs={{0,4},{1,5},{4,0},{5,1},{2,6},{3,7},{6,2},{7,3},{8,12},{9,13},{12,... | collective-permute-start | bytes 1179656 | tf_op jit(solution)/shard_map/ppermute | solution.py:337
  70.8 4.1 %pairs.13 = f32[768,128]{1,0:T(8,128)S(1)} custom-call(s32[3]{0:T(128)S(1)} %pad_add_fusion.refs_0_, f32[64,1664]{1,0:T(8,128)S(1)} %collective-permute-done.6.refs_1_.refs_2_, f32[64,1664]{1,0:T(8,128)S(1)} %collective-permute-done.6.refs_1_.refs_2_, bf16[12,256,512]{2,1,0:T(8,128)(2,1)S(1)} %get-tuple-element.32.refs_3_.refs_6_, ...), custom_call_target="tpu_custom_call" | custom-call | flops 3019898880 | bytes 2359296 | tf_op jit(solution)/shard_map/pairs/pallas_call | solution.py:153
  74.9 1.5 %collective-permute-start.14 = (f32[768,128]{1,0:T(8,128)S(1)}, f32[768,128]{1,0:T(8,128)S(1)}, u32[]{:S(2)}, u32[]{:S(2)}) collective-permute-start(f32[768,128]{1,0:T(8,128)S(1)} %pairs.13), channel_id=1, source_target_pairs={{0,2},{1,3},{2,0},{3,1},{4,6},{5,7},{6,4},{7,5},{8,10},{9,11},{10,... | collective-permute-start | bytes 1179656 | tf_op jit(solution)/shard_map/ppermute | solution.py:337
  76.4 0.0 collective-permute-done.10.refs_5_
  76.4 4.1 %pairs.14 = f32[768,128]{1,0:T(8,128)S(1)} custom-call(s32[3]{0:T(128)S(1)} %pad_add_fusion.refs_0_, f32[64,1664]{1,0:T(8,128)S(1)} %collective-permute-done.7.refs_1_.refs_3_, f32[64,1664]{1,0:T(8,128)S(1)} %collective-permute-done.8.refs_2_.refs_4_, f32[64,1664]{1,0:T(8,128)S(1)} %collective-permute-done.7.refs_1_.refs_3_, ...), custom_call_target="tpu_custom_call" | custom-call | flops 3019898880 | bytes 2359296 | tf_op jit(solution)/shard_map/pairs/pallas_call | solution.py:153
  80.6 4.1 %pairs.15 = f32[768,128]{1,0:T(8,128)S(1)} custom-call(s32[3]{0:T(128)S(1)} %pad_add_fusion.refs_0_, f32[64,1664]{1,0:T(8,128)S(1)} %collective-permute-done.6.refs_1_.refs_2_, f32[64,1664]{1,0:T(8,128)S(1)} %collective-permute-done.6.refs_1_.refs_2_, bf16[12,256,512]{2,1,0:T(8,128)(2,1)S(1)} %get-tuple-element.32.refs_3_.refs_6_, ...), custom_call_target="tpu_custom_call" | custom-call | flops 3019898880 | bytes 2359296 | tf_op jit(solution)/shard_map/pairs/pallas_call | solution.py:153
  84.6 0.6 collective-permute-start.12
  85.3 0.7 collective-permute-start.16
  85.9 0.0 collective-permute-done.15
  86.0 4.2 %collective-permute-start.11 = (f32[768,128]{1,0:T(8,128)S(1)}, f32[768,128]{1,0:T(8,128)S(1)}, u32[]{:S(2)}, u32[]{:S(2)}) collective-permute-start(f32[768,128]{1,0:T(8,128)S(1)} %pairs.14), channel_id=1, source_target_pairs={{0,4},{1,5},{4,0},{5,1},{2,6},{3,7},{6,2},{7,3},{8,12},{9,13},{12,... | collective-permute-start | bytes 1179656 | tf_op jit(solution)/shard_map/ppermute | solution.py:337
  90.2 0.0 collective-permute-done.13
  90.2 4.4 %collective-permute-done.14 = f32[768,128]{1,0:T(8,128)S(1)} collective-permute-done((f32[768,128]{1,0:T(8,128)S(1)}, f32[768,128]{1,0:T(8,128)S(1)}, u32[]{:S(2)}, u32[]{:S(2)}) %collective-permute-start.14) | collective-permute-done | bytes 393248 | tf_op jit(solution)/shard_map/ppermute | solution.py:337
  94.5 0.1 multiply_add_fusion.1.refs_1_
  94.6 1.5 %collective-permute-start.20 = (f32[768,128]{1,0:T(8,128)S(1)}, f32[768,128]{1,0:T(8,128)S(1)}, u32[]{:S(2)}, u32[]{:S(2)}) collective-permute-start(f32[768,128]{1,0:T(8,128)S(1)} %multiply_add_fusion.1.refs_1_), channel_id=1, source_target_pairs={{0,8},{8,0},{16,24},{24,16},{1,9},{9,1},{17,25},{25,17},{2,10},{10... | collective-permute-start | bytes 1179656 | tf_op jit(solution)/shard_map/ppermute | solution.py:444
  96.2 1.5 %collective-permute-start.21 = (f32[768,128]{1,0:T(8,128)S(1)}, f32[768,128]{1,0:T(8,128)S(1)}, u32[]{:S(2)}, u32[]{:S(2)}) collective-permute-start(f32[768,128]{1,0:T(8,128)S(1)} %multiply_add_fusion.1.refs_1_), channel_id=1, source_target_pairs={{0,16},{8,24},{16,0},{24,8},{1,17},{9,25},{17,1},{25,9},{2,18},{10... | collective-permute-start | bytes 1179656 | tf_op jit(solution)/shard_map/ppermute | solution.py:444
  97.7 4.7 %collective-permute-done.12 = f32[768,128]{1,0:T(8,128)S(1)} collective-permute-done((f32[768,128]{1,0:T(8,128)S(1)}, f32[768,128]{1,0:T(8,128)S(1)}, u32[]{:S(2)}, u32[]{:S(2)}) %collective-permute-start.12) | collective-permute-done | bytes 393248 | tf_op jit(solution)/shard_map/ppermute | solution.py:337
  102.4 2.5 %collective-permute-start.22 = (f32[768,128]{1,0:T(8,128)S(1)}, f32[768,128]{1,0:T(8,128)S(1)}, u32[]{:S(2)}, u32[]{:S(2)}) collective-permute-start(f32[768,128]{1,0:T(8,128)S(1)} %multiply_add_fusion.1.refs_1_), channel_id=1, source_target_pairs={{0,24},{8,16},{16,8},{24,0},{1,25},{9,17},{17,9},{25,1},{2,26},{10... | collective-permute-start | bytes 1179656 | tf_op jit(solution)/shard_map/ppermute | solution.py:444
  104.8 0.0 collective-permute-done.16
  104.8 8.6 %collective-permute-done.11 = f32[768,128]{1,0:T(8,128)S(1)} collective-permute-done((f32[768,128]{1,0:T(8,128)S(1)}, f32[768,128]{1,0:T(8,128)S(1)}, u32[]{:S(2)}, u32[]{:S(2)}) %collective-permute-start.11) | collective-permute-done | bytes 393248 | tf_op jit(solution)/shard_map/ppermute | solution.py:337
  113.4 0.1 multiply_add_fusion.refs_1_
  113.5 1.6 %collective-permute-start.17 = (f32[768,128]{1,0:T(8,128)S(1)}, f32[768,128]{1,0:T(8,128)S(1)}, u32[]{:S(2)}, u32[]{:S(2)}) collective-permute-start(f32[768,128]{1,0:T(8,128)S(1)} %multiply_add_fusion.refs_1_), channel_id=1, source_target_pairs={{0,8},{8,0},{16,24},{24,16},{1,9},{9,1},{17,25},{25,17},{2,10},{10... | collective-permute-start | bytes 1179656 | tf_op jit(solution)/shard_map/ppermute | solution.py:444
  115.1 1.5 %collective-permute-start.18 = (f32[768,128]{1,0:T(8,128)S(1)}, f32[768,128]{1,0:T(8,128)S(1)}, u32[]{:S(2)}, u32[]{:S(2)}) collective-permute-start(f32[768,128]{1,0:T(8,128)S(1)} %multiply_add_fusion.refs_1_), channel_id=1, source_target_pairs={{0,16},{8,24},{16,0},{24,8},{1,17},{9,25},{17,1},{25,9},{2,18},{10... | collective-permute-start | bytes 1179656 | tf_op jit(solution)/shard_map/ppermute | solution.py:444
  116.6 0.0 collective-permute-done.20.refs_2_
  116.6 0.5 collective-permute-start.19
  117.1 0.0 collective-permute-done.21.refs_3_
  117.1 0.0 collective-permute-done.22.refs_4_
  117.1 1.7 %spread.2.refs_5_ = f32[6144,128]{1,0:T(8,128)} custom-call(s32[4]{0:T(128)S(1)} %iota_xor_fusion.refs_0_, f32[768,128]{1,0:T(8,128)S(1)} %multiply_add_fusion.1.refs_1_, f32[768,128]{1,0:T(8,128)S(1)} %collective-permute-done.20.refs_2_, f32[768,128]{1,0:T(8,128)S(1)} %collective-permute-done.21.refs_3_, f32[768,128]{1,0:T(8,128)S(1)} %collective-permute-done.22.refs_4_), custom_call_target="tpu_custom_call" | custom-call | tf_op jit(solution)/shard_map/spread/pallas_call | solution.py:303
  118.8 6.7 %collective-permute-done.17.refs_2_ = f32[768,128]{1,0:T(8,128)S(1)} collective-permute-done((f32[768,128]{1,0:T(8,128)S(1)}, f32[768,128]{1,0:T(8,128)S(1)}, u32[]{:S(2)}, u32[]{:S(2)}) %collective-permute-start.17) | collective-permute-done | bytes 393248 | tf_op jit(solution)/shard_map/ppermute | solution.py:444
  125.5 5.4 %collective-permute-done.18.refs_3_ = f32[768,128]{1,0:T(8,128)S(1)} collective-permute-done((f32[768,128]{1,0:T(8,128)S(1)}, f32[768,128]{1,0:T(8,128)S(1)}, u32[]{:S(2)}, u32[]{:S(2)}) %collective-permute-start.18) | collective-permute-done | bytes 393248 | tf_op jit(solution)/shard_map/ppermute | solution.py:444
  130.9 0.0 collective-permute-done.19.refs_4_
  130.9 1.7 %spread.3 = f32[6144,128]{1,0:T(8,128)} custom-call(s32[4]{0:T(128)S(1)} %iota_xor_fusion.refs_0_, f32[768,128]{1,0:T(8,128)S(1)} %multiply_add_fusion.refs_1_, f32[768,128]{1,0:T(8,128)S(1)} %collective-permute-done.17.refs_2_, f32[768,128]{1,0:T(8,128)S(1)} %collective-permute-done.18.refs_3_, ...), custom_call_target="tpu_custom_call", output_to_operand_aliasing={{}: (5, {})} | custom-call | tf_op jit(solution)/shard_map/spread/pallas_call | solution.py:303
  (4 shorter events, 0.0 us)
Async XLA Ops:
  0.0 26.2 %collective-permute-start.2 = (f32[6144,128]{1,0:T(8,128)}, f32[6144,128]{1,0:T(8,128)}, u32[]{:S(2)}, u32[]{:S(2)}) collective-permute-start(f32[6144,128]{1,0:T(8,128)} %weights_ref.1), channel_id=1, source_target_pairs={{0,1},{1,0},{2,3},{3,2},{4,5},{5,4},{6,7},{7,6},{8,9},{9,8},{10,11... | collective-permute-start | bytes 9437192 | tf_op jit(solution)/shard_map/ppermute | solution.py:378
  0.5 25.7 %collective-permute-start.1 = (f32[64,6144]{1,0:T(8,128)}, f32[64,6144]{1,0:T(8,128)S(1)}, u32[]{:S(2)}, u32[]{:S(2)}) collective-permute-start(f32[64,6144]{1,0:T(8,128)} %points_ref.1), channel_id=1, source_target_pairs={{0,1},{1,0},{2,3},{3,2},{4,5},{5,4},{6,7},{7,6},{8,9},{9,8},{10,11... | collective-permute-start | bytes 4718600 | tf_op jit(solution)/shard_map/ppermute | solution.py:378
  10.7 3.7 %collective-permute-start.3 = (f32[64,256]{1,0:T(8,128)}, f32[64,256]{1,0:T(8,128)S(1)}, u32[]{:S(2)}, u32[]{:S(2)}) collective-permute-start(f32[64,256]{1,0:T(8,128)} %get-tuple-element.36), channel_id=1, source_target_pairs={{0,1},{1,0},{2,3},{3,2},{4,5},{5,4},{6,7},{7,6},{8,9},{9,8},{10,11... | collective-permute-start | bytes 196616 | tf_op jit(solution)/shard_map/ppermute | solution.py:378
  11.2 13.1 %collective-permute-start.6 = (f32[64,1664]{1,0:T(8,128)S(1)}, f32[64,1664]{1,0:T(8,128)S(1)}, u32[]{:S(2)}, u32[]{:S(2)}) collective-permute-start(f32[64,1664]{1,0:T(8,128)S(1)} %select_maximum_fusion), channel_id=1, source_target_pairs={{0,2},{1,3},{2,0},{3,1},{4,6},{5,7},{6,4},{7,5},{8,10},{9,11},{10,... | collective-permute-start | bytes 1277960 | tf_op jit(solution)/shard_map/ppermute | solution.py:337
  13.8 11.2 %collective-permute-start.5 = (f32[64,1664]{1,0:T(8,128)S(1)}, f32[64,1664]{1,0:T(8,128)S(1)}, u32[]{:S(2)}, u32[]{:S(2)}) collective-permute-start(f32[64,1664]{1,0:T(8,128)S(1)} %select_maximum_fusion), channel_id=1, source_target_pairs={{2,4},{3,5},{4,2},{5,3},{0,0},{1,1},{6,6},{7,7},{10,12},{11,13},{1... | collective-permute-start | bytes 1277960 | tf_op jit(solution)/shard_map/ppermute | solution.py:337
  14.4 1.6 %collective-permute-start.4 = (f32[256,128]{1,0:T(8,128)}, f32[256,128]{1,0:T(8,128)S(1)}, u32[]{:S(2)}, u32[]{:S(2)}) collective-permute-start(f32[256,128]{1,0:T(8,128)} %get-tuple-element.37), channel_id=1, source_target_pairs={{0,1},{1,0},{2,3},{3,2},{4,5},{5,4},{6,7},{7,6},{8,9},{9,8},{10,11... | collective-permute-start | bytes 393224 | tf_op jit(solution)/shard_map/ppermute | solution.py:378
  16.1 19.6 %collective-permute-start = (f32[64,1664]{1,0:T(8,128)S(1)}, f32[64,1664]{1,0:T(8,128)S(1)}, u32[]{:S(2)}, u32[]{:S(2)}) collective-permute-start(f32[64,1664]{1,0:T(8,128)S(1)} %select_maximum_fusion), channel_id=1, source_target_pairs={{0,6},{1,7},{6,0},{7,1},{2,2},{3,3},{4,4},{5,5},{8,14},{9,15},{14,... | collective-permute-start | bytes 1277960 | tf_op jit(solution)/shard_map/ppermute | solution.py:337
  24.2 40.3 %collective-permute-start.7 = (f32[64,1664]{1,0:T(8,128)S(1)}, f32[64,1664]{1,0:T(8,128)S(1)}, u32[]{:S(2)}, u32[]{:S(2)}) collective-permute-start(f32[64,1664]{1,0:T(8,128)S(1)} %collective-permute-done.6.refs_1_.refs_2_), channel_id=1, source_target_pairs={{2,4},{3,5},{4,2},{5,3},{10,12},{11,13},{12,10},{13,11},{18,20},{1... | collective-permute-start | bytes 1277960 | tf_op jit(solution)/shard_map/ppermute | solution.py:337
  24.9 39.6 %collective-permute-start.8 = (f32[64,1664]{1,0:T(8,128)S(1)}, f32[64,1664]{1,0:T(8,128)S(1)}, u32[]{:S(2)}, u32[]{:S(2)}) collective-permute-start(f32[64,1664]{1,0:T(8,128)S(1)} %collective-permute-done.5.refs_1_.refs_2_), channel_id=1, source_target_pairs={{2,0},{3,1},{4,6},{5,7},{10,8},{11,9},{12,14},{13,15},{18,16},{19,... | collective-permute-start | bytes 1277960 | tf_op jit(solution)/shard_map/ppermute | solution.py:337
  39.7 24.8 %collective-permute-start.9 = (f32[768,128]{1,0:T(8,128)S(1)}, f32[768,128]{1,0:T(8,128)S(1)}, u32[]{:S(2)}, u32[]{:S(2)}) collective-permute-start(f32[768,128]{1,0:T(8,128)S(1)} %pairs.8), channel_id=1, source_target_pairs={{0,2},{1,3},{6,4},{7,5},{8,10},{9,11},{14,12},{15,13},{16,18},{17,... | collective-permute-start | bytes 1179656 | tf_op jit(solution)/shard_map/ppermute | solution.py:337
  58.2 18.2 %collective-permute-start.10 = (f32[768,128]{1,0:T(8,128)S(1)}, f32[768,128]{1,0:T(8,128)S(1)}, u32[]{:S(2)}, u32[]{:S(2)}) collective-permute-start(f32[768,128]{1,0:T(8,128)S(1)} %pairs.10), channel_id=1, source_target_pairs={{0,2},{1,3},{6,4},{7,5},{8,10},{9,11},{14,12},{15,13},{16,18},{17,... | collective-permute-start | bytes 1179656 | tf_op jit(solution)/shard_map/ppermute | solution.py:337
  59.5 26.4 %collective-permute-start.15 = (f32[768,128]{1,0:T(8,128)S(1)}, f32[768,128]{1,0:T(8,128)S(1)}, u32[]{:S(2)}, u32[]{:S(2)}) collective-permute-start(f32[768,128]{1,0:T(8,128)S(1)} %pairs.9), channel_id=1, source_target_pairs={{2,4},{3,5},{4,2},{5,3},{0,0},{1,1},{6,6},{7,7},{10,12},{11,13},{1... | collective-permute-start | bytes 1179656 | tf_op jit(solution)/shard_map/ppermute | solution.py:337
  68.7 21.5 %collective-permute-start.13 = (f32[768,128]{1,0:T(8,128)S(1)}, f32[768,128]{1,0:T(8,128)S(1)}, u32[]{:S(2)}, u32[]{:S(2)}) collective-permute-start(f32[768,128]{1,0:T(8,128)S(1)} %pairs.12), channel_id=1, source_target_pairs={{0,4},{1,5},{4,0},{5,1},{2,6},{3,7},{6,2},{7,3},{8,12},{9,13},{12,... | collective-permute-start | bytes 1179656 | tf_op jit(solution)/shard_map/ppermute | solution.py:337
  74.9 19.6 %collective-permute-start.14 = (f32[768,128]{1,0:T(8,128)S(1)}, f32[768,128]{1,0:T(8,128)S(1)}, u32[]{:S(2)}, u32[]{:S(2)}) collective-permute-start(f32[768,128]{1,0:T(8,128)S(1)} %pairs.13), channel_id=1, source_target_pairs={{0,2},{1,3},{2,0},{3,1},{4,6},{5,7},{6,4},{7,5},{8,10},{9,11},{10,... | collective-permute-start | bytes 1179656 | tf_op jit(solution)/shard_map/ppermute | solution.py:337
  84.6 17.8 %collective-permute-start.12 = (f32[768,128]{1,0:T(8,128)S(1)}, f32[768,128]{1,0:T(8,128)S(1)}, u32[]{:S(2)}, u32[]{:S(2)}) collective-permute-start(f32[768,128]{1,0:T(8,128)S(1)} %pairs.15), channel_id=1, source_target_pairs={{0,2},{1,3},{2,0},{3,1},{4,6},{5,7},{6,4},{7,5},{8,10},{9,11},{10,... | collective-permute-start | bytes 1179656 | tf_op jit(solution)/shard_map/ppermute | solution.py:337
  85.3 19.6 %collective-permute-start.16 = (f32[768,128]{1,0:T(8,128)S(1)}, f32[768,128]{1,0:T(8,128)S(1)}, u32[]{:S(2)}, u32[]{:S(2)}) collective-permute-start(f32[768,128]{1,0:T(8,128)S(1)} %pairs.11), channel_id=1, source_target_pairs={{2,4},{3,5},{4,2},{5,3},{0,0},{1,1},{6,6},{7,7},{10,12},{11,13},{1... | collective-permute-start | bytes 1179656 | tf_op jit(solution)/shard_map/ppermute | solution.py:337
  86.0 27.5 %collective-permute-start.11 = (f32[768,128]{1,0:T(8,128)S(1)}, f32[768,128]{1,0:T(8,128)S(1)}, u32[]{:S(2)}, u32[]{:S(2)}) collective-permute-start(f32[768,128]{1,0:T(8,128)S(1)} %pairs.14), channel_id=1, source_target_pairs={{0,4},{1,5},{4,0},{5,1},{2,6},{3,7},{6,2},{7,3},{8,12},{9,13},{12,... | collective-permute-start | bytes 1179656 | tf_op jit(solution)/shard_map/ppermute | solution.py:337
  94.6 22.0 %collective-permute-start.20 = (f32[768,128]{1,0:T(8,128)S(1)}, f32[768,128]{1,0:T(8,128)S(1)}, u32[]{:S(2)}, u32[]{:S(2)}) collective-permute-start(f32[768,128]{1,0:T(8,128)S(1)} %multiply_add_fusion.1.refs_1_), channel_id=1, source_target_pairs={{0,8},{8,0},{16,24},{24,16},{1,9},{9,1},{17,25},{25,17},{2,10},{10... | collective-permute-start | bytes 1179656 | tf_op jit(solution)/shard_map/ppermute | solution.py:444
  96.2 20.9 %collective-permute-start.21 = (f32[768,128]{1,0:T(8,128)S(1)}, f32[768,128]{1,0:T(8,128)S(1)}, u32[]{:S(2)}, u32[]{:S(2)}) collective-permute-start(f32[768,128]{1,0:T(8,128)S(1)} %multiply_add_fusion.1.refs_1_), channel_id=1, source_target_pairs={{0,16},{8,24},{16,0},{24,8},{1,17},{9,25},{17,1},{25,9},{2,18},{10... | collective-permute-start | bytes 1179656 | tf_op jit(solution)/shard_map/ppermute | solution.py:444
  102.4 14.7 %collective-permute-start.22 = (f32[768,128]{1,0:T(8,128)S(1)}, f32[768,128]{1,0:T(8,128)S(1)}, u32[]{:S(2)}, u32[]{:S(2)}) collective-permute-start(f32[768,128]{1,0:T(8,128)S(1)} %multiply_add_fusion.1.refs_1_), channel_id=1, source_target_pairs={{0,24},{8,16},{16,8},{24,0},{1,25},{9,17},{17,9},{25,1},{2,26},{10... | collective-permute-start | bytes 1179656 | tf_op jit(solution)/shard_map/ppermute | solution.py:444
  113.5 11.9 %collective-permute-start.17 = (f32[768,128]{1,0:T(8,128)S(1)}, f32[768,128]{1,0:T(8,128)S(1)}, u32[]{:S(2)}, u32[]{:S(2)}) collective-permute-start(f32[768,128]{1,0:T(8,128)S(1)} %multiply_add_fusion.refs_1_), channel_id=1, source_target_pairs={{0,8},{8,0},{16,24},{24,16},{1,9},{9,1},{17,25},{25,17},{2,10},{10... | collective-permute-start | bytes 1179656 | tf_op jit(solution)/shard_map/ppermute | solution.py:444
  115.1 15.8 %collective-permute-start.18 = (f32[768,128]{1,0:T(8,128)S(1)}, f32[768,128]{1,0:T(8,128)S(1)}, u32[]{:S(2)}, u32[]{:S(2)}) collective-permute-start(f32[768,128]{1,0:T(8,128)S(1)} %multiply_add_fusion.refs_1_), channel_id=1, source_target_pairs={{0,16},{8,24},{16,0},{24,8},{1,17},{9,25},{17,1},{25,9},{2,18},{10... | collective-permute-start | bytes 1179656 | tf_op jit(solution)/shard_map/ppermute | solution.py:444
  116.6 14.3 %collective-permute-start.19 = (f32[768,128]{1,0:T(8,128)S(1)}, f32[768,128]{1,0:T(8,128)S(1)}, u32[]{:S(2)}, u32[]{:S(2)}) collective-permute-start(f32[768,128]{1,0:T(8,128)S(1)} %multiply_add_fusion.refs_1_), channel_id=1, source_target_pairs={{0,24},{8,16},{16,8},{24,0},{1,25},{9,17},{17,9},{25,1},{2,26},{10... | collective-permute-start | bytes 1179656 | tf_op jit(solution)/shard_map/ppermute | solution.py:444

commit v8 on v7

--- a/solution.py
+++ b/solution.py
@@ -9,7 +9,7 @@
 from jax.sharding import PartitionSpec as P
 
 
-ROUNDS = ("a0", "d0", "a1", "d1", "b0", "c0", "b1", "c1")
+ROUNDS = ("a0", "a1", "b0", "c0", "b1", "d0", "c1", "d1")
 
 F32 = jnp.float32
 BF16 = jnp.bfloat16
@@ -390,7 +390,7 @@
         middle = [(1, 2), (2, 1), (0, 0), (3, 3)]
         inward = [(0, 1), (3, 2)]
         outward = [(1, 0), (2, 3)]
-        across = [(0, 2), (2, 0), (1, 3), (3, 1)]
+        onward = [(0, 1), (3, 2), (1, 3), (2, 0)]
         cross = [(1, 2), (2, 1)]
 
         of_a = shift(parcel, ends)
@@ -415,17 +415,19 @@
             elif label[0] == "b":
                 arrived = shift(rounds[f"a{k}"], inward)
                 rounds[label] = work(of_b, arrived, k)
+            elif label[0] == "c":
+                rounds[label] = work((of_c,), None, k)
             else:
-                rounds[label] = work((of_c if label[0] == "c" else of_d,), None, k)
+                arrived = shift(rounds[f"b{k}"], onward)
+                rounds[label] = work((of_d,), arrived, k)
         done = []
         for k in range(len(chunks)):
-            from_b = shift(rounds[f"b{k}"], across)
             from_c = shift(rounds[f"c{k}"], sides)
             from_d = shift(rounds[f"d{k}"], middle)
             if done:
                 from_c, _ = lax.optimization_barrier((from_c, done[-1]))
             own = rounds[f"a{k}"] * inner
-            done.append(from_b + from_c + from_d + own)
+            done.append(from_c + from_d + own)
     else:
         sources = make_sources()
         total = None

time: 133 us -> 136 us (1.023); the launches traced: 133 us -> 134 us
  starting transfers between devices: 41.9 us -> 43.5 us
    ppermute x13, waiting for transfers between devices: 26.7 us -> 15.1 us  [shift(): return lax.ppermute(array, 'dev', along(moves))]
    ppermute x6, waiting for transfers between devices: 12.1 us -> 23.2 us  [on_device(): lax.ppermute(piece, 'grp', [(g, g ^ m) for g in range(groups)])]
    ppermute x13, starting transfers between devices: 31.5 us -> 33.1 us  [shift(): return lax.ppermute(array, 'dev', along(moves))]
  transfers between devices with their start and end apart: 23 -> 23, of which waited for: 8 -> 9; matrix products, arithmetic and copies ran while one was open for 2% -> 2% of each run, Pallas kernels for 35% -> 35%
where the time goes in v8:
time: 136 us; the launch traced here: 134 us
  Pallas kernels  48.1 us (35%)
  starting transfers between devices  43.5 us (32%)
  waiting for transfers between devices  39.7 us (29%)
  local copies, waits for them, and re-layouts  1.89 us (1%)
    ppermute x13, starting transfers between devices, shift(): return lax.ppermute(array, 'dev', along(moves))  33.1 us
    pallas_call x8, Pallas kernels, pairs(): pl.pallas_call(functools.partial(pair_kernel, plan), grid=(count // group...  32.7 us
    ppermute x6, waiting for transfers between devices, on_device(): lax.ppermute(piece, 'grp', [(g, g ^ m) for g in range(groups)])  23.2 us
    ppermute x13, waiting for transfers between devices, shift(): return lax.ppermute(array, 'dev', along(moves))  15.1 us
    pallas_call x2, Pallas kernels, prepared(): pl.pallas_call(functools.partial(body, scale), grid=(count // block,), in...  12 us
    ppermute x6, starting transfers between devices, on_device(): lax.ppermute(piece, 'grp', [(g, g ^ m) for g in range(groups)])  9.1 us
    pallas_call x2, Pallas kernels, spread(): pl.pallas_call(functools.partial(spread_kernel, groups, per, first, unit,...  3.42 us
  transfers between devices with their start and end apart: 23, of which 9 were waited for; matrix products, arithmetic and copies ran while one was open for 2% of the time, Pallas kernels for 35%

profile of v8, /device:TPU:0, one launch (start us, length us, event | category | flops | bytes accessed | tf_op | source)
XLA Modules:
  0.0 133.9 jit_solution(1359657102930723875)
XLA Ops:
  0.0 0.5 collective-permute-start.2
  0.5 0.0 collective-permute-start.1
  0.5 0.8 copy.8
  1.3 0.1 reshape.5
  1.4 0.1 pad_add_fusion.refs_0_
  1.5 1.0 constant_dynamic-slice_fusion
  2.6 8.1 %prepared.2 = (bf16[12,256,512]{2,1,0:T(8,128)(2,1)S(1)}, bf16[12,512,256]{2,1,0:T(8,128)(2,1)S(1)}, bf16[256,256]{1,0:T(8,128)(2,1)S(1)}, bf16[256,256]{1,0:T(8...) custom-call(s32[1,256]{1,0:T(1,128)} %idx_ref.1, f32[64,6144]{1,0:T(8,128)} %points_ref.1, ...), custom_call_target="tpu_custom_call" | custom-call | flops 1610612736 | bytes 20447232 | tf_op jit(solution)/shard_map/prepared/pallas_call | solution.py:268
  10.7 0.5 collective-permute-start.3
  11.2 2.6 %collective-permute-start.5 = (f32[64,1664]{1,0:T(8,128)S(1)}, f32[64,1664]{1,0:T(8,128)S(1)}, u32[]{:S(2)}, u32[]{:S(2)}) collective-permute-start(f32[64,1664]{1,0:T(8,128)S(1)} %select_maximum_fusion), channel_id=1, source_target_pairs={{0,2},{1,3},{2,0},{3,1},{4,6},{5,7},{6,4},{7,5},{8,10},{9,11},{10,... | collective-permute-start | bytes 1277960 | tf_op jit(solution)/shard_map/ppermute | solution.py:337
  13.8 0.7 collective-permute-start.7
  14.4 0.0 collective-permute-done.3.coords_ref
  14.4 0.3 collective-permute-start.4
  14.7 1.3 collective-permute-done.4.summed_ref
  16.1 4.6 %collective-permute-start = (f32[64,1664]{1,0:T(8,128)S(1)}, f32[64,1664]{1,0:T(8,128)S(1)}, u32[]{:S(2)}, u32[]{:S(2)}) collective-permute-start(f32[64,1664]{1,0:T(8,128)S(1)} %select_maximum_fusion), channel_id=1, source_target_pairs={{0,6},{1,7},{6,0},{7,1},{2,2},{3,3},{4,4},{5,5},{8,14},{9,15},{14,... | collective-permute-start | bytes 1277960 | tf_op jit(solution)/shard_map/ppermute | solution.py:337
  20.7 3.5 %collective-permute-done.5.refs_1_.refs_2_ = f32[64,1664]{1,0:T(8,128)S(1)} collective-permute-done((f32[64,1664]{1,0:T(8,128)S(1)}, f32[64,1664]{1,0:T(8,128)S(1)}, u32[]{:S(2)}, u32[]{:S(2)}) %collective-permute-start.5) | collective-permute-done | bytes 426016 | tf_op jit(solution)/shard_map/ppermute | solution.py:337
  24.2 0.7 collective-permute-start.6
  24.9 0.0 collective-permute-done.7.refs_1_.refs_2_
  24.9 1.3 collective-permute-start.8
  26.2 0.0 collective-permute-done.1.points_ref
  26.2 0.0 collective-permute-done.2.weights_ref
  26.3 3.9 %prepared.3 = (bf16[12,256,512]{2,1,0:T(8,128)(2,1)S(1)}, bf16[12,512,256]{2,1,0:T(8,128)(2,1)S(1)}, bf16[256,256]{1,0:T(8,128)(2,1)S(1)}, bf16[256,256]{1,0:T(8,128)(2,1)S(1)}) custom-call(f32[64,6144]{1,0:T(8,128)S(1)} %collective-permute-done.1.points_ref, f32[6144,128]{1,0:T(8,128)} %collective-permute-done.2.weights_ref, ...), custom_call_target="tpu_custom_call" | custom-call | flops 1610612736 | bytes 14155776 | tf_op jit(solution)/shard_map/prepared/pallas_call | solution.py:268
  30.2 5.5 %collective-permute-done.refs_1_.refs_2_ = f32[64,1664]{1,0:T(8,128)S(1)} collective-permute-done((f32[64,1664]{1,0:T(8,128)S(1)}, f32[64,1664]{1,0:T(8,128)S(1)}, u32[]{:S(2)}, u32[]{:S(2)}) %collective-permute-start) | collective-permute-done | bytes 426016 | tf_op jit(solution)/shard_map/ppermute | solution.py:337
  35.7 4.1 %pairs.8 = f32[768,128]{1,0:T(8,128)S(1)} custom-call(s32[3]{0:T(128)S(1)} %pad_add_fusion.refs_0_, f32[64,1664]{1,0:T(8,128)S(1)} %collective-permute-done.refs_1_.refs_2_, f32[64,1664]{1,0:T(8,128)S(1)} %collective-permute-done.refs_1_.refs_2_, bf16[12,256,512]{2,1,0:T(8,128)(2,1)S(1)} %get-tuple-element.32.refs_3_.refs_6_.refs_4_, ...), custom_call_target="tpu_custom_call" | custom-call | flops 3019898880 | bytes 2359296 | tf_op jit(solution)/shard_map/pairs/pallas_call | solution.py:153
  39.7 10.1 %collective-permute-start.9 = (f32[768,128]{1,0:T(8,128)S(1)}, f32[768,128]{1,0:T(8,128)S(1)}, u32[]{:S(2)}, u32[]{:S(2)}) collective-permute-start(f32[768,128]{1,0:T(8,128)S(1)} %pairs.8), channel_id=1, source_target_pairs={{0,2},{1,3},{6,4},{7,5},{8,10},{9,11},{14,12},{15,13},{16,18},{17,... | collective-permute-start | bytes 1179656 | tf_op jit(solution)/shard_map/ppermute | solution.py:337
  49.9 4.1 %pairs.9 = f32[768,128]{1,0:T(8,128)S(1)} custom-call(s32[3]{0:T(128)S(1)} %pad_add_fusion.refs_0_, f32[64,1664]{1,0:T(8,128)S(1)} %collective-permute-done.refs_1_.refs_2_, f32[64,1664]{1,0:T(8,128)S(1)} %collective-permute-done.refs_1_.refs_2_, bf16[12,256,512]{2,1,0:T(8,128)(2,1)S(1)} %get-tuple-element.32.refs_3_.refs_6_.refs_4_, ...), custom_call_target="tpu_custom_call" | custom-call | flops 3019898880 | bytes 2359296 | tf_op jit(solution)/shard_map/pairs/pallas_call | solution.py:153
  54.0 1.5 %collective-permute-start.10 = (f32[768,128]{1,0:T(8,128)S(1)}, f32[768,128]{1,0:T(8,128)S(1)}, u32[]{:S(2)}, u32[]{:S(2)}) collective-permute-start(f32[768,128]{1,0:T(8,128)S(1)} %pairs.9), channel_id=1, source_target_pairs={{0,2},{1,3},{6,4},{7,5},{8,10},{9,11},{14,12},{15,13},{16,18},{17,... | collective-permute-start | bytes 1179656 | tf_op jit(solution)/shard_map/ppermute | solution.py:337
  55.5 0.0 collective-permute-done.6.refs_1_.refs_3_
  55.5 0.0 collective-permute-done.8.refs_2_.refs_4_
  55.5 3.8 %collective-permute-done.9.refs_5_ = f32[768,128]{1,0:T(8,128)S(1)} collective-permute-done((f32[768,128]{1,0:T(8,128)S(1)}, f32[768,128]{1,0:T(8,128)S(1)}, u32[]{:S(2)}, u32[]{:S(2)}) %collective-permute-start.9) | collective-permute-done | bytes 393248 | tf_op jit(solution)/shard_map/ppermute | solution.py:337
  59.3 4.1 %pairs.10 = f32[768,128]{1,0:T(8,128)S(1)} custom-call(s32[3]{0:T(128)S(1)} %pad_add_fusion.refs_0_, f32[64,1664]{1,0:T(8,128)S(1)} %collective-permute-done.6.refs_1_.refs_3_, f32[64,1664]{1,0:T(8,128)S(1)} %collective-permute-done.8.refs_2_.refs_4_, f32[64,1664]{1,0:T(8,128)S(1)} %collective-permute-done.6.refs_1_.refs_3_, ...), custom_call_target="tpu_custom_call" | custom-call | flops 3019898880 | bytes 2359296 | tf_op jit(solution)/shard_map/pairs/pallas_call | solution.py:153
  63.5 2.5 %collective-permute-start.11 = (f32[768,128]{1,0:T(8,128)S(1)}, f32[768,128]{1,0:T(8,128)S(1)}, u32[]{:S(2)}, u32[]{:S(2)}) collective-permute-start(f32[768,128]{1,0:T(8,128)S(1)} %pairs.10), channel_id=1, source_target_pairs={{0,2},{1,3},{6,4},{7,5},{2,6},{3,7},{4,0},{5,1},{8,10},{9,11},{14,... | collective-permute-start | bytes 1179656 | tf_op jit(solution)/shard_map/ppermute | solution.py:337
  66.0 4.1 %pairs.11 = f32[768,128]{1,0:T(8,128)S(1)} custom-call(s32[3]{0:T(128)S(1)} %pad_add_fusion.refs_0_, f32[64,1664]{1,0:T(8,128)S(1)} %collective-permute-done.5.refs_1_.refs_2_, f32[64,1664]{1,0:T(8,128)S(1)} %collective-permute-done.5.refs_1_.refs_2_, bf16[12,256,512]{2,1,0:T(8,128)(2,1)S(1)} %get-tuple-element.32.refs_3_.refs_6_.refs_4_, ...), custom_call_target="tpu_custom_call" | custom-call | flops 3019898880 | bytes 2359296 | tf_op jit(solution)/shard_map/pairs/pallas_call | solution.py:153
  70.1 1.1 collective-permute-start.13
  71.1 0.0 collective-permute-done.10.refs_5_
  71.1 4.1 %pairs.12 = f32[768,128]{1,0:T(8,128)S(1)} custom-call(s32[3]{0:T(128)S(1)} %pad_add_fusion.refs_0_, f32[64,1664]{1,0:T(8,128)S(1)} %collective-permute-done.6.refs_1_.refs_3_, f32[64,1664]{1,0:T(8,128)S(1)} %collective-permute-done.8.refs_2_.refs_4_, f32[64,1664]{1,0:T(8,128)S(1)} %collective-permute-done.6.refs_1_.refs_3_, ...), custom_call_target="tpu_custom_call" | custom-call | flops 3019898880 | bytes 2359296 | tf_op jit(solution)/shard_map/pairs/pallas_call | solution.py:153
  75.3 1.3 collective-permute-start.15
  76.6 0.0 collective-permute-done.11.refs_3_
  76.6 4.1 %pairs.13 = f32[768,128]{1,0:T(8,128)S(1)} custom-call(s32[3]{0:T(128)S(1)} %pad_add_fusion.refs_0_, f32[64,1664]{1,0:T(8,128)S(1)} %collective-permute-done.7.refs_1_.refs_2_, f32[64,1664]{1,0:T(8,128)S(1)} %collective-permute-done.7.refs_1_.refs_2_, f32[768,128]{1,0:T(8,128)S(1)} %collective-permute-done.11.refs_3_, ...), custom_call_target="tpu_custom_call" | custom-call | flops 3019898880 | bytes 2359296 | tf_op jit(solution)/shard_map/pairs/pallas_call | solution.py:153
  80.7 0.7 collective-permute-start.14
  81.4 4.1 %pairs.14 = f32[768,128]{1,0:T(8,128)S(1)} custom-call(s32[3]{0:T(128)S(1)} %pad_add_fusion.refs_0_, f32[64,1664]{1,0:T(8,128)S(1)} %collective-permute-done.5.refs_1_.refs_2_, f32[64,1664]{1,0:T(8,128)S(1)} %collective-permute-done.5.refs_1_.refs_2_, bf16[12,256,512]{2,1,0:T(8,128)(2,1)S(1)} %get-tuple-element.32.refs_3_.refs_6_.refs_4_, ...), custom_call_target="tpu_custom_call" | custom-call | flops 3019898880 | bytes 2359296 | tf_op jit(solution)/shard_map/pairs/pallas_call | solution.py:153
  85.4 5.4 %collective-permute-start.12 = (f32[768,128]{1,0:T(8,128)S(1)}, f32[768,128]{1,0:T(8,128)S(1)}, u32[]{:S(2)}, u32[]{:S(2)}) collective-permute-start(f32[768,128]{1,0:T(8,128)S(1)} %pairs.14), channel_id=1, source_target_pairs={{0,2},{1,3},{2,0},{3,1},{4,6},{5,7},{6,4},{7,5},{8,10},{9,11},{10,... | collective-permute-start | bytes 1179656 | tf_op jit(solution)/shard_map/ppermute | solution.py:337
  90.8 2.2 %collective-permute-done.15.refs_3_ = f32[768,128]{1,0:T(8,128)S(1)} collective-permute-done((f32[768,128]{1,0:T(8,128)S(1)}, f32[768,128]{1,0:T(8,128)S(1)}, u32[]{:S(2)}, u32[]{:S(2)}) %collective-permute-start.15) | collective-permute-done | bytes 393248 | tf_op jit(solution)/shard_map/ppermute | solution.py:337
  93.0 4.1 %pairs.15 = f32[768,128]{1,0:T(8,128)S(1)} custom-call(s32[3]{0:T(128)S(1)} %pad_add_fusion.refs_0_, f32[64,1664]{1,0:T(8,128)S(1)} %collective-permute-done.7.refs_1_.refs_2_, f32[64,1664]{1,0:T(8,128)S(1)} %collective-permute-done.7.refs_1_.refs_2_, f32[768,128]{1,0:T(8,128)S(1)} %collective-permute-done.15.refs_3_, ...), custom_call_target="tpu_custom_call" | custom-call | flops 3019898880 | bytes 2359296 | tf_op jit(solution)/shard_map/pairs/pallas_call | solution.py:153
  97.1 0.7 collective-permute-start.16
  97.8 0.0 collective-permute-done.13
  97.8 0.0 collective-permute-done.14
  97.8 0.1 multiply_add_fusion.1.refs_1_
  97.9 1.6 %collective-permute-start.20 = (f32[768,128]{1,0:T(8,128)S(1)}, f32[768,128]{1,0:T(8,128)S(1)}, u32[]{:S(2)}, u32[]{:S(2)}) collective-permute-start(f32[768,128]{1,0:T(8,128)S(1)} %multiply_add_fusion.1.refs_1_), channel_id=1, source_target_pairs={{0,8},{8,0},{16,24},{24,16},{1,9},{9,1},{17,25},{25,17},{2,10},{10... | collective-permute-start | bytes 1179656 | tf_op jit(solution)/shard_map/ppermute | solution.py:446
  99.4 1.5 %collective-permute-start.21 = (f32[768,128]{1,0:T(8,128)S(1)}, f32[768,128]{1,0:T(8,128)S(1)}, u32[]{:S(2)}, u32[]{:S(2)}) collective-permute-start(f32[768,128]{1,0:T(8,128)S(1)} %multiply_add_fusion.1.refs_1_), channel_id=1, source_target_pairs={{0,16},{8,24},{16,0},{24,8},{1,17},{9,25},{17,1},{25,9},{2,18},{10... | collective-permute-start | bytes 1179656 | tf_op jit(solution)/shard_map/ppermute | solution.py:446
  101.0 0.5 collective-permute-start.22
  101.4 0.0 collective-permute-done.12
  101.4 0.0 collective-permute-done.16
  101.5 0.1 multiply_add_fusion.refs_1_
  101.5 1.6 %collective-permute-start.17 = (f32[768,128]{1,0:T(8,128)S(1)}, f32[768,128]{1,0:T(8,128)S(1)}, u32[]{:S(2)}, u32[]{:S(2)}) collective-permute-start(f32[768,128]{1,0:T(8,128)S(1)} %multiply_add_fusion.refs_1_), channel_id=1, source_target_pairs={{0,8},{8,0},{16,24},{24,16},{1,9},{9,1},{17,25},{25,17},{2,10},{10... | collective-permute-start | bytes 1179656 | tf_op jit(solution)/shard_map/ppermute | solution.py:446
  103.1 1.5 %collective-permute-start.18 = (f32[768,128]{1,0:T(8,128)S(1)}, f32[768,128]{1,0:T(8,128)S(1)}, u32[]{:S(2)}, u32[]{:S(2)}) collective-permute-start(f32[768,128]{1,0:T(8,128)S(1)} %multiply_add_fusion.refs_1_), channel_id=1, source_target_pairs={{0,16},{8,24},{16,0},{24,8},{1,17},{9,25},{17,1},{25,9},{2,18},{10... | collective-permute-start | bytes 1179656 | tf_op jit(solution)/shard_map/ppermute | solution.py:446
  104.6 5.3 %collective-permute-done.20.refs_2_ = f32[768,128]{1,0:T(8,128)S(1)} collective-permute-done((f32[768,128]{1,0:T(8,128)S(1)}, f32[768,128]{1,0:T(8,128)S(1)}, u32[]{:S(2)}, u32[]{:S(2)}) %collective-permute-start.20) | collective-permute-done | bytes 393248 | tf_op jit(solution)/shard_map/ppermute | solution.py:446
  109.9 2.5 %collective-permute-start.19 = (f32[768,128]{1,0:T(8,128)S(1)}, f32[768,128]{1,0:T(8,128)S(1)}, u32[]{:S(2)}, u32[]{:S(2)}) collective-permute-start(f32[768,128]{1,0:T(8,128)S(1)} %multiply_add_fusion.refs_1_), channel_id=1, source_target_pairs={{0,24},{8,16},{16,8},{24,0},{1,25},{9,17},{17,9},{25,1},{2,26},{10... | collective-permute-start | bytes 1179656 | tf_op jit(solution)/shard_map/ppermute | solution.py:446
  112.4 7.4 %collective-permute-done.21.refs_3_ = f32[768,128]{1,0:T(8,128)S(1)} collective-permute-done((f32[768,128]{1,0:T(8,128)S(1)}, f32[768,128]{1,0:T(8,128)S(1)}, u32[]{:S(2)}, u32[]{:S(2)}) %collective-permute-start.21) | collective-permute-done | bytes 393248 | tf_op jit(solution)/shard_map/ppermute | solution.py:446
  119.8 0.0 collective-permute-done.22.refs_4_
  119.8 1.7 %spread.2.refs_5_ = f32[6144,128]{1,0:T(8,128)} custom-call(s32[4]{0:T(128)S(1)} %iota_xor_fusion.refs_0_, f32[768,128]{1,0:T(8,128)S(1)} %multiply_add_fusion.1.refs_1_, f32[768,128]{1,0:T(8,128)S(1)} %collective-permute-done.20.refs_2_, f32[768,128]{1,0:T(8,128)S(1)} %collective-permute-done.21.refs_3_, f32[768,128]{1,0:T(8,128)S(1)} %collective-permute-done.22.refs_4_), custom_call_target="tpu_custom_call" | custom-call | tf_op jit(solution)/shard_map/spread/pallas_call | solution.py:303
  121.6 5.0 %collective-permute-done.17.refs_2_ = f32[768,128]{1,0:T(8,128)S(1)} collective-permute-done((f32[768,128]{1,0:T(8,128)S(1)}, f32[768,128]{1,0:T(8,128)S(1)}, u32[]{:S(2)}, u32[]{:S(2)}) %collective-permute-start.17) | collective-permute-done | bytes 393248 | tf_op jit(solution)/shard_map/ppermute | solution.py:446
  126.6 5.4 %collective-permute-done.18.refs_3_ = f32[768,128]{1,0:T(8,128)S(1)} collective-permute-done((f32[768,128]{1,0:T(8,128)S(1)}, f32[768,128]{1,0:T(8,128)S(1)}, u32[]{:S(2)}, u32[]{:S(2)}) %collective-permute-start.18) | collective-permute-done | bytes 393248 | tf_op jit(solution)/shard_map/ppermute | solution.py:446
  132.0 0.0 collective-permute-done.19.refs_4_
  132.0 1.7 %spread.3 = f32[6144,128]{1,0:T(8,128)} custom-call(s32[4]{0:T(128)S(1)} %iota_xor_fusion.refs_0_, f32[768,128]{1,0:T(8,128)S(1)} %multiply_add_fusion.refs_1_, f32[768,128]{1,0:T(8,128)S(1)} %collective-permute-done.17.refs_2_, f32[768,128]{1,0:T(8,128)S(1)} %collective-permute-done.18.refs_3_, ...), custom_call_target="tpu_custom_call", output_to_operand_aliasing={{}: (5, {})} | custom-call | tf_op jit(solution)/shard_map/spread/pallas_call | solution.py:303
  (4 shorter events, 0.0 us)
Async XLA Ops:
  0.0 26.2 %collective-permute-start.2 = (f32[6144,128]{1,0:T(8,128)}, f32[6144,128]{1,0:T(8,128)}, u32[]{:S(2)}, u32[]{:S(2)}) collective-permute-start(f32[6144,128]{1,0:T(8,128)} %weights_ref.1), channel_id=1, source_target_pairs={{0,1},{1,0},{2,3},{3,2},{4,5},{5,4},{6,7},{7,6},{8,9},{9,8},{10,11... | collective-permute-start | bytes 9437192 | tf_op jit(solution)/shard_map/ppermute | solution.py:378
  0.5 25.7 %collective-permute-start.1 = (f32[64,6144]{1,0:T(8,128)}, f32[64,6144]{1,0:T(8,128)S(1)}, u32[]{:S(2)}, u32[]{:S(2)}) collective-permute-start(f32[64,6144]{1,0:T(8,128)} %points_ref.1), channel_id=1, source_target_pairs={{0,1},{1,0},{2,3},{3,2},{4,5},{5,4},{6,7},{7,6},{8,9},{9,8},{10,11... | collective-permute-start | bytes 4718600 | tf_op jit(solution)/shard_map/ppermute | solution.py:378
  10.7 3.7 %collective-permute-start.3 = (f32[64,256]{1,0:T(8,128)}, f32[64,256]{1,0:T(8,128)S(1)}, u32[]{:S(2)}, u32[]{:S(2)}) collective-permute-start(f32[64,256]{1,0:T(8,128)} %get-tuple-element.36), channel_id=1, source_target_pairs={{0,1},{1,0},{2,3},{3,2},{4,5},{5,4},{6,7},{7,6},{8,9},{9,8},{10,11... | collective-permute-start | bytes 196616 | tf_op jit(solution)/shard_map/ppermute | solution.py:378
  11.2 13.1 %collective-permute-start.5 = (f32[64,1664]{1,0:T(8,128)S(1)}, f32[64,1664]{1,0:T(8,128)S(1)}, u32[]{:S(2)}, u32[]{:S(2)}) collective-permute-start(f32[64,1664]{1,0:T(8,128)S(1)} %select_maximum_fusion), channel_id=1, source_target_pairs={{0,2},{1,3},{2,0},{3,1},{4,6},{5,7},{6,4},{7,5},{8,10},{9,11},{10,... | collective-permute-start | bytes 1277960 | tf_op jit(solution)/shard_map/ppermute | solution.py:337
  13.8 11.2 %collective-permute-start.7 = (f32[64,1664]{1,0:T(8,128)S(1)}, f32[64,1664]{1,0:T(8,128)S(1)}, u32[]{:S(2)}, u32[]{:S(2)}) collective-permute-start(f32[64,1664]{1,0:T(8,128)S(1)} %select_maximum_fusion), channel_id=1, source_target_pairs={{2,4},{3,5},{4,2},{5,3},{0,0},{1,1},{6,6},{7,7},{10,12},{11,13},{1... | collective-permute-start | bytes 1277960 | tf_op jit(solution)/shard_map/ppermute | solution.py:337
  14.4 1.6 %collective-permute-start.4 = (f32[256,128]{1,0:T(8,128)}, f32[256,128]{1,0:T(8,128)S(1)}, u32[]{:S(2)}, u32[]{:S(2)}) collective-permute-start(f32[256,128]{1,0:T(8,128)} %get-tuple-element.37), channel_id=1, source_target_pairs={{0,1},{1,0},{2,3},{3,2},{4,5},{5,4},{6,7},{7,6},{8,9},{9,8},{10,11... | collective-permute-start | bytes 393224 | tf_op jit(solution)/shard_map/ppermute | solution.py:378
  16.1 19.6 %collective-permute-start = (f32[64,1664]{1,0:T(8,128)S(1)}, f32[64,1664]{1,0:T(8,128)S(1)}, u32[]{:S(2)}, u32[]{:S(2)}) collective-permute-start(f32[64,1664]{1,0:T(8,128)S(1)} %select_maximum_fusion), channel_id=1, source_target_pairs={{0,6},{1,7},{6,0},{7,1},{2,2},{3,3},{4,4},{5,5},{8,14},{9,15},{14,... | collective-permute-start | bytes 1277960 | tf_op jit(solution)/shard_map/ppermute | solution.py:337
  24.2 31.2 %collective-permute-start.6 = (f32[64,1664]{1,0:T(8,128)S(1)}, f32[64,1664]{1,0:T(8,128)S(1)}, u32[]{:S(2)}, u32[]{:S(2)}) collective-permute-start(f32[64,1664]{1,0:T(8,128)S(1)} %collective-permute-done.5.refs_1_.refs_2_), channel_id=1, source_target_pairs={{2,4},{3,5},{4,2},{5,3},{10,12},{11,13},{12,10},{13,11},{18,20},{1... | collective-permute-start | bytes 1277960 | tf_op jit(solution)/shard_map/ppermute | solution.py:337
  24.9 30.5 %collective-permute-start.8 = (f32[64,1664]{1,0:T(8,128)S(1)}, f32[64,1664]{1,0:T(8,128)S(1)}, u32[]{:S(2)}, u32[]{:S(2)}) collective-permute-start(f32[64,1664]{1,0:T(8,128)S(1)} %collective-permute-done.7.refs_1_.refs_2_), channel_id=1, source_target_pairs={{2,0},{3,1},{4,6},{5,7},{10,8},{11,9},{12,14},{13,15},{18,16},{19,... | collective-permute-start | bytes 1277960 | tf_op jit(solution)/shard_map/ppermute | solution.py:337
  39.7 19.6 %collective-permute-start.9 = (f32[768,128]{1,0:T(8,128)S(1)}, f32[768,128]{1,0:T(8,128)S(1)}, u32[]{:S(2)}, u32[]{:S(2)}) collective-permute-start(f32[768,128]{1,0:T(8,128)S(1)} %pairs.8), channel_id=1, source_target_pairs={{0,2},{1,3},{6,4},{7,5},{8,10},{9,11},{14,12},{15,13},{16,18},{17,... | collective-permute-start | bytes 1179656 | tf_op jit(solution)/shard_map/ppermute | solution.py:337
  54.0 17.2 %collective-permute-start.10 = (f32[768,128]{1,0:T(8,128)S(1)}, f32[768,128]{1,0:T(8,128)S(1)}, u32[]{:S(2)}, u32[]{:S(2)}) collective-permute-start(f32[768,128]{1,0:T(8,128)S(1)} %pairs.9), channel_id=1, source_target_pairs={{0,2},{1,3},{6,4},{7,5},{8,10},{9,11},{14,12},{15,13},{16,18},{17,... | collective-permute-start | bytes 1179656 | tf_op jit(solution)/shard_map/ppermute | solution.py:337
  63.5 13.1 %collective-permute-start.11 = (f32[768,128]{1,0:T(8,128)S(1)}, f32[768,128]{1,0:T(8,128)S(1)}, u32[]{:S(2)}, u32[]{:S(2)}) collective-permute-start(f32[768,128]{1,0:T(8,128)S(1)} %pairs.10), channel_id=1, source_target_pairs={{0,2},{1,3},{6,4},{7,5},{2,6},{3,7},{4,0},{5,1},{8,10},{9,11},{14,... | collective-permute-start | bytes 1179656 | tf_op jit(solution)/shard_map/ppermute | solution.py:337
  70.1 27.7 %collective-permute-start.13 = (f32[768,128]{1,0:T(8,128)S(1)}, f32[768,128]{1,0:T(8,128)S(1)}, u32[]{:S(2)}, u32[]{:S(2)}) collective-permute-start(f32[768,128]{1,0:T(8,128)S(1)} %pairs.11), channel_id=1, source_target_pairs={{0,2},{1,3},{2,0},{3,1},{4,6},{5,7},{6,4},{7,5},{8,10},{9,11},{10,... | collective-permute-start | bytes 1179656 | tf_op jit(solution)/shard_map/ppermute | solution.py:337
  75.3 17.8 %collective-permute-start.15 = (f32[768,128]{1,0:T(8,128)S(1)}, f32[768,128]{1,0:T(8,128)S(1)}, u32[]{:S(2)}, u32[]{:S(2)}) collective-permute-start(f32[768,128]{1,0:T(8,128)S(1)} %pairs.12), channel_id=1, source_target_pairs={{0,2},{1,3},{6,4},{7,5},{2,6},{3,7},{4,0},{5,1},{8,10},{9,11},{14,... | collective-permute-start | bytes 1179656 | tf_op jit(solution)/shard_map/ppermute | solution.py:337
  80.7 17.2 %collective-permute-start.14 = (f32[768,128]{1,0:T(8,128)S(1)}, f32[768,128]{1,0:T(8,128)S(1)}, u32[]{:S(2)}, u32[]{:S(2)}) collective-permute-start(f32[768,128]{1,0:T(8,128)S(1)} %pairs.13), channel_id=1, source_target_pairs={{2,4},{3,5},{4,2},{5,3},{0,0},{1,1},{6,6},{7,7},{10,12},{11,13},{1... | collective-permute-start | bytes 1179656 | tf_op jit(solution)/shard_map/ppermute | solution.py:337
  85.4 16.0 %collective-permute-start.12 = (f32[768,128]{1,0:T(8,128)S(1)}, f32[768,128]{1,0:T(8,128)S(1)}, u32[]{:S(2)}, u32[]{:S(2)}) collective-permute-start(f32[768,128]{1,0:T(8,128)S(1)} %pairs.14), channel_id=1, source_target_pairs={{0,2},{1,3},{2,0},{3,1},{4,6},{5,7},{6,4},{7,5},{8,10},{9,11},{10,... | collective-permute-start | bytes 1179656 | tf_op jit(solution)/shard_map/ppermute | solution.py:337
  97.1 4.3 %collective-permute-start.16 = (f32[768,128]{1,0:T(8,128)S(1)}, f32[768,128]{1,0:T(8,128)S(1)}, u32[]{:S(2)}, u32[]{:S(2)}) collective-permute-start(f32[768,128]{1,0:T(8,128)S(1)} %pairs.15), channel_id=1, source_target_pairs={{2,4},{3,5},{4,2},{5,3},{0,0},{1,1},{6,6},{7,7},{10,12},{11,13},{1... | collective-permute-start | bytes 1179656 | tf_op jit(solution)/shard_map/ppermute | solution.py:337
  97.9 12.1 %collective-permute-start.20 = (f32[768,128]{1,0:T(8,128)S(1)}, f32[768,128]{1,0:T(8,128)S(1)}, u32[]{:S(2)}, u32[]{:S(2)}) collective-permute-start(f32[768,128]{1,0:T(8,128)S(1)} %multiply_add_fusion.1.refs_1_), channel_id=1, source_target_pairs={{0,8},{8,0},{16,24},{24,16},{1,9},{9,1},{17,25},{25,17},{2,10},{10... | collective-permute-start | bytes 1179656 | tf_op jit(solution)/shard_map/ppermute | solution.py:446
  99.4 20.4 %collective-permute-start.21 = (f32[768,128]{1,0:T(8,128)S(1)}, f32[768,128]{1,0:T(8,128)S(1)}, u32[]{:S(2)}, u32[]{:S(2)}) collective-permute-start(f32[768,128]{1,0:T(8,128)S(1)} %multiply_add_fusion.1.refs_1_), channel_id=1, source_target_pairs={{0,16},{8,24},{16,0},{24,8},{1,17},{9,25},{17,1},{25,9},{2,18},{10... | collective-permute-start | bytes 1179656 | tf_op jit(solution)/shard_map/ppermute | solution.py:446
  101.0 18.9 %collective-permute-start.22 = (f32[768,128]{1,0:T(8,128)S(1)}, f32[768,128]{1,0:T(8,128)S(1)}, u32[]{:S(2)}, u32[]{:S(2)}) collective-permute-start(f32[768,128]{1,0:T(8,128)S(1)} %multiply_add_fusion.1.refs_1_), channel_id=1, source_target_pairs={{0,24},{8,16},{16,8},{24,0},{1,25},{9,17},{17,9},{25,1},{2,26},{10... | collective-permute-start | bytes 1179656 | tf_op jit(solution)/shard_map/ppermute | solution.py:446
  101.5 25.1 %collective-permute-start.17 = (f32[768,128]{1,0:T(8,128)S(1)}, f32[768,128]{1,0:T(8,128)S(1)}, u32[]{:S(2)}, u32[]{:S(2)}) collective-permute-start(f32[768,128]{1,0:T(8,128)S(1)} %multiply_add_fusion.refs_1_), channel_id=1, source_target_pairs={{0,8},{8,0},{16,24},{24,16},{1,9},{9,1},{17,25},{25,17},{2,10},{10... | collective-permute-start | bytes 1179656 | tf_op jit(solution)/shard_map/ppermute | solution.py:446
  103.1 28.9 %collective-permute-start.18 = (f32[768,128]{1,0:T(8,128)S(1)}, f32[768,128]{1,0:T(8,128)S(1)}, u32[]{:S(2)}, u32[]{:S(2)}) collective-permute-start(f32[768,128]{1,0:T(8,128)S(1)} %multiply_add_fusion.refs_1_), channel_id=1, source_target_pairs={{0,16},{8,24},{16,0},{24,8},{1,17},{9,25},{17,1},{25,9},{2,18},{10... | collective-permute-start | bytes 1179656 | tf_op jit(solution)/shard_map/ppermute | solution.py:446
  109.9 22.1 %collective-permute-start.19 = (f32[768,128]{1,0:T(8,128)S(1)}, f32[768,128]{1,0:T(8,128)S(1)}, u32[]{:S(2)}, u32[]{:S(2)}) collective-permute-start(f32[768,128]{1,0:T(8,128)S(1)} %multiply_add_fusion.refs_1_), channel_id=1, source_target_pairs={{0,24},{8,16},{16,8},{24,0},{1,25},{9,17},{17,9},{25,1},{2,26},{10... | collective-permute-start | bytes 1179656 | tf_op jit(solution)/shard_map/ppermute | solution.py:446

commit v9 on v8

--- a/solution.py
+++ b/solution.py
@@ -174,7 +174,8 @@
 
 
 def value_columns(values):
-    return jnp.concatenate(two_terms(values), axis=1).astype(BF16)
+    high = values.astype(BF16)
+    return jnp.concatenate([high, (values - high.astype(F32)).astype(BF16)], axis=1)
 
 
 def write_sources(points_ref, weights_ref, y_ref, w_ref, scale):
@@ -208,11 +209,13 @@
     coords_ref[...] += (
         picked[:features] + picked[features : 2 * features] + picked[2 * features :]
     )
-    p_high, p_low = two_terms(proj_ref[...])
+    whole = proj_ref[...]
+    p_high = whole.astype(BF16)
+    p_low = (whole - p_high.astype(F32)).astype(BF16)
     columns = weights_ref.shape[1]
     values = jnp.concatenate(values, axis=0)
     both = jnp.dot(
-        jnp.concatenate([p_high, p_low], axis=1).astype(BF16),
+        jnp.concatenate([p_high, p_low], axis=1),
         jnp.concatenate([values, values], axis=0),
         preferred_element_type=F32,
     )

time: 136 us -> 136 us (level)
  no operation moved by 1% of the time
where the time goes in v9:
time: 136 us; the launch traced here: 134 us
  Pallas kernels  48.1 us (35%)
  starting transfers between devices  43.5 us (32%)
  waiting for transfers between devices  39.7 us (29%)
  local copies, waits for them, and re-layouts  1.89 us (1%)
    ppermute x13, starting transfers between devices, shift(): return lax.ppermute(array, 'dev', along(moves))  33.1 us
    pallas_call x8, Pallas kernels, pairs(): pl.pallas_call(functools.partial(pair_kernel, plan), grid=(count // group...  32.7 us
    ppermute x6, waiting for transfers between devices, on_device(): lax.ppermute(piece, 'grp', [(g, g ^ m) for g in range(groups)])  23.2 us
    ppermute x13, waiting for transfers between devices, shift(): return lax.ppermute(array, 'dev', along(moves))  15.1 us
    pallas_call x2, Pallas kernels, prepared(): pl.pallas_call(functools.partial(body, scale), grid=(count // block,), in...  12 us
    ppermute x6, starting transfers between devices, on_device(): lax.ppermute(piece, 'grp', [(g, g ^ m) for g in range(groups)])  9.1 us
    pallas_call x2, Pallas kernels, spread(): pl.pallas_call(functools.partial(spread_kernel, groups, per, first, unit,...  3.42 us
  transfers between devices with their start and end apart: 23, of which 9 were waited for; matrix products, arithmetic and copies ran while one was open for 2% of the time, Pallas kernels for 35%

profile of v9, /device:TPU:0, one launch (start us, length us, event | category | flops | bytes accessed | tf_op | source)
XLA Modules:
  0.0 133.9 jit_solution(1359657102930723875)
XLA Ops:
  0.0 0.5 collective-permute-start.2
  0.5 0.0 collective-permute-start.1
  0.5 0.8 copy.8
  1.3 0.1 reshape.5
  1.4 0.1 pad_add_fusion.refs_0_
  1.5 1.0 constant_dynamic-slice_fusion
  2.6 8.1 %prepared.2 = (bf16[12,256,512]{2,1,0:T(8,128)(2,1)S(1)}, bf16[12,512,256]{2,1,0:T(8,128)(2,1)S(1)}, bf16[256,256]{1,0:T(8,128)(2,1)S(1)}, bf16[256,256]{1,0:T(8...) custom-call(s32[1,256]{1,0:T(1,128)} %idx_ref.1, f32[64,6144]{1,0:T(8,128)} %points_ref.1, ...), custom_call_target="tpu_custom_call" | custom-call | flops 1610612736 | bytes 20447232 | tf_op jit(solution)/shard_map/prepared/pallas_call | solution.py:271
  10.7 0.5 collective-permute-start.3
  11.2 2.6 %collective-permute-start.5 = (f32[64,1664]{1,0:T(8,128)S(1)}, f32[64,1664]{1,0:T(8,128)S(1)}, u32[]{:S(2)}, u32[]{:S(2)}) collective-permute-start(f32[64,1664]{1,0:T(8,128)S(1)} %select_maximum_fusion), channel_id=1, source_target_pairs={{0,2},{1,3},{2,0},{3,1},{4,6},{5,7},{6,4},{7,5},{8,10},{9,11},{10,... | collective-permute-start | bytes 1277960 | tf_op jit(solution)/shard_map/ppermute | solution.py:340
  13.8 0.7 collective-permute-start.7
  14.4 0.0 collective-permute-done.3.coords_ref
  14.4 0.3 collective-permute-start.4
  14.7 1.3 collective-permute-done.4.summed_ref
  16.1 4.6 %collective-permute-start = (f32[64,1664]{1,0:T(8,128)S(1)}, f32[64,1664]{1,0:T(8,128)S(1)}, u32[]{:S(2)}, u32[]{:S(2)}) collective-permute-start(f32[64,1664]{1,0:T(8,128)S(1)} %select_maximum_fusion), channel_id=1, source_target_pairs={{0,6},{1,7},{6,0},{7,1},{2,2},{3,3},{4,4},{5,5},{8,14},{9,15},{14,... | collective-permute-start | bytes 1277960 | tf_op jit(solution)/shard_map/ppermute | solution.py:340
  20.7 3.5 %collective-permute-done.5.refs_1_.refs_2_ = f32[64,1664]{1,0:T(8,128)S(1)} collective-permute-done((f32[64,1664]{1,0:T(8,128)S(1)}, f32[64,1664]{1,0:T(8,128)S(1)}, u32[]{:S(2)}, u32[]{:S(2)}) %collective-permute-start.5) | collective-permute-done | bytes 426016 | tf_op jit(solution)/shard_map/ppermute | solution.py:340
  24.2 0.7 collective-permute-start.6
  24.9 0.0 collective-permute-done.7.refs_1_.refs_2_
  24.9 1.3 collective-permute-start.8
  26.2 0.0 collective-permute-done.1.points_ref
  26.2 0.0 collective-permute-done.2.weights_ref
  26.3 3.9 %prepared.3 = (bf16[12,256,512]{2,1,0:T(8,128)(2,1)S(1)}, bf16[12,512,256]{2,1,0:T(8,128)(2,1)S(1)}, bf16[256,256]{1,0:T(8,128)(2,1)S(1)}, bf16[256,256]{1,0:T(8,128)(2,1)S(1)}) custom-call(f32[64,6144]{1,0:T(8,128)S(1)} %collective-permute-done.1.points_ref, f32[6144,128]{1,0:T(8,128)} %collective-permute-done.2.weights_ref, ...), custom_call_target="tpu_custom_call" | custom-call | flops 1610612736 | bytes 14155776 | tf_op jit(solution)/shard_map/prepared/pallas_call | solution.py:271
  30.2 5.5 %collective-permute-done.refs_1_.refs_2_ = f32[64,1664]{1,0:T(8,128)S(1)} collective-permute-done((f32[64,1664]{1,0:T(8,128)S(1)}, f32[64,1664]{1,0:T(8,128)S(1)}, u32[]{:S(2)}, u32[]{:S(2)}) %collective-permute-start) | collective-permute-done | bytes 426016 | tf_op jit(solution)/shard_map/ppermute | solution.py:340
  35.7 4.1 %pairs.8 = f32[768,128]{1,0:T(8,128)S(1)} custom-call(s32[3]{0:T(128)S(1)} %pad_add_fusion.refs_0_, f32[64,1664]{1,0:T(8,128)S(1)} %collective-permute-done.refs_1_.refs_2_, f32[64,1664]{1,0:T(8,128)S(1)} %collective-permute-done.refs_1_.refs_2_, bf16[12,256,512]{2,1,0:T(8,128)(2,1)S(1)} %get-tuple-element.32.refs_3_.refs_6_.refs_4_, ...), custom_call_target="tpu_custom_call" | custom-call | flops 3019898880 | bytes 2359296 | tf_op jit(solution)/shard_map/pairs/pallas_call | solution.py:153
  39.7 10.1 %collective-permute-start.9 = (f32[768,128]{1,0:T(8,128)S(1)}, f32[768,128]{1,0:T(8,128)S(1)}, u32[]{:S(2)}, u32[]{:S(2)}) collective-permute-start(f32[768,128]{1,0:T(8,128)S(1)} %pairs.8), channel_id=1, source_target_pairs={{0,2},{1,3},{6,4},{7,5},{8,10},{9,11},{14,12},{15,13},{16,18},{17,... | collective-permute-start | bytes 1179656 | tf_op jit(solution)/shard_map/ppermute | solution.py:340
  49.9 4.1 %pairs.9 = f32[768,128]{1,0:T(8,128)S(1)} custom-call(s32[3]{0:T(128)S(1)} %pad_add_fusion.refs_0_, f32[64,1664]{1,0:T(8,128)S(1)} %collective-permute-done.refs_1_.refs_2_, f32[64,1664]{1,0:T(8,128)S(1)} %collective-permute-done.refs_1_.refs_2_, bf16[12,256,512]{2,1,0:T(8,128)(2,1)S(1)} %get-tuple-element.32.refs_3_.refs_6_.refs_4_, ...), custom_call_target="tpu_custom_call" | custom-call | flops 3019898880 | bytes 2359296 | tf_op jit(solution)/shard_map/pairs/pallas_call | solution.py:153
  54.0 1.5 %collective-permute-start.10 = (f32[768,128]{1,0:T(8,128)S(1)}, f32[768,128]{1,0:T(8,128)S(1)}, u32[]{:S(2)}, u32[]{:S(2)}) collective-permute-start(f32[768,128]{1,0:T(8,128)S(1)} %pairs.9), channel_id=1, source_target_pairs={{0,2},{1,3},{6,4},{7,5},{8,10},{9,11},{14,12},{15,13},{16,18},{17,... | collective-permute-start | bytes 1179656 | tf_op jit(solution)/shard_map/ppermute | solution.py:340
  55.5 0.0 collective-permute-done.6.refs_1_.refs_3_
  55.5 0.0 collective-permute-done.8.refs_2_.refs_4_
  55.5 3.8 %collective-permute-done.9.refs_5_ = f32[768,128]{1,0:T(8,128)S(1)} collective-permute-done((f32[768,128]{1,0:T(8,128)S(1)}, f32[768,128]{1,0:T(8,128)S(1)}, u32[]{:S(2)}, u32[]{:S(2)}) %collective-permute-start.9) | collective-permute-done | bytes 393248 | tf_op jit(solution)/shard_map/ppermute | solution.py:340
  59.3 4.1 %pairs.10 = f32[768,128]{1,0:T(8,128)S(1)} custom-call(s32[3]{0:T(128)S(1)} %pad_add_fusion.refs_0_, f32[64,1664]{1,0:T(8,128)S(1)} %collective-permute-done.6.refs_1_.refs_3_, f32[64,1664]{1,0:T(8,128)S(1)} %collective-permute-done.8.refs_2_.refs_4_, f32[64,1664]{1,0:T(8,128)S(1)} %collective-permute-done.6.refs_1_.refs_3_, ...), custom_call_target="tpu_custom_call" | custom-call | flops 3019898880 | bytes 2359296 | tf_op jit(solution)/shard_map/pairs/pallas_call | solution.py:153
  63.5 2.5 %collective-permute-start.11 = (f32[768,128]{1,0:T(8,128)S(1)}, f32[768,128]{1,0:T(8,128)S(1)}, u32[]{:S(2)}, u32[]{:S(2)}) collective-permute-start(f32[768,128]{1,0:T(8,128)S(1)} %pairs.10), channel_id=1, source_target_pairs={{0,2},{1,3},{6,4},{7,5},{2,6},{3,7},{4,0},{5,1},{8,10},{9,11},{14,... | collective-permute-start | bytes 1179656 | tf_op jit(solution)/shard_map/ppermute | solution.py:340
  66.0 4.1 %pairs.11 = f32[768,128]{1,0:T(8,128)S(1)} custom-call(s32[3]{0:T(128)S(1)} %pad_add_fusion.refs_0_, f32[64,1664]{1,0:T(8,128)S(1)} %collective-permute-done.5.refs_1_.refs_2_, f32[64,1664]{1,0:T(8,128)S(1)} %collective-permute-done.5.refs_1_.refs_2_, bf16[12,256,512]{2,1,0:T(8,128)(2,1)S(1)} %get-tuple-element.32.refs_3_.refs_6_.refs_4_, ...), custom_call_target="tpu_custom_call" | custom-call | flops 3019898880 | bytes 2359296 | tf_op jit(solution)/shard_map/pairs/pallas_call | solution.py:153
  70.1 1.1 collective-permute-start.13
  71.1 0.0 collective-permute-done.10.refs_5_
  71.1 4.1 %pairs.12 = f32[768,128]{1,0:T(8,128)S(1)} custom-call(s32[3]{0:T(128)S(1)} %pad_add_fusion.refs_0_, f32[64,1664]{1,0:T(8,128)S(1)} %collective-permute-done.6.refs_1_.refs_3_, f32[64,1664]{1,0:T(8,128)S(1)} %collective-permute-done.8.refs_2_.refs_4_, f32[64,1664]{1,0:T(8,128)S(1)} %collective-permute-done.6.refs_1_.refs_3_, ...), custom_call_target="tpu_custom_call" | custom-call | flops 3019898880 | bytes 2359296 | tf_op jit(solution)/shard_map/pairs/pallas_call | solution.py:153
  75.3 1.3 collective-permute-start.15
  76.6 0.0 collective-permute-done.11.refs_3_
  76.6 4.1 %pairs.13 = f32[768,128]{1,0:T(8,128)S(1)} custom-call(s32[3]{0:T(128)S(1)} %pad_add_fusion.refs_0_, f32[64,1664]{1,0:T(8,128)S(1)} %collective-permute-done.7.refs_1_.refs_2_, f32[64,1664]{1,0:T(8,128)S(1)} %collective-permute-done.7.refs_1_.refs_2_, f32[768,128]{1,0:T(8,128)S(1)} %collective-permute-done.11.refs_3_, ...), custom_call_target="tpu_custom_call" | custom-call | flops 3019898880 | bytes 2359296 | tf_op jit(solution)/shard_map/pairs/pallas_call | solution.py:153
  80.7 0.7 collective-permute-start.14
  81.4 4.1 %pairs.14 = f32[768,128]{1,0:T(8,128)S(1)} custom-call(s32[3]{0:T(128)S(1)} %pad_add_fusion.refs_0_, f32[64,1664]{1,0:T(8,128)S(1)} %collective-permute-done.5.refs_1_.refs_2_, f32[64,1664]{1,0:T(8,128)S(1)} %collective-permute-done.5.refs_1_.refs_2_, bf16[12,256,512]{2,1,0:T(8,128)(2,1)S(1)} %get-tuple-element.32.refs_3_.refs_6_.refs_4_, ...), custom_call_target="tpu_custom_call" | custom-call | flops 3019898880 | bytes 2359296 | tf_op jit(solution)/shard_map/pairs/pallas_call | solution.py:153
  85.4 5.4 %collective-permute-start.12 = (f32[768,128]{1,0:T(8,128)S(1)}, f32[768,128]{1,0:T(8,128)S(1)}, u32[]{:S(2)}, u32[]{:S(2)}) collective-permute-start(f32[768,128]{1,0:T(8,128)S(1)} %pairs.14), channel_id=1, source_target_pairs={{0,2},{1,3},{2,0},{3,1},{4,6},{5,7},{6,4},{7,5},{8,10},{9,11},{10,... | collective-permute-start | bytes 1179656 | tf_op jit(solution)/shard_map/ppermute | solution.py:340
  90.8 2.2 %collective-permute-done.15.refs_3_ = f32[768,128]{1,0:T(8,128)S(1)} collective-permute-done((f32[768,128]{1,0:T(8,128)S(1)}, f32[768,128]{1,0:T(8,128)S(1)}, u32[]{:S(2)}, u32[]{:S(2)}) %collective-permute-start.15) | collective-permute-done | bytes 393248 | tf_op jit(solution)/shard_map/ppermute | solution.py:340
  93.0 4.1 %pairs.15 = f32[768,128]{1,0:T(8,128)S(1)} custom-call(s32[3]{0:T(128)S(1)} %pad_add_fusion.refs_0_, f32[64,1664]{1,0:T(8,128)S(1)} %collective-permute-done.7.refs_1_.refs_2_, f32[64,1664]{1,0:T(8,128)S(1)} %collective-permute-done.7.refs_1_.refs_2_, f32[768,128]{1,0:T(8,128)S(1)} %collective-permute-done.15.refs_3_, ...), custom_call_target="tpu_custom_call" | custom-call | flops 3019898880 | bytes 2359296 | tf_op jit(solution)/shard_map/pairs/pallas_call | solution.py:153
  97.1 0.7 collective-permute-start.16
  97.8 0.0 collective-permute-done.13
  97.8 0.0 collective-permute-done.14
  97.8 0.1 multiply_add_fusion.1.refs_1_
  97.9 1.6 %collective-permute-start.20 = (f32[768,128]{1,0:T(8,128)S(1)}, f32[768,128]{1,0:T(8,128)S(1)}, u32[]{:S(2)}, u32[]{:S(2)}) collective-permute-start(f32[768,128]{1,0:T(8,128)S(1)} %multiply_add_fusion.1.refs_1_), channel_id=1, source_target_pairs={{0,8},{8,0},{16,24},{24,16},{1,9},{9,1},{17,25},{25,17},{2,10},{10... | collective-permute-start | bytes 1179656 | tf_op jit(solution)/shard_map/ppermute | solution.py:449
  99.4 1.5 %collective-permute-start.21 = (f32[768,128]{1,0:T(8,128)S(1)}, f32[768,128]{1,0:T(8,128)S(1)}, u32[]{:S(2)}, u32[]{:S(2)}) collective-permute-start(f32[768,128]{1,0:T(8,128)S(1)} %multiply_add_fusion.1.refs_1_), channel_id=1, source_target_pairs={{0,16},{8,24},{16,0},{24,8},{1,17},{9,25},{17,1},{25,9},{2,18},{10... | collective-permute-start | bytes 1179656 | tf_op jit(solution)/shard_map/ppermute | solution.py:449
  101.0 0.5 collective-permute-start.22
  101.4 0.0 collective-permute-done.12
  101.4 0.0 collective-permute-done.16
  101.5 0.1 multiply_add_fusion.refs_1_
  101.5 1.6 %collective-permute-start.17 = (f32[768,128]{1,0:T(8,128)S(1)}, f32[768,128]{1,0:T(8,128)S(1)}, u32[]{:S(2)}, u32[]{:S(2)}) collective-permute-start(f32[768,128]{1,0:T(8,128)S(1)} %multiply_add_fusion.refs_1_), channel_id=1, source_target_pairs={{0,8},{8,0},{16,24},{24,16},{1,9},{9,1},{17,25},{25,17},{2,10},{10... | collective-permute-start | bytes 1179656 | tf_op jit(solution)/shard_map/ppermute | solution.py:449
  103.1 1.5 %collective-permute-start.18 = (f32[768,128]{1,0:T(8,128)S(1)}, f32[768,128]{1,0:T(8,128)S(1)}, u32[]{:S(2)}, u32[]{:S(2)}) collective-permute-start(f32[768,128]{1,0:T(8,128)S(1)} %multiply_add_fusion.refs_1_), channel_id=1, source_target_pairs={{0,16},{8,24},{16,0},{24,8},{1,17},{9,25},{17,1},{25,9},{2,18},{10... | collective-permute-start | bytes 1179656 | tf_op jit(solution)/shard_map/ppermute | solution.py:449
  104.6 5.3 %collective-permute-done.20.refs_2_ = f32[768,128]{1,0:T(8,128)S(1)} collective-permute-done((f32[768,128]{1,0:T(8,128)S(1)}, f32[768,128]{1,0:T(8,128)S(1)}, u32[]{:S(2)}, u32[]{:S(2)}) %collective-permute-start.20) | collective-permute-done | bytes 393248 | tf_op jit(solution)/shard_map/ppermute | solution.py:449
  109.9 2.5 %collective-permute-start.19 = (f32[768,128]{1,0:T(8,128)S(1)}, f32[768,128]{1,0:T(8,128)S(1)}, u32[]{:S(2)}, u32[]{:S(2)}) collective-permute-start(f32[768,128]{1,0:T(8,128)S(1)} %multiply_add_fusion.refs_1_), channel_id=1, source_target_pairs={{0,24},{8,16},{16,8},{24,0},{1,25},{9,17},{17,9},{25,1},{2,26},{10... | collective-permute-start | bytes 1179656 | tf_op jit(solution)/shard_map/ppermute | solution.py:449
  112.4 7.4 %collective-permute-done.21.refs_3_ = f32[768,128]{1,0:T(8,128)S(1)} collective-permute-done((f32[768,128]{1,0:T(8,128)S(1)}, f32[768,128]{1,0:T(8,128)S(1)}, u32[]{:S(2)}, u32[]{:S(2)}) %collective-permute-start.21) | collective-permute-done | bytes 393248 | tf_op jit(solution)/shard_map/ppermute | solution.py:449
  119.8 0.0 collective-permute-done.22.refs_4_
  119.8 1.7 %spread.2.refs_5_ = f32[6144,128]{1,0:T(8,128)} custom-call(s32[4]{0:T(128)S(1)} %iota_xor_fusion.refs_0_, f32[768,128]{1,0:T(8,128)S(1)} %multiply_add_fusion.1.refs_1_, f32[768,128]{1,0:T(8,128)S(1)} %collective-permute-done.20.refs_2_, f32[768,128]{1,0:T(8,128)S(1)} %collective-permute-done.21.refs_3_, f32[768,128]{1,0:T(8,128)S(1)} %collective-permute-done.22.refs_4_), custom_call_target="tpu_custom_call" | custom-call | tf_op jit(solution)/shard_map/spread/pallas_call | solution.py:306
  121.6 5.0 %collective-permute-done.17.refs_2_ = f32[768,128]{1,0:T(8,128)S(1)} collective-permute-done((f32[768,128]{1,0:T(8,128)S(1)}, f32[768,128]{1,0:T(8,128)S(1)}, u32[]{:S(2)}, u32[]{:S(2)}) %collective-permute-start.17) | collective-permute-done | bytes 393248 | tf_op jit(solution)/shard_map/ppermute | solution.py:449
  126.6 5.4 %collective-permute-done.18.refs_3_ = f32[768,128]{1,0:T(8,128)S(1)} collective-permute-done((f32[768,128]{1,0:T(8,128)S(1)}, f32[768,128]{1,0:T(8,128)S(1)}, u32[]{:S(2)}, u32[]{:S(2)}) %collective-permute-start.18) | collective-permute-done | bytes 393248 | tf_op jit(solution)/shard_map/ppermute | solution.py:449
  132.0 0.0 collective-permute-done.19.refs_4_
  132.0 1.7 %spread.3 = f32[6144,128]{1,0:T(8,128)} custom-call(s32[4]{0:T(128)S(1)} %iota_xor_fusion.refs_0_, f32[768,128]{1,0:T(8,128)S(1)} %multiply_add_fusion.refs_1_, f32[768,128]{1,0:T(8,128)S(1)} %collective-permute-done.17.refs_2_, f32[768,128]{1,0:T(8,128)S(1)} %collective-permute-done.18.refs_3_, ...), custom_call_target="tpu_custom_call", output_to_operand_aliasing={{}: (5, {})} | custom-call | tf_op jit(solution)/shard_map/spread/pallas_call | solution.py:306
  (4 shorter events, 0.0 us)
Async XLA Ops:
  0.0 26.2 %collective-permute-start.2 = (f32[6144,128]{1,0:T(8,128)}, f32[6144,128]{1,0:T(8,128)}, u32[]{:S(2)}, u32[]{:S(2)}) collective-permute-start(f32[6144,128]{1,0:T(8,128)} %weights_ref.1), channel_id=1, source_target_pairs={{0,1},{1,0},{2,3},{3,2},{4,5},{5,4},{6,7},{7,6},{8,9},{9,8},{10,11... | collective-permute-start | bytes 9437192 | tf_op jit(solution)/shard_map/ppermute | solution.py:381
  0.5 25.7 %collective-permute-start.1 = (f32[64,6144]{1,0:T(8,128)}, f32[64,6144]{1,0:T(8,128)S(1)}, u32[]{:S(2)}, u32[]{:S(2)}) collective-permute-start(f32[64,6144]{1,0:T(8,128)} %points_ref.1), channel_id=1, source_target_pairs={{0,1},{1,0},{2,3},{3,2},{4,5},{5,4},{6,7},{7,6},{8,9},{9,8},{10,11... | collective-permute-start | bytes 4718600 | tf_op jit(solution)/shard_map/ppermute | solution.py:381
  10.7 3.7 %collective-permute-start.3 = (f32[64,256]{1,0:T(8,128)}, f32[64,256]{1,0:T(8,128)S(1)}, u32[]{:S(2)}, u32[]{:S(2)}) collective-permute-start(f32[64,256]{1,0:T(8,128)} %get-tuple-element.36), channel_id=1, source_target_pairs={{0,1},{1,0},{2,3},{3,2},{4,5},{5,4},{6,7},{7,6},{8,9},{9,8},{10,11... | collective-permute-start | bytes 196616 | tf_op jit(solution)/shard_map/ppermute | solution.py:381
  11.2 13.1 %collective-permute-start.5 = (f32[64,1664]{1,0:T(8,128)S(1)}, f32[64,1664]{1,0:T(8,128)S(1)}, u32[]{:S(2)}, u32[]{:S(2)}) collective-permute-start(f32[64,1664]{1,0:T(8,128)S(1)} %select_maximum_fusion), channel_id=1, source_target_pairs={{0,2},{1,3},{2,0},{3,1},{4,6},{5,7},{6,4},{7,5},{8,10},{9,11},{10,... | collective-permute-start | bytes 1277960 | tf_op jit(solution)/shard_map/ppermute | solution.py:340
  13.8 11.2 %collective-permute-start.7 = (f32[64,1664]{1,0:T(8,128)S(1)}, f32[64,1664]{1,0:T(8,128)S(1)}, u32[]{:S(2)}, u32[]{:S(2)}) collective-permute-start(f32[64,1664]{1,0:T(8,128)S(1)} %select_maximum_fusion), channel_id=1, source_target_pairs={{2,4},{3,5},{4,2},{5,3},{0,0},{1,1},{6,6},{7,7},{10,12},{11,13},{1... | collective-permute-start | bytes 1277960 | tf_op jit(solution)/shard_map/ppermute | solution.py:340
  14.4 1.6 %collective-permute-start.4 = (f32[256,128]{1,0:T(8,128)}, f32[256,128]{1,0:T(8,128)S(1)}, u32[]{:S(2)}, u32[]{:S(2)}) collective-permute-start(f32[256,128]{1,0:T(8,128)} %get-tuple-element.37), channel_id=1, source_target_pairs={{0,1},{1,0},{2,3},{3,2},{4,5},{5,4},{6,7},{7,6},{8,9},{9,8},{10,11... | collective-permute-start | bytes 393224 | tf_op jit(solution)/shard_map/ppermute | solution.py:381
  16.1 19.6 %collective-permute-start = (f32[64,1664]{1,0:T(8,128)S(1)}, f32[64,1664]{1,0:T(8,128)S(1)}, u32[]{:S(2)}, u32[]{:S(2)}) collective-permute-start(f32[64,1664]{1,0:T(8,128)S(1)} %select_maximum_fusion), channel_id=1, source_target_pairs={{0,6},{1,7},{6,0},{7,1},{2,2},{3,3},{4,4},{5,5},{8,14},{9,15},{14,... | collective-permute-start | bytes 1277960 | tf_op jit(solution)/shard_map/ppermute | solution.py:340
  24.2 31.2 %collective-permute-start.6 = (f32[64,1664]{1,0:T(8,128)S(1)}, f32[64,1664]{1,0:T(8,128)S(1)}, u32[]{:S(2)}, u32[]{:S(2)}) collective-permute-start(f32[64,1664]{1,0:T(8,128)S(1)} %collective-permute-done.5.refs_1_.refs_2_), channel_id=1, source_target_pairs={{2,4},{3,5},{4,2},{5,3},{10,12},{11,13},{12,10},{13,11},{18,20},{1... | collective-permute-start | bytes 1277960 | tf_op jit(solution)/shard_map/ppermute | solution.py:340
  24.9 30.5 %collective-permute-start.8 = (f32[64,1664]{1,0:T(8,128)S(1)}, f32[64,1664]{1,0:T(8,128)S(1)}, u32[]{:S(2)}, u32[]{:S(2)}) collective-permute-start(f32[64,1664]{1,0:T(8,128)S(1)} %collective-permute-done.7.refs_1_.refs_2_), channel_id=1, source_target_pairs={{2,0},{3,1},{4,6},{5,7},{10,8},{11,9},{12,14},{13,15},{18,16},{19,... | collective-permute-start | bytes 1277960 | tf_op jit(solution)/shard_map/ppermute | solution.py:340
  39.7 19.6 %collective-permute-start.9 = (f32[768,128]{1,0:T(8,128)S(1)}, f32[768,128]{1,0:T(8,128)S(1)}, u32[]{:S(2)}, u32[]{:S(2)}) collective-permute-start(f32[768,128]{1,0:T(8,128)S(1)} %pairs.8), channel_id=1, source_target_pairs={{0,2},{1,3},{6,4},{7,5},{8,10},{9,11},{14,12},{15,13},{16,18},{17,... | collective-permute-start | bytes 1179656 | tf_op jit(solution)/shard_map/ppermute | solution.py:340
  54.0 17.2 %collective-permute-start.10 = (f32[768,128]{1,0:T(8,128)S(1)}, f32[768,128]{1,0:T(8,128)S(1)}, u32[]{:S(2)}, u32[]{:S(2)}) collective-permute-start(f32[768,128]{1,0:T(8,128)S(1)} %pairs.9), channel_id=1, source_target_pairs={{0,2},{1,3},{6,4},{7,5},{8,10},{9,11},{14,12},{15,13},{16,18},{17,... | collective-permute-start | bytes 1179656 | tf_op jit(solution)/shard_map/ppermute | solution.py:340
  63.5 13.1 %collective-permute-start.11 = (f32[768,128]{1,0:T(8,128)S(1)}, f32[768,128]{1,0:T(8,128)S(1)}, u32[]{:S(2)}, u32[]{:S(2)}) collective-permute-start(f32[768,128]{1,0:T(8,128)S(1)} %pairs.10), channel_id=1, source_target_pairs={{0,2},{1,3},{6,4},{7,5},{2,6},{3,7},{4,0},{5,1},{8,10},{9,11},{14,... | collective-permute-start | bytes 1179656 | tf_op jit(solution)/shard_map/ppermute | solution.py:340
  70.1 27.7 %collective-permute-start.13 = (f32[768,128]{1,0:T(8,128)S(1)}, f32[768,128]{1,0:T(8,128)S(1)}, u32[]{:S(2)}, u32[]{:S(2)}) collective-permute-start(f32[768,128]{1,0:T(8,128)S(1)} %pairs.11), channel_id=1, source_target_pairs={{0,2},{1,3},{2,0},{3,1},{4,6},{5,7},{6,4},{7,5},{8,10},{9,11},{10,... | collective-permute-start | bytes 1179656 | tf_op jit(solution)/shard_map/ppermute | solution.py:340
  75.3 17.8 %collective-permute-start.15 = (f32[768,128]{1,0:T(8,128)S(1)}, f32[768,128]{1,0:T(8,128)S(1)}, u32[]{:S(2)}, u32[]{:S(2)}) collective-permute-start(f32[768,128]{1,0:T(8,128)S(1)} %pairs.12), channel_id=1, source_target_pairs={{0,2},{1,3},{6,4},{7,5},{2,6},{3,7},{4,0},{5,1},{8,10},{9,11},{14,... | collective-permute-start | bytes 1179656 | tf_op jit(solution)/shard_map/ppermute | solution.py:340
  80.7 17.2 %collective-permute-start.14 = (f32[768,128]{1,0:T(8,128)S(1)}, f32[768,128]{1,0:T(8,128)S(1)}, u32[]{:S(2)}, u32[]{:S(2)}) collective-permute-start(f32[768,128]{1,0:T(8,128)S(1)} %pairs.13), channel_id=1, source_target_pairs={{2,4},{3,5},{4,2},{5,3},{0,0},{1,1},{6,6},{7,7},{10,12},{11,13},{1... | collective-permute-start | bytes 1179656 | tf_op jit(solution)/shard_map/ppermute | solution.py:340
  85.4 16.0 %collective-permute-start.12 = (f32[768,128]{1,0:T(8,128)S(1)}, f32[768,128]{1,0:T(8,128)S(1)}, u32[]{:S(2)}, u32[]{:S(2)}) collective-permute-start(f32[768,128]{1,0:T(8,128)S(1)} %pairs.14), channel_id=1, source_target_pairs={{0,2},{1,3},{2,0},{3,1},{4,6},{5,7},{6,4},{7,5},{8,10},{9,11},{10,... | collective-permute-start | bytes 1179656 | tf_op jit(solution)/shard_map/ppermute | solution.py:340
  97.1 4.3 %collective-permute-start.16 = (f32[768,128]{1,0:T(8,128)S(1)}, f32[768,128]{1,0:T(8,128)S(1)}, u32[]{:S(2)}, u32[]{:S(2)}) collective-permute-start(f32[768,128]{1,0:T(8,128)S(1)} %pairs.15), channel_id=1, source_target_pairs={{2,4},{3,5},{4,2},{5,3},{0,0},{1,1},{6,6},{7,7},{10,12},{11,13},{1... | collective-permute-start | bytes 1179656 | tf_op jit(solution)/shard_map/ppermute | solution.py:340
  97.9 12.1 %collective-permute-start.20 = (f32[768,128]{1,0:T(8,128)S(1)}, f32[768,128]{1,0:T(8,128)S(1)}, u32[]{:S(2)}, u32[]{:S(2)}) collective-permute-start(f32[768,128]{1,0:T(8,128)S(1)} %multiply_add_fusion.1.refs_1_), channel_id=1, source_target_pairs={{0,8},{8,0},{16,24},{24,16},{1,9},{9,1},{17,25},{25,17},{2,10},{10... | collective-permute-start | bytes 1179656 | tf_op jit(solution)/shard_map/ppermute | solution.py:449
  99.4 20.4 %collective-permute-start.21 = (f32[768,128]{1,0:T(8,128)S(1)}, f32[768,128]{1,0:T(8,128)S(1)}, u32[]{:S(2)}, u32[]{:S(2)}) collective-permute-start(f32[768,128]{1,0:T(8,128)S(1)} %multiply_add_fusion.1.refs_1_), channel_id=1, source_target_pairs={{0,16},{8,24},{16,0},{24,8},{1,17},{9,25},{17,1},{25,9},{2,18},{10... | collective-permute-start | bytes 1179656 | tf_op jit(solution)/shard_map/ppermute | solution.py:449
  101.0 18.9 %collective-permute-start.22 = (f32[768,128]{1,0:T(8,128)S(1)}, f32[768,128]{1,0:T(8,128)S(1)}, u32[]{:S(2)}, u32[]{:S(2)}) collective-permute-start(f32[768,128]{1,0:T(8,128)S(1)} %multiply_add_fusion.1.refs_1_), channel_id=1, source_target_pairs={{0,24},{8,16},{16,8},{24,0},{1,25},{9,17},{17,9},{25,1},{2,26},{10... | collective-permute-start | bytes 1179656 | tf_op jit(solution)/shard_map/ppermute | solution.py:449
  101.5 25.1 %collective-permute-start.17 = (f32[768,128]{1,0:T(8,128)S(1)}, f32[768,128]{1,0:T(8,128)S(1)}, u32[]{:S(2)}, u32[]{:S(2)}) collective-permute-start(f32[768,128]{1,0:T(8,128)S(1)} %multiply_add_fusion.refs_1_), channel_id=1, source_target_pairs={{0,8},{8,0},{16,24},{24,16},{1,9},{9,1},{17,25},{25,17},{2,10},{10... | collective-permute-start | bytes 1179656 | tf_op jit(solution)/shard_map/ppermute | solution.py:449
  103.1 28.9 %collective-permute-start.18 = (f32[768,128]{1,0:T(8,128)S(1)}, f32[768,128]{1,0:T(8,128)S(1)}, u32[]{:S(2)}, u32[]{:S(2)}) collective-permute-start(f32[768,128]{1,0:T(8,128)S(1)} %multiply_add_fusion.refs_1_), channel_id=1, source_target_pairs={{0,16},{8,24},{16,0},{24,8},{1,17},{9,25},{17,1},{25,9},{2,18},{10... | collective-permute-start | bytes 1179656 | tf_op jit(solution)/shard_map/ppermute | solution.py:449
  109.9 22.1 %collective-permute-start.19 = (f32[768,128]{1,0:T(8,128)S(1)}, f32[768,128]{1,0:T(8,128)S(1)}, u32[]{:S(2)}, u32[]{:S(2)}) collective-permute-start(f32[768,128]{1,0:T(8,128)S(1)} %multiply_add_fusion.refs_1_), channel_id=1, source_target_pairs={{0,24},{8,16},{16,8},{24,0},{1,25},{9,17},{17,9},{25,1},{2,26},{10... | collective-permute-start | bytes 1179656 | tf_op jit(solution)/shard_map/ppermute | solution.py:449

commit v10 on v9

--- a/solution.py
+++ b/solution.py
@@ -9,7 +9,7 @@
 from jax.sharding import PartitionSpec as P
 
 
-ROUNDS = ("a0", "a1", "b0", "c0", "b1", "d0", "c1", "d1")
+ROUNDS = ("a0", "a1", "a2", "b0", "c0", "b1", "d0", "c1", "b2", "d1", "c2", "d2")
 
 F32 = jnp.float32
 BF16 = jnp.bfloat16
@@ -127,7 +127,7 @@
     kept = own[2].shape[1]
     unit = leaf // sizes["units"]
     width = parcels[0].shape[1] - 128
-    group = math.gcd(count, 3)
+    group = 2 if count % 2 == 0 and first % 2 == 0 else 1
     assert first % group == 0
     block = group * unit
     plan = dict(
@@ -360,8 +360,8 @@
     )
     units = 2
     unit = leaf // units
-    size = -(-per * units // 2)
-    chunks = [(0, size), (size, per * units - size)]
+    size = per * units // 3
+    chunks = [(0, size), (size, size), (2 * size, per * units - 2 * size)]
     sizes = {
         "leaf": leaf,
         "per": per,

time: 136 us -> 141 us (1.037)
  the two profiles are of different devices: /device:TPU:0 before, /device:TPU:22 now
where the time goes in v10:
time: 141 us; the launch traced here: 140 us
  waiting for transfers between devices  51.6 us (37%)
  Pallas kernels  51.3 us (36%)
  starting transfers between devices  34.7 us (25%)
  local copies, waits for them, and re-layouts  1.89 us (1%)
    pallas_call x12, Pallas kernels, pairs(): pl.pallas_call(functools.partial(pair_kernel, plan), grid=(count // group...  34.6 us
    ppermute x17, starting transfers between devices, shift(): return lax.ppermute(array, 'dev', along(moves))  26.4 us
    ppermute x17, waiting for transfers between devices, shift(): return lax.ppermute(array, 'dev', along(moves))  25.8 us
    ppermute x9, waiting for transfers between devices, on_device(): lax.ppermute(piece, 'grp', [(g, g ^ m) for g in range(groups)])  24.4 us
    pallas_call x2, Pallas kernels, prepared(): pl.pallas_call(functools.partial(body, scale), grid=(count // block,), in...  12 us
    ppermute x9, starting transfers between devices, on_device(): lax.ppermute(piece, 'grp', [(g, g ^ m) for g in range(groups)])  7.54 us
    pallas_call x3, Pallas kernels, spread(): pl.pallas_call(functools.partial(spread_kernel, groups, per, first, unit,...  4.62 us
  transfers between devices with their start and end apart: 30, of which 14 were waited for; matrix products, arithmetic and copies ran while one was open for 2% of the time, Pallas kernels for 35%

profile of v10, /device:TPU:22, one launch (start us, length us, event | category | flops | bytes accessed | tf_op | source)
XLA Modules:
  0.0 140.3 jit_solution(2130731720798358552)
XLA Ops:
  0.0 0.5 collective-permute-start.1
  0.5 0.8 copy.9
  1.3 0.1 reshape.5
  1.4 0.1 pad_add_fusion.refs_0_
  1.5 1.0 constant_dynamic-slice_fusion
  2.6 8.1 %prepared.2 = (bf16[12,256,512]{2,1,0:T(8,128)(2,1)S(1)}, bf16[12,512,256]{2,1,0:T(8,128)(2,1)S(1)}, bf16[256,256]{1,0:T(8,128)(2,1)S(1)}, bf16[256,256]{1,0:T(8...) custom-call(s32[1,256]{1,0:T(1,128)} %idx_ref.1, f32[64,6144]{1,0:T(8,128)} %points_ref.1, ...), custom_call_target="tpu_custom_call" | custom-call | flops 1610612736 | bytes 20447232 | tf_op jit(solution)/shard_map/prepared/pallas_call | solution.py:271
  10.7 1.6 %collective-permute-start.5 = (f32[64,1664]{1,0:T(8,128)S(1)}, f32[64,1664]{1,0:T(8,128)S(1)}, u32[]{:S(2)}, u32[]{:S(2)}) collective-permute-start(f32[64,1664]{1,0:T(8,128)S(1)} %select_maximum_fusion), channel_id=1, source_target_pairs={{0,2},{1,3},{2,0},{3,1},{4,6},{5,7},{6,4},{7,5},{8,10},{9,11},{10,... | collective-permute-start | bytes 1277960 | tf_op jit(solution)/shard_map/ppermute | solution.py:340
  12.3 1.9 %collective-permute-start.7 = (f32[64,1664]{1,0:T(8,128)S(1)}, f32[64,1664]{1,0:T(8,128)S(1)}, u32[]{:S(2)}, u32[]{:S(2)}) collective-permute-start(f32[64,1664]{1,0:T(8,128)S(1)} %select_maximum_fusion), channel_id=1, source_target_pairs={{2,4},{3,5},{4,2},{5,3},{0,0},{1,1},{6,6},{7,7},{10,12},{11,13},{1... | collective-permute-start | bytes 1277960 | tf_op jit(solution)/shard_map/ppermute | solution.py:340
  14.2 0.3 collective-permute-start.4
  14.5 1.3 collective-permute-done.4.summed_ref
  15.8 0.7 collective-permute-start
  16.5 6.9 %collective-permute-done.5.refs_1_.refs_2_ = f32[64,1664]{1,0:T(8,128)S(1)} collective-permute-done((f32[64,1664]{1,0:T(8,128)S(1)}, f32[64,1664]{1,0:T(8,128)S(1)}, u32[]{:S(2)}, u32[]{:S(2)}) %collective-permute-start.5) | collective-permute-done | bytes 426016 | tf_op jit(solution)/shard_map/ppermute | solution.py:340
  23.4 2.3 %collective-permute-start.6 = (f32[64,1664]{1,0:T(8,128)S(1)}, f32[64,1664]{1,0:T(8,128)S(1)}, u32[]{:S(2)}, u32[]{:S(2)}) collective-permute-start(f32[64,1664]{1,0:T(8,128)S(1)} %collective-permute-done.5.refs_1_.refs_2_), channel_id=1, source_target_pairs={{2,4},{3,5},{4,2},{5,3},{10,12},{11,13},{12,10},{13,11},{18,20},{1... | collective-permute-start | bytes 1277960 | tf_op jit(solution)/shard_map/ppermute | solution.py:340
  25.8 10.2 %collective-permute-done.7.refs_1_.refs_2_ = f32[64,1664]{1,0:T(8,128)S(1)} collective-permute-done((f32[64,1664]{1,0:T(8,128)S(1)}, f32[64,1664]{1,0:T(8,128)S(1)}, u32[]{:S(2)}, u32[]{:S(2)}) %collective-permute-start.7) | collective-permute-done | bytes 426016 | tf_op jit(solution)/shard_map/ppermute | solution.py:340
  36.0 1.3 collective-permute-start.8
  37.3 3.9 %prepared.3 = (bf16[12,256,512]{2,1,0:T(8,128)(2,1)S(1)}, bf16[12,512,256]{2,1,0:T(8,128)(2,1)S(1)}, bf16[256,256]{1,0:T(8,128)(2,1)S(1)}, bf16[256,256]{1,0:T(8,128)(2,1)S(1)}) custom-call(f32[64,6144]{1,0:T(8,128)S(1)} %collective-permute-done.1.points_ref, f32[6144,128]{1,0:T(8,128)} %collective-permute-done.2.weights_ref, ...), custom_call_target="tpu_custom_call" | custom-call | flops 1610612736 | bytes 14155776 | tf_op jit(solution)/shard_map/prepared/pallas_call | solution.py:271
  41.3 2.9 %pairs.12 = f32[512,128]{1,0:T(8,128)S(1)} custom-call(s32[3]{0:T(128)S(1)} %pad_add_fusion.refs_0_, f32[64,1664]{1,0:T(8,128)S(1)} %collective-permute-done.refs_1_.refs_2_, f32[64,1664]{1,0:T(8,128)S(1)} %collective-permute-done.refs_1_.refs_2_, bf16[12,256,512]{2,1,0:T(8,128)(2,1)S(1)} %get-tuple-element.37.refs_3_.refs_6_.refs_4_, ...), custom_call_target="tpu_custom_call" | custom-call | flops 2013265920 | bytes 1572864 | tf_op jit(solution)/shard_map/pairs/pallas_call | solution.py:153
  44.1 1.3 collective-permute-start.9
  45.4 2.9 %pairs.13 = f32[512,128]{1,0:T(8,128)S(1)} custom-call(s32[3]{0:T(128)S(1)} %pad_add_fusion.refs_0_, f32[64,1664]{1,0:T(8,128)S(1)} %collective-permute-done.refs_1_.refs_2_, f32[64,1664]{1,0:T(8,128)S(1)} %collective-permute-done.refs_1_.refs_2_, bf16[12,256,512]{2,1,0:T(8,128)(2,1)S(1)} %get-tuple-element.37.refs_3_.refs_6_.refs_4_, ...), custom_call_target="tpu_custom_call" | custom-call | flops 2013265920 | bytes 1572864 | tf_op jit(solution)/shard_map/pairs/pallas_call | solution.py:153
  48.3 1.3 collective-permute-start.10
  49.6 2.9 %pairs.14 = f32[512,128]{1,0:T(8,128)S(1)} custom-call(s32[3]{0:T(128)S(1)} %pad_add_fusion.refs_0_, f32[64,1664]{1,0:T(8,128)S(1)} %collective-permute-done.refs_1_.refs_2_, f32[64,1664]{1,0:T(8,128)S(1)} %collective-permute-done.refs_1_.refs_2_, bf16[12,256,512]{2,1,0:T(8,128)(2,1)S(1)} %get-tuple-element.37.refs_3_.refs_6_.refs_4_, ...), custom_call_target="tpu_custom_call" | custom-call | flops 2013265920 | bytes 1572864 | tf_op jit(solution)/shard_map/pairs/pallas_call | solution.py:153
  52.5 1.3 collective-permute-start.12
  53.8 0.5 collective-permute-done.9.refs_5_
  54.3 2.9 %pairs.15 = f32[512,128]{1,0:T(8,128)S(1)} custom-call(s32[3]{0:T(128)S(1)} %pad_add_fusion.refs_0_, f32[64,1664]{1,0:T(8,128)S(1)} %collective-permute-done.6.refs_1_.refs_3_, f32[64,1664]{1,0:T(8,128)S(1)} %collective-permute-done.8.refs_2_.refs_4_, f32[64,1664]{1,0:T(8,128)S(1)} %collective-permute-done.6.refs_1_.refs_3_, ...), custom_call_target="tpu_custom_call" | custom-call | flops 2013265920 | bytes 1572864 | tf_op jit(solution)/shard_map/pairs/pallas_call | solution.py:153
  57.2 1.9 %collective-permute-start.11 = (f32[512,128]{1,0:T(8,128)S(1)}, f32[512,128]{1,0:T(8,128)S(1)}, u32[]{:S(2)}, u32[]{:S(2)}) collective-permute-start(f32[512,128]{1,0:T(8,128)S(1)} %pairs.15), channel_id=1, source_target_pairs={{0,2},{1,3},{6,4},{7,5},{2,6},{3,7},{4,0},{5,1},{8,10},{9,11},{14,... | collective-permute-start | bytes 786440 | tf_op jit(solution)/shard_map/ppermute | solution.py:340
  59.1 2.9 %pairs.16 = f32[512,128]{1,0:T(8,128)S(1)} custom-call(s32[3]{0:T(128)S(1)} %pad_add_fusion.refs_0_, f32[64,1664]{1,0:T(8,128)S(1)} %collective-permute-done.5.refs_1_.refs_2_, f32[64,1664]{1,0:T(8,128)S(1)} %collective-permute-done.5.refs_1_.refs_2_, bf16[12,256,512]{2,1,0:T(8,128)(2,1)S(1)} %get-tuple-element.37.refs_3_.refs_6_.refs_4_, ...), custom_call_target="tpu_custom_call" | custom-call | flops 2013265920 | bytes 1572864 | tf_op jit(solution)/shard_map/pairs/pallas_call | solution.py:153
  62.0 2.9 %pairs.17 = f32[512,128]{1,0:T(8,128)S(1)} custom-call(s32[3]{0:T(128)S(1)} %pad_add_fusion.refs_0_, f32[64,1664]{1,0:T(8,128)S(1)} %collective-permute-done.6.refs_1_.refs_3_, f32[64,1664]{1,0:T(8,128)S(1)} %collective-permute-done.8.refs_2_.refs_4_, f32[64,1664]{1,0:T(8,128)S(1)} %collective-permute-done.6.refs_1_.refs_3_, ...), custom_call_target="tpu_custom_call" | custom-call | flops 2013265920 | bytes 1572864 | tf_op jit(solution)/shard_map/pairs/pallas_call | solution.py:153
  64.9 0.4 collective-permute-start.13
  65.4 1.6 %collective-permute-start.16 = (f32[512,128]{1,0:T(8,128)S(1)}, f32[512,128]{1,0:T(8,128)S(1)}, u32[]{:S(2)}, u32[]{:S(2)}) collective-permute-start(f32[512,128]{1,0:T(8,128)S(1)} %pairs.16), channel_id=1, source_target_pairs={{0,2},{1,3},{2,0},{3,1},{4,6},{5,7},{6,4},{7,5},{8,10},{9,11},{10,... | collective-permute-start | bytes 786440 | tf_op jit(solution)/shard_map/ppermute | solution.py:340
  67.0 4.1 %collective-permute-done.11.refs_3_ = f32[512,128]{1,0:T(8,128)S(1)} collective-permute-done((f32[512,128]{1,0:T(8,128)S(1)}, f32[512,128]{1,0:T(8,128)S(1)}, u32[]{:S(2)}, u32[]{:S(2)}) %collective-permute-start.11) | collective-permute-done | bytes 262176 | tf_op jit(solution)/shard_map/ppermute | solution.py:340
  71.2 2.9 %pairs.18 = f32[512,128]{1,0:T(8,128)S(1)} custom-call(s32[3]{0:T(128)S(1)} %pad_add_fusion.refs_0_, f32[64,1664]{1,0:T(8,128)S(1)} %collective-permute-done.7.refs_1_.refs_2_, f32[64,1664]{1,0:T(8,128)S(1)} %collective-permute-done.7.refs_1_.refs_2_, f32[512,128]{1,0:T(8,128)S(1)} %collective-permute-done.11.refs_3_, ...), custom_call_target="tpu_custom_call" | custom-call | flops 2013265920 | bytes 1572864 | tf_op jit(solution)/shard_map/pairs/pallas_call | solution.py:153
  74.0 2.9 %pairs.19 = f32[512,128]{1,0:T(8,128)S(1)} custom-call(s32[3]{0:T(128)S(1)} %pad_add_fusion.refs_0_, f32[64,1664]{1,0:T(8,128)S(1)} %collective-permute-done.5.refs_1_.refs_2_, f32[64,1664]{1,0:T(8,128)S(1)} %collective-permute-done.5.refs_1_.refs_2_, bf16[12,256,512]{2,1,0:T(8,128)(2,1)S(1)} %get-tuple-element.37.refs_3_.refs_6_.refs_4_, ...), custom_call_target="tpu_custom_call" | custom-call | flops 2013265920 | bytes 1572864 | tf_op jit(solution)/shard_map/pairs/pallas_call | solution.py:153
  76.9 0.1 collective-permute-start.15
  77.0 2.5 %collective-permute-start.17 = (f32[512,128]{1,0:T(8,128)S(1)}, f32[512,128]{1,0:T(8,128)S(1)}, u32[]{:S(2)}, u32[]{:S(2)}) collective-permute-start(f32[512,128]{1,0:T(8,128)S(1)} %pairs.18), channel_id=1, source_target_pairs={{2,4},{3,5},{4,2},{5,3},{0,0},{1,1},{6,6},{7,7},{10,12},{11,13},{1... | collective-permute-start | bytes 786440 | tf_op jit(solution)/shard_map/ppermute | solution.py:340
  79.5 2.9 %pairs.20 = f32[512,128]{1,0:T(8,128)S(1)} custom-call(s32[3]{0:T(128)S(1)} %pad_add_fusion.refs_0_, f32[64,1664]{1,0:T(8,128)S(1)} %collective-permute-done.6.refs_1_.refs_3_, f32[64,1664]{1,0:T(8,128)S(1)} %collective-permute-done.8.refs_2_.refs_4_, f32[64,1664]{1,0:T(8,128)S(1)} %collective-permute-done.6.refs_1_.refs_3_, ...), custom_call_target="tpu_custom_call" | custom-call | flops 2013265920 | bytes 1572864 | tf_op jit(solution)/shard_map/pairs/pallas_call | solution.py:153
  82.4 0.5 collective-permute-start.19
  82.9 2.9 %pairs.21 = f32[512,128]{1,0:T(8,128)S(1)} custom-call(s32[3]{0:T(128)S(1)} %pad_add_fusion.refs_0_, f32[64,1664]{1,0:T(8,128)S(1)} %collective-permute-done.7.refs_1_.refs_2_, f32[64,1664]{1,0:T(8,128)S(1)} %collective-permute-done.7.refs_1_.refs_2_, f32[512,128]{1,0:T(8,128)S(1)} %collective-permute-done.13.refs_3_, ...), custom_call_target="tpu_custom_call" | custom-call | flops 2013265920 | bytes 1572864 | tf_op jit(solution)/shard_map/pairs/pallas_call | solution.py:153
  85.8 2.9 %pairs.22 = f32[512,128]{1,0:T(8,128)S(1)} custom-call(s32[3]{0:T(128)S(1)} %pad_add_fusion.refs_0_, f32[64,1664]{1,0:T(8,128)S(1)} %collective-permute-done.5.refs_1_.refs_2_, f32[64,1664]{1,0:T(8,128)S(1)} %collective-permute-done.5.refs_1_.refs_2_, bf16[12,256,512]{2,1,0:T(8,128)(2,1)S(1)} %get-tuple-element.37.refs_3_.refs_6_.refs_4_, ...), custom_call_target="tpu_custom_call" | custom-call | flops 2013265920 | bytes 1572864 | tf_op jit(solution)/shard_map/pairs/pallas_call | solution.py:153
  88.6 1.9 %collective-permute-start.14 = (f32[512,128]{1,0:T(8,128)S(1)}, f32[512,128]{1,0:T(8,128)S(1)}, u32[]{:S(2)}, u32[]{:S(2)}) collective-permute-start(f32[512,128]{1,0:T(8,128)S(1)} %pairs.22), channel_id=1, source_target_pairs={{0,2},{1,3},{2,0},{3,1},{4,6},{5,7},{6,4},{7,5},{8,10},{9,11},{10,... | collective-permute-start | bytes 786440 | tf_op jit(solution)/shard_map/ppermute | solution.py:340
  90.5 3.1 %collective-permute-done.19.refs_3_ = f32[512,128]{1,0:T(8,128)S(1)} collective-permute-done((f32[512,128]{1,0:T(8,128)S(1)}, f32[512,128]{1,0:T(8,128)S(1)}, u32[]{:S(2)}, u32[]{:S(2)}) %collective-permute-start.19) | collective-permute-done | bytes 262176 | tf_op jit(solution)/shard_map/ppermute | solution.py:340
  93.6 2.5 %collective-permute-start.18 = (f32[512,128]{1,0:T(8,128)S(1)}, f32[512,128]{1,0:T(8,128)S(1)}, u32[]{:S(2)}, u32[]{:S(2)}) collective-permute-start(f32[512,128]{1,0:T(8,128)S(1)} %pairs.21), channel_id=1, source_target_pairs={{2,4},{3,5},{4,2},{5,3},{0,0},{1,1},{6,6},{7,7},{10,12},{11,13},{1... | collective-permute-start | bytes 786440 | tf_op jit(solution)/shard_map/ppermute | solution.py:340
  96.1 2.9 %pairs.23 = f32[512,128]{1,0:T(8,128)S(1)} custom-call(s32[3]{0:T(128)S(1)} %pad_add_fusion.refs_0_, f32[64,1664]{1,0:T(8,128)S(1)} %collective-permute-done.7.refs_1_.refs_2_, f32[64,1664]{1,0:T(8,128)S(1)} %collective-permute-done.7.refs_1_.refs_2_, f32[512,128]{1,0:T(8,128)S(1)} %collective-permute-done.19.refs_3_, ...), custom_call_target="tpu_custom_call" | custom-call | flops 2013265920 | bytes 1572864 | tf_op jit(solution)/shard_map/pairs/pallas_call | solution.py:153
  99.0 3.4 %collective-permute-start.20 = (f32[512,128]{1,0:T(8,128)S(1)}, f32[512,128]{1,0:T(8,128)S(1)}, u32[]{:S(2)}, u32[]{:S(2)}) collective-permute-start(f32[512,128]{1,0:T(8,128)S(1)} %pairs.23), channel_id=1, source_target_pairs={{2,4},{3,5},{4,2},{5,3},{0,0},{1,1},{6,6},{7,7},{10,12},{11,13},{1... | collective-permute-start | bytes 786440 | tf_op jit(solution)/shard_map/ppermute | solution.py:340
  102.4 0.9 collective-permute-done.18
  103.4 0.6 collective-permute-start.24
  103.9 1.5 %collective-permute-start.27 = (f32[512,128]{1,0:T(8,128)S(1)}, f32[512,128]{1,0:T(8,128)S(1)}, u32[]{:S(2)}, u32[]{:S(2)}) collective-permute-start(f32[512,128]{1,0:T(8,128)S(1)} %multiply_add_fusion.2.refs_1_), channel_id=1, source_target_pairs={{0,8},{8,0},{16,24},{24,16},{1,9},{9,1},{17,25},{25,17},{2,10},{10... | collective-permute-start | bytes 786440 | tf_op jit(solution)/shard_map/ppermute | solution.py:449
  105.4 0.5 collective-permute-start.28
  105.9 1.5 %collective-permute-start.29 = (f32[512,128]{1,0:T(8,128)S(1)}, f32[512,128]{1,0:T(8,128)S(1)}, u32[]{:S(2)}, u32[]{:S(2)}) collective-permute-start(f32[512,128]{1,0:T(8,128)S(1)} %multiply_add_fusion.2.refs_1_), channel_id=1, source_target_pairs={{0,24},{8,16},{16,8},{24,0},{1,25},{9,17},{17,9},{25,1},{2,26},{10... | collective-permute-start | bytes 786440 | tf_op jit(solution)/shard_map/ppermute | solution.py:449
  107.4 0.1 collective-permute-done.20
  107.5 0.5 collective-permute-start.25
  108.0 0.1 multiply_add_fusion.refs_1_
  108.0 4.5 %collective-permute-done.24.refs_2_ = f32[512,128]{1,0:T(8,128)S(1)} collective-permute-done((f32[512,128]{1,0:T(8,128)S(1)}, f32[512,128]{1,0:T(8,128)S(1)}, u32[]{:S(2)}, u32[]{:S(2)}) %collective-permute-start.24) | collective-permute-done | bytes 262176 | tf_op jit(solution)/shard_map/ppermute | solution.py:449
  112.6 0.5 collective-permute-start.26
  113.1 5.1 %collective-permute-done.27.refs_2_ = f32[512,128]{1,0:T(8,128)S(1)} collective-permute-done((f32[512,128]{1,0:T(8,128)S(1)}, f32[512,128]{1,0:T(8,128)S(1)}, u32[]{:S(2)}, u32[]{:S(2)}) %collective-permute-start.27) | collective-permute-done | bytes 262176 | tf_op jit(solution)/shard_map/ppermute | solution.py:449
  118.2 0.5 collective-permute-start.21
  118.7 2.4 %collective-permute-done.28.refs_3_ = f32[512,128]{1,0:T(8,128)S(1)} collective-permute-done((f32[512,128]{1,0:T(8,128)S(1)}, f32[512,128]{1,0:T(8,128)S(1)}, u32[]{:S(2)}, u32[]{:S(2)}) %collective-permute-start.28) | collective-permute-done | bytes 262176 | tf_op jit(solution)/shard_map/ppermute | solution.py:449
  121.1 0.5 collective-permute-start.22
  121.7 2.1 %collective-permute-done.29.refs_4_ = f32[512,128]{1,0:T(8,128)S(1)} collective-permute-done((f32[512,128]{1,0:T(8,128)S(1)}, f32[512,128]{1,0:T(8,128)S(1)}, u32[]{:S(2)}, u32[]{:S(2)}) %collective-permute-start.29) | collective-permute-done | bytes 262176 | tf_op jit(solution)/shard_map/ppermute | solution.py:449
  123.8 1.5 %collective-permute-start.23 = (f32[512,128]{1,0:T(8,128)S(1)}, f32[512,128]{1,0:T(8,128)S(1)}, u32[]{:S(2)}, u32[]{:S(2)}) collective-permute-start(f32[512,128]{1,0:T(8,128)S(1)} %multiply_add_fusion.refs_1_), channel_id=1, source_target_pairs={{0,24},{8,16},{16,8},{24,0},{1,25},{9,17},{17,9},{25,1},{2,26},{10... | collective-permute-start | bytes 786440 | tf_op jit(solution)/shard_map/ppermute | solution.py:449
  125.3 1.5 %spread.3.refs_5_ = f32[6144,128]{1,0:T(8,128)} custom-call(s32[4]{0:T(128)S(1)} %iota_xor_fusion.refs_0_, f32[512,128]{1,0:T(8,128)S(1)} %multiply_add_fusion.2.refs_1_, f32[512,128]{1,0:T(8,128)S(1)} %collective-permute-done.27.refs_2_, f32[512,128]{1,0:T(8,128)S(1)} %collective-permute-done.28.refs_3_, f32[512,128]{1,0:T(8,128)S(1)} %collective-permute-done.29.refs_4_), custom_call_target="tpu_custom_call" | custom-call | tf_op jit(solution)/shard_map/spread/pallas_call | solution.py:306
  126.8 8.9 %collective-permute-done.25.refs_3_ = f32[512,128]{1,0:T(8,128)S(1)} collective-permute-done((f32[512,128]{1,0:T(8,128)S(1)}, f32[512,128]{1,0:T(8,128)S(1)}, u32[]{:S(2)}, u32[]{:S(2)}) %collective-permute-start.25) | collective-permute-done | bytes 262176 | tf_op jit(solution)/shard_map/ppermute | solution.py:449
  135.7 1.5 %spread.4.refs_5_ = f32[6144,128]{1,0:T(8,128)} custom-call(s32[4]{0:T(128)S(1)} %iota_xor_fusion.refs_0_, f32[512,128]{1,0:T(8,128)S(1)} %multiply_add_fusion.1.refs_1_, f32[512,128]{1,0:T(8,128)S(1)} %collective-permute-done.24.refs_2_, f32[512,128]{1,0:T(8,128)S(1)} %collective-permute-done.25.refs_3_, ...), custom_call_target="tpu_custom_call", output_to_operand_aliasing={{}: (5, {})} | custom-call | tf_op jit(solution)/shard_map/spread/pallas_call | solution.py:306
  137.3 1.2 collective-permute-done.22.refs_3_
  138.5 1.5 %spread.5 = f32[6144,128]{1,0:T(8,128)} custom-call(s32[4]{0:T(128)S(1)} %iota_xor_fusion.refs_0_, f32[512,128]{1,0:T(8,128)S(1)} %multiply_add_fusion.refs_1_, f32[512,128]{1,0:T(8,128)S(1)} %collective-permute-done.21.refs_2_, f32[512,128]{1,0:T(8,128)S(1)} %collective-permute-done.22.refs_3_, ...), custom_call_target="tpu_custom_call", output_to_operand_aliasing={{}: (5, {})} | custom-call | tf_op jit(solution)/shard_map/spread/pallas_call | solution.py:306
  (24 shorter events, 0.2 us)
Async XLA Ops:
  0.0 37.3 %collective-permute-start.2 = (f32[6144,128]{1,0:T(8,128)}, f32[6144,128]{1,0:T(8,128)}, u32[]{:S(2)}, u32[]{:S(2)}) collective-permute-start(f32[6144,128]{1,0:T(8,128)} %weights_ref.1), channel_id=1, source_target_pairs={{0,1},{1,0},{2,3},{3,2},{4,5},{5,4},{6,7},{7,6},{8,9},{9,8},{10,11... | collective-permute-start | bytes 9437192 | tf_op jit(solution)/shard_map/ppermute | solution.py:381
  0.0 37.3 %collective-permute-start.1 = (f32[64,6144]{1,0:T(8,128)}, f32[64,6144]{1,0:T(8,128)S(1)}, u32[]{:S(2)}, u32[]{:S(2)}) collective-permute-start(f32[64,6144]{1,0:T(8,128)} %points_ref.1), channel_id=1, source_target_pairs={{0,1},{1,0},{2,3},{3,2},{4,5},{5,4},{6,7},{7,6},{8,9},{9,8},{10,11... | collective-permute-start | bytes 4718600 | tf_op jit(solution)/shard_map/ppermute | solution.py:381
  10.7 3.5 %collective-permute-start.3 = (f32[64,256]{1,0:T(8,128)}, f32[64,256]{1,0:T(8,128)S(1)}, u32[]{:S(2)}, u32[]{:S(2)}) collective-permute-start(f32[64,256]{1,0:T(8,128)} %get-tuple-element.41), channel_id=1, source_target_pairs={{0,1},{1,0},{2,3},{3,2},{4,5},{5,4},{6,7},{7,6},{8,9},{9,8},{10,11... | collective-permute-start | bytes 196616 | tf_op jit(solution)/shard_map/ppermute | solution.py:381
  10.7 12.7 %collective-permute-start.5 = (f32[64,1664]{1,0:T(8,128)S(1)}, f32[64,1664]{1,0:T(8,128)S(1)}, u32[]{:S(2)}, u32[]{:S(2)}) collective-permute-start(f32[64,1664]{1,0:T(8,128)S(1)} %select_maximum_fusion), channel_id=1, source_target_pairs={{0,2},{1,3},{2,0},{3,1},{4,6},{5,7},{6,4},{7,5},{8,10},{9,11},{10,... | collective-permute-start | bytes 1277960 | tf_op jit(solution)/shard_map/ppermute | solution.py:340
  12.3 23.7 %collective-permute-start.7 = (f32[64,1664]{1,0:T(8,128)S(1)}, f32[64,1664]{1,0:T(8,128)S(1)}, u32[]{:S(2)}, u32[]{:S(2)}) collective-permute-start(f32[64,1664]{1,0:T(8,128)S(1)} %select_maximum_fusion), channel_id=1, source_target_pairs={{2,4},{3,5},{4,2},{5,3},{0,0},{1,1},{6,6},{7,7},{10,12},{11,13},{1... | collective-permute-start | bytes 1277960 | tf_op jit(solution)/shard_map/ppermute | solution.py:340
  14.2 1.6 %collective-permute-start.4 = (f32[256,128]{1,0:T(8,128)}, f32[256,128]{1,0:T(8,128)S(1)}, u32[]{:S(2)}, u32[]{:S(2)}) collective-permute-start(f32[256,128]{1,0:T(8,128)} %get-tuple-element.42), channel_id=1, source_target_pairs={{0,1},{1,0},{2,3},{3,2},{4,5},{5,4},{6,7},{7,6},{8,9},{9,8},{10,11... | collective-permute-start | bytes 393224 | tf_op jit(solution)/shard_map/ppermute | solution.py:381
  15.8 25.4 %collective-permute-start = (f32[64,1664]{1,0:T(8,128)S(1)}, f32[64,1664]{1,0:T(8,128)S(1)}, u32[]{:S(2)}, u32[]{:S(2)}) collective-permute-start(f32[64,1664]{1,0:T(8,128)S(1)} %select_maximum_fusion), channel_id=1, source_target_pairs={{0,6},{1,7},{6,0},{7,1},{2,2},{3,3},{4,4},{5,5},{8,14},{9,15},{14,... | collective-permute-start | bytes 1277960 | tf_op jit(solution)/shard_map/ppermute | solution.py:340
  23.4 30.4 %collective-permute-start.6 = (f32[64,1664]{1,0:T(8,128)S(1)}, f32[64,1664]{1,0:T(8,128)S(1)}, u32[]{:S(2)}, u32[]{:S(2)}) collective-permute-start(f32[64,1664]{1,0:T(8,128)S(1)} %collective-permute-done.5.refs_1_.refs_2_), channel_id=1, source_target_pairs={{2,4},{3,5},{4,2},{5,3},{10,12},{11,13},{12,10},{13,11},{18,20},{1... | collective-permute-start | bytes 1277960 | tf_op jit(solution)/shard_map/ppermute | solution.py:340
  36.0 17.8 %collective-permute-start.8 = (f32[64,1664]{1,0:T(8,128)S(1)}, f32[64,1664]{1,0:T(8,128)S(1)}, u32[]{:S(2)}, u32[]{:S(2)}) collective-permute-start(f32[64,1664]{1,0:T(8,128)S(1)} %collective-permute-done.7.refs_1_.refs_2_), channel_id=1, source_target_pairs={{2,0},{3,1},{4,6},{5,7},{10,8},{11,9},{12,14},{13,15},{18,16},{19,... | collective-permute-start | bytes 1277960 | tf_op jit(solution)/shard_map/ppermute | solution.py:340
  44.1 10.2 %collective-permute-start.9 = (f32[512,128]{1,0:T(8,128)S(1)}, f32[512,128]{1,0:T(8,128)S(1)}, u32[]{:S(2)}, u32[]{:S(2)}) collective-permute-start(f32[512,128]{1,0:T(8,128)S(1)} %pairs.12), channel_id=1, source_target_pairs={{0,2},{1,3},{6,4},{7,5},{8,10},{9,11},{14,12},{15,13},{16,18},{17,... | collective-permute-start | bytes 786440 | tf_op jit(solution)/shard_map/ppermute | solution.py:340
  48.3 13.7 %collective-permute-start.10 = (f32[512,128]{1,0:T(8,128)S(1)}, f32[512,128]{1,0:T(8,128)S(1)}, u32[]{:S(2)}, u32[]{:S(2)}) collective-permute-start(f32[512,128]{1,0:T(8,128)S(1)} %pairs.13), channel_id=1, source_target_pairs={{0,2},{1,3},{6,4},{7,5},{8,10},{9,11},{14,12},{15,13},{16,18},{17,... | collective-permute-start | bytes 786440 | tf_op jit(solution)/shard_map/ppermute | solution.py:340
  52.5 27.0 %collective-permute-start.12 = (f32[512,128]{1,0:T(8,128)S(1)}, f32[512,128]{1,0:T(8,128)S(1)}, u32[]{:S(2)}, u32[]{:S(2)}) collective-permute-start(f32[512,128]{1,0:T(8,128)S(1)} %pairs.14), channel_id=1, source_target_pairs={{0,2},{1,3},{6,4},{7,5},{8,10},{9,11},{14,12},{15,13},{16,18},{17,... | collective-permute-start | bytes 786440 | tf_op jit(solution)/shard_map/ppermute | solution.py:340
  57.2 13.9 %collective-permute-start.11 = (f32[512,128]{1,0:T(8,128)S(1)}, f32[512,128]{1,0:T(8,128)S(1)}, u32[]{:S(2)}, u32[]{:S(2)}) collective-permute-start(f32[512,128]{1,0:T(8,128)S(1)} %pairs.15), channel_id=1, source_target_pairs={{0,2},{1,3},{6,4},{7,5},{2,6},{3,7},{4,0},{5,1},{8,10},{9,11},{14,... | collective-permute-start | bytes 786440 | tf_op jit(solution)/shard_map/ppermute | solution.py:340
  64.9 18.0 %collective-permute-start.13 = (f32[512,128]{1,0:T(8,128)S(1)}, f32[512,128]{1,0:T(8,128)S(1)}, u32[]{:S(2)}, u32[]{:S(2)}) collective-permute-start(f32[512,128]{1,0:T(8,128)S(1)} %pairs.17), channel_id=1, source_target_pairs={{0,2},{1,3},{6,4},{7,5},{2,6},{3,7},{4,0},{5,1},{8,10},{9,11},{14,... | collective-permute-start | bytes 786440 | tf_op jit(solution)/shard_map/ppermute | solution.py:340
  65.4 33.6 %collective-permute-start.16 = (f32[512,128]{1,0:T(8,128)S(1)}, f32[512,128]{1,0:T(8,128)S(1)}, u32[]{:S(2)}, u32[]{:S(2)}) collective-permute-start(f32[512,128]{1,0:T(8,128)S(1)} %pairs.16), channel_id=1, source_target_pairs={{0,2},{1,3},{2,0},{3,1},{4,6},{5,7},{6,4},{7,5},{8,10},{9,11},{10,... | collective-permute-start | bytes 786440 | tf_op jit(solution)/shard_map/ppermute | solution.py:340
  76.9 25.5 %collective-permute-start.15 = (f32[512,128]{1,0:T(8,128)S(1)}, f32[512,128]{1,0:T(8,128)S(1)}, u32[]{:S(2)}, u32[]{:S(2)}) collective-permute-start(f32[512,128]{1,0:T(8,128)S(1)} %pairs.19), channel_id=1, source_target_pairs={{0,2},{1,3},{2,0},{3,1},{4,6},{5,7},{6,4},{7,5},{8,10},{9,11},{10,... | collective-permute-start | bytes 786440 | tf_op jit(solution)/shard_map/ppermute | solution.py:340
  77.0 25.4 %collective-permute-start.17 = (f32[512,128]{1,0:T(8,128)S(1)}, f32[512,128]{1,0:T(8,128)S(1)}, u32[]{:S(2)}, u32[]{:S(2)}) collective-permute-start(f32[512,128]{1,0:T(8,128)S(1)} %pairs.18), channel_id=1, source_target_pairs={{2,4},{3,5},{4,2},{5,3},{0,0},{1,1},{6,6},{7,7},{10,12},{11,13},{1... | collective-permute-start | bytes 786440 | tf_op jit(solution)/shard_map/ppermute | solution.py:340
  82.4 11.2 %collective-permute-start.19 = (f32[512,128]{1,0:T(8,128)S(1)}, f32[512,128]{1,0:T(8,128)S(1)}, u32[]{:S(2)}, u32[]{:S(2)}) collective-permute-start(f32[512,128]{1,0:T(8,128)S(1)} %pairs.20), channel_id=1, source_target_pairs={{0,2},{1,3},{6,4},{7,5},{2,6},{3,7},{4,0},{5,1},{8,10},{9,11},{14,... | collective-permute-start | bytes 786440 | tf_op jit(solution)/shard_map/ppermute | solution.py:340
  88.6 17.3 %collective-permute-start.14 = (f32[512,128]{1,0:T(8,128)S(1)}, f32[512,128]{1,0:T(8,128)S(1)}, u32[]{:S(2)}, u32[]{:S(2)}) collective-permute-start(f32[512,128]{1,0:T(8,128)S(1)} %pairs.22), channel_id=1, source_target_pairs={{0,2},{1,3},{2,0},{3,1},{4,6},{5,7},{6,4},{7,5},{8,10},{9,11},{10,... | collective-permute-start | bytes 786440 | tf_op jit(solution)/shard_map/ppermute | solution.py:340
  93.6 9.7 %collective-permute-start.18 = (f32[512,128]{1,0:T(8,128)S(1)}, f32[512,128]{1,0:T(8,128)S(1)}, u32[]{:S(2)}, u32[]{:S(2)}) collective-permute-start(f32[512,128]{1,0:T(8,128)S(1)} %pairs.21), channel_id=1, source_target_pairs={{2,4},{3,5},{4,2},{5,3},{0,0},{1,1},{6,6},{7,7},{10,12},{11,13},{1... | collective-permute-start | bytes 786440 | tf_op jit(solution)/shard_map/ppermute | solution.py:340
  99.0 8.5 %collective-permute-start.20 = (f32[512,128]{1,0:T(8,128)S(1)}, f32[512,128]{1,0:T(8,128)S(1)}, u32[]{:S(2)}, u32[]{:S(2)}) collective-permute-start(f32[512,128]{1,0:T(8,128)S(1)} %pairs.23), channel_id=1, source_target_pairs={{2,4},{3,5},{4,2},{5,3},{0,0},{1,1},{6,6},{7,7},{10,12},{11,13},{1... | collective-permute-start | bytes 786440 | tf_op jit(solution)/shard_map/ppermute | solution.py:340
  103.4 9.2 %collective-permute-start.24 = (f32[512,128]{1,0:T(8,128)S(1)}, f32[512,128]{1,0:T(8,128)S(1)}, u32[]{:S(2)}, u32[]{:S(2)}) collective-permute-start(f32[512,128]{1,0:T(8,128)S(1)} %multiply_add_fusion.1.refs_1_), channel_id=1, source_target_pairs={{0,8},{8,0},{16,24},{24,16},{1,9},{9,1},{17,25},{25,17},{2,10},{10... | collective-permute-start | bytes 786440 | tf_op jit(solution)/shard_map/ppermute | solution.py:449
  103.9 14.3 %collective-permute-start.27 = (f32[512,128]{1,0:T(8,128)S(1)}, f32[512,128]{1,0:T(8,128)S(1)}, u32[]{:S(2)}, u32[]{:S(2)}) collective-permute-start(f32[512,128]{1,0:T(8,128)S(1)} %multiply_add_fusion.2.refs_1_), channel_id=1, source_target_pairs={{0,8},{8,0},{16,24},{24,16},{1,9},{9,1},{17,25},{25,17},{2,10},{10... | collective-permute-start | bytes 786440 | tf_op jit(solution)/shard_map/ppermute | solution.py:449
  105.4 15.7 %collective-permute-start.28 = (f32[512,128]{1,0:T(8,128)S(1)}, f32[512,128]{1,0:T(8,128)S(1)}, u32[]{:S(2)}, u32[]{:S(2)}) collective-permute-start(f32[512,128]{1,0:T(8,128)S(1)} %multiply_add_fusion.2.refs_1_), channel_id=1, source_target_pairs={{0,16},{8,24},{16,0},{24,8},{1,17},{9,25},{17,1},{25,9},{2,18},{10... | collective-permute-start | bytes 786440 | tf_op jit(solution)/shard_map/ppermute | solution.py:449
  105.9 17.8 %collective-permute-start.29 = (f32[512,128]{1,0:T(8,128)S(1)}, f32[512,128]{1,0:T(8,128)S(1)}, u32[]{:S(2)}, u32[]{:S(2)}) collective-permute-start(f32[512,128]{1,0:T(8,128)S(1)} %multiply_add_fusion.2.refs_1_), channel_id=1, source_target_pairs={{0,24},{8,16},{16,8},{24,0},{1,25},{9,17},{17,9},{25,1},{2,26},{10... | collective-permute-start | bytes 786440 | tf_op jit(solution)/shard_map/ppermute | solution.py:449
  107.5 28.2 %collective-permute-start.25 = (f32[512,128]{1,0:T(8,128)S(1)}, f32[512,128]{1,0:T(8,128)S(1)}, u32[]{:S(2)}, u32[]{:S(2)}) collective-permute-start(f32[512,128]{1,0:T(8,128)S(1)} %multiply_add_fusion.1.refs_1_), channel_id=1, source_target_pairs={{0,16},{8,24},{16,0},{24,8},{1,17},{9,25},{17,1},{25,9},{2,18},{10... | collective-permute-start | bytes 786440 | tf_op jit(solution)/shard_map/ppermute | solution.py:449
  112.6 23.1 %collective-permute-start.26 = (f32[512,128]{1,0:T(8,128)S(1)}, f32[512,128]{1,0:T(8,128)S(1)}, u32[]{:S(2)}, u32[]{:S(2)}) collective-permute-start(f32[512,128]{1,0:T(8,128)S(1)} %multiply_add_fusion.1.refs_1_), channel_id=1, source_target_pairs={{0,24},{8,16},{16,8},{24,0},{1,25},{9,17},{17,9},{25,1},{2,26},{10... | collective-permute-start | bytes 786440 | tf_op jit(solution)/shard_map/ppermute | solution.py:449
  118.2 19.1 %collective-permute-start.21 = (f32[512,128]{1,0:T(8,128)S(1)}, f32[512,128]{1,0:T(8,128)S(1)}, u32[]{:S(2)}, u32[]{:S(2)}) collective-permute-start(f32[512,128]{1,0:T(8,128)S(1)} %multiply_add_fusion.refs_1_), channel_id=1, source_target_pairs={{0,8},{8,0},{16,24},{24,16},{1,9},{9,1},{17,25},{25,17},{2,10},{10... | collective-permute-start | bytes 786440 | tf_op jit(solution)/shard_map/ppermute | solution.py:449
  121.1 17.4 %collective-permute-start.22 = (f32[512,128]{1,0:T(8,128)S(1)}, f32[512,128]{1,0:T(8,128)S(1)}, u32[]{:S(2)}, u32[]{:S(2)}) collective-permute-start(f32[512,128]{1,0:T(8,128)S(1)} %multiply_add_fusion.refs_1_), channel_id=1, source_target_pairs={{0,16},{8,24},{16,0},{24,8},{1,17},{9,25},{17,1},{25,9},{2,18},{10... | collective-permute-start | bytes 786440 | tf_op jit(solution)/shard_map/ppermute | solution.py:449
  123.8 14.8 %collective-permute-start.23 = (f32[512,128]{1,0:T(8,128)S(1)}, f32[512,128]{1,0:T(8,128)S(1)}, u32[]{:S(2)}, u32[]{:S(2)}) collective-permute-start(f32[512,128]{1,0:T(8,128)S(1)} %multiply_add_fusion.refs_1_), channel_id=1, source_target_pairs={{0,24},{8,16},{16,8},{24,0},{1,25},{9,17},{17,9},{25,1},{2,26},{10... | collective-permute-start | bytes 786440 | tf_op jit(solution)/shard_map/ppermute | solution.py:449
